TPU v7x, 32 devices: a whole 2x2x4 slice. The times are simulated.
32 devices in a mesh: role: 2 (over x), seq: 4 (over y, core), mp: 4 (over z).
Axes of the slice: x: 2, y: 2, z: 4, core: 2. Of those that a mesh axis runs over, the one named last changes fastest.
Arguments:
- rollout: bfloat16 [2, 1536, 64], P('role', 'seq'), may hold values from -6.5 to 6.5
- w_embed: bfloat16 [64, 5120], replicated, may hold values from -0.75 to 0.75
- w_qkv: bfloat16 [5120, 3, 2560], P('seq', None, 'mp'), may hold values from -0.5 to 0.5
- w_out: bfloat16 [2560, 64], P('mp'), may hold values from -0.5 to 0.5
- momentum: float32 [2560, 2, 3, 2560], P('seq', 'role', None, 'mp'), may hold values from -3 to 3
- rewards: float32 [32], replicated, may hold values from 0 to 1
- group_ids: int32 [32], replicated, may hold values from 0 to 3
- timestep: int32 [1], replicated, may hold values from 10 to 40
Outputs:
- new_momentum: float32 [2560, 2, 3, 2560], P('seq', 'role', None, 'mp')
- new_w_qkv: bfloat16 [5120, 3, 2560], P('seq', None, 'mp')
All inputs are finite; a program needn't handle non-finite values.
Results may differ from a plain program's by a relative error of at most 0.0075.
Values may be sent and summed in bfloat16 or wider, within the bound.
No kernel may reach another device: no remote copies, remote signals or barrier semaphores. Data moves between devices by JAX's collectives and lax.ppermute only.
A program may use at most 128 MiB of HBM per device.

v0:
```python
import jax
import jax.numpy as jnp
from jax import lax
from jax.sharding import PartitionSpec as P

HD = 128
TILE = 192
STEPS = 50


SHIFT_FACTOR = 5.0
NOISE_LEVEL = 0.7
MOMENTUM_DECAY = 0.9
LEARNING_RATE = 0.004
LOSS_SCALE = 16384.0
REWARD_FLOOR = 0.1
MASKED = -1e30


def from_behind(block, axis, distance):
    devices = range(lax.axis_size(axis))
    route = [(i - distance, i) for i in devices if i - distance in devices]
    return lax.ppermute(block, axis, route)


def with_halo(cells, sides, width):
    for axis, dim in sides:
        count = lax.axis_size(axis)
        ends = count - 1
        head = lax.slice_in_dim(cells, 0, width, axis=dim)
        tail = lax.slice_in_dim(cells, cells.shape[dim] - width, cells.shape[dim], axis=dim)
        cells = jnp.concatenate(
            [
                lax.ppermute(tail, axis, [(i, (i + 1) % count) for i in range(ends)]),
                cells,
                lax.ppermute(head, axis, [((i + 1) % count, i) for i in range(ends)]),
            ],
            axis=dim,
        )
    return cells


def sigma_at(index, total_steps):
    fraction = index.astype(jnp.float32) / total_steps
    return SHIFT_FACTOR * fraction / (1.0 + (SHIFT_FACTOR - 1.0) * fraction)


def advantage_of(rewards, group_ids):
    members = (group_ids == group_ids[0]).astype(jnp.float32)
    member_total = jnp.sum(members)
    group_mean = jnp.sum(members * rewards) / member_total
    spread = jnp.sqrt(jnp.sum(members * (rewards - group_mean) ** 2) / member_total)
    return (rewards[0] - group_mean) / jnp.maximum(spread, REWARD_FLOOR)


def allowed_keys(seq_index, tok_dev, seq_count):
    tiles_dev = tok_dev // TILE
    query_tile = jnp.arange(tok_dev, dtype=jnp.int32) // TILE
    key_tile = jnp.arange(tok_dev + 2 * TILE, dtype=jnp.int32) // TILE
    in_band = (key_tile[None, :] >= query_tile[:, None]) & (
        key_tile[None, :] <= query_tile[:, None] + 2
    )
    global_tile = seq_index * tiles_dev - 1 + key_tile
    inside = (global_tile >= 0) & (global_tile < seq_count * tiles_dev)
    return in_band & inside[None, :]


def body(rollout, w_embed, w_qkv, w_out, momentum, rewards, group_ids, timestep):
    seq_count = lax.axis_size("seq")
    seq_index = lax.axis_index("seq")
    role_index = lax.axis_index("role")
    latent_next = rollout[0]
    latent_now = from_behind(rollout, "role", 1)[0]
    tok_dev = latent_now.shape[0]
    rows_dev = w_qkv.shape[0]
    width = w_qkv.shape[2]
    heads_dev = width // HD
    extent = tok_dev + 2 * TILE
    scale = HD ** (-0.5)
    embedded = jnp.dot(latent_now, w_embed, preferred_element_type=jnp.float32).astype(jnp.bfloat16)
    columns = embedded
    projected = jnp.einsum(
        "tr,rmc->tmc",
        columns,
        lax.all_gather(w_qkv, "seq", axis=0, tiled=True),
        preferred_element_type=jnp.float32,
    )
    projected = projected.astype(jnp.bfloat16)
    queries = projected[:, 0].reshape(tok_dev, heads_dev, HD)
    nearby = with_halo(projected[:, 1:3], (("seq", 0),), TILE)
    keys_near = nearby[:, 0].reshape(extent, heads_dev, HD)
    values_near = nearby[:, 1].reshape(extent, heads_dev, HD)
    allowed = allowed_keys(seq_index, tok_dev, seq_count)
    scores = (
        jnp.einsum("thd,ehd->hte", queries, keys_near, preferred_element_type=jnp.float32) * scale
    )
    scores = jnp.where(allowed[None], scores, MASKED)
    highest = jnp.max(scores, axis=2, keepdims=True)
    weights = jnp.exp(scores - highest)
    probs = weights / jnp.sum(weights, axis=2, keepdims=True)
    probs_low = probs.astype(jnp.bfloat16)
    attended = jnp.einsum(
        "hte,ehd->thd", probs_low, values_near, preferred_element_type=jnp.float32
    )
    attended = attended.astype(jnp.bfloat16).reshape(tok_dev, width)
    partial_pred = jnp.dot(attended, w_out, preferred_element_type=jnp.float32)
    prediction = lax.psum(partial_pred.astype(jnp.bfloat16), "mp").astype(jnp.float32)
    advantage = advantage_of(rewards, group_ids)
    sigma_now = sigma_at(timestep[0], STEPS)
    step_size = sigma_at(timestep[0] - 1, STEPS) - sigma_now
    tokens_all = tok_dev * seq_count
    coefficient = (
        advantage * LOSS_SCALE * (1.0 - sigma_now) / (NOISE_LEVEL**2 * sigma_now * tokens_all)
    )
    step_mean = latent_now.astype(jnp.float32) + step_size * prediction
    pred_grad = (coefficient * (latent_next.astype(jnp.float32) - step_mean)).astype(jnp.bfloat16)
    attended_grad = jnp.einsum("tc,kc->tk", pred_grad, w_out, preferred_element_type=jnp.float32)
    attended_grad = attended_grad.astype(jnp.bfloat16).reshape(tok_dev, heads_dev, HD)
    prob_grad = jnp.einsum(
        "thd,ehd->hte", attended_grad, values_near, preferred_element_type=jnp.float32
    )
    row_dot = jnp.sum(probs * prob_grad, axis=2, keepdims=True)
    score_grad = (probs * (prob_grad - row_dot) * scale).astype(jnp.bfloat16)
    query_grad = jnp.einsum(
        "hte,ehd->thd", score_grad, keys_near, preferred_element_type=jnp.float32
    ).reshape(tok_dev, width)
    key_grad = jnp.einsum(
        "hte,thd->ehd", score_grad, queries, preferred_element_type=jnp.float32
    ).reshape(extent, width)
    value_grad = jnp.einsum(
        "hte,thd->ehd", probs_low, attended_grad, preferred_element_type=jnp.float32
    ).reshape(extent, width)
    near_grads = jnp.stack([key_grad, value_grad], axis=1)
    rim_pair = jnp.concatenate([near_grads[:TILE], near_grads[extent - TILE :]], axis=0).astype(
        jnp.bfloat16
    )
    arrived = with_halo(rim_pair, (("seq", 0),), TILE)
    from_left = arrived[:TILE].astype(jnp.float32)
    from_right = arrived[3 * TILE :].astype(jnp.float32)
    owned = near_grads[TILE : TILE + tok_dev]
    owned = owned + jnp.pad(from_left, ((0, tok_dev - TILE), (0, 0), (0, 0)))
    owned = owned + jnp.pad(from_right, ((tok_dev - TILE, 0), (0, 0), (0, 0)))
    qkv_grad = jnp.concatenate([query_grad[:, None], owned], axis=1).astype(jnp.bfloat16)
    pair_rows = rows_dev // 2
    columns = embedded
    block_grad = (
        lax.psum_scatter(
            jnp.einsum("tr,tmc->rmc", columns, qkv_grad, preferred_element_type=jnp.float32).astype(
                jnp.bfloat16
            ),
            "seq",
            scatter_dimension=0,
            tiled=True,
        )
        .astype(jnp.float32)
        .reshape(pair_rows, 2, 3, width)
    )
    sent_half = from_behind(block_grad[:, 0:1].astype(jnp.bfloat16), "role", -1).astype(jnp.float32)
    own_grad = jnp.where(role_index == 0, sent_half, block_grad[:, 1:2])
    new_momentum = MOMENTUM_DECAY * momentum + own_grad
    own_weights = lax.dynamic_slice_in_dim(w_qkv.reshape(pair_rows, 2, 3, width), role_index, 1, 1)
    new_half = (own_weights.astype(jnp.float32) - LEARNING_RATE * new_momentum).astype(jnp.bfloat16)
    new_w_qkv = lax.all_gather(new_half, "role", axis=1, tiled=True).reshape(rows_dev, 3, width)
    return (new_momentum, new_w_qkv)


def solution(mesh):
    in_specs = (
        P("role", "seq", None),
        P(),
        P("seq", None, "mp"),
        P("mp", None),
        P("seq", "role", None, "mp"),
        P(),
        P(),
        P(),
    )
    out_specs = (P("seq", "role", None, "mp"), P("seq", None, "mp"))
    return jax.shard_map(body, mesh=mesh, in_specs=in_specs, out_specs=out_specs, check_vma=False)
```

profile of v0, /device:TPU:0, one launch (start us, length us, event | category | flops | bytes accessed | tf_op | source)
XLA Modules:
  0.0 593.6 jit_solution(4470652563330857601)
XLA Ops:
  7.2 0.0 copy-start
  7.2 0.0 all-gather.3.cloned.1.call-start
  7.3 0.7 all-gather.3.cloned.1.call-update
  7.9 0.0 reduce-scatter.2.cloned.1.call-start
  8.0 0.1 copy-done.6
  8.0 4.8 collective-permute-start
  12.9 0.6 convert_reduce_fusion
  14.9 0.6 select_reduce_fusion
  15.5 0.0 collective-permute-done
  15.5 3.1 fusion.2
  18.7 117.0 %all-gather.3.cloned.1.call-done = bf16[5120,3,640]{2,0,1:T(8,128)(2,1)} async-done(((bf16[1280,3,640]{2,0,1:T(8,128)(2,1)}), bf16[5120,3,640]{2,0,1:T(8,128)(2,1)}) %all-gather.3.cloned.1.call-update) | async-done | bytes 19660816 | tf_op jit(solution)/shard_map/all_gather | solution.py:85
  135.6 13.0 %convolution_convert_fusion.2 = bf16[384,3,640]{2,0,1:T(8,128)(2,1)S(1)} fusion(bf16[384,5120,1]{1,0,2:T(8,128)(2,1)} %fusion.2, bf16[5120,3,640]{2,0,1:T(8,128)(2,1)} %all-gather.3.cloned.1.call-done), kind=kOutput, calls=%fused_computation.31 | convolution fusion | flops 7550484480 | bytes 25067520 | tf_op jit(solution)/shard_map/tr,rmc->tmc/dot_general | solution.py:82
  148.7 1.0 fusion.64
  149.7 3.0 collective-permute-start.1
  152.7 1.3 collective-permute-start.2
  156.2 0.3 and_and_fusion
  156.5 0.1 slice.64
  156.7 1.0 copy.95
  157.7 0.0 collective-permute-done.1
  157.7 0.0 collective-permute-done.2
  157.7 1.4 pad_maximum_fusion.1
  159.0 0.0 copy-start.3
  159.0 0.2 fusion.63
  159.2 1.3 copy.94
  160.6 0.6 copy.98
  161.2 6.0 %fusion.65 = (f32[5,384]{1,0:T(8,128)S(1)}, f32[5,384,768]{2,1,0:T(8,128)}) fusion(pred[384,768]{1,0:T(8,128)(4,1)S(1)} %and_and_fusion, bf16[384,5,128]{0,2,1:T(8,128)(2,1)S(1)} %bitcast.71, bf16[768,5,128]{0,2,1:T(8,128)(2,1)} %bitcast.68), kind=kOutput, calls=%fused_computation.85 | convolution fusion | flops 383386368 | bytes 7675392 | tf_op jit(solution)/shard_map/sub | solution.py:99
  167.2 3.8 fusion.31
  171.0 0.2 convolution_convert_fusion.4
  171.3 19.6 %psum.7 = bf16[384,64]{0,1:T(8,128)(2,1)S(1)} all-reduce(bf16[384,64]{0,1:T(8,128)(2,1)S(1)} %convolution_convert_fusion.4), channel_id=1, replica_groups=mesh['role'=2,'seq'=4,'mp'=4] {'mp'}, use_global_device_ids=true, to_apply=%region_5.6 | all-reduce | flops 24576 | bytes 98304 | tf_op jit(solution)/shard_map/psum | solution.py:107
  190.8 0.3 convolution_convert_fusion.3
  191.2 0.3 copy.99
  191.4 3.5 fusion.66
  195.0 4.7 fusion.27
  199.7 1.9 copy.103
  201.6 14.8 %fusion.10 = f32[5,128,768]{2,1,0:T(8,128)} fusion(bf16[384,5,128]{0,2,1:T(8,128)(2,1)S(1)} %bitcast.72, f32[5,384,768]{2,1,0:T(8,128)} %fusion.66, f32[5,384,768]{2,1,0:T(8,128)} %get-tuple-element.25, f32[5,384]{1,0:T(8,128)S(1)} %get-tuple-element.24), kind=kOutput, calls=%fused_computation.18 | convolution fusion | flops 387811968 | bytes 14261760 | tf_op jit(solution)/shard_map/hte,thd->ehd/dot_general | solution.py:127
  216.4 2.9 copy.102
  219.3 1.8 fusion.8
  221.1 1.0 fusion.62
  222.2 3.2 collective-permute-start.3
  225.4 1.3 collective-permute-start.4
  226.7 19.7 %fusion.34 = bf16[5,128,384]{2,1,0:T(8,128)(2,1)} fusion(bf16[768,5,128]{0,2,1:T(8,128)(2,1)} %bitcast.69, f32[5,384,768]{2,1,0:T(8,128)} %fusion.66, f32[5,384,768]{2,1,0:T(8,128)} %get-tuple-element.25, f32[5,384]{1,0:T(8,128)S(1)} %get-tuple-element.24), kind=kOutput, calls=%fused_computation.40 | convolution fusion | flops 388057728 | bytes 13278720 | tf_op jit(solution)/shard_map/hte,ehd->thd/dot_general | solution.py:124
  246.5 2.0 copy.104
  248.5 0.0 collective-permute-done.3
  248.5 0.0 collective-permute-done.4
  248.5 1.5 fusion.23
  250.0 0.9 copy-done.2
  250.9 0.1 copy-done.4
  251.0 13.9 %convolution_convert_fusion = bf16[5120,3,640]{2,0,1:T(8,128)(2,1)} fusion(bf16[384,5120,1]{1,0,2:T(8,128)(2,1)S(1)} %copy-done.2, bf16[384,2,640]{2,0,1:T(8,128)(2,1)S(1)} %fusion.23, bf16[384,1,640]{2,0,1:T(8,128)(2,1)S(1)} %copy-done.4), kind=kOutput, calls=%fused_computation.2 | convolution fusion | flops 7562526720 | bytes 25067520 | tf_op jit(solution)/shard_map/tr,tmc->rmc/dot_general | solution.py:148
  264.9 0.0 reduce-scatter.2.cloned.1.call-update
  264.9 0.3 all-gather.5.cloned.1.call-start
  265.2 147.0 %reduce-scatter.2.cloned.1.call-done = bf16[1280,3,640]{2,0,1:T(8,128)(2,1)} async-done(((bf16[5120,3,640]{2,0,1:T(8,128)(2,1)}), bf16[1280,3,640]{2,0,1:T(8,128)(2,1)}) %reduce-scatter.2.cloned.1.call-update) | async-done | bytes 4915216 | tf_op jit(solution)/shard_map/reduce_scatter | solution.py:147
  412.1 10.6 %reshape.150 = bf16[640,2,3,640]{3,1,0,2:T(2,128)(2,1)} reshape(bf16[1280,3,640]{2,0,1:T(8,128)(2,1)} %reduce-scatter.2.cloned.1.call-done) | data formatting | bytes 9830400 | tf_op jit(solution)/shard_map/reshape | solution.py:156
  422.7 11.3 %fusion.61 = (bf16[640,1,3,640]{3,1,0,2:T(2,128)(2,1)S(1)}, bf16[640,1,3,640]{3,1,0,2:T(2,128)(2,1)}) fusion(bf16[640,2,3,640]{3,1,0,2:T(2,128)(2,1)} %reshape.150), kind=kLoop, calls=%fused_computation.81 | loop fusion | bytes 9830400 | tf_op jit(solution)/shard_map/slice | solution.py:158
  434.0 0.4 copy.106
  434.4 1.3 collective-permute-start.5
  435.7 10.6 %reshape.151 = bf16[640,2,3,640]{3,1,0,2:T(2,128)(2,1)} reshape(bf16[1280,3,640]{2,0,1:T(8,128)(2,1)} %param.10) | data formatting | bytes 9830400 | tf_op jit(solution)/shard_map/reshape | solution.py:161
  446.3 9.7 %constant_dynamic-slice_fusion = bf16[640,1,3,640]{3,1,0,2:T(2,128)(2,1)} fusion(bf16[640,2,3,640]{3,1,0,2:T(2,128)(2,1)} %reshape.151, s32[]{:T(128)S(6)} %select_n.46), kind=kLoop, calls=%fused_computation.75 | loop fusion | bytes 4915204 | tf_op jit(solution)/shard_map/dynamic_slice | solution.py:161
  456.0 35.5 %collective-permute-done.5 = bf16[640,1,3,640]{3,0,2,1:T(8,128)(2,1)} collective-permute-done((bf16[640,1,3,640]{3,0,2,1:T(8,128)(2,1)S(1)}, bf16[640,1,3,640]{3,0,2,1:T(8,128)(2,1)}, u32[]{:S(2)}, u32[]{:S(2)}) %collective-permute-start.5) | collective-permute-done | bytes 2457632 | tf_op jit(solution)/shard_map/ppermute | solution.py:23
  491.5 10.3 %subtract_convert_fusion = (bf16[640,1,3,640]{3,0,2,1:T(8,128)(2,1)}, f32[640,1,3,640]{3,0,2,1:T(8,128)}) fusion(bf16[640,1,3,640]{3,1,0,2:T(2,128)(2,1)} %constant_dynamic-slice_fusion, bf16[640,1,3,640]{3,1,0,2:T(2,128)(2,1)} %get-tuple-element.17, bf16[640,1,3,640]{3,0,2,1:T(8,128)(2,1)} %collective-permute-done.5, pred[]{:T(512)S(6)} %eq.9, ...), kind=kLoop, calls=%fused_computation.12 | loop fusion | flops 11059200 | bytes 19660800 | tf_op jit(solution)/shard_map/convert_element_type | solution.py:162
  501.8 0.0 all-gather.5.cloned.1.call-update
  501.8 9.7 %copy.110 = f32[640,1,3,640]{3,1,2,0:T(1,128)} copy(f32[640,1,3,640]{3,0,2,1:T(8,128)} %get-tuple-element.15) | data formatting | bytes 9830400
  511.5 54.4 %all-gather.5.cloned.1.call-done = bf16[640,2,3,640]{3,0,2,1:T(8,128)(2,1)} async-done(((bf16[640,1,3,640]{3,0,2,1:T(8,128)(2,1)}), bf16[640,2,3,640]{3,0,2,1:T(8,128)(2,1)}) %all-gather.5.cloned.1.call-update) | async-done | bytes 4915216 | tf_op jit(solution)/shard_map/all_gather | solution.py:163
  565.9 9.8 %copy.109 = bf16[640,2,3,640]{3,1,0,2:T(2,128)(2,1)} copy(bf16[640,2,3,640]{3,0,2,1:T(8,128)(2,1)} %all-gather.5.cloned.1.call-done) | data formatting | bytes 9830400 | tf_op jit(solution)/shard_map/all_gather | solution.py:163
  575.7 11.0 %reshape.152 = bf16[1280,3,640]{2,0,1:T(8,128)(2,1)} reshape(bf16[640,2,3,640]{3,1,0,2:T(2,128)(2,1)} %copy.109) | data formatting | bytes 9830400 | tf_op jit(solution)/shard_map/reshape | solution.py:163
  (17 shorter events, 0.1 us)
Async XLA Ops:
  7.2 8.4 %copy-start = (bf16[64,5120]{1,0:T(8,128)(2,1)S(1)}, bf16[64,5120]{1,0:T(8,128)(2,1)}, u32[]{:S(2)}) copy-start(bf16[64,5120]{1,0:T(8,128)(2,1)} %param.9) | copy-start | bytes 1966084
  7.2 0.9 copy-start.6
  7.2 5.7 copy-start.7
  7.2 5.7 copy-start.8
  7.2 128.4 %all-gather.3.cloned.1.call-start = ((), (), s32[]{:S(2)}) async-start(), calls=%async_computation.1 | async-start | bytes 24576000 | tf_op jit(solution)/shard_map/all_gather | solution.py:85
  7.9 404.2 %reduce-scatter.2.cloned.1.call-start = ((), (), s32[]{:S(2)}) async-start(), calls=%async_computation.2 | async-start | bytes 24576000 | tf_op jit(solution)/shard_map/reduce_scatter | solution.py:147
  8.0 7.5 %collective-permute-start = (bf16[1,384,64]{1,2,0:T(8,128)(2,1)S(1)}, bf16[1,384,64]{1,2,0:T(8,128)(2,1)S(1)}, u32[]{:S(2)}, u32[]{:S(2)}) collective-permute-start(bf16[1,384,64]{1,2,0:T(8,128)(2,1)S(1)} %copy-done.6), channel_id=1, source_target_pairs={{0,16},{1,17},{2,18},{3,19},{4,20},{5,21},{6,22},{7,23},{8,24},{9,... | collective-permute-start | bytes 147464 | tf_op jit(solution)/shard_map/ppermute | solution.py:23
  149.7 8.0 %collective-permute-start.1 = (bf16[192,2,640]{2,0,1:T(8,128)(2,1)}, bf16[192,2,640]{2,0,1:T(8,128)(2,1)}, u32[]{:S(2)}, u32[]{:S(2)}) collective-permute-start(bf16[192,2,640]{2,0,1:T(8,128)(2,1)} %get-tuple-element.22), channel_id=1, source_target_pairs={{0,4},{4,8},{8,12},{1,5},{5,9},{9,13},{2,6},{6,10},{10,14},{3,7},{... | collective-permute-start | bytes 1474568 | tf_op jit(solution)/shard_map/ppermute | solution.py:34
  152.7 5.0 collective-permute-start.2
  159.0 2.2 copy-start.3
  167.2 3.8 copy-start.5
  222.2 26.3 %collective-permute-start.3 = (bf16[192,2,640]{2,0,1:T(8,128)(2,1)}, bf16[192,2,640]{2,0,1:T(8,128)(2,1)S(1)}, u32[]{:S(2)}, u32[]{:S(2)}) collective-permute-start(bf16[192,2,640]{2,0,1:T(8,128)(2,1)} %get-tuple-element.18), channel_id=1, source_target_pairs={{0,4},{4,8},{8,12},{1,5},{5,9},{9,13},{2,6},{6,10},{10,14},{3,7},{... | collective-permute-start | bytes 1474568 | tf_op jit(solution)/shard_map/ppermute | solution.py:34
  225.4 23.1 %collective-permute-start.4 = (bf16[192,2,640]{2,0,1:T(8,128)(2,1)}, bf16[192,2,640]{2,0,1:T(8,128)(2,1)S(1)}, u32[]{:S(2)}, u32[]{:S(2)}) collective-permute-start(bf16[192,2,640]{2,0,1:T(8,128)(2,1)} %get-tuple-element.19), channel_id=1, source_target_pairs={{4,0},{8,4},{12,8},{5,1},{9,5},{13,9},{6,2},{10,6},{14,10},{7,3},{... | collective-permute-start | bytes 1474568 | tf_op jit(solution)/shard_map/ppermute | solution.py:36
  248.5 2.4 copy-start.2
  248.5 2.5 copy-start.4
  264.9 301.0 %all-gather.5.cloned.1.call-start = ((), (), s32[]{:S(2)}) async-start(), calls=%async_computation.3 | async-start | bytes 7372800 | tf_op jit(solution)/shard_map/all_gather | solution.py:163
  434.4 57.1 %collective-permute-start.5 = (bf16[640,1,3,640]{3,0,2,1:T(8,128)(2,1)S(1)}, bf16[640,1,3,640]{3,0,2,1:T(8,128)(2,1)}, u32[]{:S(2)}, u32[]{:S(2)}) collective-permute-start(bf16[640,1,3,640]{3,0,2,1:T(8,128)(2,1)S(1)} %copy.106), channel_id=1, source_target_pairs={{16,0},{17,1},{18,2},{19,3},{20,4},{21,5},{22,6},{23,7},{24,8},{25... | collective-permute-start | bytes 7372808 | tf_op jit(solution)/shard_map/ppermute | solution.py:23
  565.9 20.7 %copy-start.1 = (bf16[64,5120]{1,0:T(8,128)(2,1)S(1)}, bf16[64,5120]{1,0:T(8,128)(2,1)}, u32[]{:S(2)}) copy-start(bf16[64,5120]{1,0:T(8,128)(2,1)} %param.9) | copy-start | bytes 1966084
Sparse Core Ops, SparseCore 0:
  9.6 125.9 all-gather.2
  265.0 147.0 reduce-scatter.1
  501.9 63.9 all-gather.4
where the time goes:
time: 602 us; the launch traced here: 594 us
  waiting for transfers between devices  355 us (59%)
  local copies, waits for them, and re-layouts  86.5 us (14%)
  matrix products  83.1 us (14%)
  blocking collectives  19.6 us (3%)
  between operations  18 us (3%)
  other arithmetic  16.7 us (3%)
  starting transfers between devices  15.2 us (3%)
    reduce_scatter x1, waiting for transfers between devices, body(): lax.psum_scatter(jnp.einsum('tr,tmc->rmc', columns, qkv_grad, preferred_e...  147 us
    all_gather x1, waiting for transfers between devices, body(): lax.all_gather(w_qkv, 'seq', axis=0, tiled=True)  117 us
    all_gather x1, waiting for transfers between devices, body(): lax.all_gather(new_half, 'role', axis=1, tiled=True)  54.4 us
    ppermute x2, waiting for transfers between devices, from_behind(): return lax.ppermute(block, axis, route)  35.5 us
    dot_general x1, matrix products, body(): jnp.einsum('hte,ehd->thd', score_grad, keys_near, preferred_element_type=...  19.7 us
    psum x1, blocking collectives, body(): lax.psum(partial_pred.astype(jnp.bfloat16), 'mp').astype(jnp.float32)  19.6 us
    dot_general x1, matrix products, body(): jnp.einsum('hte,thd->ehd', score_grad, queries, preferred_element_type=jn...  14.8 us
    dot_general x1, matrix products, body(): jnp.einsum('tr,tmc->rmc', columns, qkv_grad, preferred_element_type=jnp.f...  13.9 us
  transfers between devices with their start and end apart: 9, of which 4 were waited for; matrix products, arithmetic and copies ran while one was open for 10% of the time, Pallas kernels for 0%

commit v1 on v0

v1 whole, which is shorter than its diff:
```python
import functools

import jax
import jax.numpy as jnp
from jax import lax
from jax.experimental import pallas as pl
from jax.experimental.pallas import tpu as pltpu
from jax.sharding import PartitionSpec as P

HD = 128
TILE = 192
STEPS = 50
CH = 64
WINDOW = 640
ONE_LANE = 64
BIAS_LANE = 65
LOW_LANE = 66

SHIFT_FACTOR = 5.0
NOISE_LEVEL = 0.7
MOMENTUM_DECAY = 0.9
LEARNING_RATE = 0.004
LOSS_SCALE = 16384.0
REWARD_FLOOR = 0.1
MASKED = -1e30
LOG2E = 1.4426950408889634

F32 = jnp.float32
BF16 = jnp.bfloat16
NT = (((1,), (1,)), ((), ()))
TN = (((0,), (0,)), ((), ()))
NN = (((1,), (0,)), ((), ()))


def dot(a, b, dims=NN):
    return lax.dot_general(a, b, dims, preferred_element_type=F32)


def sigma_at(index, total_steps):
    fraction = index.astype(F32) / total_steps
    return SHIFT_FACTOR * fraction / (1.0 + (SHIFT_FACTOR - 1.0) * fraction)


def advantage_of(rewards, group_ids):
    members = (group_ids == group_ids[0]).astype(F32)
    member_total = jnp.sum(members)
    group_mean = jnp.sum(members * rewards) / member_total
    spread = jnp.sqrt(jnp.sum(members * (rewards - group_mean) ** 2) / member_total)
    return (rewards[0] - group_mean) / jnp.maximum(spread, REWARD_FLOOR)


def swap(x, axis, bit):
    return lax.ppermute(x, axis, [(i, i ^ bit) for i in range(lax.axis_size(axis))])


def butterfly(x, axis):
    bit = 1
    while bit < lax.axis_size(axis):
        x = (x.astype(F32) + swap(x, axis, bit).astype(F32)).astype(x.dtype)
        bit *= 2
    return x


def fold_kernel(e_ref, w_ref, o_ref):
    o_ref[0] = dot(e_ref[...], w_ref[0]).astype(BF16)


def fold(e_rows, w):
    _, rows, width = w.shape
    return pl.pallas_call(
        fold_kernel,
        grid=(3,),
        in_specs=[
            pl.BlockSpec((CH, rows), lambda m: (0, 0)),
            pl.BlockSpec((1, rows, width), lambda m: (m, 0, 0)),
        ],
        out_specs=pl.BlockSpec((1, CH, width), lambda m: (m, 0, 0)),
        out_shape=jax.ShapeDtypeStruct((3, CH, width), BF16),
        name="fold",
    )(e_rows, w)


def forward_kernel(tiles, heads, win_ref, m_ref, wot_ref, e_ref, u_ref, il_ref, pred_ref, mk_ref, att_ref):
    mk_ref[...] = jnp.zeros_like(mk_ref)
    mk_ref[0:CH, :] = m_ref[1]
    lane = lax.broadcasted_iota(jnp.int32, (TILE, HD), 1)
    unit = jnp.where(lane == BIAS_LANE, 1.0, 0.0)
    factor = LOG2E * HD ** (-0.5)
    for j in range(tiles):
        own = win_ref[j, TILE : 2 * TILE, 0:CH]
        queries = dot(own, m_ref[0]).astype(BF16)
        keys = win_ref[j]
        for h in range(heads):
            cols = slice(h * HD, (h + 1) * HD)
            t = dot(queries[:, cols], mk_ref[:, cols], NT) * factor + unit
            s = dot(t.astype(BF16), keys, NT)
            e = jnp.exp2(s - jnp.max(s, axis=1, keepdims=True)).astype(BF16)
            at = slice((j * heads + h) * TILE, (j * heads + h + 1) * TILE)
            e_ref[at, :] = e
            u = dot(e, keys)
            inv = 1.0 / u[:, ONE_LANE : ONE_LANE + 1]
            u = (u * inv).astype(BF16)
            u_ref[at, :] = u
            il_ref[at, :] = jnp.broadcast_to(inv, (TILE, HD))
            att_ref[j * TILE : (j + 1) * TILE, cols] = dot(u[:, 0:CH], m_ref[2, :, cols]).astype(BF16)
    pred_ref[...] = dot(att_ref[...], wot_ref[...], NT).astype(BF16)


def forward(win, m, wot, tiles, heads):
    rows = tiles * heads * TILE
    width = heads * HD
    vm = pl.BlockSpec(memory_space=pltpu.VMEM)
    return pl.pallas_call(
        functools.partial(forward_kernel, tiles, heads),
        in_specs=[vm] * 3,
        out_specs=[vm] * 4,
        out_shape=[
            jax.ShapeDtypeStruct((rows, WINDOW), BF16),
            jax.ShapeDtypeStruct((rows, HD), BF16),
            jax.ShapeDtypeStruct((rows, HD), F32),
            jax.ShapeDtypeStruct((tiles * TILE, CH), BF16),
        ],
        scratch_shapes=[pltpu.VMEM((HD, width), BF16), pltpu.VMEM((tiles * TILE, width), BF16)],
        compiler_params=pltpu.CompilerParams(vmem_limit_bytes=48 * 1024 * 1024),
        name="attend",
    )(win, m, wot)


def backward_kernel(tiles, heads, *refs):
    (sc_ref, win_ref, m_ref, wot_ref, e_ref, u_ref, il_ref, next_ref) = refs[:8]
    pred_refs = refs[8:-3]
    zy_ref, mv_ref, v_ref = refs[-3:]
    width = heads * HD
    mv_ref[...] = jnp.zeros_like(mv_ref)
    mv_ref[0:CH, :] = m_ref[2]
    lane = lax.broadcasted_iota(jnp.int32, (TILE, HD), 1)
    half_lane = lax.broadcasted_iota(jnp.int32, (CH, HD), 1)
    scale = HD ** (-0.5)
    pred = pred_refs[0][...].astype(F32)
    for ref in pred_refs[1:]:
        pred = pred + ref[...].astype(F32)
    pgs = []
    for j in range(tiles):
        at = slice(j * TILE, (j + 1) * TILE)
        now = win_ref[j, TILE : 2 * TILE, 0:CH].astype(F32)
        step_mean = now + sc_ref[1] * pred[at]
        pg = (sc_ref[0] * (next_ref[at, :].astype(F32) - step_mean)).astype(BF16)
        pgs.append(pg)
        ag = dot(pg, wot_ref[...]).astype(BF16)
        keys = win_ref[j]
        for h in range(heads):
            cols = slice(h * HD, (h + 1) * HD)
            rows = slice((j * heads + h) * TILE, (j * heads + h + 1) * TILE)
            w = dot(ag[:, cols], mv_ref[:, cols], NT).astype(BF16).astype(F32)
            u = u_ref[rows, :].astype(F32)
            row_dot = jnp.sum(w * u, axis=1, keepdims=True)
            factor = scale * il_ref[rows, :]
            w = w * factor
            row_dot = row_dot * factor
            high = row_dot.astype(BF16).astype(F32)
            low = row_dot - high
            w = jnp.where(lane == ONE_LANE, -high, jnp.where(lane == LOW_LANE, -low, w))
            x = dot(w.astype(BF16), keys, NT)
            ds = (e_ref[rows, :].astype(F32) * x).astype(BF16)
            v_ref[h, at, :] = dot(ds, keys).astype(BF16)
    pg_all = jnp.concatenate(pgs, axis=0)
    pg_all = jnp.concatenate([jnp.zeros_like(pg_all), pg_all], axis=1)
    own = jnp.concatenate([win_ref[j, TILE : 2 * TILE, 0:CH] for j in range(tiles)], axis=0)
    for h in range(heads):
        z = dot(own, v_ref[h], TN)
        u = jnp.concatenate(
            [u_ref[(j * heads + h) * TILE : (j * heads + h + 1) * TILE, 0:CH] for j in range(tiles)], axis=0
        )
        y = dot(u, pg_all, TN)
        zy_ref[h * CH : (h + 1) * CH, :] = jnp.where(half_lane < CH, z, y).astype(BF16)


def backward(scalars, win, m, wot, e, u, il, latent_next, preds, tiles, heads):
    vm = pl.BlockSpec(memory_space=pltpu.VMEM)
    width = heads * HD
    return pl.pallas_call(
        functools.partial(backward_kernel, tiles, heads),
        in_specs=[pl.BlockSpec(memory_space=pltpu.SMEM)] + [vm] * (7 + len(preds)),
        out_specs=vm,
        out_shape=jax.ShapeDtypeStruct((heads * CH, HD), BF16),
        scratch_shapes=[pltpu.VMEM((HD, width), BF16), pltpu.VMEM((heads, tiles * TILE, HD), BF16)],
        compiler_params=pltpu.CompilerParams(vmem_limit_bytes=48 * 1024 * 1024),
        name="attend_grad",
    )(scalars, win, m, wot, e, u, il, latent_next, *preds)


def update_kernel(heads, steps, pairs, aliased, *refs):
    role_ref, zy_ref, m_ref, wot_ref, et_ref, mom_ref, w_ref = refs[:7]
    recv_refs = refs[7 : 7 + steps]
    onm_ref, ow_ref, g_ref, gs_ref, rs_ref, fs_ref = refs[7 + steps + aliased :]
    width = heads * HD
    lanes = width // HD
    stride = 3 * lanes
    step = pl.program_id(0)
    role = role_ref[0]

    @pl.when(step == 0)
    def _():
        for h in range(heads):
            cols = slice(h * HD, (h + 1) * HD)
            zy = zy_ref[h * CH : (h + 1) * CH, :]
            z = zy[:, 0:CH]
            y = zy[:, CH : 2 * CH]
            g_ref[0, :, cols] = dot(z, m_ref[1, :, cols]).astype(BF16)
            g_ref[1, :, cols] = dot(z, m_ref[0, :, cols], TN).astype(BF16)
            g_ref[2, :, cols] = dot(y, wot_ref[:, cols]).astype(BF16)

    for s in range(steps):

        @pl.when(step == s)
        def _():
            rs_ref[...] = recv_refs[s][...].astype(F32)

    for part in range(3):
        g = dot(et_ref[...], g_ref[part])
        for b in range(lanes):
            cols = slice(b * HD, (b + 1) * HD)
            at = pl.ds(part * lanes + b, pairs, stride=stride)
            gs_ref[...] = g[:, cols]
            own = MOMENTUM_DECAY * mom_ref[at, :] + gs_ref[pl.ds(role, pairs, stride=2), :]
            other = MOMENTUM_DECAY * rs_ref[at, :] + gs_ref[pl.ds(1 - role, pairs, stride=2), :]
            onm_ref[at, :] = own
            fs_ref[pl.ds(role, pairs, stride=2), :] = own
            fs_ref[pl.ds(1 - role, pairs, stride=2), :] = other
            ow_ref[part, :, cols] = (w_ref[part, :, cols].astype(F32) - LEARNING_RATE * fs_ref[...]).astype(BF16)


def update(role, zy, m, wot, et, mom, w, received, first, pairs, before, heads):
    steps = len(received)
    width = heads * HD
    lin = pairs * 3 * heads
    any_space = pl.BlockSpec(memory_space=pl.ANY)
    whole = lambda a: pl.BlockSpec(a.shape, lambda i: (0,) * a.ndim)
    args = [role, zy, m, wot, et, mom, w, *received, *before]
    return pl.pallas_call(
        functools.partial(update_kernel, heads, steps, pairs, len(before)),
        grid=(steps,),
        in_specs=[
            pl.BlockSpec(memory_space=pltpu.SMEM),
            whole(zy),
            whole(m),
            whole(wot),
            pl.BlockSpec((2 * pairs, CH), lambda i: (first + i, 0)),
            pl.BlockSpec((lin, HD), lambda i: (first + i, 0)),
            pl.BlockSpec((3, 2 * pairs, width), lambda i: (0, first + i, 0)),
        ]
        + [whole(a) for a in received]
        + [any_space] * len(before),
        out_specs=[
            pl.BlockSpec((lin, HD), lambda i: (first + i, 0)),
            pl.BlockSpec((3, 2 * pairs, width), lambda i: (0, first + i, 0)),
        ],
        out_shape=[jax.ShapeDtypeStruct(mom.shape, F32), jax.ShapeDtypeStruct(w.shape, BF16)],
        input_output_aliases={7 + steps + k: k for k in range(len(before))},
        scratch_shapes=[
            pltpu.VMEM((3, CH, width), BF16),
            pltpu.VMEM((2 * pairs, HD), F32),
            pltpu.VMEM((lin, HD), F32),
            pltpu.VMEM((2 * pairs, HD), F32),
        ],
        compiler_params=pltpu.CompilerParams(vmem_limit_bytes=48 * 1024 * 1024),
        name="update",
    )(*args)


def body(rollout, w_embed, w_qkv, w_out, momentum, rewards, group_ids, timestep):
    seq_count = lax.axis_size("seq")
    seq_index = lax.axis_index("seq")
    role_index = lax.axis_index("role")
    rows_dev = w_qkv.shape[0]
    width = w_qkv.shape[2]
    heads = width // HD
    tok_dev = rollout.shape[1]
    tiles = tok_dev // TILE
    pair_rows = rows_dev // 2

    mine = rollout[0]
    other = lax.ppermute(mine, "role", [(0, 1), (1, 0)])
    latent_now = jnp.where(role_index == 0, mine, other)
    latent_next = jnp.where(role_index == 0, other, mine)

    mom = momentum.reshape(pair_rows * 3 * heads, HD)
    chunks = 5
    pairs = pair_rows // chunks
    lin = pairs * 3 * heads
    received = []
    for c in range(chunks):
        piece = lax.slice_in_dim(mom, c * lin, (c + 1) * lin, axis=0).astype(BF16)
        received.append(lax.ppermute(piece, "role", [(0, 1), (1, 0)]))

    e_rows = lax.dynamic_slice_in_dim(w_embed, seq_index * rows_dev, rows_dev, axis=1)
    w = w_qkv.transpose(1, 0, 2)
    m = butterfly(fold(e_rows, w), "seq")

    left = lax.ppermute(latent_now[tok_dev - TILE :], "seq", [(i, i + 1) for i in range(seq_count - 1)])
    right = lax.ppermute(latent_now[:TILE], "seq", [(i + 1, i) for i in range(seq_count - 1)])
    near = jnp.concatenate([left, latent_now, right, jnp.zeros((WINDOW - 3 * TILE, CH), BF16)], axis=0)
    key_tile = jnp.arange(near.shape[0], dtype=jnp.int32) // TILE + seq_index * tiles - 1
    inside = (key_tile >= 0) & (key_tile < seq_count * tiles)
    windows = []
    for j in range(tiles):
        seen = inside[j * TILE : j * TILE + WINDOW] & (jnp.arange(WINDOW) < 3 * TILE)
        bias = jnp.where(seen, 0.0, MASKED).astype(BF16)[:, None]
        ones = jnp.ones((WINDOW, 1), BF16)
        rest = jnp.zeros((WINDOW, HD - LOW_LANE - 1), BF16)
        windows.append(jnp.concatenate([near[j * TILE : j * TILE + WINDOW], ones, bias, ones, rest], axis=1))
    win = jnp.stack(windows)

    advantage = advantage_of(rewards, group_ids)
    sigma_now = sigma_at(timestep[0], STEPS)
    step_size = sigma_at(timestep[0] - 1, STEPS) - sigma_now
    tokens_all = tok_dev * seq_count
    coefficient = advantage * LOSS_SCALE * (1.0 - sigma_now) / (NOISE_LEVEL**2 * sigma_now * tokens_all)
    scalars = jnp.stack([coefficient, step_size])

    wot = w_out.T
    e, u, il, partial_pred = forward(win, m, wot, tiles, heads)
    mp_count = lax.axis_size("mp")
    preds = [partial_pred] + [
        lax.ppermute(partial_pred, "mp", [(i, (i + d) % mp_count) for i in range(mp_count)])
        for d in range(1, mp_count)
    ]
    zy = backward(scalars, win, m, wot, e, u, il, latent_next, preds, tiles, heads)
    zy = butterfly(zy, "seq")

    et = e_rows.T
    role = role_index[None]
    first = update(role, zy, m, wot, et, mom, w, received[:-1], 0, pairs, [], heads)
    nm, nw = update(role, zy, m, wot, et, mom, w, received[-1:], chunks - 1, pairs, first, heads)
    return nm.reshape(momentum.shape), nw.transpose(1, 0, 2)


def solution(mesh):
    in_specs = (
        P("role", "seq", None),
        P(),
        P("seq", None, "mp"),
        P("mp", None),
        P("seq", "role", None, "mp"),
        P(),
        P(),
        P(),
    )
    out_specs = (P("seq", "role", None, "mp"), P("seq", None, "mp"))
    return jax.shard_map(body, mesh=mesh, in_specs=in_specs, out_specs=out_specs, check_vma=False)
```

time: 602 us -> 140 us (0.23); the launches traced: 594 us -> 139 us
  waiting for transfers between devices: 355 us -> 45.4 us
  matrix products: 83.1 us -> 0 us
  local copies, waits for them, and re-layouts: 86.5 us -> 29 us
  Pallas kernels: 0 us -> 28.7 us
  blocking collectives: 19.6 us -> 0 us
  between operations: 18 us -> 4.4 us
    all_gather x2 -> x0, waiting for transfers between devices: 171 us -> none  [the longest x1 117 us: body(): lax.all_gather(w_qkv, 'seq', axis=0, tiled=True)]
    reduce_scatter x1 -> x0, waiting for transfers between devices: 147 us -> none  [body(): lax.psum_scatter(jnp.einsum('tr,tmc->rmc', columns, qkv_grad, preferred_e...]
    dot_general x10 -> x0, matrix products: 77.1 us -> none  [the longest x1 19.7 us: body(): jnp.einsum('hte,ehd->thd', score_grad, keys_near, preferred_element_type=...]
    reshape x3 -> x0, local copies, waits for them, and re-layouts: 32.1 us -> none  [the longest x1 11 us: body(): lax.all_gather(new_half, 'role', axis=1, tiled=True)]
    pallas_call x0 -> x5, Pallas kernels: none -> 28.7 us  [the longest x2 12.7 us: update(): pl.pallas_call(functools.partial(update_kernel, heads, steps, pairs, len(...]
    psum x1 -> x0, blocking collectives: 19.6 us -> none  [body(): lax.psum(partial_pred.astype(jnp.bfloat16), 'mp').astype(jnp.float32)]
    ppermute x6 -> x15, waiting for transfers between devices: 35.5 us -> 45.4 us  [the longest x5 32.8 us: body(): received.append(lax.ppermute(piece, 'role', [(0, 1), (1, 0)]))]
    all_gather x1 -> x0, local copies, waits for them, and re-layouts: 9.76 us -> none  [body(): lax.all_gather(new_half, 'role', axis=1, tiled=True)]
  transfers between devices with their start and end apart: 9 -> 15, of which waited for: 4 -> 8; matrix products, arithmetic and copies ran while one was open for 10% -> 28% of each run, Pallas kernels for 0% -> 10%
where the time goes in v1:
time: 140 us; the launch traced here: 139 us
  waiting for transfers between devices  45.4 us (32%)
  local copies, waits for them, and re-layouts  29 us (21%)
  Pallas kernels  28.7 us (20%)
  starting transfers between devices  19.8 us (14%)
  other arithmetic  11.7 us (8%)
  between operations  4.4 us (3%)
    ppermute x5, waiting for transfers between devices, body(): received.append(lax.ppermute(piece, 'role', [(0, 1), (1, 0)]))  32.8 us
    slice x1, local copies, waits for them, and re-layouts, body(): piece = lax.slice_in_dim(mom, c * lin, (c + 1) * lin, axis=0).astype(BF16)  15.5 us
    pallas_call x2, Pallas kernels, update(): pl.pallas_call(functools.partial(update_kernel, heads, steps, pairs, len(...  12.7 us
    convert_element_type x5, local copies, waits for them, and re-layouts, body(): piece = lax.slice_in_dim(mom, c * lin, (c + 1) * lin, axis=0).astype(BF16)  8.95 us
    another operation x1, other arithmetic  8.01 us
    ppermute x3, waiting for transfers between devices, body(): lax.ppermute(partial_pred, 'mp', [(i, (i + d) % mp_count) for i in range(...  7.3 us
    pallas_call x1, Pallas kernels, forward(): pl.pallas_call(functools.partial(forward_kernel, tiles, heads), in_specs=...  6.36 us
    ppermute x4, waiting for transfers between devices, swap(): lax.ppermute(x, axis, [(i, i ^ bit) for i in range(lax.axis_size(axis))])  5.32 us
  transfers between devices with their start and end apart: 15, of which 8 were waited for; matrix products, arithmetic and copies ran while one was open for 28% of the time, Pallas kernels for 10%

profile of v1, /device:TPU:0, one launch (start us, length us, event | category | flops | bytes accessed | tf_op | source)
XLA Modules:
  0.0 139.1 jit_solution(7065000667714058021)
XLA Ops:
  0.6 0.0 copy-start
  0.6 0.0 copy-start.4
  0.7 0.0 copy-start.5
  0.7 1.0 copy.16
  1.6 3.0 %collective-permute-start = (bf16[384,64]{1,0:T(8,128)(2,1)S(1)}, bf16[384,64]{1,0:T(8,128)(2,1)S(1)}, u32[]{:S(2)}, u32[]{:S(2)}) collective-permute-start(bf16[384,64]{1,0:T(8,128)(2,1)S(1)} %bitcast.36), channel_id=1, source_target_pairs={{0,16},{16,0},{1,17},{17,1},{2,18},{18,2},{3,19},{19,3},{4,20},{20... | collective-permute-start | bytes 147464 | tf_op jit(solution)/shard_map/ppermute | solution.py:283
  4.7 0.7 constant_dynamic-slice_fusion.e_ref
  5.3 4.4 %fold.1 = bf16[3,64,640]{2,1,0:T(8,128)(2,1)} custom-call(bf16[64,1280]{1,0:T(8,128)(2,1)} %constant_dynamic-slice_fusion.e_ref, bf16[3,1280,640]{2,1,0:T(8,128)(2,1)} %bitcast.29), custom_call_target="tpu_custom_call" | custom-call | tf_op jit(solution)/shard_map/fold/pallas_call | solution.py:70
  9.7 0.0 collective-permute-start.3
  9.8 0.1 select_convert_fusion.1
  9.8 0.0 copy-done.4
  9.8 0.7 convert_reduce_fusion
  11.8 0.6 select_reduce_fusion
  14.6 0.1 broadcast_in_dim.28
  14.8 0.1 broadcast_in_dim.29
  15.0 0.1 pad.4.clone
  15.1 0.0 collective-permute-done
  15.1 2.4 %collective-permute-start.1 = (bf16[192,64]{1,0:T(8,128)(2,1)S(1)}, bf16[192,64]{1,0:T(8,128)(2,1)S(1)}, u32[]{:S(2)}, u32[]{:S(2)}) collective-permute-start(bf16[192,64]{1,0:T(8,128)(2,1)S(1)} %get-tuple-element.33), channel_id=1, source_target_pairs={{0,4},{4,8},{8,12},{1,5},{5,9},{9,13},{2,6},{6,10},{10,14},{3,7},{... | collective-permute-start | bytes 73736 | tf_op jit(solution)/shard_map/ppermute | solution.py:300
  17.6 1.3 collective-permute-start.2
  18.9 0.0 collective-permute-done.3
  18.9 1.0 add_convert_fusion.1
  19.9 3.4 %collective-permute-start.4 = (bf16[3,64,640]{2,1,0:T(8,128)(2,1)S(1)}, bf16[3,64,640]{2,1,0:T(8,128)(2,1)S(1)}, u32[]{:S(2)}, u32[]{:S(2)}) collective-permute-start(bf16[3,64,640]{2,1,0:T(8,128)(2,1)S(1)} %add_convert_fusion.1), channel_id=1, source_target_pairs={{0,8},{4,12},{8,0},{12,4},{1,9},{5,13},{9,1},{13,5},{2,10},{6,14},... | collective-permute-start | bytes 737288 | tf_op jit(solution)/shard_map/ppermute | solution.py:53
  23.3 0.0 collective-permute-done.1
  23.3 0.0 collective-permute-done.2
  23.3 0.2 pad_maximum_fusion.1
  23.6 0.3 concatenate.14
  23.9 0.3 concatenate.16
  24.3 5.3 %collective-permute-done.4 = bf16[3,64,640]{2,1,0:T(8,128)(2,1)S(1)} collective-permute-done((bf16[3,64,640]{2,1,0:T(8,128)(2,1)S(1)}, bf16[3,64,640]{2,1,0:T(8,128)(2,1)S(1)}, u32[]{:S(2)}, u32[]{:S(2)}) %collective-permute-start.4) | collective-permute-done | bytes 245792 | tf_op jit(solution)/shard_map/ppermute | solution.py:53
  29.6 0.1 add_convert_fusion.m_ref.refs_2_
  29.7 6.4 %attend.1 = (bf16[1920,640]{1,0:T(8,128)(2,1)S(1)}, bf16[1920,128]{1,0:T(8,128)(2,1)S(1)}, f32[1920,128]{1,0:T(8,128)S(1)}, bf16[384,64]{1,0:T(8,128)(2,1)S(1)}) custom-call(bf16[2,640,128]{2,1,0:T(8,128)(2,1)S(1)} %pad_maximum_fusion.win_ref.refs_1_, bf16[3,64,640]{2,1,0:T(8,128)(2,1)S(1)} %add_convert_fusion.m_ref.refs_2_, bf16[64,640]{1,0:T(8,128)(2,1)S(1)} %bitcast.25), custom_call_target="tpu_custom_call" | custom-call | tf_op jit(solution)/shard_map/attend/pallas_call | solution.py:113
  36.0 3.7 %collective-permute-start.7 = (bf16[384,64]{1,0:T(8,128)(2,1)S(1)}, bf16[384,64]{1,0:T(8,128)(2,1)S(1)}, u32[]{:S(2)}, u32[]{:S(2)}) collective-permute-start(bf16[384,64]{1,0:T(8,128)(2,1)S(1)} %get-tuple-element.13.refs_8_), channel_id=1, source_target_pairs={{0,3},{1,0},{2,1},{3,2},{4,7},{5,4},{6,5},{7,6},{8,11},{9,8},{10,9... | collective-permute-start | bytes 147464 | tf_op jit(solution)/shard_map/ppermute | solution.py:325
  39.7 0.0 collective-permute-start.6
  39.7 1.0 collective-permute-start.5
  40.7 0.1 pad_maximum_fusion.3.refs_0_
  40.8 2.1 %collective-permute-done.7.refs_11_ = bf16[384,64]{1,0:T(8,128)(2,1)S(1)} collective-permute-done((bf16[384,64]{1,0:T(8,128)(2,1)S(1)}, bf16[384,64]{1,0:T(8,128)(2,1)S(1)}, u32[]{:S(2)}, u32[]{:S(2)}) %collective-permute-start.7) | collective-permute-done | bytes 49184 | tf_op jit(solution)/shard_map/ppermute | solution.py:325
  42.9 5.2 %collective-permute-done.6.refs_10_ = bf16[384,64]{1,0:T(8,128)(2,1)S(1)} collective-permute-done((bf16[384,64]{1,0:T(8,128)(2,1)S(1)}, bf16[384,64]{1,0:T(8,128)(2,1)S(1)}, u32[]{:S(2)}, u32[]{:S(2)}) %collective-permute-start.6) | collective-permute-done | bytes 49184 | tf_op jit(solution)/shard_map/ppermute | solution.py:325
  48.1 0.0 collective-permute-done.5.refs_9_
  48.1 5.2 %attend_grad.1 = bf16[320,128]{1,0:T(8,128)(2,1)S(1)} custom-call(f32[2]{0:T(128)S(1)} %pad_maximum_fusion.3.refs_0_, bf16[2,640,128]{2,1,0:T(8,128)(2,1)S(1)} %pad_maximum_fusion.win_ref.refs_1_, bf16[3,64,640]{2,1,0:T(8,128)(2,1)S(1)} %add_convert_fusion.m_ref.refs_2_, bf16[64,640]{1,0:T(8,128)(2,1)S(1)} %bitcast.26, ...), custom_call_target="tpu_custom_call" | custom-call | tf_op jit(solution)/shard_map/attend_grad/pallas_call | solution.py:181
  53.3 0.1 collective-permute-start.8
  53.3 8.0 %convert.7 = bf16[640,1,3,640]{3,1,2,0:T(2,128)(2,1)} convert(f32[640,1,3,640]{3,1,2,0:T(1,128)} %param.12) | non-fusion elementwise | flops 1228800 | bytes 7372800 | tf_op jit(solution)/shard_map/convert.4
  61.4 0.0 collective-permute-done.8
  61.4 0.0 copy-start.2
  61.4 0.3 collective-permute-start.9
  61.8 15.5 %slice_reduce_fusion = (bf16[128,3,640]{2,1,0:T(4,128)(2,1)}, bf16[128,3,640]{2,1,0:T(4,128)(2,1)}, bf16[128,3,640]{2,1,0:T(4,128)(2,1)S(1)}, bf16[128,3,640]{2,1,0:T(4,128)(2,1)}, bf16[128,3,640]{2,1,0:T(4,128)(2,1)S(1)}) fusion(bf16[640,1,3,640]{3,1,2,0:T(2,128)(2,1)} %convert.7), kind=kLoop, calls=%fused_computation | loop fusion | bytes 4915200 | tf_op jit(solution)/shard_map/slice | solution.py:293
  77.2 2.2 %convert_element_type.91 = bf16[1920,128]{1,0:T(8,128)(2,1)} reshape(bf16[128,3,640]{2,1,0:T(4,128)(2,1)} %get-tuple-element.25) | data formatting | bytes 983040 | tf_op jit(solution)/shard_map/convert_element_type | solution.py:293
  79.4 0.5 collective-permute-start.11
  79.9 1.2 convert_element_type.92
  81.2 1.5 %collective-permute-start.12 = (bf16[1920,128]{1,0:T(8,128)(2,1)}, bf16[1920,128]{1,0:T(8,128)(2,1)S(1)}, u32[]{:S(2)}, u32[]{:S(2)}) collective-permute-start(bf16[1920,128]{1,0:T(8,128)(2,1)} %convert_element_type.92), channel_id=1, source_target_pairs={{0,16},{16,0},{1,17},{17,1},{2,18},{18,2},{3,19},{19,3},{4,20},{20... | collective-permute-start | bytes 1474568 | tf_op jit(solution)/shard_map/ppermute | solution.py:294
  82.6 2.2 %convert_element_type.93 = bf16[1920,128]{1,0:T(8,128)(2,1)} reshape(bf16[128,3,640]{2,1,0:T(4,128)(2,1)} %get-tuple-element.23) | data formatting | bytes 983040 | tf_op jit(solution)/shard_map/convert_element_type | solution.py:293
  84.8 0.5 collective-permute-start.13
  85.4 2.2 %convert_element_type.94 = bf16[1920,128]{1,0:T(8,128)(2,1)} reshape(bf16[128,3,640]{2,1,0:T(4,128)(2,1)} %get-tuple-element.22) | data formatting | bytes 983040 | tf_op jit(solution)/shard_map/convert_element_type | solution.py:293
  87.5 1.5 %collective-permute-start.14 = (bf16[1920,128]{1,0:T(8,128)(2,1)}, bf16[1920,128]{1,0:T(8,128)(2,1)}, u32[]{:S(2)}, u32[]{:S(2)}) collective-permute-start(bf16[1920,128]{1,0:T(8,128)(2,1)} %convert_element_type.94), channel_id=1, source_target_pairs={{0,16},{16,0},{1,17},{17,1},{2,18},{18,2},{3,19},{19,3},{4,20},{20... | collective-permute-start | bytes 1474568 | tf_op jit(solution)/shard_map/ppermute | solution.py:294
  89.0 1.2 convert_element_type.90
  90.2 0.0 collective-permute-done.9
  90.2 0.6 copy-done.3
  90.9 0.5 collective-permute-start.10
  91.4 1.2 copy.22
  92.6 1.0 add_convert_fusion.2.refs_1_
  93.6 0.1 collective-permute-done.11.refs_7_
  93.7 10.5 %collective-permute-done.12.refs_8_ = bf16[1920,128]{1,0:T(8,128)(2,1)S(1)} collective-permute-done((bf16[1920,128]{1,0:T(8,128)(2,1)}, bf16[1920,128]{1,0:T(8,128)(2,1)S(1)}, u32[]{:S(2)}, u32[]{:S(2)}) %collective-permute-start.12) | collective-permute-done | bytes 491552 | tf_op jit(solution)/shard_map/ppermute | solution.py:294
  104.2 10.5 %collective-permute-done.13.refs_9_ = bf16[1920,128]{1,0:T(8,128)(2,1)S(1)} collective-permute-done((bf16[1920,128]{1,0:T(8,128)(2,1)}, bf16[1920,128]{1,0:T(8,128)(2,1)S(1)}, u32[]{:S(2)}, u32[]{:S(2)}) %collective-permute-start.13) | collective-permute-done | bytes 491552 | tf_op jit(solution)/shard_map/ppermute | solution.py:294
  114.7 10.6 %collective-permute-done.14.refs_10_ = bf16[1920,128]{1,0:T(8,128)(2,1)} collective-permute-done((bf16[1920,128]{1,0:T(8,128)(2,1)}, bf16[1920,128]{1,0:T(8,128)(2,1)}, u32[]{:S(2)}, u32[]{:S(2)}) %collective-permute-start.14) | collective-permute-done | bytes 491552 | tf_op jit(solution)/shard_map/ppermute | solution.py:294
  125.4 8.9 %update.2 = (f32[9600,128]{1,0:T(8,128)}, bf16[3,1280,640]{2,1,0:T(8,128)(2,1)}) custom-call(s32[1]{0:T(128)} %bitcast.refs_0_, bf16[320,128]{1,0:T(8,128)(2,1)S(1)} %add_convert_fusion.2.refs_1_, bf16[3,64,640]{2,1,0:T(8,128)(2,1)S(1)} %add_convert_fusion.m_ref.refs_2_, bf16[64,640]{1,0:T(8,128)(2,1)S(1)} %bitcast.27, bf16[1280,64]{1,0:T(8,128)(2,1)S(1)} %bitcast.23, ...), custom_call_target="tpu_custom_call" | custom-call | tf_op jit(solution)/shard_map/update/pallas_call | solution.py:240
  134.2 1.0 collective-permute-done.10.refs_7_
  135.2 3.9 %update.3 = (f32[9600,128]{1,0:T(8,128)}, bf16[3,1280,640]{2,1,0:T(8,128)(2,1)}) custom-call(s32[1]{0:T(128)} %bitcast.refs_0_, bf16[320,128]{1,0:T(8,128)(2,1)S(1)} %add_convert_fusion.2.refs_1_, bf16[3,64,640]{2,1,0:T(8,128)(2,1)S(1)} %add_convert_fusion.m_ref.refs_2_, bf16[64,640]{1,0:T(8,128)(2,1)S(1)} %bitcast.28, ...), custom_call_target="tpu_custom_call", output_to_operand_aliasing={{0}: (8, {}), {1}: (9, {})} | custom-call | tf_op jit(solution)/shard_map/update/pallas_call | solution.py:240
  (19 shorter events, 0.2 us)
Async XLA Ops:
  0.6 4.0 %copy-start = (bf16[64,5120]{1,0:T(8,128)(2,1)S(1)}, bf16[64,5120]{1,0:T(8,128)(2,1)}, u32[]{:S(2)}) copy-start(bf16[64,5120]{1,0:T(8,128)(2,1)} %param.9) | copy-start | bytes 1966084
  0.6 9.2 %copy-start.4 = (s32[32]{0:T(128)S(1)}, s32[32]{0:T(128)}, u32[]{:S(2)}) copy-start(s32[32]{0:T(128)} %param.14) | copy-start | bytes 388
  0.7 9.2 %copy-start.5 = (f32[32]{0:T(128)S(1)}, f32[32]{0:T(128)}, u32[]{:S(2)}) copy-start(f32[32]{0:T(128)} %param.13) | copy-start | bytes 388
  1.6 13.5 %collective-permute-start = (bf16[384,64]{1,0:T(8,128)(2,1)S(1)}, bf16[384,64]{1,0:T(8,128)(2,1)S(1)}, u32[]{:S(2)}, u32[]{:S(2)}) collective-permute-start(bf16[384,64]{1,0:T(8,128)(2,1)S(1)} %bitcast.36), channel_id=1, source_target_pairs={{0,16},{16,0},{1,17},{17,1},{2,18},{18,2},{3,19},{19,3},{4,20},{20... | collective-permute-start | bytes 147464 | tf_op jit(solution)/shard_map/ppermute | solution.py:283
  5.3 24.3 %copy-start.1 = (bf16[640,64]{0,1:T(8,128)(2,1)S(1)}, bf16[640,64]{0,1:T(8,128)(2,1)}, u32[]{:S(2)}) copy-start(bf16[640,64]{0,1:T(8,128)(2,1)} %param.11) | copy-start | bytes 245764
  9.7 9.1 %collective-permute-start.3 = (bf16[3,64,640]{2,1,0:T(8,128)(2,1)}, bf16[3,64,640]{2,1,0:T(8,128)(2,1)S(1)}, u32[]{:S(2)}, u32[]{:S(2)}) collective-permute-start(bf16[3,64,640]{2,1,0:T(8,128)(2,1)} %fold.1), channel_id=1, source_target_pairs={{0,4},{4,0},{8,12},{12,8},{1,5},{5,1},{9,13},{13,9},{2,6},{6,2},{1... | collective-permute-start | bytes 737288 | tf_op jit(solution)/shard_map/ppermute | solution.py:53
  15.1 8.2 %collective-permute-start.1 = (bf16[192,64]{1,0:T(8,128)(2,1)S(1)}, bf16[192,64]{1,0:T(8,128)(2,1)S(1)}, u32[]{:S(2)}, u32[]{:S(2)}) collective-permute-start(bf16[192,64]{1,0:T(8,128)(2,1)S(1)} %get-tuple-element.33), channel_id=1, source_target_pairs={{0,4},{4,8},{8,12},{1,5},{5,9},{9,13},{2,6},{6,10},{10,14},{3,7},{... | collective-permute-start | bytes 73736 | tf_op jit(solution)/shard_map/ppermute | solution.py:300
  17.6 5.8 %collective-permute-start.2 = (bf16[192,64]{1,0:T(8,128)(2,1)S(1)}, bf16[192,64]{1,0:T(8,128)(2,1)S(1)}, u32[]{:S(2)}, u32[]{:S(2)}) collective-permute-start(bf16[192,64]{1,0:T(8,128)(2,1)S(1)} %get-tuple-element.34), channel_id=1, source_target_pairs={{4,0},{8,4},{12,8},{5,1},{9,5},{13,9},{6,2},{10,6},{14,10},{7,3},{... | collective-permute-start | bytes 73736 | tf_op jit(solution)/shard_map/ppermute | solution.py:301
  19.9 9.7 %collective-permute-start.4 = (bf16[3,64,640]{2,1,0:T(8,128)(2,1)S(1)}, bf16[3,64,640]{2,1,0:T(8,128)(2,1)S(1)}, u32[]{:S(2)}, u32[]{:S(2)}) collective-permute-start(bf16[3,64,640]{2,1,0:T(8,128)(2,1)S(1)} %add_convert_fusion.1), channel_id=1, source_target_pairs={{0,8},{4,12},{8,0},{12,4},{1,9},{5,13},{9,1},{13,5},{2,10},{6,14},... | collective-permute-start | bytes 737288 | tf_op jit(solution)/shard_map/ppermute | solution.py:53
  36.0 6.9 %collective-permute-start.7 = (bf16[384,64]{1,0:T(8,128)(2,1)S(1)}, bf16[384,64]{1,0:T(8,128)(2,1)S(1)}, u32[]{:S(2)}, u32[]{:S(2)}) collective-permute-start(bf16[384,64]{1,0:T(8,128)(2,1)S(1)} %get-tuple-element.13.refs_8_), channel_id=1, source_target_pairs={{0,3},{1,0},{2,1},{3,2},{4,7},{5,4},{6,5},{7,6},{8,11},{9,8},{10,9... | collective-permute-start | bytes 147464 | tf_op jit(solution)/shard_map/ppermute | solution.py:325
  39.7 8.4 %collective-permute-start.6 = (bf16[384,64]{1,0:T(8,128)(2,1)S(1)}, bf16[384,64]{1,0:T(8,128)(2,1)S(1)}, u32[]{:S(2)}, u32[]{:S(2)}) collective-permute-start(bf16[384,64]{1,0:T(8,128)(2,1)S(1)} %get-tuple-element.13.refs_8_), channel_id=1, source_target_pairs={{0,2},{1,3},{2,0},{3,1},{4,6},{5,7},{6,4},{7,5},{8,10},{9,11},{10,... | collective-permute-start | bytes 147464 | tf_op jit(solution)/shard_map/ppermute | solution.py:325
  39.7 8.4 %collective-permute-start.5 = (bf16[384,64]{1,0:T(8,128)(2,1)S(1)}, bf16[384,64]{1,0:T(8,128)(2,1)S(1)}, u32[]{:S(2)}, u32[]{:S(2)}) collective-permute-start(bf16[384,64]{1,0:T(8,128)(2,1)S(1)} %get-tuple-element.13.refs_8_), channel_id=1, source_target_pairs={{0,1},{1,2},{2,3},{3,0},{4,5},{5,6},{6,7},{7,4},{8,9},{9,10},{10,1... | collective-permute-start | bytes 147464 | tf_op jit(solution)/shard_map/ppermute | solution.py:325
  53.3 8.1 %collective-permute-start.8 = (bf16[320,128]{1,0:T(8,128)(2,1)S(1)}, bf16[320,128]{1,0:T(8,128)(2,1)S(1)}, u32[]{:S(2)}, u32[]{:S(2)}) collective-permute-start(bf16[320,128]{1,0:T(8,128)(2,1)S(1)} %attend_grad.1), channel_id=1, source_target_pairs={{0,4},{4,0},{8,12},{12,8},{1,5},{5,1},{9,13},{13,9},{2,6},{6,2},{1... | collective-permute-start | bytes 245768 | tf_op jit(solution)/shard_map/ppermute | solution.py:53
  61.4 19.8 %copy-start.2 = (bf16[320,128]{1,0:T(8,128)(2,1)}, bf16[320,128]{1,0:T(8,128)(2,1)S(1)}, u32[]{:S(2)}) copy-start(bf16[320,128]{1,0:T(8,128)(2,1)S(1)} %add_convert_fusion.3) | copy-start | bytes 245764
  61.4 28.8 %collective-permute-start.9 = (bf16[320,128]{1,0:T(8,128)(2,1)S(1)}, bf16[320,128]{1,0:T(8,128)(2,1)S(1)}, u32[]{:S(2)}, u32[]{:S(2)}) collective-permute-start(bf16[320,128]{1,0:T(8,128)(2,1)S(1)} %add_convert_fusion.3), channel_id=1, source_target_pairs={{0,8},{4,12},{8,0},{12,4},{1,9},{5,13},{9,1},{13,5},{2,10},{6,14},... | collective-permute-start | bytes 245768 | tf_op jit(solution)/shard_map/ppermute | solution.py:53
  79.4 14.3 %collective-permute-start.11 = (bf16[1920,128]{1,0:T(8,128)(2,1)}, bf16[1920,128]{1,0:T(8,128)(2,1)S(1)}, u32[]{:S(2)}, u32[]{:S(2)}) collective-permute-start(bf16[1920,128]{1,0:T(8,128)(2,1)} %convert_element_type.91), channel_id=1, source_target_pairs={{0,16},{16,0},{1,17},{17,1},{2,18},{18,2},{3,19},{19,3},{4,20},{20... | collective-permute-start | bytes 1474568 | tf_op jit(solution)/shard_map/ppermute | solution.py:294
  81.2 23.0 %collective-permute-start.12 = (bf16[1920,128]{1,0:T(8,128)(2,1)}, bf16[1920,128]{1,0:T(8,128)(2,1)S(1)}, u32[]{:S(2)}, u32[]{:S(2)}) collective-permute-start(bf16[1920,128]{1,0:T(8,128)(2,1)} %convert_element_type.92), channel_id=1, source_target_pairs={{0,16},{16,0},{1,17},{17,1},{2,18},{18,2},{3,19},{19,3},{4,20},{20... | collective-permute-start | bytes 1474568 | tf_op jit(solution)/shard_map/ppermute | solution.py:294
  84.8 29.9 %collective-permute-start.13 = (bf16[1920,128]{1,0:T(8,128)(2,1)}, bf16[1920,128]{1,0:T(8,128)(2,1)S(1)}, u32[]{:S(2)}, u32[]{:S(2)}) collective-permute-start(bf16[1920,128]{1,0:T(8,128)(2,1)} %convert_element_type.93), channel_id=1, source_target_pairs={{0,16},{16,0},{1,17},{17,1},{2,18},{18,2},{3,19},{19,3},{4,20},{20... | collective-permute-start | bytes 1474568 | tf_op jit(solution)/shard_map/ppermute | solution.py:294
  87.5 37.8 %collective-permute-start.14 = (bf16[1920,128]{1,0:T(8,128)(2,1)}, bf16[1920,128]{1,0:T(8,128)(2,1)}, u32[]{:S(2)}, u32[]{:S(2)}) collective-permute-start(bf16[1920,128]{1,0:T(8,128)(2,1)} %convert_element_type.94), channel_id=1, source_target_pairs={{0,16},{16,0},{1,17},{17,1},{2,18},{18,2},{3,19},{19,3},{4,20},{20... | collective-permute-start | bytes 1474568 | tf_op jit(solution)/shard_map/ppermute | solution.py:294
  90.2 0.6 copy-start.3
  90.9 44.3 %collective-permute-start.10 = (bf16[1920,128]{1,0:T(8,128)(2,1)}, bf16[1920,128]{1,0:T(8,128)(2,1)}, u32[]{:S(2)}, u32[]{:S(2)}) collective-permute-start(bf16[1920,128]{1,0:T(8,128)(2,1)} %convert_element_type.90), channel_id=1, source_target_pairs={{0,16},{16,0},{1,17},{17,1},{2,18},{18,2},{3,19},{19,3},{4,20},{20... | collective-permute-start | bytes 1474568 | tf_op jit(solution)/shard_map/ppermute | solution.py:294
  91.4 43.8 %slice-start = ((s8[4915200]{0:T(1024)(128)(4,1)}), s8[720896]{0:T(1024)(128)(4,1)S(1)}, s32[]{:S(2)}) async-start(s8[4915200]{0:T(1024)(128)(4,1)} %bitcast.20), calls=%async_computation | async-start | bytes 1441792
  125.4 9.8 %slice-start.1 = ((s8[4915200]{0:T(1024)(128)(4,1)}), s8[4194304]{0:T(1024)(128)(4,1)S(1)}, s32[]{:S(2)}) async-start(s8[4915200]{0:T(1024)(128)(4,1)} %bitcast.20), calls=%async_computation.1 | async-start | bytes 8388608

commit v2 on v1

v2 whole, which is shorter than its diff:
```python
import functools

import jax
import jax.numpy as jnp
from jax import lax
from jax.experimental import pallas as pl
from jax.experimental.pallas import tpu as pltpu
from jax.sharding import PartitionSpec as P

HD = 128
TILE = 192
STEPS = 50
CH = 64
WINDOW = 640
ONE_LANE = 64
BIAS_LANE = 65
LOW_LANE = 66

SHIFT_FACTOR = 5.0
NOISE_LEVEL = 0.7
MOMENTUM_DECAY = 0.9
LEARNING_RATE = 0.004
LOSS_SCALE = 16384.0
REWARD_FLOOR = 0.1
MASKED = -1e30
LOG2E = 1.4426950408889634

F32 = jnp.float32
BF16 = jnp.bfloat16
NT = (((1,), (1,)), ((), ()))
TN = (((0,), (0,)), ((), ()))
NN = (((1,), (0,)), ((), ()))


def dot(a, b, dims=NN):
    return lax.dot_general(a, b, dims, preferred_element_type=F32)


def sigma_at(index, total_steps):
    fraction = index.astype(F32) / total_steps
    return SHIFT_FACTOR * fraction / (1.0 + (SHIFT_FACTOR - 1.0) * fraction)


def advantage_of(rewards, group_ids):
    members = (group_ids == group_ids[:, 0:1]).astype(F32)
    member_total = jnp.sum(members, axis=1, keepdims=True)
    group_mean = jnp.sum(members * rewards, axis=1, keepdims=True) / member_total
    spread = jnp.sqrt(jnp.sum(members * (rewards - group_mean) ** 2, axis=1, keepdims=True) / member_total)
    return (rewards[:, 0:1] - group_mean) / jnp.maximum(spread, REWARD_FLOOR)


def swap(x, axis, bit):
    return lax.ppermute(x, axis, [(i, i ^ bit) for i in range(lax.axis_size(axis))])


def butterfly(x, axis):
    bit = 1
    while bit < lax.axis_size(axis):
        x = (x.astype(F32) + swap(x, axis, bit).astype(F32)).astype(x.dtype)
        bit *= 2
    return x


def fold_kernel(at_ref, e_ref, w_ref, o_ref, et_ref):
    o_ref[0] = dot(e_ref[...], w_ref[0]).astype(BF16)

    @pl.when(pl.program_id(0) == 0)
    def _():
        et_ref[...] = e_ref[...].astype(F32).T.astype(BF16)


def fold(seq, w_embed, w):
    _, rows, width = w.shape
    return pl.pallas_call(
        fold_kernel,
        grid_spec=pltpu.PrefetchScalarGridSpec(
            num_scalar_prefetch=1,
            grid=(3,),
            in_specs=[
                pl.BlockSpec((CH, rows), lambda m, at: (0, at[0])),
                pl.BlockSpec((1, rows, width), lambda m, at: (m, 0, 0)),
            ],
            out_specs=[
                pl.BlockSpec((1, CH, width), lambda m, at: (m, 0, 0)),
                pl.BlockSpec((rows, CH), lambda m, at: (0, 0)),
            ],
        ),
        out_shape=[jax.ShapeDtypeStruct((3, CH, width), BF16), jax.ShapeDtypeStruct((rows, CH), BF16)],
        name="fold",
    )(seq, w_embed, w)


def narrow_kernel(sizes, stride, unit, mom_ref, *out_refs):
    step = pl.program_id(0)
    start = 0
    for size, ref in zip(sizes, out_refs):

        @pl.when((step >= start) & (step < start + size))
        def _():
            for q in range(stride):
                ref[0, q] = (MOMENTUM_DECAY * mom_ref[pl.ds(q, unit, stride=stride), :]).astype(BF16)

        start += size


def narrow(mom, first, sizes, stride, unit):
    starts = [sum(sizes[:k]) for k in range(len(sizes))]
    return pl.pallas_call(
        functools.partial(narrow_kernel, sizes, stride, unit),
        grid=(sum(sizes),),
        in_specs=[pl.BlockSpec((unit * stride, HD), lambda i: (first + i, 0))],
        out_specs=[
            pl.BlockSpec((1, stride, unit, HD), lambda i, a=a, n=n: (jnp.clip(i - a, 0, n - 1), 0, 0, 0))
            for a, n in zip(starts, sizes)
        ],
        out_shape=[jax.ShapeDtypeStruct((n, stride, unit, HD), BF16) for n in sizes],
        name="narrow",
    )(mom)


def forward_kernel(tiles, heads, win_ref, m_ref, wot_ref, e_ref, u_ref, il_ref, pred_ref, mk_ref, att_ref):
    mk_ref[...] = jnp.zeros_like(mk_ref)
    mk_ref[0:CH, :] = m_ref[1]
    lane = lax.broadcasted_iota(jnp.int32, (TILE, HD), 1)
    unit = jnp.where(lane == BIAS_LANE, 1.0, 0.0)
    factor = LOG2E * HD ** (-0.5)
    for j in range(tiles):
        own = win_ref[j, TILE : 2 * TILE, 0:CH]
        queries = dot(own, m_ref[0]).astype(BF16)
        keys = win_ref[j]
        for h in range(heads):
            cols = slice(h * HD, (h + 1) * HD)
            t = dot(queries[:, cols], mk_ref[:, cols], NT) * factor + unit
            s = dot(t.astype(BF16), keys, NT)
            e = jnp.exp2(s - jnp.max(s, axis=1, keepdims=True)).astype(BF16)
            at = slice((j * heads + h) * TILE, (j * heads + h + 1) * TILE)
            e_ref[at, :] = e
            u = dot(e, keys)
            inv = 1.0 / u[:, ONE_LANE : ONE_LANE + 1]
            u = (u * inv).astype(BF16)
            u_ref[at, :] = u
            il_ref[at, :] = jnp.broadcast_to(inv, (TILE, HD))
            att_ref[j * TILE : (j + 1) * TILE, cols] = dot(u[:, 0:CH], m_ref[2, :, cols]).astype(BF16)
    pred_ref[...] = dot(att_ref[...], wot_ref[...], NT).astype(BF16)


def forward(win, m, wot, tiles, heads):
    rows = tiles * heads * TILE
    width = heads * HD
    vm = pl.BlockSpec(memory_space=pltpu.VMEM)
    return pl.pallas_call(
        functools.partial(forward_kernel, tiles, heads),
        in_specs=[vm] * 3,
        out_specs=[vm] * 4,
        out_shape=[
            jax.ShapeDtypeStruct((rows, WINDOW), BF16),
            jax.ShapeDtypeStruct((rows, HD), BF16),
            jax.ShapeDtypeStruct((rows, HD), F32),
            jax.ShapeDtypeStruct((tiles * TILE, CH), BF16),
        ],
        scratch_shapes=[pltpu.VMEM((HD, width), BF16), pltpu.VMEM((tiles * TILE, width), BF16)],
        compiler_params=pltpu.CompilerParams(vmem_limit_bytes=48 * 1024 * 1024),
        name="attend",
    )(win, m, wot)


def backward_kernel(tiles, heads, tokens_all, *refs):
    (time_ref, rewards_ref, groups_ref, win_ref, m_ref, wot_ref, e_ref, u_ref, il_ref, next_ref) = refs[:10]
    pred_refs = refs[10:-3]
    zy_ref, mv_ref, v_ref = refs[-3:]
    width = heads * HD
    mv_ref[...] = jnp.zeros_like(mv_ref)
    mv_ref[0:CH, :] = m_ref[2]
    lane = lax.broadcasted_iota(jnp.int32, (TILE, HD), 1)
    half_lane = lax.broadcasted_iota(jnp.int32, (CH, HD), 1)
    scale = HD ** (-0.5)
    advantage = advantage_of(rewards_ref[...], groups_ref[...])
    index = jnp.full((1, 1), time_ref[0], jnp.int32)
    sigma_now = sigma_at(index, STEPS)
    step_size = sigma_at(index - 1, STEPS) - sigma_now
    coefficient = advantage * LOSS_SCALE * (1.0 - sigma_now) / (NOISE_LEVEL**2 * sigma_now * tokens_all)
    pred = pred_refs[0][...].astype(F32)
    for ref in pred_refs[1:]:
        pred = pred + ref[...].astype(F32)
    pgs = []
    for j in range(tiles):
        at = slice(j * TILE, (j + 1) * TILE)
        now = win_ref[j, TILE : 2 * TILE, 0:CH].astype(F32)
        step_mean = now + step_size * pred[at]
        pg = (coefficient * (next_ref[at, :].astype(F32) - step_mean)).astype(BF16)
        pgs.append(pg)
        ag = dot(pg, wot_ref[...]).astype(BF16)
        keys = win_ref[j]
        for h in range(heads):
            cols = slice(h * HD, (h + 1) * HD)
            rows = slice((j * heads + h) * TILE, (j * heads + h + 1) * TILE)
            w = dot(ag[:, cols], mv_ref[:, cols], NT).astype(BF16).astype(F32)
            u = u_ref[rows, :].astype(F32)
            row_dot = jnp.sum(w * u, axis=1, keepdims=True)
            factor = scale * il_ref[rows, :]
            w = w * factor
            row_dot = row_dot * factor
            high = row_dot.astype(BF16).astype(F32)
            low = row_dot - high
            w = jnp.where(lane == ONE_LANE, -high, jnp.where(lane == LOW_LANE, -low, w))
            x = dot(w.astype(BF16), keys, NT)
            ds = (e_ref[rows, :].astype(F32) * x).astype(BF16)
            v_ref[h, at, :] = dot(ds, keys).astype(BF16)
    pg_all = jnp.concatenate(pgs, axis=0)
    pg_all = jnp.concatenate([jnp.zeros_like(pg_all), pg_all], axis=1)
    own = jnp.concatenate([win_ref[j, TILE : 2 * TILE, 0:CH] for j in range(tiles)], axis=0)
    for h in range(heads):
        z = dot(own, v_ref[h], TN)
        u = jnp.concatenate(
            [u_ref[(j * heads + h) * TILE : (j * heads + h + 1) * TILE, 0:CH] for j in range(tiles)], axis=0
        )
        y = dot(u, pg_all, TN)
        zy_ref[h * CH : (h + 1) * CH, :] = jnp.where(half_lane < CH, z, y).astype(BF16)


def backward(timestep, rewards, group_ids, win, m, wot, e, u, il, latent_next, preds, tiles, heads, tokens_all):
    vm = pl.BlockSpec(memory_space=pltpu.VMEM)
    width = heads * HD
    return pl.pallas_call(
        functools.partial(backward_kernel, tiles, heads, tokens_all),
        in_specs=[pl.BlockSpec(memory_space=pltpu.SMEM)] + [vm] * (9 + len(preds)),
        out_specs=vm,
        out_shape=jax.ShapeDtypeStruct((heads * CH, HD), BF16),
        scratch_shapes=[pltpu.VMEM((HD, width), BF16), pltpu.VMEM((heads, tiles * TILE, HD), BF16)],
        compiler_params=pltpu.CompilerParams(vmem_limit_bytes=48 * 1024 * 1024),
        name="attend_grad",
    )(timestep, rewards, group_ids, win, m, wot, e, u, il, latent_next, *preds)


def update_kernel(heads, sizes, unit, later, *refs):
    role_ref, et_ref, mom_ref, w_ref = refs[:4]
    recv_refs = refs[4 : 4 + len(sizes)]
    rest = refs[4 + len(sizes) :]
    if later:
        g_ref = rest[0]
        onm_ref, ow_ref, gs_ref, fs_ref = rest[3:]
    else:
        zy_ref, m_ref, wot_ref, onm_ref, ow_ref, g_ref, gs_ref, fs_ref = rest
    width = heads * HD
    stride = 3 * heads
    step = pl.program_id(0)
    role = role_ref[0]

    if not later:

        @pl.when(step == 0)
        def _():
            for h in range(heads):
                cols = slice(h * HD, (h + 1) * HD)
                zy = zy_ref[h * CH : (h + 1) * CH, :]
                z = zy[:, 0:CH]
                y = zy[:, CH : 2 * CH]
                g_ref[0, :, cols] = dot(z, m_ref[1, :, cols]).astype(BF16)
                g_ref[1, :, cols] = dot(z, m_ref[0, :, cols], TN).astype(BF16)
                g_ref[2, :, cols] = dot(y, wot_ref[:, cols]).astype(BF16)

    def run(recv_ref):
        for part in range(3):
            g = dot(et_ref[...], g_ref[part])
            for b in range(heads):
                cols = slice(b * HD, (b + 1) * HD)
                at = pl.ds(part * heads + b, unit, stride=stride)
                gs_ref[...] = g[:, cols]
                own = MOMENTUM_DECAY * mom_ref[at, :] + gs_ref[pl.ds(role, unit, stride=2), :]
                other = recv_ref[0, part * heads + b].astype(F32) + gs_ref[pl.ds(1 - role, unit, stride=2), :]
                onm_ref[at, :] = own
                fs_ref[pl.ds(role, unit, stride=2), :] = own
                fs_ref[pl.ds(1 - role, unit, stride=2), :] = other
                ow_ref[part, :, cols] = (w_ref[part, :, cols].astype(F32) - LEARNING_RATE * fs_ref[...]).astype(BF16)

    start = 0
    for size, ref in zip(sizes, recv_refs):

        @pl.when((step >= start) & (step < start + size))
        def _():
            run(ref)

        start += size


def update(role, et, mom, w, received, first, unit, heads, sources=None, before=None):
    sizes = [a.shape[0] for a in received]
    starts = [sum(sizes[:k]) for k in range(len(sizes))]
    width = heads * HD
    stride = 3 * heads
    any_space = pl.BlockSpec(memory_space=pl.ANY)
    whole = lambda a: pl.BlockSpec(a.shape, lambda i: (0,) * a.ndim)
    args = [role, et, mom, w, *received]
    in_specs = [
        pl.BlockSpec(memory_space=pltpu.SMEM),
        pl.BlockSpec((2 * unit, CH), lambda i: (first + i, 0)),
        pl.BlockSpec((unit * stride, HD), lambda i: (first + i, 0)),
        pl.BlockSpec((3, 2 * unit, width), lambda i: (0, first + i, 0)),
    ] + [
        pl.BlockSpec((1, stride, unit, HD), lambda i, a=a, n=n: (jnp.clip(i - a, 0, n - 1), 0, 0, 0))
        for a, n in zip(starts, sizes)
    ]
    out_specs = [
        pl.BlockSpec((unit * stride, HD), lambda i: (first + i, 0)),
        pl.BlockSpec((3, 2 * unit, width), lambda i: (0, first + i, 0)),
    ]
    out_shape = [jax.ShapeDtypeStruct(mom.shape, F32), jax.ShapeDtypeStruct(w.shape, BF16)]
    aliases = {}
    if before is None:
        args += sources
        in_specs += [whole(a) for a in sources]
        g_shape = (3, CH, width)
        out_specs.append(pl.BlockSpec(g_shape, lambda i: (0, 0, 0)))
        out_shape.append(jax.ShapeDtypeStruct(g_shape, BF16))
    else:
        new_mom, new_w, g = before
        aliases = {len(args) + 1: 0, len(args) + 2: 1}
        args += [g, new_mom, new_w]
        in_specs += [whole(g), any_space, any_space]
    return pl.pallas_call(
        functools.partial(update_kernel, heads, sizes, unit, before is not None),
        grid=(sum(sizes),),
        in_specs=in_specs,
        out_specs=out_specs,
        out_shape=out_shape,
        input_output_aliases=aliases,
        scratch_shapes=[pltpu.VMEM((2 * unit, HD), F32), pltpu.VMEM((2 * unit, HD), F32)],
        compiler_params=pltpu.CompilerParams(vmem_limit_bytes=48 * 1024 * 1024),
        name="update",
    )(*args)


def exchange(x):
    return lax.ppermute(x, "role", [(0, 1), (1, 0)])


def body(rollout, w_embed, w_qkv, w_out, momentum, rewards, group_ids, timestep):
    seq_count = lax.axis_size("seq")
    seq_index = lax.axis_index("seq")
    role_index = lax.axis_index("role")
    rows_dev = w_qkv.shape[0]
    width = w_qkv.shape[2]
    heads = width // HD
    tok_dev = rollout.shape[1]
    tiles = tok_dev // TILE
    pair_rows = rows_dev // 2

    mine = rollout[0]
    other = exchange(mine)
    latent_now = jnp.where(role_index == 0, mine, other)
    latent_next = jnp.where(role_index == 0, other, mine)

    stride = 3 * heads
    mom = momentum.reshape(pair_rows * stride, HD)
    unit = pair_rows // 10
    w = w_qkv.transpose(1, 0, 2)
    (piece,) = narrow(mom, 0, (3,), stride, unit)
    w_embed, piece = lax.optimization_barrier((w_embed, piece))
    received = [exchange(piece)]
    if rows_dev % HD == 0:
        m, et = fold(seq_index[None], w_embed, w)
    else:
        m, et = fold(
            jnp.zeros((1,), jnp.int32), lax.dynamic_slice_in_dim(w_embed, seq_index * rows_dev, rows_dev, axis=1), w
        )
    mom_late, m = lax.optimization_barrier((mom, m))
    pieces = narrow(mom_late, 3, (3, 3, 1), stride, unit)
    received += [exchange(p) for p in pieces]
    m = butterfly(m, "seq")

    left = lax.ppermute(latent_now[tok_dev - TILE :], "seq", [(i, i + 1) for i in range(seq_count - 1)])
    right = lax.ppermute(latent_now[:TILE], "seq", [(i + 1, i) for i in range(seq_count - 1)])
    near = jnp.concatenate([left, latent_now, right, jnp.zeros((WINDOW - 3 * TILE, CH), BF16)], axis=0)
    key_tile = jnp.arange(near.shape[0], dtype=jnp.int32) // TILE + seq_index * tiles - 1
    inside = (key_tile >= 0) & (key_tile < seq_count * tiles)
    windows = []
    for j in range(tiles):
        seen = inside[j * TILE : j * TILE + WINDOW] & (jnp.arange(WINDOW) < 3 * TILE)
        bias = jnp.where(seen, 0.0, MASKED).astype(BF16)[:, None]
        ones = jnp.ones((WINDOW, 1), BF16)
        rest = jnp.zeros((WINDOW, HD - LOW_LANE - 1), BF16)
        windows.append(jnp.concatenate([near[j * TILE : j * TILE + WINDOW], ones, bias, ones, rest], axis=1))
    win = jnp.stack(windows)

    wot = w_out.T
    e, u, il, partial_pred = forward(win, m, wot, tiles, heads)
    mp_count = lax.axis_size("mp")
    preds = [partial_pred] + [
        lax.ppermute(partial_pred, "mp", [(i, (i + d) % mp_count) for i in range(mp_count)])
        for d in range(1, mp_count)
    ]
    zy = backward(
        timestep, rewards[None], group_ids[None], win, m, wot, e, u, il, latent_next, preds, tiles, heads, tok_dev * seq_count
    )
    zy = butterfly(zy, "seq")

    role = role_index[None]
    first = update(role, et, mom, w, received[:-1], 0, unit, heads, sources=[zy, m, wot])
    nm, nw = update(role, et, mom, w, received[-1:], 9, unit, heads, before=first)
    return nm.reshape(momentum.shape), nw.transpose(1, 0, 2)


def solution(mesh):
    in_specs = (
        P("role", "seq", None),
        P(),
        P("seq", None, "mp"),
        P("mp", None),
        P("seq", "role", None, "mp"),
        P(),
        P(),
        P(),
    )
    out_specs = (P("seq", "role", None, "mp"), P("seq", None, "mp"))
    return jax.shard_map(body, mesh=mesh, in_specs=in_specs, out_specs=out_specs, check_vma=False)
```

time: 140 us -> 84.1 us (0.60)
  waiting for transfers between devices: 45.4 us -> 15.2 us
  local copies, waits for them, and re-layouts: 29 us -> 6.01 us
  Pallas kernels: 28.7 us -> 39 us
  other arithmetic: 11.7 us -> 3.1 us
  between operations: 4.4 us -> 1.53 us
  starting transfers between devices: 19.8 us -> 18.4 us
    ppermute x6 -> x5, waiting for transfers between devices: 32.8 us -> 0.01 us  [exchange(): return lax.ppermute(x, 'role', [(0, 1), (1, 0)])]
    slice x1 -> x0, local copies, waits for them, and re-layouts: 15.5 us -> none  [body(): piece = lax.slice_in_dim(mom, c * lin, (c + 1) * lin, axis=0).astype(BF16)]
    pallas_call x4 -> x6, Pallas kernels: 22.3 us -> 32.7 us  [the longest x2 14.2 us: update(): pl.pallas_call(functools.partial(update_kernel, heads, sizes, unit, befor...]
    convert_element_type x5 -> x0, local copies, waits for them, and re-layouts: 8.95 us -> none  [body(): piece = lax.slice_in_dim(mom, c * lin, (c + 1) * lin, axis=0).astype(BF16)]
    another operation x2 -> x0, other arithmetic: 8.09 us -> none
    concatenate x2, local copies, waits for them, and re-layouts: 0.65 us -> 3.27 us  [body(): jnp.concatenate([near[j * TILE:j * TILE + WINDOW], ones, bias, ones, rest...]
    ppermute x3, waiting for transfers between devices: 7.3 us -> 9.33 us  [body(): lax.ppermute(partial_pred, 'mp', [(i, (i + d) % mp_count) for i in range(...]
    unnamed x18 -> x17, local copies, waits for them, and re-layouts: 2.84 us -> 0.95 us
  transfers between devices with their start and end apart: 15 -> 14, of which waited for: 8 -> 6; matrix products, arithmetic and copies ran while one was open for 28% -> 10% of each run, Pallas kernels for 10% -> 44%
where the time goes in v2:
time: 84.1 us; the launch traced here: 83.3 us
  Pallas kernels  39 us (46%)
  starting transfers between devices  18.4 us (22%)
  waiting for transfers between devices  15.2 us (18%)
  local copies, waits for them, and re-layouts  6.01 us (7%)
  other arithmetic  3.1 us (4%)
  between operations  1.53 us (2%)
    pallas_call x2, Pallas kernels, update(): pl.pallas_call(functools.partial(update_kernel, heads, sizes, unit, befor...  14.2 us
    ppermute x3, waiting for transfers between devices, body(): lax.ppermute(partial_pred, 'mp', [(i, (i + d) % mp_count) for i in range(...  9.33 us
    pallas_call x2, Pallas kernels, narrow(): pl.pallas_call(functools.partial(narrow_kernel, sizes, stride, unit), gri...  8.76 us
    ppermute x5, starting transfers between devices, exchange(): return lax.ppermute(x, 'role', [(0, 1), (1, 0)])  6.72 us
    pallas_call x1, Pallas kernels, forward(): pl.pallas_call(functools.partial(forward_kernel, tiles, heads), in_specs=...  6.35 us
    ppermute x4, waiting for transfers between devices, swap(): lax.ppermute(x, axis, [(i, i ^ bit) for i in range(lax.axis_size(axis))])  5.86 us
    pallas_call x1, Pallas kernels, backward(): pl.pallas_call(functools.partial(backward_kernel, tiles, heads, tokens_al...  4.97 us
    ppermute x4, starting transfers between devices, swap(): lax.ppermute(x, axis, [(i, i ^ bit) for i in range(lax.axis_size(axis))])  4.77 us
  transfers between devices with their start and end apart: 14, of which 6 were waited for; matrix products, arithmetic and copies ran while one was open for 10% of the time, Pallas kernels for 44%

profile of v2, /device:TPU:0, one launch (start us, length us, event | category | flops | bytes accessed | tf_op | source)
XLA Modules:
  0.0 83.3 jit_solution(13877871415234335449)
XLA Ops:
  0.6 0.9 %copy.14 = bf16[1,384,64]{2,1,0:T(8,128)(2,1)S(1)} copy(bf16[1,384,64]{1,2,0:T(8,128)(2,1)} %param.8) | data formatting | bytes 98304 | tf_op args[0]
  1.5 3.0 %collective-permute-start.4 = (bf16[384,64]{1,0:T(8,128)(2,1)S(1)}, bf16[384,64]{1,0:T(8,128)(2,1)S(1)}, u32[]{:S(2)}, u32[]{:S(2)}) collective-permute-start(bf16[384,64]{1,0:T(8,128)(2,1)S(1)} %bitcast.32), channel_id=1, source_target_pairs={{0,16},{16,0},{1,17},{17,1},{2,18},{18,2},{3,19},{19,3},{4,20},{20... | collective-permute-start | bytes 147464 | tf_op jit(solution)/shard_map/ppermute | solution.py:334
  4.6 3.1 %narrow.2 = bf16[3,15,64,128]{3,2,1,0:T(8,128)(2,1)} custom-call(f32[9600,128]{1,0:T(8,128)} %bitcast.14), custom_call_target="tpu_custom_call" | custom-call | tf_op jit(solution)/shard_map/narrow/pallas_call | solution.py:108
  7.6 4.7 %fold.1 = (bf16[3,64,640]{2,1,0:T(8,128)(2,1)}, bf16[1280,64]{1,0:T(8,128)(2,1)}) custom-call(s32[1]{0:T(128)} %bitcast.1.at_ref, bf16[64,5120]{1,0:T(8,128)(2,1)} %e_ref, bf16[3,1280,640]{2,1,0:T(8,128)(2,1)} %bitcast.25), custom_call_target="tpu_custom_call" | custom-call | tf_op jit(solution)/shard_map/fold/pallas_call | solution.py:74
  12.3 0.0 copy-start.4
  12.3 0.0 copy-start.1
  12.3 0.0 copy-start.2
  12.4 0.0 copy-start.3
  12.4 0.1 collective-permute-start.7
  12.5 0.1 collective-permute-start.1
  12.6 5.7 %narrow.3 = (bf16[3,15,64,128]{3,2,1,0:T(8,128)(2,1)}, bf16[3,15,64,128]{3,2,1,0:T(8,128)(2,1)}, bf16[1,15,64,128]{3,2,1,0:T(8,128)(2,1)}) custom-call(f32[9600,128]{1,0:T(8,128)} %bitcast.15), custom_call_target="tpu_custom_call" | custom-call | tf_op jit(solution)/shard_map/narrow/pallas_call | solution.py:108
  18.2 2.0 %collective-permute-start.2 = (bf16[3,15,64,128]{3,2,1,0:T(8,128)(2,1)}, bf16[3,15,64,128]{3,2,1,0:T(8,128)(2,1)S(1)}, u32[]{:S(2)}, u32[]{:S(2)}) collective-permute-start(bf16[3,15,64,128]{3,2,1,0:T(8,128)(2,1)} %get-tuple-element.26), channel_id=1, source_target_pairs={{0,16},{16,0},{1,17},{17,1},{2,18},{18,2},{3,19},{19,3},{4,20},{20... | collective-permute-start | bytes 2211848 | tf_op jit(solution)/shard_map/ppermute | solution.py:334
  20.2 0.1 collective-permute-start.3
  20.3 0.1 select_convert_fusion.1
  20.4 0.8 broadcast_in_dim.40
  21.2 0.8 broadcast_in_dim.41
  22.0 0.1 pad.4.clone
  22.1 0.0 collective-permute-done.4
  22.1 1.8 %collective-permute-start.5 = (bf16[192,64]{1,0:T(8,128)(2,1)S(1)}, bf16[192,64]{1,0:T(8,128)(2,1)S(1)}, u32[]{:S(2)}, u32[]{:S(2)}) collective-permute-start(bf16[192,64]{1,0:T(8,128)(2,1)S(1)} %get-tuple-element.46), channel_id=1, source_target_pairs={{0,4},{4,8},{8,12},{1,5},{5,9},{9,13},{2,6},{6,10},{10,14},{3,7},{... | collective-permute-start | bytes 73736 | tf_op jit(solution)/shard_map/ppermute | solution.py:371
  23.9 0.0 collective-permute-done.7
  23.9 1.3 %collective-permute-start.6 = (bf16[192,64]{1,0:T(8,128)(2,1)S(1)}, bf16[192,64]{1,0:T(8,128)(2,1)S(1)}, u32[]{:S(2)}, u32[]{:S(2)}) collective-permute-start(bf16[192,64]{1,0:T(8,128)(2,1)S(1)} %get-tuple-element.47), channel_id=1, source_target_pairs={{4,0},{8,4},{12,8},{5,1},{9,5},{13,9},{6,2},{10,6},{14,10},{7,3},{... | collective-permute-start | bytes 73736 | tf_op jit(solution)/shard_map/ppermute | solution.py:372
  25.2 0.0 copy-done.4
  25.2 0.1 add_convert_fusion.1
  25.3 0.0 collective-permute-done.5
  25.3 4.6 %collective-permute-start.8 = (bf16[3,64,640]{2,1,0:T(8,128)(2,1)S(1)}, bf16[3,64,640]{2,1,0:T(8,128)(2,1)}, u32[]{:S(2)}, u32[]{:S(2)}) collective-permute-start(bf16[3,64,640]{2,1,0:T(8,128)(2,1)S(1)} %add_convert_fusion.1), channel_id=1, source_target_pairs={{0,8},{4,12},{8,0},{12,4},{1,9},{5,13},{9,1},{13,5},{2,10},{6,14},... | collective-permute-start | bytes 737288 | tf_op jit(solution)/shard_map/ppermute | solution.py:53
  29.9 0.0 collective-permute-done.6
  29.9 0.9 %pad_maximum_fusion.1 = (bf16[640,64]{1,0:T(8,128)(2,1)}, bf16[640,64]{1,0:T(8,128)(2,1)}) fusion(bf16[192,64]{1,0:T(8,128)(2,1)S(1)} %collective-permute-done.6, bf16[384,64]{1,0:T(8,128)(2,1)S(1)} %get-tuple-element.43, bf16[192,64]{1,0:T(8,128)(2,1)S(1)} %collective-permute-done.5, bf16[640]{0:T(1024)(128)(2,1)S(1)} %pad.4.clone), kind=kLoop, calls=%fused_computation.3 | loop fusion | flops 491520 | bytes 263424 | tf_op jit(solution)/shard_map/concatenate | solution.py:373
  30.7 0.0 copy-start
  30.8 1.3 %concatenate.14 = bf16[640,128]{1,0:T(8,128)(2,1)S(1)} concatenate(bf16[640,64]{1,0:T(8,128)(2,1)} %get-tuple-element.44, bf16[640,1]{1,0:T(8,128)(2,1)S(1)} %broadcast.13, bf16[640,1]{1,0:T(8,128)(2,1)} %broadcast_in_dim.40, bf16[640,1]{1,0:T(8,128)(2,1)S(1)} %broadcast.13, bf16[640,61]{1,0:T(8,128)(2,1)S(1)} %broadcast.16), dimensions={1} | concatenate | bytes 327680 | tf_op jit(solution)/shard_map/concatenate | solution.py:382
  32.1 1.9 %concatenate.16 = bf16[640,128]{1,0:T(8,128)(2,1)} concatenate(bf16[640,64]{1,0:T(8,128)(2,1)} %get-tuple-element.45, bf16[640,1]{1,0:T(8,128)(2,1)S(1)} %broadcast.13, bf16[640,1]{1,0:T(8,128)(2,1)} %broadcast_in_dim.41, bf16[640,1]{1,0:T(8,128)(2,1)S(1)} %broadcast.13, bf16[640,61]{1,0:T(8,128)(2,1)S(1)} %broadcast.16), dimensions={1} | concatenate | bytes 327680 | tf_op jit(solution)/shard_map/concatenate | solution.py:382
  34.1 0.0 copy-start.5
  34.1 1.0 %pad_maximum_fusion.win_ref.refs_3_ = bf16[2,640,128]{2,1,0:T(8,128)(2,1)S(1)} fusion(bf16[1,640,128]{2,1,0:T(8,128)(2,1)} %bitcast.31, bf16[1,640,128]{2,1,0:T(8,128)(2,1)S(1)} %bitcast.30), kind=kLoop, calls=%fused_computation.2 | loop fusion | flops 163840 | bytes 655360 | tf_op jit(solution)/shard_map/stack | solution.py:383
  35.1 1.7 %collective-permute-done.8 = bf16[3,64,640]{2,1,0:T(8,128)(2,1)} collective-permute-done((bf16[3,64,640]{2,1,0:T(8,128)(2,1)S(1)}, bf16[3,64,640]{2,1,0:T(8,128)(2,1)}, u32[]{:S(2)}, u32[]{:S(2)}) %collective-permute-start.8) | collective-permute-done | bytes 245792 | tf_op jit(solution)/shard_map/ppermute | solution.py:53
  36.7 1.0 %add_convert_fusion.m_ref.refs_4_.refs_8_ = bf16[3,64,640]{2,1,0:T(8,128)(2,1)S(1)} fusion(bf16[3,64,640]{2,1,0:T(8,128)(2,1)} %collective-permute-done.8, bf16[3,64,640]{2,1,0:T(8,128)(2,1)S(1)} %add_convert_fusion.1), kind=kLoop, calls=%fused_computation | loop fusion | flops 491520 | bytes 737280 | tf_op jit(solution)/shard_map/convert_element_type | solution.py:59
  37.8 0.0 copy-done.1
  37.8 6.4 %attend.1 = (bf16[1920,640]{1,0:T(8,128)(2,1)S(1)}, bf16[1920,128]{1,0:T(8,128)(2,1)S(1)}, f32[1920,128]{1,0:T(8,128)S(1)}, bf16[384,64]{1,0:T(8,128)(2,1)S(1)}) custom-call(bf16[2,640,128]{2,1,0:T(8,128)(2,1)S(1)} %pad_maximum_fusion.win_ref.refs_3_, bf16[3,64,640]{2,1,0:T(8,128)(2,1)S(1)} %add_convert_fusion.m_ref.refs_4_.refs_8_, bf16[64,640]{1,0:T(8,128)(2,1)S(1)} %bitcast.20), custom_call_target="tpu_custom_call" | custom-call | tf_op jit(solution)/shard_map/attend/pallas_call | solution.py:151
  44.1 3.7 %collective-permute-start.11 = (bf16[384,64]{1,0:T(8,128)(2,1)S(1)}, bf16[384,64]{1,0:T(8,128)(2,1)S(1)}, u32[]{:S(2)}, u32[]{:S(2)}) collective-permute-start(bf16[384,64]{1,0:T(8,128)(2,1)S(1)} %get-tuple-element.32.refs_10_), channel_id=1, source_target_pairs={{0,3},{1,0},{2,1},{3,2},{4,7},{5,4},{6,5},{7,6},{8,11},{9,8},{10,9... | collective-permute-start | bytes 147464 | tf_op jit(solution)/shard_map/ppermute | solution.py:389
  47.8 0.0 collective-permute-start.10
  47.8 3.2 %collective-permute-done.11.refs_13_ = bf16[384,64]{1,0:T(8,128)(2,1)S(1)} collective-permute-done((bf16[384,64]{1,0:T(8,128)(2,1)S(1)}, bf16[384,64]{1,0:T(8,128)(2,1)S(1)}, u32[]{:S(2)}, u32[]{:S(2)}) %collective-permute-start.11) | collective-permute-done | bytes 49184 | tf_op jit(solution)/shard_map/ppermute | solution.py:389
  51.0 0.2 collective-permute-start.9
  51.9 4.0 %collective-permute-done.10.refs_12_ = bf16[384,64]{1,0:T(8,128)(2,1)S(1)} collective-permute-done((bf16[384,64]{1,0:T(8,128)(2,1)S(1)}, bf16[384,64]{1,0:T(8,128)(2,1)S(1)}, u32[]{:S(2)}, u32[]{:S(2)}) %collective-permute-start.10) | collective-permute-done | bytes 49184 | tf_op jit(solution)/shard_map/ppermute | solution.py:389
  55.9 2.1 %collective-permute-done.9.refs_11_ = bf16[384,64]{1,0:T(8,128)(2,1)S(1)} collective-permute-done((bf16[384,64]{1,0:T(8,128)(2,1)S(1)}, bf16[384,64]{1,0:T(8,128)(2,1)S(1)}, u32[]{:S(2)}, u32[]{:S(2)}) %collective-permute-start.9) | collective-permute-done | bytes 49184 | tf_op jit(solution)/shard_map/ppermute | solution.py:389
  58.0 0.0 copy-done.2
  58.0 0.0 copy-done.3
  58.0 5.0 %attend_grad.1 = bf16[320,128]{1,0:T(8,128)(2,1)S(1)} custom-call(s32[1]{0:T(128)S(6)} %copy.20.refs_0_, f32[1,32]{1,0:T(1,128)S(1)} %bitcast.23, s32[1,32]{1,0:T(1,128)S(1)} %bitcast.24, bf16[2,640,128]{2,1,0:T(8,128)(2,1)S(1)} %pad_maximum_fusion.win_ref.refs_3_, bf16[3,64,640]{2,1,0:T(8,128)(2,1)S(1)} %add_convert_fusion.m_ref.refs_4_.refs_8_, ...), custom_call_target="tpu_custom_call" | custom-call | tf_op jit(solution)/shard_map/attend_grad/pallas_call | solution.py:224
  63.0 0.1 collective-permute-start.12
  63.1 1.3 %collective-permute-done.12 = bf16[320,128]{1,0:T(8,128)(2,1)S(1)} collective-permute-done((bf16[320,128]{1,0:T(8,128)(2,1)S(1)}, bf16[320,128]{1,0:T(8,128)(2,1)S(1)}, u32[]{:S(2)}, u32[]{:S(2)}) %collective-permute-start.12) | collective-permute-done | bytes 81952 | tf_op jit(solution)/shard_map/ppermute | solution.py:53
  64.3 0.0 slice-start
  64.4 0.1 collective-permute-start.13
  64.4 0.0 copy-done.5
  64.4 1.6 %collective-permute-start = (bf16[1,15,64,128]{3,2,1,0:T(8,128)(2,1)S(1)}, bf16[1,15,64,128]{3,2,1,0:T(8,128)(2,1)S(1)}, u32[]{:S(2)}, u32[]{:S(2)}) collective-permute-start(bf16[1,15,64,128]{3,2,1,0:T(8,128)(2,1)S(1)} %copy-done.5), channel_id=1, source_target_pairs={{0,16},{16,0},{1,17},{17,1},{2,18},{18,2},{3,19},{19,3},{4,20},{20... | collective-permute-start | bytes 737288 | tf_op jit(solution)/shard_map/ppermute | solution.py:334
  66.0 2.9 %collective-permute-done.13 = bf16[320,128]{1,0:T(8,128)(2,1)S(1)} collective-permute-done((bf16[320,128]{1,0:T(8,128)(2,1)S(1)}, bf16[320,128]{1,0:T(8,128)(2,1)S(1)}, u32[]{:S(2)}, u32[]{:S(2)}) %collective-permute-start.13) | collective-permute-done | bytes 81952 | tf_op jit(solution)/shard_map/ppermute | solution.py:53
  69.0 0.0 collective-permute-done.1.refs_4_
  69.0 0.0 collective-permute-done.2.refs_5_
  69.0 0.0 collective-permute-done.3.refs_6_
  69.0 0.0 copy-done
  69.0 0.0 slice-start.1
  69.0 11.7 %update.2 = (f32[9600,128]{1,0:T(8,128)}, bf16[3,1280,640]{2,1,0:T(8,128)(2,1)}, bf16[3,64,640]{2,1,0:T(8,128)(2,1)S(1)}) custom-call(s32[1]{0:T(128)} %bitcast.refs_0_, bf16[1280,64]{1,0:T(8,128)(2,1)S(1)} %copy-done, f32[9600,128]{1,0:T(8,128)} %bitcast.16, bf16[3,1280,640]{2,1,0:T(8,128)(2,1)} %bitcast.26, ...), custom_call_target="tpu_custom_call" | custom-call | tf_op jit(solution)/shard_map/update/pallas_call | solution.py:320
  80.7 0.0 collective-permute-done.refs_4_
  80.7 0.0 slice-done
  80.7 0.0 slice-done.1
  80.7 2.6 %update.3 = (f32[9600,128]{1,0:T(8,128)}, bf16[3,1280,640]{2,1,0:T(8,128)(2,1)}) custom-call(s32[1]{0:T(128)} %bitcast.refs_0_, bf16[1280,64]{1,0:T(8,128)(2,1)S(1)} %copy-done, f32[9600,128]{1,0:T(8,128)S(1)} %bitcast.19, bf16[3,1280,640]{2,1,0:T(8,128)(2,1)} %bitcast.27, ...), custom_call_target="tpu_custom_call", output_to_operand_aliasing={{0}: (6, {}), {1}: (7, {})} | custom-call | tf_op jit(solution)/shard_map/update/pallas_call | solution.py:320
  (9 shorter events, 0.1 us)
Async XLA Ops:
  1.5 20.6 %collective-permute-start.4 = (bf16[384,64]{1,0:T(8,128)(2,1)S(1)}, bf16[384,64]{1,0:T(8,128)(2,1)S(1)}, u32[]{:S(2)}, u32[]{:S(2)}) collective-permute-start(bf16[384,64]{1,0:T(8,128)(2,1)S(1)} %bitcast.32), channel_id=1, source_target_pairs={{0,16},{16,0},{1,17},{17,1},{2,18},{18,2},{3,19},{19,3},{4,20},{20... | collective-permute-start | bytes 147464 | tf_op jit(solution)/shard_map/ppermute | solution.py:334
  12.3 12.9 %copy-start.4 = (bf16[3,64,640]{2,1,0:T(8,128)(2,1)S(1)}, bf16[3,64,640]{2,1,0:T(8,128)(2,1)}, u32[]{:S(2)}) copy-start(bf16[3,64,640]{2,1,0:T(8,128)(2,1)} %get-tuple-element.28) | copy-start | bytes 737284
  12.3 25.4 %copy-start.1 = (bf16[640,64]{0,1:T(8,128)(2,1)S(1)}, bf16[640,64]{0,1:T(8,128)(2,1)}, u32[]{:S(2)}) copy-start(bf16[640,64]{0,1:T(8,128)(2,1)} %param.11) | copy-start | bytes 245764
  12.3 45.7 %copy-start.2 = (f32[32]{0:T(128)S(1)}, f32[32]{0:T(128)}, u32[]{:S(2)}) copy-start(f32[32]{0:T(128)} %param.13) | copy-start | bytes 388
  12.4 45.7 %copy-start.3 = (s32[32]{0:T(128)S(1)}, s32[32]{0:T(128)}, u32[]{:S(2)}) copy-start(s32[32]{0:T(128)} %param.14) | copy-start | bytes 388
  12.4 11.5 %collective-permute-start.7 = (bf16[3,64,640]{2,1,0:T(8,128)(2,1)}, bf16[3,64,640]{2,1,0:T(8,128)(2,1)S(1)}, u32[]{:S(2)}, u32[]{:S(2)}) collective-permute-start(bf16[3,64,640]{2,1,0:T(8,128)(2,1)} %get-tuple-element.28), channel_id=1, source_target_pairs={{0,4},{4,0},{8,12},{12,8},{1,5},{5,1},{9,13},{13,9},{2,6},{6,2},{1... | collective-permute-start | bytes 737288 | tf_op jit(solution)/shard_map/ppermute | solution.py:53
  12.5 56.5 %collective-permute-start.1 = (bf16[3,15,64,128]{3,2,1,0:T(8,128)(2,1)}, bf16[3,15,64,128]{3,2,1,0:T(8,128)(2,1)S(1)}, u32[]{:S(2)}, u32[]{:S(2)}) collective-permute-start(bf16[3,15,64,128]{3,2,1,0:T(8,128)(2,1)} %narrow.2), channel_id=1, source_target_pairs={{0,16},{16,0},{1,17},{17,1},{2,18},{18,2},{3,19},{19,3},{4,20},{20... | collective-permute-start | bytes 2211848 | tf_op jit(solution)/shard_map/ppermute | solution.py:334
  18.2 50.8 %collective-permute-start.2 = (bf16[3,15,64,128]{3,2,1,0:T(8,128)(2,1)}, bf16[3,15,64,128]{3,2,1,0:T(8,128)(2,1)S(1)}, u32[]{:S(2)}, u32[]{:S(2)}) collective-permute-start(bf16[3,15,64,128]{3,2,1,0:T(8,128)(2,1)} %get-tuple-element.26), channel_id=1, source_target_pairs={{0,16},{16,0},{1,17},{17,1},{2,18},{18,2},{3,19},{19,3},{4,20},{20... | collective-permute-start | bytes 2211848 | tf_op jit(solution)/shard_map/ppermute | solution.py:334
  20.2 48.8 %collective-permute-start.3 = (bf16[3,15,64,128]{3,2,1,0:T(8,128)(2,1)}, bf16[3,15,64,128]{3,2,1,0:T(8,128)(2,1)S(1)}, u32[]{:S(2)}, u32[]{:S(2)}) collective-permute-start(bf16[3,15,64,128]{3,2,1,0:T(8,128)(2,1)} %get-tuple-element.27), channel_id=1, source_target_pairs={{0,16},{16,0},{1,17},{17,1},{2,18},{18,2},{3,19},{19,3},{4,20},{20... | collective-permute-start | bytes 2211848 | tf_op jit(solution)/shard_map/ppermute | solution.py:334
  22.1 3.2 %collective-permute-start.5 = (bf16[192,64]{1,0:T(8,128)(2,1)S(1)}, bf16[192,64]{1,0:T(8,128)(2,1)S(1)}, u32[]{:S(2)}, u32[]{:S(2)}) collective-permute-start(bf16[192,64]{1,0:T(8,128)(2,1)S(1)} %get-tuple-element.46), channel_id=1, source_target_pairs={{0,4},{4,8},{8,12},{1,5},{5,9},{9,13},{2,6},{6,10},{10,14},{3,7},{... | collective-permute-start | bytes 73736 | tf_op jit(solution)/shard_map/ppermute | solution.py:371
  23.9 6.0 %collective-permute-start.6 = (bf16[192,64]{1,0:T(8,128)(2,1)S(1)}, bf16[192,64]{1,0:T(8,128)(2,1)S(1)}, u32[]{:S(2)}, u32[]{:S(2)}) collective-permute-start(bf16[192,64]{1,0:T(8,128)(2,1)S(1)} %get-tuple-element.47), channel_id=1, source_target_pairs={{4,0},{8,4},{12,8},{5,1},{9,5},{13,9},{6,2},{10,6},{14,10},{7,3},{... | collective-permute-start | bytes 73736 | tf_op jit(solution)/shard_map/ppermute | solution.py:372
  25.3 11.4 %collective-permute-start.8 = (bf16[3,64,640]{2,1,0:T(8,128)(2,1)S(1)}, bf16[3,64,640]{2,1,0:T(8,128)(2,1)}, u32[]{:S(2)}, u32[]{:S(2)}) collective-permute-start(bf16[3,64,640]{2,1,0:T(8,128)(2,1)S(1)} %add_convert_fusion.1), channel_id=1, source_target_pairs={{0,8},{4,12},{8,0},{12,4},{1,9},{5,13},{9,1},{13,5},{2,10},{6,14},... | collective-permute-start | bytes 737288 | tf_op jit(solution)/shard_map/ppermute | solution.py:53
  30.7 38.2 %copy-start = (bf16[1280,64]{1,0:T(8,128)(2,1)S(1)}, bf16[1280,64]{1,0:T(8,128)(2,1)}, u32[]{:S(2)}) copy-start(bf16[1280,64]{1,0:T(8,128)(2,1)} %get-tuple-element.21.refs_1_) | copy-start | bytes 491524
  34.1 30.4 %copy-start.5 = (bf16[1,15,64,128]{3,2,1,0:T(8,128)(2,1)S(1)}, bf16[1,15,64,128]{3,2,1,0:T(8,128)(2,1)}, u32[]{:S(2)}) copy-start(bf16[1,15,64,128]{3,2,1,0:T(8,128)(2,1)} %get-tuple-element.24) | copy-start | bytes 737284
  44.1 6.9 %collective-permute-start.11 = (bf16[384,64]{1,0:T(8,128)(2,1)S(1)}, bf16[384,64]{1,0:T(8,128)(2,1)S(1)}, u32[]{:S(2)}, u32[]{:S(2)}) collective-permute-start(bf16[384,64]{1,0:T(8,128)(2,1)S(1)} %get-tuple-element.32.refs_10_), channel_id=1, source_target_pairs={{0,3},{1,0},{2,1},{3,2},{4,7},{5,4},{6,5},{7,6},{8,11},{9,8},{10,9... | collective-permute-start | bytes 147464 | tf_op jit(solution)/shard_map/ppermute | solution.py:389
  47.8 8.1 %collective-permute-start.10 = (bf16[384,64]{1,0:T(8,128)(2,1)S(1)}, bf16[384,64]{1,0:T(8,128)(2,1)S(1)}, u32[]{:S(2)}, u32[]{:S(2)}) collective-permute-start(bf16[384,64]{1,0:T(8,128)(2,1)S(1)} %get-tuple-element.32.refs_10_), channel_id=1, source_target_pairs={{0,2},{1,3},{2,0},{3,1},{4,6},{5,7},{6,4},{7,5},{8,10},{9,11},{10,... | collective-permute-start | bytes 147464 | tf_op jit(solution)/shard_map/ppermute | solution.py:389
  51.0 7.0 %collective-permute-start.9 = (bf16[384,64]{1,0:T(8,128)(2,1)S(1)}, bf16[384,64]{1,0:T(8,128)(2,1)S(1)}, u32[]{:S(2)}, u32[]{:S(2)}) collective-permute-start(bf16[384,64]{1,0:T(8,128)(2,1)S(1)} %get-tuple-element.32.refs_10_), channel_id=1, source_target_pairs={{0,1},{1,2},{2,3},{3,0},{4,5},{5,6},{6,7},{7,4},{8,9},{9,10},{10,1... | collective-permute-start | bytes 147464 | tf_op jit(solution)/shard_map/ppermute | solution.py:389
  63.0 1.3 %collective-permute-start.12 = (bf16[320,128]{1,0:T(8,128)(2,1)S(1)}, bf16[320,128]{1,0:T(8,128)(2,1)S(1)}, u32[]{:S(2)}, u32[]{:S(2)}) collective-permute-start(bf16[320,128]{1,0:T(8,128)(2,1)S(1)} %attend_grad.1), channel_id=1, source_target_pairs={{0,4},{4,0},{8,12},{12,8},{1,5},{5,1},{9,13},{13,9},{2,6},{6,2},{1... | collective-permute-start | bytes 245768 | tf_op jit(solution)/shard_map/ppermute | solution.py:53
  64.3 16.4 %slice-start = ((s8[4915200]{0:T(1024)(128)(4,1)}), s8[4194304]{0:T(1024)(128)(4,1)S(1)}, s32[]{:S(2)}) async-start(s8[4915200]{0:T(1024)(128)(4,1)} %bitcast.17), calls=%async_computation | async-start | bytes 8388608
  64.4 4.6 %collective-permute-start.13 = (bf16[320,128]{1,0:T(8,128)(2,1)S(1)}, bf16[320,128]{1,0:T(8,128)(2,1)S(1)}, u32[]{:S(2)}, u32[]{:S(2)}) collective-permute-start(bf16[320,128]{1,0:T(8,128)(2,1)S(1)} %add_convert_fusion.3), channel_id=1, source_target_pairs={{0,8},{4,12},{8,0},{12,4},{1,9},{5,13},{9,1},{13,5},{2,10},{6,14},... | collective-permute-start | bytes 245768 | tf_op jit(solution)/shard_map/ppermute | solution.py:53
  64.4 16.2 %collective-permute-start = (bf16[1,15,64,128]{3,2,1,0:T(8,128)(2,1)S(1)}, bf16[1,15,64,128]{3,2,1,0:T(8,128)(2,1)S(1)}, u32[]{:S(2)}, u32[]{:S(2)}) collective-permute-start(bf16[1,15,64,128]{3,2,1,0:T(8,128)(2,1)S(1)} %copy-done.5), channel_id=1, source_target_pairs={{0,16},{16,0},{1,17},{17,1},{2,18},{18,2},{3,19},{19,3},{4,20},{20... | collective-permute-start | bytes 737288 | tf_op jit(solution)/shard_map/ppermute | solution.py:334
  69.0 11.7 %slice-start.1 = ((s8[4915200]{0:T(1024)(128)(4,1)}), s8[720896]{0:T(1024)(128)(4,1)S(1)}, s32[]{:S(2)}) async-start(s8[4915200]{0:T(1024)(128)(4,1)} %bitcast.17), calls=%async_computation.1 | async-start | bytes 1441792

commit v3 on v2

v3 whole, which is shorter than its diff:
```python
import functools

import jax
import jax.numpy as jnp
from jax import lax
from jax.experimental import pallas as pl
from jax.experimental.pallas import tpu as pltpu
from jax.sharding import PartitionSpec as P

HD = 128
TILE = 192
STEPS = 50
CH = 64
WINDOW = 640
ONE_LANE = 64
BIAS_LANE = 65
LOW_LANE = 66

SHIFT_FACTOR = 5.0
NOISE_LEVEL = 0.7
MOMENTUM_DECAY = 0.9
LEARNING_RATE = 0.004
LOSS_SCALE = 16384.0
REWARD_FLOOR = 0.1
MASKED = -1e30
LOG2E = 1.4426950408889634

F32 = jnp.float32
BF16 = jnp.bfloat16
NT = (((1,), (1,)), ((), ()))
TN = (((0,), (0,)), ((), ()))
NN = (((1,), (0,)), ((), ()))


VMEM = pl.BlockSpec(memory_space=pltpu.VMEM)
SMEM = pl.BlockSpec(memory_space=pltpu.SMEM)
HBM = pl.BlockSpec(memory_space=pltpu.HBM)
MIB = 1024 * 1024


def in_hbm(x):
    return pltpu.with_memory_space_constraint(x, pltpu.HBM)


def in_vmem(x):
    return pltpu.with_memory_space_constraint(x, pltpu.VMEM)


def params(mib):
    return pltpu.CompilerParams(vmem_limit_bytes=mib * MIB)


def dot(a, b, dims=NN):
    return lax.dot_general(a, b, dims, preferred_element_type=F32)


def sigma_at(index, total_steps):
    fraction = index.astype(F32) / total_steps
    return SHIFT_FACTOR * fraction / (1.0 + (SHIFT_FACTOR - 1.0) * fraction)


def advantage_of(rewards, group_ids):
    members = (group_ids == group_ids[:, 0:1]).astype(F32)
    member_total = jnp.sum(members, axis=1, keepdims=True)
    group_mean = jnp.sum(members * rewards, axis=1, keepdims=True) / member_total
    spread = jnp.sqrt(jnp.sum(members * (rewards - group_mean) ** 2, axis=1, keepdims=True) / member_total)
    return (rewards[:, 0:1] - group_mean) / jnp.maximum(spread, REWARD_FLOOR)


def swap(x, axis, bit):
    return lax.ppermute(x, axis, [(i, i ^ bit) for i in range(lax.axis_size(axis))])


def add_kernel(a_ref, b_ref, o_ref):
    o_ref[...] = (a_ref[...].astype(F32) + b_ref[...].astype(F32)).astype(BF16)


def add(a, b):
    return pl.pallas_call(
        add_kernel,
        in_specs=[VMEM, VMEM],
        out_specs=VMEM,
        out_shape=pltpu.VMEM(a.shape, BF16),
        compiler_params=params(4),
        name="add",
    )(a, b)


def butterfly(x, axis):
    bit = 1
    while 2 * bit < lax.axis_size(axis):
        x = add(x, swap(x, axis, bit))
        bit *= 2
    return x, swap(x, axis, bit)


def pick_kernel(place_ref, mine_ref, other_ref, now_ref, next_ref, head_ref, tail_ref):
    mine = mine_ref[...]
    other = other_ref[...]
    sampler = place_ref[1] == 0
    now = jnp.where(sampler, mine.astype(F32), other.astype(F32)).astype(BF16)
    now_ref[...] = now
    next_ref[...] = jnp.where(sampler, other.astype(F32), mine.astype(F32)).astype(BF16)
    spare = head_ref.shape[1]
    head_ref[...] = now[:, :spare]
    tail_ref[...] = now[:, now.shape[1] - spare :]


def pick(place, mine, other, spare):
    shape = pltpu.VMEM(mine.shape, BF16)
    edge = pltpu.VMEM((mine.shape[0], spare), BF16)
    return pl.pallas_call(
        pick_kernel,
        in_specs=[SMEM, VMEM, VMEM],
        out_specs=[VMEM] * 4,
        out_shape=[shape, shape, edge, edge],
        compiler_params=params(4),
        name="pick",
    )(place, mine, other)


def lead_kernel(stride, unit, mom_ref, o_ref):
    for q in range(stride):
        o_ref[0, q] = (MOMENTUM_DECAY * mom_ref[pl.ds(q, unit, stride=stride), :]).astype(BF16)


def lead(mom, stride, unit):
    return pl.pallas_call(
        functools.partial(lead_kernel, stride, unit),
        grid=(1,),
        in_specs=[pl.BlockSpec((unit * stride, HD), lambda i: (0, 0))],
        out_specs=pl.BlockSpec((1, stride, unit, HD), lambda i: (0, 0, 0, 0)),
        out_shape=jax.ShapeDtypeStruct((1, stride, unit, HD), BF16),
        name="lead",
    )(mom)


def prepare_kernel(sizes, stride, unit, sliced, at_ref, e_hbm, mom_hbm, w_hbm, m_ref, et_ref, w_ref, mom_ref, *rest):
    pieces = rest[: len(sizes)]
    e_ref, e_sem, w_sem, mom_sem = rest[len(sizes) :]
    rows = w_ref.shape[1]
    half = rows // 2
    count = mom_ref.shape[0] // 5
    if sliced:
        e_src = e_hbm
    else:
        e_src = e_hbm.at[:, pl.ds(pl.multiple_of(at_ref[0] * rows, HD), rows)]
    e_copy = pltpu.make_async_copy(e_src, e_ref, e_sem)
    e_copy.start()
    w_copies = []
    for m in range(3):
        for k in range(2):
            at = pl.ds(k * half, half)
            w_copies.append(pltpu.make_async_copy(w_hbm.at[m, at], w_ref.at[m, at], w_sem.at[2 * m + k]))
    mom_copies = [
        pltpu.make_async_copy(mom_hbm.at[pl.ds(k * count, count)], mom_ref.at[pl.ds(k * count, count)], mom_sem.at[k])
        for k in range(5)
    ]
    for copy in w_copies[:2] + mom_copies[:2] + w_copies[2:4] + mom_copies[2:4] + w_copies[4:] + mom_copies[4:]:
        copy.start()
    e_copy.wait()
    et_ref[...] = e_ref[...].astype(F32).T.astype(BF16)
    waited = 0
    done = 0
    for m in range(3):
        w_copies[2 * m].wait()
        w_copies[2 * m + 1].wait()
        m_ref[m] = dot(e_ref[...], w_ref[m]).astype(BF16)
        target = 2 * m + 2 if m < 2 else 5
        while waited < target:
            mom_copies[waited].wait()
            waited += 1
        for u in range(done, 2 * target):
            if u > 0:
                k, first = 0, 1
                while u >= first + sizes[k]:
                    first += sizes[k]
                    k += 1
                for q in range(stride):
                    part = mom_ref[pl.ds(u * unit * stride + q, unit, stride=stride), :]
                    pieces[k][u - first, q] = (MOMENTUM_DECAY * part).astype(BF16)
        done = 2 * target


def prepare(place, w_embed, mom, w, sizes, stride, unit):
    _, rows, width = w.shape
    sliced = rows % HD != 0
    if sliced:
        w_embed = lax.dynamic_slice_in_dim(w_embed, place[0] * rows, rows, axis=1)
    return pl.pallas_call(
        functools.partial(prepare_kernel, sizes, stride, unit, sliced),
        in_specs=[SMEM, HBM, HBM, HBM],
        out_specs=[VMEM] * (4 + len(sizes)),
        out_shape=[
            pltpu.VMEM((3, CH, width), BF16),
            pltpu.VMEM((rows, CH), BF16),
            pltpu.VMEM(w.shape, BF16),
            pltpu.VMEM(mom.shape, F32),
        ]
        + [pltpu.VMEM((n, stride, unit, HD), BF16) for n in sizes],
        scratch_shapes=[
            pltpu.VMEM((CH, rows), BF16),
            pltpu.SemaphoreType.DMA(()),
            pltpu.SemaphoreType.DMA((6,)),
            pltpu.SemaphoreType.DMA((5,)),
        ],
        compiler_params=params(4),
        name="prepare",
    )(place, in_hbm(w_embed), in_hbm(mom), in_hbm(w))


def forward_kernel(tiles, heads, ends, *refs):
    place_ref, left_ref, now_ref, right_ref, ma_ref, mb_ref, wot_ref = refs[:7]
    m_ref, win_ref, e_ref, u_ref, il_ref, pred_ref, mk_ref, att_ref = refs[7:]
    tok = tiles * TILE
    m_ref[...] = (ma_ref[...].astype(F32) + mb_ref[...].astype(F32)).astype(BF16)
    mk_ref[...] = jnp.zeros_like(mk_ref)
    mk_ref[0:CH, :] = m_ref[1]

    spare = left_ref.shape[1]
    left = left_ref[...].astype(F32).T[spare - TILE :]
    now = now_ref[...].astype(F32).T
    right = right_ref[...].astype(F32).T[:TILE]
    blocks = [left] + [now[j * TILE : (j + 1) * TILE] for j in range(tiles)] + [right]
    lane = lax.broadcasted_iota(jnp.int32, (TILE, CH), 1) + CH
    flags = jnp.where((lane == ONE_LANE) | (lane == LOW_LANE), 1.0, 0.0)
    seq = place_ref[0]
    for j in range(tiles):
        for k in range(3):
            extra = flags
            if j + k == 0:
                extra = jnp.where(lane == BIAS_LANE, jnp.where(seq == 0, MASKED, 0.0), flags)
            if j + k == tiles + 1:
                extra = jnp.where(lane == BIAS_LANE, jnp.where(seq == ends, MASKED, 0.0), flags)
            win_ref[j, k * TILE : (k + 1) * TILE, :] = jnp.concatenate([blocks[j + k], extra], axis=1).astype(BF16)
        pad_lane = lax.broadcasted_iota(jnp.int32, (WINDOW - 3 * TILE, HD), 1)
        win_ref[j, 3 * TILE :, :] = jnp.where(pad_lane == BIAS_LANE, MASKED, 0.0).astype(BF16)

    lane = lax.broadcasted_iota(jnp.int32, (TILE, HD), 1)
    unit = jnp.where(lane == BIAS_LANE, 1.0, 0.0)
    factor = LOG2E * HD ** (-0.5)
    for j in range(tiles):
        own = win_ref[j, TILE : 2 * TILE, 0:CH]
        queries = dot(own, m_ref[0]).astype(BF16)
        keys = win_ref[j]
        for h in range(heads):
            cols = slice(h * HD, (h + 1) * HD)
            t = dot(queries[:, cols], mk_ref[:, cols], NT) * factor + unit
            s = dot(t.astype(BF16), keys, NT)
            e = jnp.exp2(s - jnp.max(s, axis=1, keepdims=True)).astype(BF16)
            at = slice(h * tok + j * TILE, h * tok + (j + 1) * TILE)
            e_ref[at, :] = e
            u = dot(e, keys)
            inv = 1.0 / u[:, ONE_LANE : ONE_LANE + 1]
            u = (u * inv).astype(BF16)
            u_ref[at, :] = u
            il_ref[at, :] = jnp.broadcast_to(inv, (TILE, HD))
            att_ref[j * TILE : (j + 1) * TILE, cols] = dot(u[:, 0:CH], m_ref[2, :, cols]).astype(BF16)
    pred_ref[...] = dot(wot_ref[...], att_ref[...], NT).astype(BF16)


def forward(place, left, now, right, ma, mb, wot, tiles, heads, seq_count):
    tok = tiles * TILE
    rows = heads * tok
    width = heads * HD
    return pl.pallas_call(
        functools.partial(forward_kernel, tiles, heads, seq_count - 1),
        in_specs=[SMEM] + [VMEM] * 6,
        out_specs=[VMEM] * 6,
        out_shape=[
            pltpu.VMEM((3, CH, width), BF16),
            pltpu.VMEM((tiles, WINDOW, HD), BF16),
            pltpu.VMEM((rows, WINDOW), BF16),
            pltpu.VMEM((rows, HD), BF16),
            pltpu.VMEM((rows, HD), F32),
            pltpu.VMEM((CH, tok), BF16),
        ],
        scratch_shapes=[pltpu.VMEM((HD, width), BF16), pltpu.VMEM((tok, width), BF16)],
        compiler_params=params(8),
        name="attend",
    )(place, left, now, right, ma, mb, wot)


def backward_kernel(tiles, heads, tokens_all, *refs):
    (time_ref, rewards_ref, groups_ref, win_ref, m_ref, wot_ref, e_ref, u_ref, il_ref, now_ref, next_ref) = refs[:11]
    pred_refs = refs[11:-3]
    zy_ref, mv_ref, v_ref = refs[-3:]
    tok = tiles * TILE
    mv_ref[...] = jnp.zeros_like(mv_ref)
    mv_ref[0:CH, :] = m_ref[2]
    lane = lax.broadcasted_iota(jnp.int32, (TILE, HD), 1)
    scale = HD ** (-0.5)
    advantage = advantage_of(rewards_ref[...], groups_ref[...])
    index = jnp.full((1, 1), time_ref[0], jnp.int32)
    sigma_now = sigma_at(index, STEPS)
    step_size = sigma_at(index - 1, STEPS) - sigma_now
    coefficient = advantage * LOSS_SCALE * (1.0 - sigma_now) / (NOISE_LEVEL**2 * sigma_now * tokens_all)
    pred = pred_refs[0][...].astype(F32)
    for ref in pred_refs[1:]:
        pred = pred + ref[...].astype(F32)
    step_mean = now_ref[...].astype(F32) + step_size * pred
    pg_flat = coefficient * (next_ref[...].astype(F32) - step_mean)
    pg = pg_flat.T.astype(BF16)
    pg_flat = pg_flat.astype(BF16)
    ag_all = dot(pg, wot_ref[...]).astype(BF16)
    for j in range(tiles):
        at = slice(j * TILE, (j + 1) * TILE)
        ag = ag_all[at]
        keys = win_ref[j]
        for h in range(heads):
            cols = slice(h * HD, (h + 1) * HD)
            rows = slice(h * tok + j * TILE, h * tok + (j + 1) * TILE)
            w = dot(ag[:, cols], mv_ref[:, cols], NT).astype(BF16).astype(F32)
            u = u_ref[rows, :].astype(F32)
            row_dot = jnp.sum(w * u, axis=1, keepdims=True)
            factor = scale * il_ref[rows, :]
            w = w * factor
            row_dot = row_dot * factor
            high = row_dot.astype(BF16).astype(F32)
            low = row_dot - high
            w = jnp.where(lane == ONE_LANE, -high, jnp.where(lane == LOW_LANE, -low, w))
            x = dot(w.astype(BF16), keys, NT)
            ds = (e_ref[rows, :].astype(F32) * x).astype(BF16)
            v_ref[rows, :] = dot(ds, keys).astype(BF16)
    now = now_ref[...]
    for h in range(heads):
        rows = slice(h * tok, (h + 1) * tok)
        z = dot(now, v_ref[rows, :])
        y = dot(pg_flat, u_ref[rows, :])
        zy_ref[h * CH : (h + 1) * CH, :] = jnp.concatenate([z[:, 0:CH], y[:, 0:CH]], axis=1).astype(BF16)


def backward(timestep, rewards, group_ids, win, m, wot, e, u, il, now, later, preds, tiles, heads, tokens_all):
    width = heads * HD
    return pl.pallas_call(
        functools.partial(backward_kernel, tiles, heads, tokens_all),
        in_specs=[SMEM] + [VMEM] * (10 + len(preds)),
        out_specs=VMEM,
        out_shape=pltpu.VMEM((heads * CH, HD), BF16),
        scratch_shapes=[pltpu.VMEM((HD, width), BF16), pltpu.VMEM((heads * tiles * TILE, HD), BF16)],
        compiler_params=params(8),
        name="attend_grad",
    )(timestep, rewards, group_ids, win, m, wot, e, u, il, now, later, *preds)


def update_kernel(heads, sizes, first, unit, later, *refs):
    place_ref, et_ref, mom_ref, w_ref = refs[:4]
    recv_refs = refs[4 : 4 + len(sizes)]
    rest = refs[4 + len(sizes) :]
    if later:
        g_ref = rest[0]
        onm_hbm, ow_hbm, gs_ref, fs_ref, onm_ref, ow_ref, sems = rest[3:]
    else:
        za_ref, zb_ref, m_ref, wot_ref, onm_hbm, ow_hbm, g_ref, gs_ref, fs_ref, onm_ref, ow_ref, sems = rest
    stride = 3 * heads
    lin = unit * stride
    role = place_ref[1]
    slots = onm_ref.shape[0]

    if not later:
        for h in range(heads):
            cols = slice(h * HD, (h + 1) * HD)
            rows = slice(h * CH, (h + 1) * CH)
            zy = (za_ref[rows, :].astype(F32) + zb_ref[rows, :].astype(F32)).astype(BF16)
            z = zy[:, 0:CH]
            y = zy[:, CH : 2 * CH]
            g_ref[0, :, cols] = dot(z, m_ref[1, :, cols]).astype(BF16)
            g_ref[1, :, cols] = dot(z, m_ref[0, :, cols], TN).astype(BF16)
            g_ref[2, :, cols] = dot(y, wot_ref[:, cols], TN).astype(BF16)

    def copies(u, slot):
        rows = pl.ds(u * 2 * unit, 2 * unit)
        return [
            pltpu.make_async_copy(onm_ref.at[slot], onm_hbm.at[pl.ds(u * lin, lin)], sems.at[0, slot]),
            pltpu.make_async_copy(ow_ref.at[slot], ow_hbm.at[:, rows], sems.at[1, slot]),
        ]

    order = [(k, i) for k, size in enumerate(sizes) for i in range(size)]
    for step, (k, i) in enumerate(order):
        u = first + step
        slot = step % slots
        if step >= slots:
            for copy in copies(u - slots, slot):
                copy.wait()
        natural = slice(u * 2 * unit, (u + 1) * 2 * unit)
        for part in range(3):
            g = dot(et_ref[natural, :], g_ref[part])
            for b in range(heads):
                q = part * heads + b
                cols = slice(b * HD, (b + 1) * HD)
                gs_ref[q] = g[:, cols]
                own = MOMENTUM_DECAY * mom_ref[pl.ds(u * lin + q, unit, stride=stride), :]
                own = own + gs_ref[q, pl.ds(role, unit, stride=2), :]
                other = recv_refs[k][i, q].astype(F32) + gs_ref[q, pl.ds(1 - role, unit, stride=2), :]
                onm_ref[slot, pl.ds(q, unit, stride=stride), :] = own
                fs_ref[q, pl.ds(role, unit, stride=2), :] = own
                fs_ref[q, pl.ds(1 - role, unit, stride=2), :] = other
                new = w_ref[part, natural, cols].astype(F32) - LEARNING_RATE * fs_ref[q]
                ow_ref[slot, part, :, cols] = new.astype(BF16)
        for copy in copies(u, slot):
            copy.start()
    steps = len(order)
    for step in range(max(steps - slots, 0), steps):
        for copy in copies(first + step, step % slots):
            copy.wait()


def update(place, et, mom, w, received, first, unit, heads, sources=None, before=None):
    sizes = [a.shape[0] for a in received]
    width = heads * HD
    stride = 3 * heads
    slots = min(sum(sizes), 4)
    args = [place, et, in_vmem(mom), in_vmem(w), *received]
    in_specs = [SMEM] + [VMEM] * (3 + len(received))
    out_specs = [HBM, HBM]
    out_shape = [jax.ShapeDtypeStruct(mom.shape, F32), jax.ShapeDtypeStruct(w.shape, BF16)]
    aliases = {}
    if before is None:
        args += sources
        in_specs += [VMEM] * len(sources)
        out_specs.append(VMEM)
        out_shape.append(pltpu.VMEM((3, CH, width), BF16))
    else:
        new_mom, new_w, g = before
        aliases = {len(args) + 1: 0, len(args) + 2: 1}
        args += [g, new_mom, new_w]
        in_specs += [VMEM, HBM, HBM]
    return pl.pallas_call(
        functools.partial(update_kernel, heads, sizes, first, unit, before is not None),
        in_specs=in_specs,
        out_specs=out_specs,
        out_shape=out_shape,
        input_output_aliases=aliases,
        scratch_shapes=[
            pltpu.VMEM((stride, 2 * unit, HD), F32),
            pltpu.VMEM((stride, 2 * unit, HD), F32),
            pltpu.VMEM((slots, unit * stride, HD), F32),
            pltpu.VMEM((slots, 3, 2 * unit, width), BF16),
            pltpu.SemaphoreType.DMA((2, slots)),
        ],
        compiler_params=params(10),
        name="update",
    )(*args)


def exchange(x):
    return lax.ppermute(x, "role", [(0, 1), (1, 0)])


def body(rollout, w_embed, w_qkv, w_out, momentum, rewards, group_ids, timestep):
    seq_count = lax.axis_size("seq")
    seq_index = lax.axis_index("seq")
    role_index = lax.axis_index("role")
    rows_dev = w_qkv.shape[0]
    width = w_qkv.shape[2]
    heads = width // HD
    tok_dev = rollout.shape[1]
    tiles = tok_dev // TILE
    pair_rows = rows_dev // 2

    stride = 3 * heads
    unit = pair_rows // 10
    sizes = (4, 4, 1)
    mom = momentum.reshape(pair_rows * stride, HD)
    w = w_qkv.transpose(1, 0, 2)
    wot = w_out.T
    place = jnp.stack([seq_index, role_index])

    piece = lead(mom, stride, unit)
    received = [exchange(piece)]
    mine = rollout[0].T
    other = exchange(mine)
    mom, piece = lax.optimization_barrier((mom, piece))
    m, et, w, mom, *pieces = prepare(place, w_embed, mom, w, sizes, stride, unit)
    m, received[0], other, pieces = lax.optimization_barrier((m, received[0], other, pieces))
    received += [exchange(p) for p in pieces]
    ma, mb = butterfly(m, "seq")

    latent_now, latent_next, head, tail = pick(place, mine, other, min(2 * HD, tok_dev))
    left = lax.ppermute(tail, "seq", [(i, i + 1) for i in range(seq_count - 1)])
    right = lax.ppermute(head, "seq", [(i + 1, i) for i in range(seq_count - 1)])

    m, win, e, u, il, partial_pred = forward(place, left, latent_now, right, ma, mb, wot, tiles, heads, seq_count)
    mp_count = lax.axis_size("mp")
    preds = [partial_pred] + [
        lax.ppermute(partial_pred, "mp", [(i, (i + d) % mp_count) for i in range(mp_count)])
        for d in range(1, mp_count)
    ]
    za, zb = butterfly(
        backward(
            timestep,
            rewards[None],
            group_ids[None],
            win,
            m,
            wot,
            e,
            u,
            il,
            latent_now,
            latent_next,
            preds,
            tiles,
            heads,
            tok_dev * seq_count,
        ),
        "seq",
    )

    first = update(place, et, mom, w, received[:-1], 0, unit, heads, sources=[za, zb, m, wot])
    nm, nw = update(place, et, mom, w, received[-1:], 10 - sizes[-1], unit, heads, before=first)
    return nm.reshape(momentum.shape), nw.transpose(1, 0, 2)


def solution(mesh):
    in_specs = (
        P("role", "seq", None),
        P(),
        P("seq", None, "mp"),
        P("mp", None),
        P("seq", "role", None, "mp"),
        P(),
        P(),
        P(),
    )
    out_specs = (P("seq", "role", None, "mp"), P("seq", None, "mp"))
    return jax.shard_map(body, mesh=mesh, in_specs=in_specs, out_specs=out_specs, check_vma=False)
```

time: 84.1 us -> 67.9 us (0.81)
  Pallas kernels: 39 us -> 29.4 us
  local copies, waits for them, and re-layouts: 6.01 us -> 0.02 us
  other arithmetic: 3.1 us -> 0.07 us
  waiting for transfers between devices: 15.2 us -> 18 us
    pallas_call x6 -> x8, Pallas kernels: 34 us -> 24.5 us  [the longest x2 9.15 us: update(): pl.pallas_call(functools.partial(update_kernel, heads, sizes, first, unit...]
    ppermute x5, waiting for transfers between devices: 0.01 us -> 5.17 us  [exchange(): return lax.ppermute(x, 'role', [(0, 1), (1, 0)])]
    ppermute x3, waiting for transfers between devices: 9.33 us -> 5.05 us  [body(): lax.ppermute(partial_pred, 'mp', [(i, (i + d) % mp_count) for i in range(...]
    concatenate x3 -> x0, local copies, waits for them, and re-layouts: 3.35 us -> none  [the longest x2 3.27 us: body(): jnp.concatenate([near[j * TILE:j * TILE + WINDOW], ones, bias, ones, rest...]
    ppermute x2, waiting for transfers between devices: 0.01 us -> 1.81 us  [the longest x1 1.81 us: body(): lax.ppermute(head, 'seq', [(i + 1, i) for i in range(seq_count - 1)])]
    broadcast_in_dim x3 -> x0, local copies, waits for them, and re-layouts: 1.65 us -> none  [the longest x2 1.64 us: body(): bias = jnp.where(seen, 0.0, MASKED).astype(BF16)[:, None]]
    convert_element_type x5 -> x0, other arithmetic: 1.22 us -> none  [the longest x4 1.14 us: butterfly(): x = (x.astype(F32) + swap(x, axis, bit).astype(F32)).astype(x.dtype)]
    unnamed x17 -> x8, local copies, waits for them, and re-layouts: 0.95 us -> 0.02 us
  transfers between devices with their start and end apart: 14 -> 14, of which waited for: 6 -> 10; matrix products, arithmetic and copies ran while one was open for 10% -> 0% of each run, Pallas kernels for 44% -> 38%
where the time goes in v3:
time: 67.9 us; the launch traced here: 67.7 us
  Pallas kernels  29.4 us (43%)
  starting transfers between devices  18.6 us (27%)
  waiting for transfers between devices  18 us (27%)
  between operations  1.53 us (2%)
    pallas_call x2, Pallas kernels, update(): pl.pallas_call(functools.partial(update_kernel, heads, sizes, first, unit...  9.15 us
    pallas_call x1, Pallas kernels, forward(): pl.pallas_call(functools.partial(forward_kernel, tiles, heads, seq_count...  7.02 us
    ppermute x5, starting transfers between devices, exchange(): return lax.ppermute(x, 'role', [(0, 1), (1, 0)])  6.48 us
    ppermute x4, waiting for transfers between devices, swap(): lax.ppermute(x, axis, [(i, i ^ bit) for i in range(lax.axis_size(axis))])  5.99 us
    pallas_call x1, Pallas kernels, prepare(): pl.pallas_call(functools.partial(prepare_kernel, sizes, stride, unit, sli...  5.85 us
    ppermute x5, waiting for transfers between devices, exchange(): return lax.ppermute(x, 'role', [(0, 1), (1, 0)])  5.17 us
    ppermute x3, waiting for transfers between devices, body(): lax.ppermute(partial_pred, 'mp', [(i, (i + d) % mp_count) for i in range(...  5.05 us
    pallas_call x1, Pallas kernels, backward(): pl.pallas_call(functools.partial(backward_kernel, tiles, heads, tokens_al...  4.96 us
  transfers between devices with their start and end apart: 14, of which 10 were waited for; matrix products, arithmetic and copies ran while one was open for 0% of the time, Pallas kernels for 38%

profile of v3, /device:TPU:0, one launch (start us, length us, event | category | flops | bytes accessed | tf_op | source)
XLA Modules:
  0.0 67.7 jit_solution(14697045870374082574)
XLA Ops:
  0.6 0.0 copy-start.1
  0.6 1.8 %lead.1 = bf16[1,15,64,128]{3,2,1,0:T(8,128)(2,1)} custom-call(f32[9600,128]{1,0:T(8,128)} %bitcast.19), custom_call_target="tpu_custom_call" | custom-call | tf_op jit(solution)/shard_map/lead/pallas_call | solution.py:128
  2.4 2.9 %collective-permute-start = (bf16[1,15,64,128]{3,2,1,0:T(8,128)(2,1)}, bf16[1,15,64,128]{3,2,1,0:T(8,128)(2,1)S(1)}, u32[]{:S(2)}, u32[]{:S(2)}) collective-permute-start(bf16[1,15,64,128]{3,2,1,0:T(8,128)(2,1)} %lead.1), channel_id=1, source_target_pairs={{0,16},{16,0},{1,17},{17,1},{2,18},{18,2},{3,19},{19,3},{4,20},{20... | collective-permute-start | bytes 737288 | tf_op jit(solution)/shard_map/ppermute | solution.py:447
  5.4 0.0 copy-done.1
  5.4 0.0 collective-permute-start.1
  5.4 0.1 pad_add_fusion.at_ref.place_ref.refs_0_
  5.5 0.0 copy-start
  5.5 0.0 copy-start.2
  5.5 0.0 copy-start.3
  5.5 5.8 %prepare.1 = (bf16[3,64,640]{2,1,0:T(8,128)(2,1)S(1)}, bf16[1280,64]{1,0:T(8,128)(2,1)S(1)}, bf16[3,1280,640]{2,1,0:T(8,128)(2,1)S(1)}, f32[9600,128]{1,0:T(8,12...) custom-call(s32[2]{0:T(128)S(1)} %pad_add_fusion.at_ref.place_ref.re, ...), custom_call_target="tpu_custom_call" | custom-call | tf_op jit(solution)/shard_map/prepare/pallas_call | solution.py:190
  11.3 1.2 %collective-permute-done.1.other_ref = bf16[64,384]{1,0:T(8,128)(2,1)S(1)} collective-permute-done((bf16[64,384]{1,0:T(8,128)(2,1)S(1)}, bf16[64,384]{1,0:T(8,128)(2,1)S(1)}, u32[]{:S(2)}, u32[]{:S(2)}) %collective-permute-start.1) | collective-permute-done | bytes 49184 | tf_op jit(solution)/shard_map/ppermute | solution.py:447
  12.6 0.0 collective-permute-done.refs_4_
  12.6 1.7 %collective-permute-start.3 = (bf16[4,15,64,128]{3,2,1,0:T(8,128)(2,1)S(1)}, bf16[4,15,64,128]{3,2,1,0:T(8,128)(2,1)S(1)}, u32[]{:S(2)}, u32[]{:S(2)}) collective-permute-start(bf16[4,15,64,128]{3,2,1,0:T(8,128)(2,1)S(1)} %get-tuple-element.41), channel_id=1, source_target_pairs={{0,16},{16,0},{1,17},{17,1},{2,18},{18,2},{3,19},{19,3},{4,20},{20... | collective-permute-start | bytes 2949128 | tf_op jit(solution)/shard_map/ppermute | solution.py:447
  14.3 0.3 collective-permute-start.4
  14.6 0.0 collective-permute-start.7
  14.6 1.5 %collective-permute-done.7.b_ref = bf16[3,64,640]{2,1,0:T(8,128)(2,1)S(1)} collective-permute-done((bf16[3,64,640]{2,1,0:T(8,128)(2,1)S(1)}, bf16[3,64,640]{2,1,0:T(8,128)(2,1)S(1)}, u32[]{:S(2)}, u32[]{:S(2)}) %collective-permute-start.7) | collective-permute-done | bytes 245792 | tf_op jit(solution)/shard_map/ppermute | solution.py:71
  16.1 0.1 add.4.refs_4_
  16.2 1.8 %collective-permute-start.8 = (bf16[3,64,640]{2,1,0:T(8,128)(2,1)S(1)}, bf16[3,64,640]{2,1,0:T(8,128)(2,1)S(1)}, u32[]{:S(2)}, u32[]{:S(2)}) collective-permute-start(bf16[3,64,640]{2,1,0:T(8,128)(2,1)S(1)} %add.4.refs_4_), channel_id=1, source_target_pairs={{0,8},{4,12},{8,0},{12,4},{1,9},{5,13},{9,1},{13,5},{2,10},{6,14},... | collective-permute-start | bytes 737288 | tf_op jit(solution)/shard_map/ppermute | solution.py:71
  18.0 0.6 pick.1
  18.6 1.8 %collective-permute-start.5 = (bf16[64,256]{1,0:T(8,128)(2,1)S(1)}, bf16[64,256]{1,0:T(8,128)(2,1)S(1)}, u32[]{:S(2)}, u32[]{:S(2)}) collective-permute-start(bf16[64,256]{1,0:T(8,128)(2,1)S(1)} %get-tuple-element.44), channel_id=1, source_target_pairs={{0,4},{4,8},{8,12},{1,5},{5,9},{9,13},{2,6},{6,10},{10,14},{3,7},{... | collective-permute-start | bytes 98312 | tf_op jit(solution)/shard_map/ppermute | solution.py:480
  20.4 1.3 %collective-permute-start.6 = (bf16[64,256]{1,0:T(8,128)(2,1)S(1)}, bf16[64,256]{1,0:T(8,128)(2,1)S(1)}, u32[]{:S(2)}, u32[]{:S(2)}) collective-permute-start(bf16[64,256]{1,0:T(8,128)(2,1)S(1)} %get-tuple-element.46), channel_id=1, source_target_pairs={{4,0},{8,4},{12,8},{5,1},{9,5},{13,9},{6,2},{10,6},{14,10},{7,3},{... | collective-permute-start | bytes 98312 | tf_op jit(solution)/shard_map/ppermute | solution.py:481
  21.7 0.0 collective-permute-done.5.refs_1_
  21.7 1.8 %collective-permute-done.6.refs_3_ = bf16[64,256]{1,0:T(8,128)(2,1)S(1)} collective-permute-done((bf16[64,256]{1,0:T(8,128)(2,1)S(1)}, bf16[64,256]{1,0:T(8,128)(2,1)S(1)}, u32[]{:S(2)}, u32[]{:S(2)}) %collective-permute-start.6) | collective-permute-done | bytes 32800 | tf_op jit(solution)/shard_map/ppermute | solution.py:481
  23.5 0.8 %collective-permute-done.8.refs_5_ = bf16[3,64,640]{2,1,0:T(8,128)(2,1)S(1)} collective-permute-done((bf16[3,64,640]{2,1,0:T(8,128)(2,1)S(1)}, bf16[3,64,640]{2,1,0:T(8,128)(2,1)S(1)}, u32[]{:S(2)}, u32[]{:S(2)}) %collective-permute-start.8) | collective-permute-done | bytes 245792 | tf_op jit(solution)/shard_map/ppermute | solution.py:71
  24.3 0.0 copy-done
  24.3 7.0 %attend.1 = (bf16[3,64,640]{2,1,0:T(8,128)(2,1)S(1)}, bf16[2,640,128]{2,1,0:T(8,128)(2,1)S(1)}, bf16[1920,640]{1,0:T(8,128)(2,1)S(1)}, bf16[1920,128]{1,0:T(8,12...) custom-call(s32[2]{0:T(128)S(1)} %pad_add_fusion.at_ref.place_ref.refs_0_, ...), custom_call_target="tpu_custom_call" | custom-call | tf_op jit(solution)/shard_map/attend/pallas_call | solution.py:266
  31.3 3.9 %collective-permute-start.11 = (bf16[64,384]{1,0:T(8,128)(2,1)S(1)}, bf16[64,384]{1,0:T(8,128)(2,1)S(1)}, u32[]{:S(2)}, u32[]{:S(2)}) collective-permute-start(bf16[64,384]{1,0:T(8,128)(2,1)S(1)} %get-tuple-element.54.refs_11_), channel_id=1, source_target_pairs={{0,3},{1,0},{2,1},{3,2},{4,7},{5,4},{6,5},{7,6},{8,11},{9,8},{10,9... | collective-permute-start | bytes 147464 | tf_op jit(solution)/shard_map/ppermute | solution.py:486
  35.2 1.5 %collective-permute-start.2 = (bf16[1,15,64,128]{3,2,1,0:T(8,128)(2,1)S(1)}, bf16[1,15,64,128]{3,2,1,0:T(8,128)(2,1)S(1)}, u32[]{:S(2)}, u32[]{:S(2)}) collective-permute-start(bf16[1,15,64,128]{3,2,1,0:T(8,128)(2,1)S(1)} %get-tuple-element.39), channel_id=1, source_target_pairs={{0,16},{16,0},{1,17},{17,1},{2,18},{18,2},{3,19},{19,3},{4,20},{20... | collective-permute-start | bytes 737288 | tf_op jit(solution)/shard_map/ppermute | solution.py:447
  36.7 0.0 collective-permute-start.10
  36.7 0.3 collective-permute-done.11.refs_14_
  36.9 0.8 %collective-permute-start.9 = (bf16[64,384]{1,0:T(8,128)(2,1)S(1)}, bf16[64,384]{1,0:T(8,128)(2,1)S(1)}, u32[]{:S(2)}, u32[]{:S(2)}) collective-permute-start(bf16[64,384]{1,0:T(8,128)(2,1)S(1)} %get-tuple-element.54.refs_11_), channel_id=1, source_target_pairs={{0,1},{1,2},{2,3},{3,0},{4,5},{5,6},{6,7},{7,4},{8,9},{9,10},{10,1... | collective-permute-start | bytes 147464 | tf_op jit(solution)/shard_map/ppermute | solution.py:486
  38.4 3.3 %collective-permute-done.10.refs_13_ = bf16[64,384]{1,0:T(8,128)(2,1)S(1)} collective-permute-done((bf16[64,384]{1,0:T(8,128)(2,1)S(1)}, bf16[64,384]{1,0:T(8,128)(2,1)S(1)}, u32[]{:S(2)}, u32[]{:S(2)}) %collective-permute-start.10) | collective-permute-done | bytes 49184 | tf_op jit(solution)/shard_map/ppermute | solution.py:486
  41.7 1.5 %collective-permute-done.9.refs_12_ = bf16[64,384]{1,0:T(8,128)(2,1)S(1)} collective-permute-done((bf16[64,384]{1,0:T(8,128)(2,1)S(1)}, bf16[64,384]{1,0:T(8,128)(2,1)S(1)}, u32[]{:S(2)}, u32[]{:S(2)}) %collective-permute-start.9) | collective-permute-done | bytes 49184 | tf_op jit(solution)/shard_map/ppermute | solution.py:486
  43.1 0.0 copy-done.2
  43.1 0.0 copy-done.3
  43.1 5.0 %attend_grad.1.a_ref = bf16[320,128]{1,0:T(8,128)(2,1)S(1)} custom-call(s32[1]{0:T(128)S(6)} %copy.16.refs_0_, f32[1,32]{1,0:T(1,128)S(1)} %bitcast.17, s32[1,32]{1,0:T(1,128)S(1)} %bitcast.18, bf16[2,640,128]{2,1,0:T(8,128)(2,1)S(1)} %get-tuple-element.48.refs_3_, bf16[3,64,640]{2,1,0:T(8,128)(2,1)S(1)} %get-tuple-element.49.refs_4_.refs_9_, ...), custom_call_target="tpu_custom_call" | custom-call | tf_op jit(solution)/shard_map/attend_grad/pallas_call | solution.py:335
  48.1 0.5 collective-permute-start.12
  48.7 0.9 %collective-permute-done.12.b_ref = bf16[320,128]{1,0:T(8,128)(2,1)S(1)} collective-permute-done((bf16[320,128]{1,0:T(8,128)(2,1)S(1)}, bf16[320,128]{1,0:T(8,128)(2,1)S(1)}, u32[]{:S(2)}, u32[]{:S(2)}) %collective-permute-start.12) | collective-permute-done | bytes 81952 | tf_op jit(solution)/shard_map/ppermute | solution.py:71
  49.6 2.1 %collective-permute-start.13 = (bf16[320,128]{1,0:T(8,128)(2,1)S(1)}, bf16[320,128]{1,0:T(8,128)(2,1)S(1)}, u32[]{:S(2)}, u32[]{:S(2)}) collective-permute-start(bf16[320,128]{1,0:T(8,128)(2,1)S(1)} %add.5.refs_7_), channel_id=1, source_target_pairs={{0,8},{4,12},{8,0},{12,4},{1,9},{5,13},{9,1},{13,5},{2,10},{6,14},... | collective-permute-start | bytes 245768 | tf_op jit(solution)/shard_map/ppermute | solution.py:71
  51.7 2.8 %collective-permute-done.13.refs_8_ = bf16[320,128]{1,0:T(8,128)(2,1)S(1)} collective-permute-done((bf16[320,128]{1,0:T(8,128)(2,1)S(1)}, bf16[320,128]{1,0:T(8,128)(2,1)S(1)}, u32[]{:S(2)}, u32[]{:S(2)}) %collective-permute-start.13) | collective-permute-done | bytes 81952 | tf_op jit(solution)/shard_map/ppermute | solution.py:71
  54.4 0.0 collective-permute-done.3.refs_5_
  54.4 3.9 %collective-permute-done.4.refs_6_ = bf16[4,15,64,128]{3,2,1,0:T(8,128)(2,1)S(1)} collective-permute-done((bf16[4,15,64,128]{3,2,1,0:T(8,128)(2,1)S(1)}, bf16[4,15,64,128]{3,2,1,0:T(8,128)(2,1)S(1)}, u32[]{:S(2)}, u32[]{:S(2)}) %collective-permute-start.4) | collective-permute-done | bytes 983072 | tf_op jit(solution)/shard_map/ppermute | solution.py:447
  58.3 7.2 %update.2 = (f32[9600,128]{1,0:T(8,128)}, bf16[3,1280,640]{2,1,0:T(8,128)(2,1)}, bf16[3,64,640]{2,1,0:T(8,128)(2,1)S(1)}) custom-call(s32[2]{0:T(128)S(1)} %pad_add_fusion.at_ref.place_ref.refs_0_, bf16[1280,64]{1,0:T(8,128)(2,1)S(1)} %get-tuple-element.32.refs_1_, f32[9600,128]{1,0:T(8,128)S(1)} %get-tuple-element.33.refs_2_, ...), custom_call_target="tpu_custom_call" | custom-call | tf_op jit(solution)/shard_map/update/pallas_call | solution.py:428
  65.5 0.0 collective-permute-done.2.refs_4_
  65.5 2.0 %update.3 = (f32[9600,128]{1,0:T(8,128)}, bf16[3,1280,640]{2,1,0:T(8,128)(2,1)}) custom-call(s32[2]{0:T(128)S(1)} %pad_add_fusion.at_ref.place_ref.refs_0_, bf16[1280,64]{1,0:T(8,128)(2,1)S(1)} %get-tuple-element.32.refs_1_, f32[9600,128]{1,0:T(8,128)S(1)} %get-tuple-element.33.refs_2_, ...), custom_call_target="tpu_custom_call", output_to_operand_aliasing={{0}: (6, {}), {1}: (7, {})} | custom-call | tf_op jit(solution)/shard_map/update/pallas_call | solution.py:428
  (1 shorter events, 0.0 us)
Async XLA Ops:
  0.6 4.7 %copy-start.1 = (bf16[1,384,64]{1,2,0:T(8,128)(2,1)S(1)}, bf16[1,384,64]{1,2,0:T(8,128)(2,1)}, u32[]{:S(2)}) copy-start(bf16[1,384,64]{1,2,0:T(8,128)(2,1)} %param.8) | copy-start | bytes 147460
  2.4 10.2 %collective-permute-start = (bf16[1,15,64,128]{3,2,1,0:T(8,128)(2,1)}, bf16[1,15,64,128]{3,2,1,0:T(8,128)(2,1)S(1)}, u32[]{:S(2)}, u32[]{:S(2)}) collective-permute-start(bf16[1,15,64,128]{3,2,1,0:T(8,128)(2,1)} %lead.1), channel_id=1, source_target_pairs={{0,16},{16,0},{1,17},{17,1},{2,18},{18,2},{3,19},{19,3},{4,20},{20... | collective-permute-start | bytes 737288 | tf_op jit(solution)/shard_map/ppermute | solution.py:447
  5.4 7.2 %collective-permute-start.1 = (bf16[64,384]{1,0:T(8,128)(2,1)S(1)}, bf16[64,384]{1,0:T(8,128)(2,1)S(1)}, u32[]{:S(2)}, u32[]{:S(2)}) collective-permute-start(bf16[64,384]{1,0:T(8,128)(2,1)S(1)} %bitcast.15), channel_id=1, source_target_pairs={{0,16},{16,0},{1,17},{17,1},{2,18},{18,2},{3,19},{19,3},{4,20},{20... | collective-permute-start | bytes 147464 | tf_op jit(solution)/shard_map/ppermute | solution.py:447
  5.5 18.8 %copy-start = (bf16[640,64]{0,1:T(8,128)(2,1)S(1)}, bf16[640,64]{0,1:T(8,128)(2,1)}, u32[]{:S(2)}) copy-start(bf16[640,64]{0,1:T(8,128)(2,1)} %param.11) | copy-start | bytes 245764
  5.5 37.7 %copy-start.2 = (f32[32]{0:T(128)S(1)}, f32[32]{0:T(128)}, u32[]{:S(2)}) copy-start(f32[32]{0:T(128)} %param.13) | copy-start | bytes 388
  5.5 37.7 %copy-start.3 = (s32[32]{0:T(128)S(1)}, s32[32]{0:T(128)}, u32[]{:S(2)}) copy-start(s32[32]{0:T(128)} %param.14) | copy-start | bytes 388
  12.6 41.8 %collective-permute-start.3 = (bf16[4,15,64,128]{3,2,1,0:T(8,128)(2,1)S(1)}, bf16[4,15,64,128]{3,2,1,0:T(8,128)(2,1)S(1)}, u32[]{:S(2)}, u32[]{:S(2)}) collective-permute-start(bf16[4,15,64,128]{3,2,1,0:T(8,128)(2,1)S(1)} %get-tuple-element.41), channel_id=1, source_target_pairs={{0,16},{16,0},{1,17},{17,1},{2,18},{18,2},{3,19},{19,3},{4,20},{20... | collective-permute-start | bytes 2949128 | tf_op jit(solution)/shard_map/ppermute | solution.py:447
  14.3 44.0 %collective-permute-start.4 = (bf16[4,15,64,128]{3,2,1,0:T(8,128)(2,1)S(1)}, bf16[4,15,64,128]{3,2,1,0:T(8,128)(2,1)S(1)}, u32[]{:S(2)}, u32[]{:S(2)}) collective-permute-start(bf16[4,15,64,128]{3,2,1,0:T(8,128)(2,1)S(1)} %get-tuple-element.42), channel_id=1, source_target_pairs={{0,16},{16,0},{1,17},{17,1},{2,18},{18,2},{3,19},{19,3},{4,20},{20... | collective-permute-start | bytes 2949128 | tf_op jit(solution)/shard_map/ppermute | solution.py:447
  14.6 1.5 %collective-permute-start.7 = (bf16[3,64,640]{2,1,0:T(8,128)(2,1)S(1)}, bf16[3,64,640]{2,1,0:T(8,128)(2,1)S(1)}, u32[]{:S(2)}, u32[]{:S(2)}) collective-permute-start(bf16[3,64,640]{2,1,0:T(8,128)(2,1)S(1)} %get-tuple-element.47.a_ref), channel_id=1, source_target_pairs={{0,4},{4,0},{8,12},{12,8},{1,5},{5,1},{9,13},{13,9},{2,6},{6,2},{1... | collective-permute-start | bytes 737288 | tf_op jit(solution)/shard_map/ppermute | solution.py:71
  16.2 8.1 %collective-permute-start.8 = (bf16[3,64,640]{2,1,0:T(8,128)(2,1)S(1)}, bf16[3,64,640]{2,1,0:T(8,128)(2,1)S(1)}, u32[]{:S(2)}, u32[]{:S(2)}) collective-permute-start(bf16[3,64,640]{2,1,0:T(8,128)(2,1)S(1)} %add.4.refs_4_), channel_id=1, source_target_pairs={{0,8},{4,12},{8,0},{12,4},{1,9},{5,13},{9,1},{13,5},{2,10},{6,14},... | collective-permute-start | bytes 737288 | tf_op jit(solution)/shard_map/ppermute | solution.py:71
  18.6 3.1 %collective-permute-start.5 = (bf16[64,256]{1,0:T(8,128)(2,1)S(1)}, bf16[64,256]{1,0:T(8,128)(2,1)S(1)}, u32[]{:S(2)}, u32[]{:S(2)}) collective-permute-start(bf16[64,256]{1,0:T(8,128)(2,1)S(1)} %get-tuple-element.44), channel_id=1, source_target_pairs={{0,4},{4,8},{8,12},{1,5},{5,9},{9,13},{2,6},{6,10},{10,14},{3,7},{... | collective-permute-start | bytes 98312 | tf_op jit(solution)/shard_map/ppermute | solution.py:480
  20.4 3.1 %collective-permute-start.6 = (bf16[64,256]{1,0:T(8,128)(2,1)S(1)}, bf16[64,256]{1,0:T(8,128)(2,1)S(1)}, u32[]{:S(2)}, u32[]{:S(2)}) collective-permute-start(bf16[64,256]{1,0:T(8,128)(2,1)S(1)} %get-tuple-element.46), channel_id=1, source_target_pairs={{4,0},{8,4},{12,8},{5,1},{9,5},{13,9},{6,2},{10,6},{14,10},{7,3},{... | collective-permute-start | bytes 98312 | tf_op jit(solution)/shard_map/ppermute | solution.py:481
  31.3 5.6 %collective-permute-start.11 = (bf16[64,384]{1,0:T(8,128)(2,1)S(1)}, bf16[64,384]{1,0:T(8,128)(2,1)S(1)}, u32[]{:S(2)}, u32[]{:S(2)}) collective-permute-start(bf16[64,384]{1,0:T(8,128)(2,1)S(1)} %get-tuple-element.54.refs_11_), channel_id=1, source_target_pairs={{0,3},{1,0},{2,1},{3,2},{4,7},{5,4},{6,5},{7,6},{8,11},{9,8},{10,9... | collective-permute-start | bytes 147464 | tf_op jit(solution)/shard_map/ppermute | solution.py:486
  35.2 30.3 %collective-permute-start.2 = (bf16[1,15,64,128]{3,2,1,0:T(8,128)(2,1)S(1)}, bf16[1,15,64,128]{3,2,1,0:T(8,128)(2,1)S(1)}, u32[]{:S(2)}, u32[]{:S(2)}) collective-permute-start(bf16[1,15,64,128]{3,2,1,0:T(8,128)(2,1)S(1)} %get-tuple-element.39), channel_id=1, source_target_pairs={{0,16},{16,0},{1,17},{17,1},{2,18},{18,2},{3,19},{19,3},{4,20},{20... | collective-permute-start | bytes 737288 | tf_op jit(solution)/shard_map/ppermute | solution.py:447
  36.7 5.0 %collective-permute-start.10 = (bf16[64,384]{1,0:T(8,128)(2,1)S(1)}, bf16[64,384]{1,0:T(8,128)(2,1)S(1)}, u32[]{:S(2)}, u32[]{:S(2)}) collective-permute-start(bf16[64,384]{1,0:T(8,128)(2,1)S(1)} %get-tuple-element.54.refs_11_), channel_id=1, source_target_pairs={{0,2},{1,3},{2,0},{3,1},{4,6},{5,7},{6,4},{7,5},{8,10},{9,11},{10,... | collective-permute-start | bytes 147464 | tf_op jit(solution)/shard_map/ppermute | solution.py:486
  36.9 6.2 %collective-permute-start.9 = (bf16[64,384]{1,0:T(8,128)(2,1)S(1)}, bf16[64,384]{1,0:T(8,128)(2,1)S(1)}, u32[]{:S(2)}, u32[]{:S(2)}) collective-permute-start(bf16[64,384]{1,0:T(8,128)(2,1)S(1)} %get-tuple-element.54.refs_11_), channel_id=1, source_target_pairs={{0,1},{1,2},{2,3},{3,0},{4,5},{5,6},{6,7},{7,4},{8,9},{9,10},{10,1... | collective-permute-start | bytes 147464 | tf_op jit(solution)/shard_map/ppermute | solution.py:486
  48.1 1.5 %collective-permute-start.12 = (bf16[320,128]{1,0:T(8,128)(2,1)S(1)}, bf16[320,128]{1,0:T(8,128)(2,1)S(1)}, u32[]{:S(2)}, u32[]{:S(2)}) collective-permute-start(bf16[320,128]{1,0:T(8,128)(2,1)S(1)} %attend_grad.1.a_ref), channel_id=1, source_target_pairs={{0,4},{4,0},{8,12},{12,8},{1,5},{5,1},{9,13},{13,9},{2,6},{6,2},{1... | collective-permute-start | bytes 245768 | tf_op jit(solution)/shard_map/ppermute | solution.py:71
  49.6 4.8 %collective-permute-start.13 = (bf16[320,128]{1,0:T(8,128)(2,1)S(1)}, bf16[320,128]{1,0:T(8,128)(2,1)S(1)}, u32[]{:S(2)}, u32[]{:S(2)}) collective-permute-start(bf16[320,128]{1,0:T(8,128)(2,1)S(1)} %add.5.refs_7_), channel_id=1, source_target_pairs={{0,8},{4,12},{8,0},{12,4},{1,9},{5,13},{9,1},{13,5},{2,10},{6,14},... | collective-permute-start | bytes 245768 | tf_op jit(solution)/shard_map/ppermute | solution.py:71

commit v4 on v3

v4 whole, which is shorter than its diff:
```python
import functools

import jax
import jax.numpy as jnp
from jax import lax
from jax.experimental import pallas as pl
from jax.experimental.pallas import tpu as pltpu
from jax.sharding import PartitionSpec as P

HD = 128
TILE = 192
STEPS = 50
CH = 64
WINDOW = 640
ONE_LANE = 64
BIAS_LANE = 65
LOW_LANE = 66

SHIFT_FACTOR = 5.0
NOISE_LEVEL = 0.7
MOMENTUM_DECAY = 0.9
LEARNING_RATE = 0.004
LOSS_SCALE = 16384.0
REWARD_FLOOR = 0.1
MASKED = -1e30
LOG2E = 1.4426950408889634

F32 = jnp.float32
BF16 = jnp.bfloat16
NT = (((1,), (1,)), ((), ()))
TN = (((0,), (0,)), ((), ()))
NN = (((1,), (0,)), ((), ()))


VMEM = pl.BlockSpec(memory_space=pltpu.VMEM)
SMEM = pl.BlockSpec(memory_space=pltpu.SMEM)
HBM = pl.BlockSpec(memory_space=pltpu.HBM)
MIB = 1024 * 1024


def in_hbm(x):
    return pltpu.with_memory_space_constraint(x, pltpu.HBM)


def in_vmem(x):
    return pltpu.with_memory_space_constraint(x, pltpu.VMEM)


def params(mib):
    return pltpu.CompilerParams(vmem_limit_bytes=mib * MIB)


def cost(flops, nbytes, exps=0):
    return pl.CostEstimate(flops=flops, bytes_accessed=nbytes, transcendentals=exps)


def dot(a, b, dims=NN):
    return lax.dot_general(a, b, dims, preferred_element_type=F32)


def sigma_at(index, total_steps):
    fraction = index.astype(F32) / total_steps
    return SHIFT_FACTOR * fraction / (1.0 + (SHIFT_FACTOR - 1.0) * fraction)


def advantage_of(rewards, group_ids):
    members = (group_ids == group_ids[:, 0:1]).astype(F32)
    member_total = jnp.sum(members, axis=1, keepdims=True)
    group_mean = jnp.sum(members * rewards, axis=1, keepdims=True) / member_total
    spread = jnp.sqrt(jnp.sum(members * (rewards - group_mean) ** 2, axis=1, keepdims=True) / member_total)
    return (rewards[:, 0:1] - group_mean) / jnp.maximum(spread, REWARD_FLOOR)


def swap(x, axis, bit):
    return lax.ppermute(x, axis, [(i, i ^ bit) for i in range(lax.axis_size(axis))])


def add_kernel(a_ref, b_ref, o_ref):
    o_ref[...] = (a_ref[...].astype(F32) + b_ref[...].astype(F32)).astype(BF16)


def add(a, b):
    return pl.pallas_call(
        add_kernel,
        in_specs=[VMEM, VMEM],
        out_specs=VMEM,
        out_shape=pltpu.VMEM(a.shape, BF16),
        compiler_params=params(4),
        cost_estimate=cost(a.size, 6 * a.size),
        name="add",
    )(a, b)


def butterfly(x, axis):
    bit = 1
    while 2 * bit < lax.axis_size(axis):
        x = add(x, swap(x, axis, bit))
        bit *= 2
    return x, swap(x, axis, bit)


def pick_kernel(place_ref, mine_ref, other_ref, now_ref, next_ref, head_ref, tail_ref):
    mine = mine_ref[...]
    other = other_ref[...]
    sampler = place_ref[1] == 0
    now = jnp.where(sampler, mine.astype(F32), other.astype(F32)).astype(BF16)
    now_ref[...] = now
    next_ref[...] = jnp.where(sampler, other.astype(F32), mine.astype(F32)).astype(BF16)
    spare = head_ref.shape[1]
    head_ref[...] = now[:, :spare]
    tail_ref[...] = now[:, now.shape[1] - spare :]


def pick(place, mine, other, spare):
    shape = pltpu.VMEM(mine.shape, BF16)
    edge = pltpu.VMEM((mine.shape[0], spare), BF16)
    return pl.pallas_call(
        pick_kernel,
        in_specs=[SMEM, VMEM, VMEM],
        out_specs=[VMEM] * 4,
        out_shape=[shape, shape, edge, edge],
        compiler_params=params(4),
        cost_estimate=cost(mine.size, 10 * mine.size),
        name="pick",
    )(place, mine, other)


def narrow(mom_ref, o_ref, stride, first, count, at=0):
    for q in range(stride):
        part = mom_ref[pl.ds(first * stride + q, count, stride=stride), :]
        o_ref[q, pl.ds(at, count), :] = (MOMENTUM_DECAY * part).astype(BF16)


def lead_kernel(stride, count, steps, mom_hbm, o_ref, mom_ref, sems):
    copies = []
    for k in range(steps):
        rows = pl.ds(k * count * stride, count * stride)
        copies.append(pltpu.make_async_copy(mom_hbm.at[rows], mom_ref.at[rows], sems.at[k]))
        copies[-1].start()
    for k in range(steps):
        copies[k].wait()
        narrow(mom_ref, o_ref, stride, k * count, count, k * count)


def lead(mom, stride, count, steps):
    pairs = count * steps
    return pl.pallas_call(
        functools.partial(lead_kernel, stride, count, steps),
        in_specs=[HBM],
        out_specs=VMEM,
        out_shape=pltpu.VMEM((stride, pairs, HD), BF16),
        scratch_shapes=[pltpu.VMEM((pairs * stride, HD), F32), pltpu.SemaphoreType.DMA((steps,))],
        compiler_params=params(4),
        cost_estimate=cost(pairs * stride * HD, 6 * pairs * stride * HD),
        name="lead",
    )(in_hbm(mom))


def prepare_kernel(sizes, stride, skip, sliced, place_ref, e_hbm, mom_hbm, w_hbm, m_ref, et_ref, w_ref, mom_ref, *rest):
    pieces = rest[: len(sizes)]
    e_ref, e_sem, w_sem, mom_sem = rest[len(sizes) :]
    rows = w_ref.shape[1]
    half = rows // 2
    if sliced:
        e_src = e_hbm
    else:
        e_src = e_hbm.at[:, pl.ds(pl.multiple_of(place_ref[0] * rows, HD), rows)]
    e_copy = pltpu.make_async_copy(e_src, e_ref, e_sem)
    e_copy.start()
    w_copies = []
    for m in range(3):
        for k in range(2):
            at = pl.ds(k * half, half)
            w_copies.append(pltpu.make_async_copy(w_hbm.at[m, at], w_ref.at[m, at], w_sem.at[2 * m + k]))
    cuts = [(0, skip, -1, 0)]
    first = skip
    for k, size in enumerate(sizes):
        cuts += [(first + at, skip, k, at) for at in range(0, size, skip)]
        first += size
    mom_copies = []
    for k, (first, count, _, _) in enumerate(cuts):
        rows = pl.ds(first * stride, count * stride)
        mom_copies.append(pltpu.make_async_copy(mom_hbm.at[rows], mom_ref.at[rows], mom_sem.at[k]))
    for copy in w_copies + mom_copies:
        copy.start()
    e_copy.wait()
    et_ref[...] = e_ref[...].astype(F32).T.astype(BF16)
    for m in range(3):
        w_copies[2 * m].wait()
        w_copies[2 * m + 1].wait()
        m_ref[m] = dot(e_ref[...], w_ref[m]).astype(BF16)
    for (first, count, k, at), copy in zip(cuts, mom_copies):
        copy.wait()
        if k >= 0:
            narrow(mom_ref, pieces[k], stride, first, count, at)


def prepare(place, w_embed, mom, w, sizes, stride, skip):
    _, rows, width = w.shape
    sliced = rows % HD != 0
    if sliced:
        w_embed = lax.dynamic_slice_in_dim(w_embed, place[0] * rows, rows, axis=1)
    return pl.pallas_call(
        functools.partial(prepare_kernel, sizes, stride, skip, sliced),
        in_specs=[SMEM, HBM, HBM, HBM],
        out_specs=[VMEM] * (4 + len(sizes)),
        out_shape=[
            pltpu.VMEM((3, CH, width), BF16),
            pltpu.VMEM((rows, CH), BF16),
            pltpu.VMEM(w.shape, BF16),
            pltpu.VMEM(mom.shape, F32),
        ]
        + [pltpu.VMEM((stride, n, HD), BF16) for n in sizes],
        scratch_shapes=[
            pltpu.VMEM((CH, rows), BF16),
            pltpu.SemaphoreType.DMA(()),
            pltpu.SemaphoreType.DMA((6,)),
            pltpu.SemaphoreType.DMA((1 + sum(sizes) // skip,)),
        ],
        compiler_params=params(4),
        cost_estimate=cost(2 * CH * w.size, 4 * w.size + 10 * mom.size),
        name="prepare",
    )(place, in_hbm(w_embed), in_hbm(mom), in_hbm(w))


def forward_kernel(tiles, heads, ends, *refs):
    place_ref, left_ref, now_ref, right_ref, ma_ref, mb_ref, wot_ref = refs[:7]
    m_ref, win_ref, e_ref, u_ref, il_ref, pred_ref, mk_ref, att_ref, t_ref, s_ref = refs[7:]
    tok = tiles * TILE
    m_ref[...] = (ma_ref[...].astype(F32) + mb_ref[...].astype(F32)).astype(BF16)
    mk_ref[...] = jnp.zeros_like(mk_ref)
    mk_ref[0:CH, :] = m_ref[1]

    spare = left_ref.shape[1]
    left = left_ref[...].astype(F32).T[spare - TILE :]
    now = now_ref[...].astype(F32).T
    right = right_ref[...].astype(F32).T[:TILE]
    blocks = [left] + [now[j * TILE : (j + 1) * TILE] for j in range(tiles)] + [right]
    lane = lax.broadcasted_iota(jnp.int32, (TILE, CH), 1) + CH
    flags = jnp.where((lane == ONE_LANE) | (lane == LOW_LANE), 1.0, 0.0)
    seq = place_ref[0]
    for j in range(tiles):
        for k in range(3):
            extra = flags
            if j + k == 0:
                extra = jnp.where(lane == BIAS_LANE, jnp.where(seq == 0, MASKED, 0.0), flags)
            if j + k == tiles + 1:
                extra = jnp.where(lane == BIAS_LANE, jnp.where(seq == ends, MASKED, 0.0), flags)
            win_ref[j, k * TILE : (k + 1) * TILE, :] = jnp.concatenate([blocks[j + k], extra], axis=1).astype(BF16)
        pad_lane = lax.broadcasted_iota(jnp.int32, (WINDOW - 3 * TILE, HD), 1)
        win_ref[j, 3 * TILE :, :] = jnp.where(pad_lane == BIAS_LANE, MASKED, 0.0).astype(BF16)

    lane = lax.broadcasted_iota(jnp.int32, (tok, HD), 1)
    unit = jnp.where(lane == BIAS_LANE, 1.0, 0.0)
    factor = LOG2E * HD ** (-0.5)
    queries = dot(now.astype(BF16), m_ref[0]).astype(BF16)
    for h in range(heads):
        cols = slice(h * HD, (h + 1) * HD)
        t = (dot(queries[:, cols], mk_ref[:, cols], NT) * factor + unit).astype(BF16)
        for j in range(tiles):
            t_ref[j, h * TILE : (h + 1) * TILE, :] = t[j * TILE : (j + 1) * TILE]
    for j in range(tiles):
        keys = win_ref[j]
        s_ref[...] = dot(t_ref[j], keys, NT)
        for h in range(heads):
            rows = slice(h * TILE, (h + 1) * TILE)
            s = s_ref[rows, :]
            e_ref[j, rows, :] = jnp.exp2(s - jnp.max(s, axis=1, keepdims=True)).astype(BF16)
        u = dot(e_ref[j], keys)
        inv = 1.0 / u[:, ONE_LANE : ONE_LANE + 1]
        u = (u * inv).astype(BF16)
        inv = jnp.broadcast_to(inv, u.shape)
        for h in range(heads):
            rows = slice(h * TILE, (h + 1) * TILE)
            at = slice(h * tok + j * TILE, h * tok + (j + 1) * TILE)
            u_ref[at, :] = u[rows]
            il_ref[at, :] = inv[rows]
    for h in range(heads):
        cols = slice(h * HD, (h + 1) * HD)
        att_ref[:, cols] = dot(u_ref[h * tok : (h + 1) * tok, 0:CH], m_ref[2, :, cols]).astype(BF16)
    pred_ref[...] = dot(wot_ref[...], att_ref[...], NT).astype(BF16)


def forward(place, left, now, right, ma, mb, wot, tiles, heads, seq_count):
    tok = tiles * TILE
    rows = heads * tok
    width = heads * HD
    return pl.pallas_call(
        functools.partial(forward_kernel, tiles, heads, seq_count - 1),
        in_specs=[SMEM] + [VMEM] * 6,
        out_specs=[VMEM] * 6,
        out_shape=[
            pltpu.VMEM((3, CH, width), BF16),
            pltpu.VMEM((tiles, WINDOW, HD), BF16),
            pltpu.VMEM((tiles, heads * TILE, WINDOW), BF16),
            pltpu.VMEM((rows, HD), BF16),
            pltpu.VMEM((rows, HD), F32),
            pltpu.VMEM((CH, tok), BF16),
        ],
        scratch_shapes=[
            pltpu.VMEM((HD, width), BF16),
            pltpu.VMEM((tok, width), BF16),
            pltpu.VMEM((tiles, heads * TILE, HD), BF16),
            pltpu.VMEM((heads * TILE, WINDOW), F32),
        ],
        compiler_params=params(12),
        cost_estimate=cost(rows * (WINDOW + CH) * 4 * HD, 20 * rows * WINDOW, rows * WINDOW),
        name="attend",
    )(place, left, now, right, ma, mb, wot)


def backward_kernel(tiles, heads, tokens_all, *refs):
    (time_ref, rewards_ref, groups_ref, win_ref, m_ref, wot_ref, e_ref, u_ref, il_ref, now_ref, next_ref) = refs[:11]
    pred_refs = refs[11:-6]
    zy_ref, mv_ref, v_ref, t_ref, s_ref, d_ref = refs[-6:]
    tok = tiles * TILE
    mv_ref[...] = jnp.zeros_like(mv_ref)
    mv_ref[0:CH, :] = m_ref[2]
    lane = lax.broadcasted_iota(jnp.int32, (tok, HD), 1)
    scale = HD ** (-0.5)
    advantage = advantage_of(rewards_ref[...], groups_ref[...])
    index = jnp.full((1, 1), time_ref[0], jnp.int32)
    sigma_now = sigma_at(index, STEPS)
    step_size = sigma_at(index - 1, STEPS) - sigma_now
    coefficient = advantage * LOSS_SCALE * (1.0 - sigma_now) / (NOISE_LEVEL**2 * sigma_now * tokens_all)
    pred = pred_refs[0][...].astype(F32)
    for ref in pred_refs[1:]:
        pred = pred + ref[...].astype(F32)
    step_mean = now_ref[...].astype(F32) + step_size * pred
    pg_flat = coefficient * (next_ref[...].astype(F32) - step_mean)
    pg = pg_flat.T.astype(BF16)
    pg_flat = pg_flat.astype(BF16)
    ag_all = dot(pg, wot_ref[...]).astype(BF16)
    for h in range(heads):
        cols = slice(h * HD, (h + 1) * HD)
        rows = slice(h * tok, (h + 1) * tok)
        w = dot(ag_all[:, cols], mv_ref[:, cols], NT).astype(BF16).astype(F32)
        row_dot = jnp.sum(w * u_ref[rows, :].astype(F32), axis=1, keepdims=True)
        factor = scale * il_ref[rows, :]
        w = w * factor
        row_dot = row_dot * factor
        high = row_dot.astype(BF16).astype(F32)
        low = row_dot - high
        w = jnp.where(lane == ONE_LANE, -high, jnp.where(lane == LOW_LANE, -low, w)).astype(BF16)
        for j in range(tiles):
            t_ref[j, h * TILE : (h + 1) * TILE, :] = w[j * TILE : (j + 1) * TILE]
    for j in range(tiles):
        keys = win_ref[j]
        s_ref[...] = dot(t_ref[j], keys, NT)
        for h in range(heads):
            rows = slice(h * TILE, (h + 1) * TILE)
            d_ref[rows, :] = (e_ref[j, rows, :].astype(F32) * s_ref[rows, :]).astype(BF16)
        v = dot(d_ref[...], keys).astype(BF16)
        for h in range(heads):
            v_ref[h * tok + j * TILE : h * tok + (j + 1) * TILE, :] = v[h * TILE : (h + 1) * TILE]
    now = now_ref[...]
    for h in range(heads):
        rows = slice(h * tok, (h + 1) * tok)
        z = dot(now, v_ref[rows, :])
        y = dot(pg_flat, u_ref[rows, :])
        zy_ref[h * CH : (h + 1) * CH, :] = jnp.concatenate([z[:, 0:CH], y[:, 0:CH]], axis=1).astype(BF16)


def backward(timestep, rewards, group_ids, win, m, wot, e, u, il, now, later, preds, tiles, heads, tokens_all):
    width = heads * HD
    return pl.pallas_call(
        functools.partial(backward_kernel, tiles, heads, tokens_all),
        in_specs=[SMEM] + [VMEM] * (10 + len(preds)),
        out_specs=VMEM,
        out_shape=pltpu.VMEM((heads * CH, HD), BF16),
        scratch_shapes=[
            pltpu.VMEM((HD, width), BF16),
            pltpu.VMEM((heads * tiles * TILE, HD), BF16),
            pltpu.VMEM((tiles, heads * TILE, HD), BF16),
            pltpu.VMEM((heads * TILE, WINDOW), F32),
            pltpu.VMEM((heads * TILE, WINDOW), BF16),
        ],
        compiler_params=params(12),
        cost_estimate=cost(width * tiles * TILE * (WINDOW + CH) * 4, 20 * heads * tiles * TILE * WINDOW),
        name="attend_grad",
    )(timestep, rewards, group_ids, win, m, wot, e, u, il, now, later, *preds)


def update_kernel(heads, unit, sizes, first, later, *refs):
    place_ref, et_ref, mom_ref, w_ref = refs[:4]
    recv_refs = refs[4 : 4 + len(sizes)]
    rest = refs[4 + len(sizes) :]
    if later:
        g_ref = rest[0]
        onm_hbm, ow_hbm, gs_ref, fs_ref, onm_ref, ow_ref, sems = rest[3:]
    else:
        za_ref, zb_ref, m_ref, wot_ref, onm_hbm, ow_hbm, g_ref, gs_ref, fs_ref, onm_ref, ow_ref, sems = rest
    stride = 3 * heads
    role = place_ref[1]
    slots = onm_ref.shape[0]

    if not later:
        for h in range(heads):
            cols = slice(h * HD, (h + 1) * HD)
            rows = slice(h * CH, (h + 1) * CH)
            zy = (za_ref[rows, :].astype(F32) + zb_ref[rows, :].astype(F32)).astype(BF16)
            z = zy[:, 0:CH]
            y = zy[:, CH : 2 * CH]
            g_ref[0, :, cols] = dot(z, m_ref[1, :, cols]).astype(BF16)
            g_ref[1, :, cols] = dot(z, m_ref[0, :, cols], TN).astype(BF16)
            g_ref[2, :, cols] = dot(y, wot_ref[:, cols], TN).astype(BF16)

    total = sum(sizes)
    for part in range(3):
        g = dot(et_ref[2 * first : 2 * (first + total), :], g_ref[part])
        for b in range(heads):
            gs_ref[part * heads + b] = g[:, b * HD : (b + 1) * HD]

    def copies(pair, count, slot):
        lin = pl.ds(pair * stride, count * stride)
        rows = pl.ds(2 * pair, 2 * count)
        return [
            pltpu.make_async_copy(onm_ref.at[slot, pl.ds(0, count * stride)], onm_hbm.at[lin], sems.at[0, slot]),
            pltpu.make_async_copy(ow_ref.at[slot, :, pl.ds(0, 2 * count)], ow_hbm.at[:, rows], sems.at[1, slot]),
        ]

    order = []
    pair = first
    for k, size in enumerate(sizes):
        count = 2 * unit if size % (2 * unit) == 0 else unit
        for i in range(size // count):
            order.append((k, i * count, pair, count))
            pair += count
    for step, (k, at, pair, count) in enumerate(order):
        slot = step % slots
        if step >= slots:
            for copy in copies(*order[step - slots][2:], slot):
                copy.wait()
        natural = slice(2 * pair, 2 * (pair + count))
        local = 2 * (pair - first)
        mine = pl.ds(role, count, stride=2)
        theirs = pl.ds(1 - role, count, stride=2)
        for q in range(stride):
            part, b = divmod(q, heads)
            cols = slice(b * HD, (b + 1) * HD)
            own = MOMENTUM_DECAY * mom_ref[pl.ds(pair * stride + q, count, stride=stride), :]
            own = own + gs_ref[q, pl.ds(local + role, count, stride=2), :]
            other = recv_refs[k][q, at : at + count, :].astype(F32)
            other = other + gs_ref[q, pl.ds(local + 1 - role, count, stride=2), :]
            onm_ref[slot, pl.ds(q, count, stride=stride), :] = own
            fs_ref[q, mine, :] = own
            fs_ref[q, theirs, :] = other
            new = w_ref[part, natural, cols].astype(F32) - LEARNING_RATE * fs_ref[q, 0 : 2 * count, :]
            ow_ref[slot, part, 0 : 2 * count, cols] = new.astype(BF16)
        for copy in copies(pair, count, slot):
            copy.start()
    for step in range(max(len(order) - slots, 0), len(order)):
        for copy in copies(*order[step][2:], step % slots):
            copy.wait()


def update(place, et, mom, w, received, first, unit, heads, sources=None, before=None):
    sizes = [a.shape[1] for a in received]
    _, rows, width = w.shape
    stride = 3 * heads
    slots = min(sum(sizes) // unit, 4)
    most = max(2 * unit if n % (2 * unit) == 0 else unit for n in sizes)
    args = [place, et, in_vmem(mom), in_vmem(w), *received]
    in_specs = [SMEM] + [VMEM] * (3 + len(received))
    out_specs = [HBM, HBM]
    out_shape = [jax.ShapeDtypeStruct((rows // 2 * stride, HD), F32), jax.ShapeDtypeStruct(w.shape, BF16)]
    aliases = {}
    if before is None:
        args += sources
        in_specs += [VMEM] * len(sources)
        out_specs.append(VMEM)
        out_shape.append(pltpu.VMEM((3, CH, width), BF16))
    else:
        new_mom, new_w, g = before
        aliases = {len(args) + 1: 0, len(args) + 2: 1}
        args += [g, new_mom, new_w]
        in_specs += [VMEM, HBM, HBM]
    return pl.pallas_call(
        functools.partial(update_kernel, heads, unit, sizes, first, before is not None),
        in_specs=in_specs,
        out_specs=out_specs,
        out_shape=out_shape,
        input_output_aliases=aliases,
        scratch_shapes=[
            pltpu.VMEM((stride, 2 * sum(sizes), HD), F32),
            pltpu.VMEM((stride, 2 * most, HD), F32),
            pltpu.VMEM((slots, most * stride, HD), F32),
            pltpu.VMEM((slots, 3, 2 * most, width), BF16),
            pltpu.SemaphoreType.DMA((2, slots)),
        ],
        compiler_params=params(14),
        cost_estimate=cost(2 * sum(sizes) * stride * HD * 2 * CH, 22 * sum(sizes) * stride * HD),
        name="update",
    )(*args)


def exchange(x):
    return lax.ppermute(x, "role", [(0, 1), (1, 0)])


def body(rollout, w_embed, w_qkv, w_out, momentum, rewards, group_ids, timestep):
    seq_count = lax.axis_size("seq")
    seq_index = lax.axis_index("seq")
    role_index = lax.axis_index("role")
    rows_dev = w_qkv.shape[0]
    width = w_qkv.shape[2]
    heads = width // HD
    tok_dev = rollout.shape[1]
    tiles = tok_dev // TILE
    pair_rows = rows_dev // 2

    stride = 3 * heads
    unit = pair_rows // 20
    sizes = (2 * unit, 10 * unit, 6 * unit, 2 * unit)
    mom = momentum.reshape(pair_rows * stride, HD)
    w = w_qkv.transpose(1, 0, 2)
    wot = w_out.T
    place = jnp.stack([seq_index, role_index])

    mine = rollout[0].T
    other = exchange(mine)
    piece = lead(mom, stride, unit, 2)
    received = [exchange(piece)]
    mom, piece = lax.optimization_barrier((mom, piece))
    m, et, w, mom, *pieces = prepare(place, w_embed, mom, w, sizes[1:], stride, sizes[0])
    other, pieces = lax.optimization_barrier((other, pieces))
    received += [exchange(p) for p in pieces[:-1]]
    m, received[0] = lax.optimization_barrier((m, received[0]))
    ma, mb = butterfly(m, "seq")

    latent_now, latent_next, head, tail = pick(place, mine, other, min(2 * HD, tok_dev))
    left = lax.ppermute(tail, "seq", [(i, i + 1) for i in range(seq_count - 1)])
    right = lax.ppermute(head, "seq", [(i + 1, i) for i in range(seq_count - 1)])

    m, win, e, u, il, partial_pred = forward(place, left, latent_now, right, ma, mb, wot, tiles, heads, seq_count)
    mp_count = lax.axis_size("mp")
    preds = [partial_pred] + [
        lax.ppermute(partial_pred, "mp", [(i, (i + d) % mp_count) for i in range(mp_count)])
        for d in range(1, mp_count)
    ]
    za, zb = butterfly(
        backward(
            timestep,
            rewards[None],
            group_ids[None],
            win,
            m,
            wot,
            e,
            u,
            il,
            latent_now,
            latent_next,
            preds,
            tiles,
            heads,
            tok_dev * seq_count,
        ),
        "seq",
    )

    zb, last = lax.optimization_barrier((zb, pieces[-1]))
    received.append(exchange(last))
    done = update(place, et, mom, w, received[:2], 0, unit, heads, sources=[za, zb, m, wot])
    g = done[2]
    first = sizes[0] + sizes[1]
    done = update(place, et, mom, w, received[2:3], first, unit, heads, before=[*done[:2], g])
    nm, nw = update(place, et, mom, w, received[3:], first + sizes[2], unit, heads, before=[*done, g])
    return nm.reshape(momentum.shape), nw.transpose(1, 0, 2)


def solution(mesh):
    in_specs = (
        P("role", "seq", None),
        P(),
        P("seq", None, "mp"),
        P("mp", None),
        P("seq", "role", None, "mp"),
        P(),
        P(),
        P(),
    )
    out_specs = (P("seq", "role", None, "mp"), P("seq", None, "mp"))
    return jax.shard_map(body, mesh=mesh, in_specs=in_specs, out_specs=out_specs, check_vma=False)
```

time: 67.9 us -> 62.9 us (0.926)
  Pallas kernels: 29.4 us -> 24.1 us
    pallas_call x1, Pallas kernels: 7.02 us -> 3.63 us  [forward(): pl.pallas_call(functools.partial(forward_kernel, tiles, heads, seq_count...]
    pallas_call x1, Pallas kernels: 4.96 us -> 2.88 us  [backward(): pl.pallas_call(functools.partial(backward_kernel, tiles, heads, tokens_al...]
    ppermute x3, waiting for transfers between devices: 5.05 us -> 4.23 us  [body(): lax.ppermute(partial_pred, 'mp', [(i, (i + d) % mp_count) for i in range(...]
    ppermute x5, starting transfers between devices: 6.48 us -> 7.18 us  [exchange(): return lax.ppermute(x, 'role', [(0, 1), (1, 0)])]
    pallas_call x4 -> x5, Pallas kernels: 16.8 us -> 16.9 us  [the longest x3 9.74 us: update(): pl.pallas_call(functools.partial(update_kernel, heads, unit, sizes, first...]
  transfers between devices with their start and end apart: 14 -> 14, of which waited for: 10 -> 10; matrix products, arithmetic and copies ran while one was open for 0% -> 0% of each run, Pallas kernels for 38% -> 35%
where the time goes in v4:
time: 62.9 us; the launch traced here: 62.7 us
  Pallas kernels  24.1 us (38%)
  starting transfers between devices  19 us (30%)
  waiting for transfers between devices  18.1 us (29%)
  between operations  1.54 us (2%)
    pallas_call x3, Pallas kernels, update(): pl.pallas_call(functools.partial(update_kernel, heads, unit, sizes, first...  9.74 us
    ppermute x5, starting transfers between devices, exchange(): return lax.ppermute(x, 'role', [(0, 1), (1, 0)])  7.18 us
    ppermute x4, waiting for transfers between devices, swap(): lax.ppermute(x, axis, [(i, i ^ bit) for i in range(lax.axis_size(axis))])  6.41 us
    pallas_call x1, Pallas kernels, prepare(): pl.pallas_call(functools.partial(prepare_kernel, sizes, stride, skip, sli...  6.05 us
    ppermute x5, waiting for transfers between devices, exchange(): return lax.ppermute(x, 'role', [(0, 1), (1, 0)])  5.51 us
    ppermute x3, starting transfers between devices, body(): lax.ppermute(partial_pred, 'mp', [(i, (i + d) % mp_count) for i in range(...  4.66 us
    ppermute x4, starting transfers between devices, swap(): lax.ppermute(x, axis, [(i, i ^ bit) for i in range(lax.axis_size(axis))])  4.36 us
    ppermute x3, waiting for transfers between devices, body(): lax.ppermute(partial_pred, 'mp', [(i, (i + d) % mp_count) for i in range(...  4.23 us
  transfers between devices with their start and end apart: 14, of which 10 were waited for; matrix products, arithmetic and copies ran while one was open for 0% of the time, Pallas kernels for 35%

profile of v4, /device:TPU:0, one launch (start us, length us, event | category | flops | bytes accessed | tf_op | source)
XLA Modules:
  0.0 62.7 jit_solution(2557890134825595493)
XLA Ops:
  0.6 3.0 %collective-permute-start = (bf16[64,384]{1,0:T(8,128)(2,1)}, bf16[64,384]{1,0:T(8,128)(2,1)S(1)}, u32[]{:S(2)}, u32[]{:S(2)}) collective-permute-start(bf16[64,384]{1,0:T(8,128)(2,1)} %bitcast.15), channel_id=1, source_target_pairs={{0,16},{16,0},{1,17},{17,1},{2,18},{18,2},{3,19},{19,3},{4,20},{20... | collective-permute-start | bytes 147464 | tf_op jit(solution)/shard_map/ppermute | solution.py:498
  3.6 1.1 %lead.1 = bf16[15,64,128]{2,1,0:T(8,128)(2,1)S(1)} custom-call(f32[9600,128]{1,0:T(8,128)} %bitcast.19), custom_call_target="tpu_custom_call" | custom-call | flops 122880 | bytes 737280 | tf_op jit(solution)/shard_map/lead/pallas_call | solution.py:147
  4.7 0.1 collective-permute-start.3
  4.8 0.1 pad_add_fusion.place_ref.refs_0_
  4.9 0.0 copy-start.1
  4.9 0.0 copy-start
  4.9 0.0 copy-start.2
  4.9 0.0 copy-start.3
  4.9 6.0 %prepare.1 = (bf16[3,64,640]{2,1,0:T(8,128)(2,1)S(1)}, bf16[1280,64]{1,0:T(8,128)(2,1)S(1)}, bf16[3,1280,640]{2,1,0:T(8,128)(2,1)S(1)}, f32[9600,128]{1,0:T(8,12...) custom-call(s32[2]{0:T(128)S(1)} %pad_add_fusion.place_ref.refs_0_, ...), custom_call_target="tpu_custom_call" | custom-call | flops 314572800 | bytes 22118400 | tf_op jit(solution)/shard_map/prepare/pallas_call | solution.py:203
  11.0 0.0 collective-permute-done.other_ref
  11.0 2.1 %collective-permute-start.12 = (bf16[15,320,128]{2,1,0:T(8,128)(2,1)S(1)}, bf16[15,320,128]{2,1,0:T(8,128)(2,1)S(1)}, u32[]{:S(2)}, u32[]{:S(2)}) collective-permute-start(bf16[15,320,128]{2,1,0:T(8,128)(2,1)S(1)} %get-tuple-element.58), channel_id=1, source_target_pairs={{0,16},{16,0},{1,17},{17,1},{2,18},{18,2},{3,19},{19,3},{4,20},{20... | collective-permute-start | bytes 3686408 | tf_op jit(solution)/shard_map/ppermute | solution.py:498
  13.1 0.0 collective-permute-done.3.refs_4_
  13.1 0.0 collective-permute-start.4
  13.1 1.5 %collective-permute-done.4.b_ref = bf16[3,64,640]{2,1,0:T(8,128)(2,1)S(1)} collective-permute-done((bf16[3,64,640]{2,1,0:T(8,128)(2,1)S(1)}, bf16[3,64,640]{2,1,0:T(8,128)(2,1)S(1)}, u32[]{:S(2)}, u32[]{:S(2)}) %collective-permute-start.4) | collective-permute-done | bytes 245792 | tf_op jit(solution)/shard_map/ppermute | solution.py:75
  14.6 0.1 add.4.refs_4_
  14.6 1.6 %collective-permute-start.5 = (bf16[3,64,640]{2,1,0:T(8,128)(2,1)S(1)}, bf16[3,64,640]{2,1,0:T(8,128)(2,1)S(1)}, u32[]{:S(2)}, u32[]{:S(2)}) collective-permute-start(bf16[3,64,640]{2,1,0:T(8,128)(2,1)S(1)} %add.4.refs_4_), channel_id=1, source_target_pairs={{0,8},{4,12},{8,0},{12,4},{1,9},{5,13},{9,1},{13,5},{2,10},{6,14},... | collective-permute-start | bytes 737288 | tf_op jit(solution)/shard_map/ppermute | solution.py:75
  16.2 0.5 collective-permute-start.13
  16.8 0.0 copy-done.1
  16.8 0.6 pick.1
  17.3 1.5 %collective-permute-start.1 = (bf16[64,256]{1,0:T(8,128)(2,1)S(1)}, bf16[64,256]{1,0:T(8,128)(2,1)S(1)}, u32[]{:S(2)}, u32[]{:S(2)}) collective-permute-start(bf16[64,256]{1,0:T(8,128)(2,1)S(1)} %get-tuple-element.43), channel_id=1, source_target_pairs={{0,4},{4,8},{8,12},{1,5},{5,9},{9,13},{2,6},{6,10},{10,14},{3,7},{... | collective-permute-start | bytes 98312 | tf_op jit(solution)/shard_map/ppermute | solution.py:532
  18.8 1.3 %collective-permute-start.2 = (bf16[64,256]{1,0:T(8,128)(2,1)S(1)}, bf16[64,256]{1,0:T(8,128)(2,1)S(1)}, u32[]{:S(2)}, u32[]{:S(2)}) collective-permute-start(bf16[64,256]{1,0:T(8,128)(2,1)S(1)} %get-tuple-element.45), channel_id=1, source_target_pairs={{4,0},{8,4},{12,8},{5,1},{9,5},{13,9},{6,2},{10,6},{14,10},{7,3},{... | collective-permute-start | bytes 98312 | tf_op jit(solution)/shard_map/ppermute | solution.py:533
  20.1 0.0 collective-permute-done.1.refs_1_
  20.1 1.9 %collective-permute-done.2.refs_3_ = bf16[64,256]{1,0:T(8,128)(2,1)S(1)} collective-permute-done((bf16[64,256]{1,0:T(8,128)(2,1)S(1)}, bf16[64,256]{1,0:T(8,128)(2,1)S(1)}, u32[]{:S(2)}, u32[]{:S(2)}) %collective-permute-start.2) | collective-permute-done | bytes 32800 | tf_op jit(solution)/shard_map/ppermute | solution.py:533
  22.0 0.7 %collective-permute-done.5.refs_5_ = bf16[3,64,640]{2,1,0:T(8,128)(2,1)S(1)} collective-permute-done((bf16[3,64,640]{2,1,0:T(8,128)(2,1)S(1)}, bf16[3,64,640]{2,1,0:T(8,128)(2,1)S(1)}, u32[]{:S(2)}, u32[]{:S(2)}) %collective-permute-start.5) | collective-permute-done | bytes 245792 | tf_op jit(solution)/shard_map/ppermute | solution.py:75
  22.7 0.0 copy-done
  22.7 3.6 %attend.1 = (bf16[3,64,640]{2,1,0:T(8,128)(2,1)S(1)}, bf16[2,640,128]{2,1,0:T(8,128)(2,1)S(1)}, bf16[2,960,640]{2,1,0:T(8,128)(2,1)S(1)}, bf16[1920,128]{1,0:T(8...) custom-call(s32[2]{0:T(128)S(1)} %pad_add_fusion.place_ref.refs_0_, ...), custom_call_target="tpu_custom_call" | custom-call | flops 692060160 | bytes 24576000 | tf_op jit(solution)/shard_map/attend/pallas_call | solution.py:288
  26.3 3.6 %collective-permute-start.8 = (bf16[64,384]{1,0:T(8,128)(2,1)S(1)}, bf16[64,384]{1,0:T(8,128)(2,1)S(1)}, u32[]{:S(2)}, u32[]{:S(2)}) collective-permute-start(bf16[64,384]{1,0:T(8,128)(2,1)S(1)} %get-tuple-element.54.refs_11_), channel_id=1, source_target_pairs={{0,3},{1,0},{2,1},{3,2},{4,7},{5,4},{6,5},{7,6},{8,11},{9,8},{10,9... | collective-permute-start | bytes 147464 | tf_op jit(solution)/shard_map/ppermute | solution.py:538
  30.0 0.0 collective-permute-start.7
  30.0 1.0 %collective-permute-start.6 = (bf16[64,384]{1,0:T(8,128)(2,1)S(1)}, bf16[64,384]{1,0:T(8,128)(2,1)S(1)}, u32[]{:S(2)}, u32[]{:S(2)}) collective-permute-start(bf16[64,384]{1,0:T(8,128)(2,1)S(1)} %get-tuple-element.54.refs_11_), channel_id=1, source_target_pairs={{0,1},{1,2},{2,3},{3,0},{4,5},{5,6},{6,7},{7,4},{8,9},{9,10},{10,1... | collective-permute-start | bytes 147464 | tf_op jit(solution)/shard_map/ppermute | solution.py:538
  31.7 0.1 collective-permute-done.8.refs_14_
  31.7 3.6 %collective-permute-done.7.refs_13_ = bf16[64,384]{1,0:T(8,128)(2,1)S(1)} collective-permute-done((bf16[64,384]{1,0:T(8,128)(2,1)S(1)}, bf16[64,384]{1,0:T(8,128)(2,1)S(1)}, u32[]{:S(2)}, u32[]{:S(2)}) %collective-permute-start.7) | collective-permute-done | bytes 49184 | tf_op jit(solution)/shard_map/ppermute | solution.py:538
  35.3 0.6 collective-permute-done.6.refs_12_
  35.9 0.0 copy-done.2
  35.9 0.0 copy-done.3
  35.9 2.9 %attend_grad.1.a_ref = bf16[320,128]{1,0:T(8,128)(2,1)S(1)} custom-call(s32[1]{0:T(128)S(6)} %copy.20.refs_0_, f32[1,32]{1,0:T(1,128)S(1)} %bitcast.17, s32[1,32]{1,0:T(1,128)S(1)} %bitcast.18, bf16[2,640,128]{2,1,0:T(8,128)(2,1)S(1)} %get-tuple-element.48.refs_3_, bf16[3,64,640]{2,1,0:T(8,128)(2,1)S(1)} %get-tuple-element.49.refs_4_.refs_8_, ...), custom_call_target="tpu_custom_call" | custom-call | flops 692060160 | bytes 24576000 | tf_op jit(solution)/shard_map/attend_grad/pallas_call | solution.py:366
  38.8 1.3 %collective-permute-start.9 = (bf16[320,128]{1,0:T(8,128)(2,1)S(1)}, bf16[320,128]{1,0:T(8,128)(2,1)S(1)}, u32[]{:S(2)}, u32[]{:S(2)}) collective-permute-start(bf16[320,128]{1,0:T(8,128)(2,1)S(1)} %attend_grad.1.a_ref), channel_id=1, source_target_pairs={{0,4},{4,0},{8,12},{12,8},{1,5},{5,1},{9,13},{13,9},{2,6},{6,2},{1... | collective-permute-start | bytes 245768 | tf_op jit(solution)/shard_map/ppermute | solution.py:75
  40.1 0.9 %collective-permute-done.9.b_ref = bf16[320,128]{1,0:T(8,128)(2,1)S(1)} collective-permute-done((bf16[320,128]{1,0:T(8,128)(2,1)S(1)}, bf16[320,128]{1,0:T(8,128)(2,1)S(1)}, u32[]{:S(2)}, u32[]{:S(2)}) %collective-permute-start.9) | collective-permute-done | bytes 81952 | tf_op jit(solution)/shard_map/ppermute | solution.py:75
  41.0 1.4 %collective-permute-start.10 = (bf16[320,128]{1,0:T(8,128)(2,1)S(1)}, bf16[320,128]{1,0:T(8,128)(2,1)S(1)}, u32[]{:S(2)}, u32[]{:S(2)}) collective-permute-start(bf16[320,128]{1,0:T(8,128)(2,1)S(1)} %add.5.refs_6_), channel_id=1, source_target_pairs={{0,8},{4,12},{8,0},{12,4},{1,9},{5,13},{9,1},{13,5},{2,10},{6,14},... | collective-permute-start | bytes 245768 | tf_op jit(solution)/shard_map/ppermute | solution.py:75
  42.5 3.3 %collective-permute-done.10.refs_7_ = bf16[320,128]{1,0:T(8,128)(2,1)S(1)} collective-permute-done((bf16[320,128]{1,0:T(8,128)(2,1)S(1)}, bf16[320,128]{1,0:T(8,128)(2,1)S(1)}, u32[]{:S(2)}, u32[]{:S(2)}) %collective-permute-start.10) | collective-permute-done | bytes 81952 | tf_op jit(solution)/shard_map/ppermute | solution.py:75
  45.8 1.5 %collective-permute-start.11 = (bf16[15,64,128]{2,1,0:T(8,128)(2,1)S(1)}, bf16[15,64,128]{2,1,0:T(8,128)(2,1)S(1)}, u32[]{:S(2)}, u32[]{:S(2)}) collective-permute-start(bf16[15,64,128]{2,1,0:T(8,128)(2,1)S(1)} %get-tuple-element.56), channel_id=1, source_target_pairs={{0,16},{16,0},{1,17},{17,1},{2,18},{18,2},{3,19},{19,3},{4,20},{20... | collective-permute-start | bytes 737288 | tf_op jit(solution)/shard_map/ppermute | solution.py:498
  47.3 0.0 collective-permute-done.12.refs_5_
  47.3 4.7 %update.3 = (f32[9600,128]{1,0:T(8,128)}, bf16[3,1280,640]{2,1,0:T(8,128)(2,1)}, bf16[3,64,640]{2,1,0:T(8,128)(2,1)S(1)}) custom-call(s32[2]{0:T(128)S(1)} %pad_add_fusion.place_ref.refs_0_, bf16[1280,64]{1,0:T(8,128)(2,1)S(1)} %get-tuple-element.36.refs_1_, f32[9600,128]{1,0:T(8,128)S(1)} %get-tuple-element.37.refs_2_, ...), custom_call_target="tpu_custom_call" | custom-call | flops 188743680 | bytes 16220160 | tf_op jit(solution)/shard_map/update/pallas_call | solution.py:478
  52.1 4.7 %collective-permute-done.13.refs_4_ = bf16[15,192,128]{2,1,0:T(8,128)(2,1)S(1)} collective-permute-done((bf16[15,192,128]{2,1,0:T(8,128)(2,1)S(1)}, bf16[15,192,128]{2,1,0:T(8,128)(2,1)S(1)}, u32[]{:S(2)}, u32[]{:S(2)}) %collective-permute-start.13) | collective-permute-done | bytes 737312 | tf_op jit(solution)/shard_map/ppermute | solution.py:498
  56.8 3.0 %update.4 = (f32[9600,128]{1,0:T(8,128)}, bf16[3,1280,640]{2,1,0:T(8,128)(2,1)}) custom-call(s32[2]{0:T(128)S(1)} %pad_add_fusion.place_ref.refs_0_, bf16[1280,64]{1,0:T(8,128)(2,1)S(1)} %get-tuple-element.36.refs_1_, f32[9600,128]{1,0:T(8,128)S(1)} %get-tuple-element.37.refs_2_, ...), custom_call_target="tpu_custom_call", output_to_operand_aliasing={{0}: (6, {}), {1}: (7, {})} | custom-call | flops 94371840 | bytes 8110080 | tf_op jit(solution)/shard_map/update/pallas_call | solution.py:478
  59.8 0.8 %collective-permute-done.11.refs_4_ = bf16[15,64,128]{2,1,0:T(8,128)(2,1)S(1)} collective-permute-done((bf16[15,64,128]{2,1,0:T(8,128)(2,1)S(1)}, bf16[15,64,128]{2,1,0:T(8,128)(2,1)S(1)}, u32[]{:S(2)}, u32[]{:S(2)}) %collective-permute-start.11) | collective-permute-done | bytes 245792 | tf_op jit(solution)/shard_map/ppermute | solution.py:498
  60.6 2.0 %update.5 = (f32[9600,128]{1,0:T(8,128)}, bf16[3,1280,640]{2,1,0:T(8,128)(2,1)}) custom-call(s32[2]{0:T(128)S(1)} %pad_add_fusion.place_ref.refs_0_, bf16[1280,64]{1,0:T(8,128)(2,1)S(1)} %get-tuple-element.36.refs_1_, f32[9600,128]{1,0:T(8,128)S(1)} %get-tuple-element.37.refs_2_, ...), custom_call_target="tpu_custom_call", output_to_operand_aliasing={{0}: (6, {}), {1}: (7, {})} | custom-call | flops 31457280 | bytes 2703360 | tf_op jit(solution)/shard_map/update/pallas_call | solution.py:478
  (1 shorter events, 0.0 us)
Async XLA Ops:
  0.6 10.3 %collective-permute-start = (bf16[64,384]{1,0:T(8,128)(2,1)}, bf16[64,384]{1,0:T(8,128)(2,1)S(1)}, u32[]{:S(2)}, u32[]{:S(2)}) collective-permute-start(bf16[64,384]{1,0:T(8,128)(2,1)} %bitcast.15), channel_id=1, source_target_pairs={{0,16},{16,0},{1,17},{17,1},{2,18},{18,2},{3,19},{19,3},{4,20},{20... | collective-permute-start | bytes 147464 | tf_op jit(solution)/shard_map/ppermute | solution.py:498
  4.7 8.3 %collective-permute-start.3 = (bf16[15,64,128]{2,1,0:T(8,128)(2,1)S(1)}, bf16[15,64,128]{2,1,0:T(8,128)(2,1)S(1)}, u32[]{:S(2)}, u32[]{:S(2)}) collective-permute-start(bf16[15,64,128]{2,1,0:T(8,128)(2,1)S(1)} %lead.1), channel_id=1, source_target_pairs={{0,16},{16,0},{1,17},{17,1},{2,18},{18,2},{3,19},{19,3},{4,20},{20... | collective-permute-start | bytes 737288 | tf_op jit(solution)/shard_map/ppermute | solution.py:498
  4.9 11.9 %copy-start.1 = (bf16[1,384,64]{1,2,0:T(8,128)(2,1)S(1)}, bf16[1,384,64]{1,2,0:T(8,128)(2,1)}, u32[]{:S(2)}) copy-start(bf16[1,384,64]{1,2,0:T(8,128)(2,1)} %param.8) | copy-start | bytes 147460
  4.9 17.8 %copy-start = (bf16[640,64]{0,1:T(8,128)(2,1)S(1)}, bf16[640,64]{0,1:T(8,128)(2,1)}, u32[]{:S(2)}) copy-start(bf16[640,64]{0,1:T(8,128)(2,1)} %param.11) | copy-start | bytes 245764
  4.9 31.0 %copy-start.2 = (f32[32]{0:T(128)S(1)}, f32[32]{0:T(128)}, u32[]{:S(2)}) copy-start(f32[32]{0:T(128)} %param.13) | copy-start | bytes 388
  4.9 31.0 %copy-start.3 = (s32[32]{0:T(128)S(1)}, s32[32]{0:T(128)}, u32[]{:S(2)}) copy-start(s32[32]{0:T(128)} %param.14) | copy-start | bytes 388
  11.0 36.3 %collective-permute-start.12 = (bf16[15,320,128]{2,1,0:T(8,128)(2,1)S(1)}, bf16[15,320,128]{2,1,0:T(8,128)(2,1)S(1)}, u32[]{:S(2)}, u32[]{:S(2)}) collective-permute-start(bf16[15,320,128]{2,1,0:T(8,128)(2,1)S(1)} %get-tuple-element.58), channel_id=1, source_target_pairs={{0,16},{16,0},{1,17},{17,1},{2,18},{18,2},{3,19},{19,3},{4,20},{20... | collective-permute-start | bytes 3686408 | tf_op jit(solution)/shard_map/ppermute | solution.py:498
  13.1 1.5 %collective-permute-start.4 = (bf16[3,64,640]{2,1,0:T(8,128)(2,1)S(1)}, bf16[3,64,640]{2,1,0:T(8,128)(2,1)S(1)}, u32[]{:S(2)}, u32[]{:S(2)}) collective-permute-start(bf16[3,64,640]{2,1,0:T(8,128)(2,1)S(1)} %get-tuple-element.47.a_ref), channel_id=1, source_target_pairs={{0,4},{4,0},{8,12},{12,8},{1,5},{5,1},{9,13},{13,9},{2,6},{6,2},{1... | collective-permute-start | bytes 737288 | tf_op jit(solution)/shard_map/ppermute | solution.py:75
  14.6 8.1 %collective-permute-start.5 = (bf16[3,64,640]{2,1,0:T(8,128)(2,1)S(1)}, bf16[3,64,640]{2,1,0:T(8,128)(2,1)S(1)}, u32[]{:S(2)}, u32[]{:S(2)}) collective-permute-start(bf16[3,64,640]{2,1,0:T(8,128)(2,1)S(1)} %add.4.refs_4_), channel_id=1, source_target_pairs={{0,8},{4,12},{8,0},{12,4},{1,9},{5,13},{9,1},{13,5},{2,10},{6,14},... | collective-permute-start | bytes 737288 | tf_op jit(solution)/shard_map/ppermute | solution.py:75
  16.2 40.6 %collective-permute-start.13 = (bf16[15,192,128]{2,1,0:T(8,128)(2,1)S(1)}, bf16[15,192,128]{2,1,0:T(8,128)(2,1)S(1)}, u32[]{:S(2)}, u32[]{:S(2)}) collective-permute-start(bf16[15,192,128]{2,1,0:T(8,128)(2,1)S(1)} %get-tuple-element.61), channel_id=1, source_target_pairs={{0,16},{16,0},{1,17},{17,1},{2,18},{18,2},{3,19},{19,3},{4,20},{20... | collective-permute-start | bytes 2211848 | tf_op jit(solution)/shard_map/ppermute | solution.py:498
  17.3 2.8 %collective-permute-start.1 = (bf16[64,256]{1,0:T(8,128)(2,1)S(1)}, bf16[64,256]{1,0:T(8,128)(2,1)S(1)}, u32[]{:S(2)}, u32[]{:S(2)}) collective-permute-start(bf16[64,256]{1,0:T(8,128)(2,1)S(1)} %get-tuple-element.43), channel_id=1, source_target_pairs={{0,4},{4,8},{8,12},{1,5},{5,9},{9,13},{2,6},{6,10},{10,14},{3,7},{... | collective-permute-start | bytes 98312 | tf_op jit(solution)/shard_map/ppermute | solution.py:532
  18.8 3.2 %collective-permute-start.2 = (bf16[64,256]{1,0:T(8,128)(2,1)S(1)}, bf16[64,256]{1,0:T(8,128)(2,1)S(1)}, u32[]{:S(2)}, u32[]{:S(2)}) collective-permute-start(bf16[64,256]{1,0:T(8,128)(2,1)S(1)} %get-tuple-element.45), channel_id=1, source_target_pairs={{4,0},{8,4},{12,8},{5,1},{9,5},{13,9},{6,2},{10,6},{14,10},{7,3},{... | collective-permute-start | bytes 98312 | tf_op jit(solution)/shard_map/ppermute | solution.py:533
  26.3 5.4 %collective-permute-start.8 = (bf16[64,384]{1,0:T(8,128)(2,1)S(1)}, bf16[64,384]{1,0:T(8,128)(2,1)S(1)}, u32[]{:S(2)}, u32[]{:S(2)}) collective-permute-start(bf16[64,384]{1,0:T(8,128)(2,1)S(1)} %get-tuple-element.54.refs_11_), channel_id=1, source_target_pairs={{0,3},{1,0},{2,1},{3,2},{4,7},{5,4},{6,5},{7,6},{8,11},{9,8},{10,9... | collective-permute-start | bytes 147464 | tf_op jit(solution)/shard_map/ppermute | solution.py:538
  30.0 5.3 %collective-permute-start.7 = (bf16[64,384]{1,0:T(8,128)(2,1)S(1)}, bf16[64,384]{1,0:T(8,128)(2,1)S(1)}, u32[]{:S(2)}, u32[]{:S(2)}) collective-permute-start(bf16[64,384]{1,0:T(8,128)(2,1)S(1)} %get-tuple-element.54.refs_11_), channel_id=1, source_target_pairs={{0,2},{1,3},{2,0},{3,1},{4,6},{5,7},{6,4},{7,5},{8,10},{9,11},{10,... | collective-permute-start | bytes 147464 | tf_op jit(solution)/shard_map/ppermute | solution.py:538
  30.0 5.9 %collective-permute-start.6 = (bf16[64,384]{1,0:T(8,128)(2,1)S(1)}, bf16[64,384]{1,0:T(8,128)(2,1)S(1)}, u32[]{:S(2)}, u32[]{:S(2)}) collective-permute-start(bf16[64,384]{1,0:T(8,128)(2,1)S(1)} %get-tuple-element.54.refs_11_), channel_id=1, source_target_pairs={{0,1},{1,2},{2,3},{3,0},{4,5},{5,6},{6,7},{7,4},{8,9},{9,10},{10,1... | collective-permute-start | bytes 147464 | tf_op jit(solution)/shard_map/ppermute | solution.py:538
  38.8 2.2 %collective-permute-start.9 = (bf16[320,128]{1,0:T(8,128)(2,1)S(1)}, bf16[320,128]{1,0:T(8,128)(2,1)S(1)}, u32[]{:S(2)}, u32[]{:S(2)}) collective-permute-start(bf16[320,128]{1,0:T(8,128)(2,1)S(1)} %attend_grad.1.a_ref), channel_id=1, source_target_pairs={{0,4},{4,0},{8,12},{12,8},{1,5},{5,1},{9,13},{13,9},{2,6},{6,2},{1... | collective-permute-start | bytes 245768 | tf_op jit(solution)/shard_map/ppermute | solution.py:75
  41.0 4.8 %collective-permute-start.10 = (bf16[320,128]{1,0:T(8,128)(2,1)S(1)}, bf16[320,128]{1,0:T(8,128)(2,1)S(1)}, u32[]{:S(2)}, u32[]{:S(2)}) collective-permute-start(bf16[320,128]{1,0:T(8,128)(2,1)S(1)} %add.5.refs_6_), channel_id=1, source_target_pairs={{0,8},{4,12},{8,0},{12,4},{1,9},{5,13},{9,1},{13,5},{2,10},{6,14},... | collective-permute-start | bytes 245768 | tf_op jit(solution)/shard_map/ppermute | solution.py:75
  45.8 14.8 %collective-permute-start.11 = (bf16[15,64,128]{2,1,0:T(8,128)(2,1)S(1)}, bf16[15,64,128]{2,1,0:T(8,128)(2,1)S(1)}, u32[]{:S(2)}, u32[]{:S(2)}) collective-permute-start(bf16[15,64,128]{2,1,0:T(8,128)(2,1)S(1)} %get-tuple-element.56), channel_id=1, source_target_pairs={{0,16},{16,0},{1,17},{17,1},{2,18},{18,2},{3,19},{19,3},{4,20},{20... | collective-permute-start | bytes 737288 | tf_op jit(solution)/shard_map/ppermute | solution.py:498

commit v5 on v4

--- a/solution.py
+++ b/solution.py
@@ -125,6 +125,10 @@
     )(place, mine, other)
 
 
+def chunk_of(size, unit):
+    return 2 * unit if size % (2 * unit) == 0 else unit
+
+
 def narrow(mom_ref, o_ref, stride, first, count, at=0):
     for q in range(stride):
         part = mom_ref[pl.ds(first * stride + q, count, stride=stride), :]
@@ -156,7 +160,7 @@
     )(in_hbm(mom))
 
 
-def prepare_kernel(sizes, stride, skip, sliced, place_ref, e_hbm, mom_hbm, w_hbm, m_ref, et_ref, w_ref, mom_ref, *rest):
+def prepare_kernel(sizes, stride, skip, unit, sliced, place_ref, e_hbm, mom_hbm, w_hbm, m_ref, et_ref, w_ref, mom_ref, *rest):
     pieces = rest[: len(sizes)]
     e_ref, e_sem, w_sem, mom_sem = rest[len(sizes) :]
     rows = w_ref.shape[1]
@@ -175,7 +179,8 @@
     cuts = [(0, skip, -1, 0)]
     first = skip
     for k, size in enumerate(sizes):
-        cuts += [(first + at, skip, k, at) for at in range(0, size, skip)]
+        step = chunk_of(size, unit)
+        cuts += [(first + at, step, k, at) for at in range(0, size, step)]
         first += size
     mom_copies = []
     for k, (first, count, _, _) in enumerate(cuts):
@@ -195,13 +200,13 @@
             narrow(mom_ref, pieces[k], stride, first, count, at)
 
 
-def prepare(place, w_embed, mom, w, sizes, stride, skip):
+def prepare(place, w_embed, mom, w, sizes, stride, skip, unit):
     _, rows, width = w.shape
     sliced = rows % HD != 0
     if sliced:
         w_embed = lax.dynamic_slice_in_dim(w_embed, place[0] * rows, rows, axis=1)
     return pl.pallas_call(
-        functools.partial(prepare_kernel, sizes, stride, skip, sliced),
+        functools.partial(prepare_kernel, sizes, stride, skip, unit, sliced),
         in_specs=[SMEM, HBM, HBM, HBM],
         out_specs=[VMEM] * (4 + len(sizes)),
         out_shape=[
@@ -215,7 +220,7 @@
             pltpu.VMEM((CH, rows), BF16),
             pltpu.SemaphoreType.DMA(()),
             pltpu.SemaphoreType.DMA((6,)),
-            pltpu.SemaphoreType.DMA((1 + sum(sizes) // skip,)),
+            pltpu.SemaphoreType.DMA((1 + sum(sizes) // unit,)),
         ],
         compiler_params=params(4),
         cost_estimate=cost(2 * CH * w.size, 4 * w.size + 10 * mom.size),
@@ -381,58 +386,59 @@
     )(timestep, rewards, group_ids, win, m, wot, e, u, il, now, later, *preds)
 
 
-def update_kernel(heads, unit, sizes, first, later, *refs):
-    place_ref, et_ref, mom_ref, w_ref = refs[:4]
-    recv_refs = refs[4 : 4 + len(sizes)]
-    rest = refs[4 + len(sizes) :]
-    if later:
-        g_ref = rest[0]
-        onm_hbm, ow_hbm, gs_ref, fs_ref, onm_ref, ow_ref, sems = rest[3:]
-    else:
-        za_ref, zb_ref, m_ref, wot_ref, onm_hbm, ow_hbm, g_ref, gs_ref, fs_ref, onm_ref, ow_ref, sems = rest
+def update_kernel(heads, unit, sizes, *refs):
+    place_ref, et_ref, mom_ref, w_ref, za_ref, zb_ref, m_ref, wot_ref = refs[:8]
+    here = len(sizes) - 1
+    recv_refs = refs[8 : 8 + here]
+    onm_hbm, ow_hbm, base_ref, g_ref, gs_ref, fs_ref, onm_ref, ow_ref, sems = refs[8 + here :]
     stride = 3 * heads
     role = place_ref[1]
     slots = onm_ref.shape[0]
-
-    if not later:
-        for h in range(heads):
-            cols = slice(h * HD, (h + 1) * HD)
-            rows = slice(h * CH, (h + 1) * CH)
-            zy = (za_ref[rows, :].astype(F32) + zb_ref[rows, :].astype(F32)).astype(BF16)
-            z = zy[:, 0:CH]
-            y = zy[:, CH : 2 * CH]
-            g_ref[0, :, cols] = dot(z, m_ref[1, :, cols]).astype(BF16)
-            g_ref[1, :, cols] = dot(z, m_ref[0, :, cols], TN).astype(BF16)
-            g_ref[2, :, cols] = dot(y, wot_ref[:, cols], TN).astype(BF16)
-
-    total = sum(sizes)
-    for part in range(3):
-        g = dot(et_ref[2 * first : 2 * (first + total), :], g_ref[part])
-        for b in range(heads):
-            gs_ref[part * heads + b] = g[:, b * HD : (b + 1) * HD]
-
-    def copies(pair, count, slot):
-        lin = pl.ds(pair * stride, count * stride)
-        rows = pl.ds(2 * pair, 2 * count)
-        return [
-            pltpu.make_async_copy(onm_ref.at[slot, pl.ds(0, count * stride)], onm_hbm.at[lin], sems.at[0, slot]),
-            pltpu.make_async_copy(ow_ref.at[slot, :, pl.ds(0, 2 * count)], ow_hbm.at[:, rows], sems.at[1, slot]),
-        ]
-
+    for h in range(heads):
+        cols = slice(h * HD, (h + 1) * HD)
+        rows = slice(h * CH, (h + 1) * CH)
+        zy = (za_ref[rows, :].astype(F32) + zb_ref[rows, :].astype(F32)).astype(BF16)
+        z = zy[:, 0:CH]
+        y = zy[:, CH : 2 * CH]
+        g_ref[0, :, cols] = dot(z, m_ref[1, :, cols]).astype(BF16)
+        g_ref[1, :, cols] = dot(z, m_ref[0, :, cols], TN).astype(BF16)
+        g_ref[2, :, cols] = dot(y, wot_ref[:, cols], TN).astype(BF16)
+
+    arrived = sum(sizes[:here])
     order = []
-    pair = first
+    pair = 0
     for k, size in enumerate(sizes):
-        count = 2 * unit if size % (2 * unit) == 0 else unit
+        count = chunk_of(size, unit)
         for i in range(size // count):
             order.append((k, i * count, pair, count))
             pair += count
+
+    def copies(k, at, pair, count, slot):
+        lin = pl.ds(pair * stride, count * stride)
+        rows = pl.ds(2 * pair, 2 * count)
+        out = [pltpu.make_async_copy(onm_ref.at[slot, pl.ds(0, count * stride)], onm_hbm.at[lin], sems.at[0, slot])]
+        if k < here:
+            out.append(
+                pltpu.make_async_copy(ow_ref.at[slot, :, pl.ds(0, 2 * count)], ow_hbm.at[:, rows], sems.at[1, slot])
+            )
+        return out
+
+    group = -1
     for step, (k, at, pair, count) in enumerate(order):
+        if group != (k == here):
+            group = k == here
+            origin = arrived if group else 0
+            span = sizes[here] if group else arrived
+            for part in range(3):
+                g = dot(et_ref[2 * origin : 2 * (origin + span), :], g_ref[part])
+                for b in range(heads):
+                    gs_ref[part * heads + b, 0 : 2 * span, :] = g[:, b * HD : (b + 1) * HD]
         slot = step % slots
         if step >= slots:
-            for copy in copies(*order[step - slots][2:], slot):
+            for copy in copies(*order[step - slots], slot):
                 copy.wait()
         natural = slice(2 * pair, 2 * (pair + count))
-        local = 2 * (pair - first)
+        local = 2 * (pair - origin)
         mine = pl.ds(role, count, stride=2)
         theirs = pl.ds(1 - role, count, stride=2)
         for q in range(stride):
@@ -440,58 +446,92 @@
             cols = slice(b * HD, (b + 1) * HD)
             own = MOMENTUM_DECAY * mom_ref[pl.ds(pair * stride + q, count, stride=stride), :]
             own = own + gs_ref[q, pl.ds(local + role, count, stride=2), :]
-            other = recv_refs[k][q, at : at + count, :].astype(F32)
-            other = other + gs_ref[q, pl.ds(local + 1 - role, count, stride=2), :]
+            other = gs_ref[q, pl.ds(local + 1 - role, count, stride=2), :]
+            if k < here:
+                other = other + recv_refs[k][q, at : at + count, :].astype(F32)
             onm_ref[slot, pl.ds(q, count, stride=stride), :] = own
             fs_ref[q, mine, :] = own
             fs_ref[q, theirs, :] = other
             new = w_ref[part, natural, cols].astype(F32) - LEARNING_RATE * fs_ref[q, 0 : 2 * count, :]
-            ow_ref[slot, part, 0 : 2 * count, cols] = new.astype(BF16)
-        for copy in copies(pair, count, slot):
+            if k < here:
+                ow_ref[slot, part, 0 : 2 * count, cols] = new.astype(BF16)
+            else:
+                base_ref[q, local : local + 2 * count, :] = new
+        for copy in copies(k, at, pair, count, slot):
             copy.start()
     for step in range(max(len(order) - slots, 0), len(order)):
-        for copy in copies(*order[step][2:], step % slots):
+        for copy in copies(*order[step], step % slots):
             copy.wait()
 
 
-def update(place, et, mom, w, received, first, unit, heads, sources=None, before=None):
-    sizes = [a.shape[1] for a in received]
+def update(place, et, mom, w, received, rest, unit, heads, sources):
+    sizes = [a.shape[1] for a in received] + [rest]
     _, rows, width = w.shape
     stride = 3 * heads
-    slots = min(sum(sizes) // unit, 4)
-    most = max(2 * unit if n % (2 * unit) == 0 else unit for n in sizes)
-    args = [place, et, in_vmem(mom), in_vmem(w), *received]
-    in_specs = [SMEM] + [VMEM] * (3 + len(received))
-    out_specs = [HBM, HBM]
-    out_shape = [jax.ShapeDtypeStruct((rows // 2 * stride, HD), F32), jax.ShapeDtypeStruct(w.shape, BF16)]
-    aliases = {}
-    if before is None:
-        args += sources
-        in_specs += [VMEM] * len(sources)
-        out_specs.append(VMEM)
-        out_shape.append(pltpu.VMEM((3, CH, width), BF16))
-    else:
-        new_mom, new_w, g = before
-        aliases = {len(args) + 1: 0, len(args) + 2: 1}
-        args += [g, new_mom, new_w]
-        in_specs += [VMEM, HBM, HBM]
-    return pl.pallas_call(
-        functools.partial(update_kernel, heads, unit, sizes, first, before is not None),
-        in_specs=in_specs,
-        out_specs=out_specs,
-        out_shape=out_shape,
-        input_output_aliases=aliases,
+    slots = 4
+    return pl.pallas_call(
+        functools.partial(update_kernel, heads, unit, sizes),
+        in_specs=[SMEM] + [VMEM] * (7 + len(received)),
+        out_specs=[HBM, HBM, VMEM],
+        out_shape=[
+            jax.ShapeDtypeStruct(mom.shape, F32),
+            jax.ShapeDtypeStruct(w.shape, BF16),
+            pltpu.VMEM((stride, 2 * rest, HD), F32),
+        ],
         scratch_shapes=[
-            pltpu.VMEM((stride, 2 * sum(sizes), HD), F32),
-            pltpu.VMEM((stride, 2 * most, HD), F32),
-            pltpu.VMEM((slots, most * stride, HD), F32),
-            pltpu.VMEM((slots, 3, 2 * most, width), BF16),
+            pltpu.VMEM((3, CH, width), BF16),
+            pltpu.VMEM((stride, 2 * max(sum(sizes) - rest, rest), HD), F32),
+            pltpu.VMEM((stride, 4 * unit, HD), F32),
+            pltpu.VMEM((slots, 2 * unit * stride, HD), F32),
+            pltpu.VMEM((slots, 3, 4 * unit, width), BF16),
             pltpu.SemaphoreType.DMA((2, slots)),
         ],
-        compiler_params=params(14),
-        cost_estimate=cost(2 * sum(sizes) * stride * HD * 2 * CH, 22 * sum(sizes) * stride * HD),
+        compiler_params=params(16),
+        cost_estimate=cost(4 * CH * w.size, 22 * mom.size),
         name="update",
-    )(*args)
+    )(place, et, in_vmem(mom), in_vmem(w), *sources, *received)
+
+
+def finish_kernel(heads, unit, first, local, place_ref, base_ref, recv_ref, old_hbm, ow_hbm, fs_ref, ow_ref, sems):
+    del old_hbm
+    stride, size, _ = recv_ref.shape
+    role = place_ref[1]
+    count = chunk_of(size, unit)
+    fs_ref[...] = jnp.zeros_like(fs_ref)
+    copies = []
+    for step in range(size // count):
+        at = 2 * step * count
+        for q in range(stride):
+            part, b = divmod(q, heads)
+            fs_ref[q, pl.ds(1 - role, count, stride=2), :] = recv_ref[q, at // 2 : at // 2 + count, :].astype(F32)
+            new = base_ref[q, 2 * local + at : 2 * local + at + 2 * count, :] - LEARNING_RATE * fs_ref[q]
+            ow_ref[part, at : at + 2 * count, b * HD : (b + 1) * HD] = new.astype(BF16)
+        source = ow_ref.at[:, pl.ds(at, 2 * count)]
+        target = ow_hbm.at[:, pl.ds(2 * first + at, 2 * count)]
+        copies.append(pltpu.make_async_copy(source, target, sems.at[step]))
+        copies[-1].start()
+    for copy in copies:
+        copy.wait()
+
+
+def finish(place, base, recv, old, first, local, unit, heads):
+    stride, size, _ = recv.shape
+    count = chunk_of(size, unit)
+    return pl.pallas_call(
+        functools.partial(finish_kernel, heads, unit, first, local),
+        in_specs=[SMEM, VMEM, VMEM, HBM],
+        out_specs=HBM,
+        out_shape=jax.ShapeDtypeStruct(old.shape, BF16),
+        input_output_aliases={3: 0},
+        scratch_shapes=[
+            pltpu.VMEM((stride, 2 * count, HD), F32),
+            pltpu.VMEM((3, 2 * size, heads * HD), BF16),
+            pltpu.SemaphoreType.DMA((size // count,)),
+        ],
+        compiler_params=params(4),
+        cost_estimate=cost(2 * recv.size, 14 * recv.size),
+        name="finish",
+    )(place, in_vmem(base), recv, old)
 
 
 def exchange(x):
@@ -511,19 +551,18 @@
 
     stride = 3 * heads
     unit = pair_rows // 20
-    sizes = (2 * unit, 10 * unit, 6 * unit, 2 * unit)
+    sizes = (3 * unit, 10 * unit, 6 * unit, unit)
     mom = momentum.reshape(pair_rows * stride, HD)
     w = w_qkv.transpose(1, 0, 2)
     wot = w_out.T
     place = jnp.stack([seq_index, role_index])
 
-    mine = rollout[0].T
+    piece = lead(mom, stride, unit, 3)
+    mine, piece = lax.optimization_barrier((rollout[0].T, piece))
     other = exchange(mine)
-    piece = lead(mom, stride, unit, 2)
     received = [exchange(piece)]
-    mom, piece = lax.optimization_barrier((mom, piece))
-    m, et, w, mom, *pieces = prepare(place, w_embed, mom, w, sizes[1:], stride, sizes[0])
-    other, pieces = lax.optimization_barrier((other, pieces))
+    mom, other = lax.optimization_barrier((mom, other))
+    m, et, w, mom, *pieces = prepare(place, w_embed, mom, w, sizes[1:], stride, sizes[0], unit)
     received += [exchange(p) for p in pieces[:-1]]
     m, received[0] = lax.optimization_barrier((m, received[0]))
     ma, mb = butterfly(m, "seq")
@@ -561,11 +600,11 @@
 
     zb, last = lax.optimization_barrier((zb, pieces[-1]))
     received.append(exchange(last))
-    done = update(place, et, mom, w, received[:2], 0, unit, heads, sources=[za, zb, m, wot])
-    g = done[2]
+    rest = sizes[2] + sizes[3]
+    nm, nw, base = update(place, et, mom, w, received[:2], rest, unit, heads, [za, zb, m, wot])
     first = sizes[0] + sizes[1]
-    done = update(place, et, mom, w, received[2:3], first, unit, heads, before=[*done[:2], g])
-    nm, nw = update(place, et, mom, w, received[3:], first + sizes[2], unit, heads, before=[*done, g])
+    nw = finish(place, base, received[2], nw, first, 0, unit, heads)
+    nw = finish(place, base, received[3], nw, first + sizes[2], sizes[2], unit, heads)
     return nm.reshape(momentum.shape), nw.transpose(1, 0, 2)
 
 

time: 62.9 us -> 62.1 us (0.987)
  starting transfers between devices: 19 us -> 18.3 us
where the time goes in v5:
time: 62.1 us; the launch traced here: 61.9 us
  Pallas kernels  24.5 us (39%)
  starting transfers between devices  18.3 us (29%)
  waiting for transfers between devices  17.5 us (28%)
  between operations  1.56 us (3%)
    ppermute x5, starting transfers between devices, exchange(): return lax.ppermute(x, 'role', [(0, 1), (1, 0)])  6.68 us
    pallas_call x1, Pallas kernels, update(): pl.pallas_call(functools.partial(update_kernel, heads, unit, sizes), in_s...  6.57 us
    pallas_call x1, Pallas kernels, prepare(): pl.pallas_call(functools.partial(prepare_kernel, sizes, stride, skip, uni...  6.16 us
    ppermute x4, waiting for transfers between devices, swap(): lax.ppermute(x, axis, [(i, i ^ bit) for i in range(lax.axis_size(axis))])  6.04 us
    ppermute x5, waiting for transfers between devices, exchange(): return lax.ppermute(x, 'role', [(0, 1), (1, 0)])  5.14 us
    ppermute x3, starting transfers between devices, body(): lax.ppermute(partial_pred, 'mp', [(i, (i + d) % mp_count) for i in range(...  4.67 us
    ppermute x3, waiting for transfers between devices, body(): lax.ppermute(partial_pred, 'mp', [(i, (i + d) % mp_count) for i in range(...  4.28 us
    ppermute x4, starting transfers between devices, swap(): lax.ppermute(x, axis, [(i, i ^ bit) for i in range(lax.axis_size(axis))])  3.87 us
  transfers between devices with their start and end apart: 14, of which 10 were waited for; matrix products, arithmetic and copies ran while one was open for 0% of the time, Pallas kernels for 35%

profile of v5, /device:TPU:0, one launch (start us, length us, event | category | flops | bytes accessed | tf_op | source)
XLA Modules:
  0.0 61.9 jit_solution(2214945186648211120)
XLA Ops:
  0.6 0.0 copy-start.1
  0.6 1.2 %lead.1 = bf16[15,96,128]{2,1,0:T(8,128)(2,1)S(1)} custom-call(f32[9600,128]{1,0:T(8,128)} %bitcast.19), custom_call_target="tpu_custom_call" | custom-call | flops 184320 | bytes 1105920 | tf_op jit(solution)/shard_map/lead/pallas_call | solution.py:151
  1.9 0.0 copy-done.1
  1.9 3.0 %collective-permute-start = (bf16[64,384]{1,0:T(8,128)(2,1)S(1)}, bf16[64,384]{1,0:T(8,128)(2,1)S(1)}, u32[]{:S(2)}, u32[]{:S(2)}) collective-permute-start(bf16[64,384]{1,0:T(8,128)(2,1)S(1)} %bitcast.15), channel_id=1, source_target_pairs={{0,16},{16,0},{1,17},{17,1},{2,18},{18,2},{3,19},{19,3},{4,20},{20... | collective-permute-start | bytes 147464 | tf_op jit(solution)/shard_map/ppermute | solution.py:538
  4.9 0.1 collective-permute-start.3
  5.0 0.1 pad_add_fusion.place_ref.refs_0_
  5.1 2.0 %collective-permute-done.other_ref = bf16[64,384]{1,0:T(8,128)(2,1)S(1)} collective-permute-done((bf16[64,384]{1,0:T(8,128)(2,1)S(1)}, bf16[64,384]{1,0:T(8,128)(2,1)S(1)}, u32[]{:S(2)}, u32[]{:S(2)}) %collective-permute-start) | collective-permute-done | bytes 49184 | tf_op jit(solution)/shard_map/ppermute | solution.py:538
  7.1 0.0 copy-start
  7.1 0.0 copy-start.2
  7.1 0.0 copy-start.3
  7.1 6.2 %prepare.1 = (bf16[3,64,640]{2,1,0:T(8,128)(2,1)S(1)}, bf16[1280,64]{1,0:T(8,128)(2,1)S(1)}, bf16[3,1280,640]{2,1,0:T(8,128)(2,1)S(1)}, f32[9600,128]{1,0:T(8,12...) custom-call(s32[2]{0:T(128)S(1)} %pad_add_fusion.place_ref.refs_0_, ...), custom_call_target="tpu_custom_call" | custom-call | flops 314572800 | bytes 22118400 | tf_op jit(solution)/shard_map/prepare/pallas_call | solution.py:208
  13.2 2.5 %collective-permute-start.11 = (bf16[15,320,128]{2,1,0:T(8,128)(2,1)S(1)}, bf16[15,320,128]{2,1,0:T(8,128)(2,1)S(1)}, u32[]{:S(2)}, u32[]{:S(2)}) collective-permute-start(bf16[15,320,128]{2,1,0:T(8,128)(2,1)S(1)} %get-tuple-element.52), channel_id=1, source_target_pairs={{0,16},{16,0},{1,17},{17,1},{2,18},{18,2},{3,19},{19,3},{4,20},{20... | collective-permute-start | bytes 3686408 | tf_op jit(solution)/shard_map/ppermute | solution.py:538
  15.8 0.0 collective-permute-done.3.refs_8_
  15.8 0.0 collective-permute-start.4
  15.8 0.5 collective-permute-start.13
  16.3 1.0 %collective-permute-done.4.b_ref = bf16[3,64,640]{2,1,0:T(8,128)(2,1)S(1)} collective-permute-done((bf16[3,64,640]{2,1,0:T(8,128)(2,1)S(1)}, bf16[3,64,640]{2,1,0:T(8,128)(2,1)S(1)}, u32[]{:S(2)}, u32[]{:S(2)}) %collective-permute-start.4) | collective-permute-done | bytes 245792 | tf_op jit(solution)/shard_map/ppermute | solution.py:75
  17.3 0.1 add.4.refs_4_
  17.4 1.6 %collective-permute-start.5 = (bf16[3,64,640]{2,1,0:T(8,128)(2,1)S(1)}, bf16[3,64,640]{2,1,0:T(8,128)(2,1)S(1)}, u32[]{:S(2)}, u32[]{:S(2)}) collective-permute-start(bf16[3,64,640]{2,1,0:T(8,128)(2,1)S(1)} %add.4.refs_4_), channel_id=1, source_target_pairs={{0,8},{4,12},{8,0},{12,4},{1,9},{5,13},{9,1},{13,5},{2,10},{6,14},... | collective-permute-start | bytes 737288 | tf_op jit(solution)/shard_map/ppermute | solution.py:75
  18.9 0.6 pick.1
  19.5 1.8 %collective-permute-start.1 = (bf16[64,256]{1,0:T(8,128)(2,1)S(1)}, bf16[64,256]{1,0:T(8,128)(2,1)S(1)}, u32[]{:S(2)}, u32[]{:S(2)}) collective-permute-start(bf16[64,256]{1,0:T(8,128)(2,1)S(1)} %get-tuple-element.36), channel_id=1, source_target_pairs={{0,4},{4,8},{8,12},{1,5},{5,9},{9,13},{2,6},{6,10},{10,14},{3,7},{... | collective-permute-start | bytes 98312 | tf_op jit(solution)/shard_map/ppermute | solution.py:571
  21.3 1.3 %collective-permute-start.2 = (bf16[64,256]{1,0:T(8,128)(2,1)S(1)}, bf16[64,256]{1,0:T(8,128)(2,1)S(1)}, u32[]{:S(2)}, u32[]{:S(2)}) collective-permute-start(bf16[64,256]{1,0:T(8,128)(2,1)S(1)} %get-tuple-element.38), channel_id=1, source_target_pairs={{4,0},{8,4},{12,8},{5,1},{9,5},{13,9},{6,2},{10,6},{14,10},{7,3},{... | collective-permute-start | bytes 98312 | tf_op jit(solution)/shard_map/ppermute | solution.py:572
  22.6 0.0 collective-permute-done.1.refs_1_
  22.6 2.1 %collective-permute-done.2.refs_3_ = bf16[64,256]{1,0:T(8,128)(2,1)S(1)} collective-permute-done((bf16[64,256]{1,0:T(8,128)(2,1)S(1)}, bf16[64,256]{1,0:T(8,128)(2,1)S(1)}, u32[]{:S(2)}, u32[]{:S(2)}) %collective-permute-start.2) | collective-permute-done | bytes 32800 | tf_op jit(solution)/shard_map/ppermute | solution.py:572
  24.7 0.8 %collective-permute-done.5.refs_5_ = bf16[3,64,640]{2,1,0:T(8,128)(2,1)S(1)} collective-permute-done((bf16[3,64,640]{2,1,0:T(8,128)(2,1)S(1)}, bf16[3,64,640]{2,1,0:T(8,128)(2,1)S(1)}, u32[]{:S(2)}, u32[]{:S(2)}) %collective-permute-start.5) | collective-permute-done | bytes 245792 | tf_op jit(solution)/shard_map/ppermute | solution.py:75
  25.4 0.0 copy-done
  25.4 3.6 %attend.1 = (bf16[3,64,640]{2,1,0:T(8,128)(2,1)S(1)}, bf16[2,640,128]{2,1,0:T(8,128)(2,1)S(1)}, bf16[2,960,640]{2,1,0:T(8,128)(2,1)S(1)}, bf16[1920,128]{1,0:T(8...) custom-call(s32[2]{0:T(128)S(1)} %pad_add_fusion.place_ref.refs_0_, ...), custom_call_target="tpu_custom_call" | custom-call | flops 692060160 | bytes 24576000 | tf_op jit(solution)/shard_map/attend/pallas_call | solution.py:293
  29.1 3.7 %collective-permute-start.8 = (bf16[64,384]{1,0:T(8,128)(2,1)S(1)}, bf16[64,384]{1,0:T(8,128)(2,1)S(1)}, u32[]{:S(2)}, u32[]{:S(2)}) collective-permute-start(bf16[64,384]{1,0:T(8,128)(2,1)S(1)} %get-tuple-element.48.refs_11_), channel_id=1, source_target_pairs={{0,3},{1,0},{2,1},{3,2},{4,7},{5,4},{6,5},{7,6},{8,11},{9,8},{10,9... | collective-permute-start | bytes 147464 | tf_op jit(solution)/shard_map/ppermute | solution.py:577
  32.7 0.0 collective-permute-start.7
  32.7 1.0 %collective-permute-start.6 = (bf16[64,384]{1,0:T(8,128)(2,1)S(1)}, bf16[64,384]{1,0:T(8,128)(2,1)S(1)}, u32[]{:S(2)}, u32[]{:S(2)}) collective-permute-start(bf16[64,384]{1,0:T(8,128)(2,1)S(1)} %get-tuple-element.48.refs_11_), channel_id=1, source_target_pairs={{0,1},{1,2},{2,3},{3,0},{4,5},{5,6},{6,7},{7,4},{8,9},{9,10},{10,1... | collective-permute-start | bytes 147464 | tf_op jit(solution)/shard_map/ppermute | solution.py:577
  34.4 0.1 collective-permute-done.8.refs_14_
  34.5 3.2 %collective-permute-done.7.refs_13_ = bf16[64,384]{1,0:T(8,128)(2,1)S(1)} collective-permute-done((bf16[64,384]{1,0:T(8,128)(2,1)S(1)}, bf16[64,384]{1,0:T(8,128)(2,1)S(1)}, u32[]{:S(2)}, u32[]{:S(2)}) %collective-permute-start.7) | collective-permute-done | bytes 49184 | tf_op jit(solution)/shard_map/ppermute | solution.py:577
  37.7 1.0 %collective-permute-done.6.refs_12_ = bf16[64,384]{1,0:T(8,128)(2,1)S(1)} collective-permute-done((bf16[64,384]{1,0:T(8,128)(2,1)S(1)}, bf16[64,384]{1,0:T(8,128)(2,1)S(1)}, u32[]{:S(2)}, u32[]{:S(2)}) %collective-permute-start.6) | collective-permute-done | bytes 49184 | tf_op jit(solution)/shard_map/ppermute | solution.py:577
  38.7 0.0 copy-done.2
  38.7 0.0 copy-done.3
  38.7 2.9 %attend_grad.1.a_ref = bf16[320,128]{1,0:T(8,128)(2,1)S(1)} custom-call(s32[1]{0:T(128)S(6)} %copy.16.refs_0_, f32[1,32]{1,0:T(1,128)S(1)} %bitcast.17, s32[1,32]{1,0:T(1,128)S(1)} %bitcast.18, bf16[2,640,128]{2,1,0:T(8,128)(2,1)S(1)} %get-tuple-element.42.refs_3_, bf16[3,64,640]{2,1,0:T(8,128)(2,1)S(1)} %get-tuple-element.43.refs_4_.refs_6_, ...), custom_call_target="tpu_custom_call" | custom-call | flops 692060160 | bytes 24576000 | tf_op jit(solution)/shard_map/attend_grad/pallas_call | solution.py:371
  41.6 0.9 %collective-permute-start.9 = (bf16[320,128]{1,0:T(8,128)(2,1)S(1)}, bf16[320,128]{1,0:T(8,128)(2,1)S(1)}, u32[]{:S(2)}, u32[]{:S(2)}) collective-permute-start(bf16[320,128]{1,0:T(8,128)(2,1)S(1)} %attend_grad.1.a_ref), channel_id=1, source_target_pairs={{0,4},{4,0},{8,12},{12,8},{1,5},{5,1},{9,13},{13,9},{2,6},{6,2},{1... | collective-permute-start | bytes 245768 | tf_op jit(solution)/shard_map/ppermute | solution.py:75
  42.4 0.9 %collective-permute-done.9.b_ref = bf16[320,128]{1,0:T(8,128)(2,1)S(1)} collective-permute-done((bf16[320,128]{1,0:T(8,128)(2,1)S(1)}, bf16[320,128]{1,0:T(8,128)(2,1)S(1)}, u32[]{:S(2)}, u32[]{:S(2)}) %collective-permute-start.9) | collective-permute-done | bytes 81952 | tf_op jit(solution)/shard_map/ppermute | solution.py:75
  43.4 1.4 %collective-permute-start.10 = (bf16[320,128]{1,0:T(8,128)(2,1)S(1)}, bf16[320,128]{1,0:T(8,128)(2,1)S(1)}, u32[]{:S(2)}, u32[]{:S(2)}) collective-permute-start(bf16[320,128]{1,0:T(8,128)(2,1)S(1)} %add.5.refs_4_), channel_id=1, source_target_pairs={{0,8},{4,12},{8,0},{12,4},{1,9},{5,13},{9,1},{13,5},{2,10},{6,14},... | collective-permute-start | bytes 245768 | tf_op jit(solution)/shard_map/ppermute | solution.py:75
  44.8 3.4 %collective-permute-done.10.refs_5_ = bf16[320,128]{1,0:T(8,128)(2,1)S(1)} collective-permute-done((bf16[320,128]{1,0:T(8,128)(2,1)S(1)}, bf16[320,128]{1,0:T(8,128)(2,1)S(1)}, u32[]{:S(2)}, u32[]{:S(2)}) %collective-permute-start.10) | collective-permute-done | bytes 81952 | tf_op jit(solution)/shard_map/ppermute | solution.py:75
  48.1 0.5 collective-permute-start.12
  48.7 0.0 collective-permute-done.11.refs_9_
  48.7 6.6 %update.1 = (f32[9600,128]{1,0:T(8,128)}, bf16[3,1280,640]{2,1,0:T(8,128)(2,1)}, f32[15,448,128]{2,1,0:T(8,128)S(1)}) custom-call(s32[2]{0:T(128)S(1)} %pad_add_fusion.place_ref.refs_0_, bf16[1280,64]{1,0:T(8,128)(2,1)S(1)} %get-tuple-element.32.refs_1_, f32[9600,128]{1,0:T(8,128)S(1)} %get-tuple-element.33.refs_2_, ...), custom_call_target="tpu_custom_call" | custom-call | flops 629145600 | bytes 27033600 | tf_op jit(solution)/shard_map/update/pallas_call | solution.py:472
  55.3 3.1 %collective-permute-done.13.recv_ref = bf16[15,192,128]{2,1,0:T(8,128)(2,1)S(1)} collective-permute-done((bf16[15,192,128]{2,1,0:T(8,128)(2,1)S(1)}, bf16[15,192,128]{2,1,0:T(8,128)(2,1)S(1)}, u32[]{:S(2)}, u32[]{:S(2)}) %collective-permute-start.13) | collective-permute-done | bytes 737312 | tf_op jit(solution)/shard_map/ppermute | solution.py:538
  58.4 2.0 %finish.2.old_hbm = bf16[3,1280,640]{2,1,0:T(8,128)(2,1)} custom-call(s32[2]{0:T(128)S(1)} %pad_add_fusion.place_ref.refs_0_, f32[15,448,128]{2,1,0:T(8,128)S(1)} %get-tuple-element.54.base_ref, bf16[15,192,128]{2,1,0:T(8,128)(2,1)S(1)} %collective-permute-done.13.recv_ref, ...), custom_call_target="tpu_custom_call", output_to_operand_aliasing={{}: (3, {})} | custom-call | flops 737280 | bytes 5160960 | tf_op jit(solution)/shard_map/finish/pallas_call | solution.py:520
  60.4 0.0 collective-permute-done.12.recv_ref
  60.4 1.4 %finish.3 = bf16[3,1280,640]{2,1,0:T(8,128)(2,1)} custom-call(s32[2]{0:T(128)S(1)} %pad_add_fusion.place_ref.refs_0_, f32[15,448,128]{2,1,0:T(8,128)S(1)} %get-tuple-element.54.base_ref, bf16[15,32,128]{2,1,0:T(8,128)(2,1)S(1)} %collective-permute-done.12.recv_ref, bf16[3,1280,640]{2,1,0:T(8,128)(2,1)} %finish.2.old_hbm), custom_call_target="tpu_custom_call", output_to_operand_aliasing={{}: (3, {})} | custom-call | flops 122880 | bytes 860160 | tf_op jit(solution)/shard_map/finish/pallas_call | solution.py:520
  (1 shorter events, 0.0 us)
Async XLA Ops:
  0.6 1.3 %copy-start.1 = (bf16[1,384,64]{1,2,0:T(8,128)(2,1)S(1)}, bf16[1,384,64]{1,2,0:T(8,128)(2,1)}, u32[]{:S(2)}) copy-start(bf16[1,384,64]{1,2,0:T(8,128)(2,1)} %param.8) | copy-start | bytes 147460
  1.9 5.2 %collective-permute-start = (bf16[64,384]{1,0:T(8,128)(2,1)S(1)}, bf16[64,384]{1,0:T(8,128)(2,1)S(1)}, u32[]{:S(2)}, u32[]{:S(2)}) collective-permute-start(bf16[64,384]{1,0:T(8,128)(2,1)S(1)} %bitcast.15), channel_id=1, source_target_pairs={{0,16},{16,0},{1,17},{17,1},{2,18},{18,2},{3,19},{19,3},{4,20},{20... | collective-permute-start | bytes 147464 | tf_op jit(solution)/shard_map/ppermute | solution.py:538
  4.9 10.9 %collective-permute-start.3 = (bf16[15,96,128]{2,1,0:T(8,128)(2,1)S(1)}, bf16[15,96,128]{2,1,0:T(8,128)(2,1)S(1)}, u32[]{:S(2)}, u32[]{:S(2)}) collective-permute-start(bf16[15,96,128]{2,1,0:T(8,128)(2,1)S(1)} %lead.1), channel_id=1, source_target_pairs={{0,16},{16,0},{1,17},{17,1},{2,18},{18,2},{3,19},{19,3},{4,20},{20... | collective-permute-start | bytes 1105928 | tf_op jit(solution)/shard_map/ppermute | solution.py:538
  7.1 18.4 %copy-start = (bf16[640,64]{0,1:T(8,128)(2,1)S(1)}, bf16[640,64]{0,1:T(8,128)(2,1)}, u32[]{:S(2)}) copy-start(bf16[640,64]{0,1:T(8,128)(2,1)} %param.11) | copy-start | bytes 245764
  7.1 31.6 %copy-start.2 = (f32[32]{0:T(128)S(1)}, f32[32]{0:T(128)}, u32[]{:S(2)}) copy-start(f32[32]{0:T(128)} %param.13) | copy-start | bytes 388
  7.1 31.6 %copy-start.3 = (s32[32]{0:T(128)S(1)}, s32[32]{0:T(128)}, u32[]{:S(2)}) copy-start(s32[32]{0:T(128)} %param.14) | copy-start | bytes 388
  13.2 35.5 %collective-permute-start.11 = (bf16[15,320,128]{2,1,0:T(8,128)(2,1)S(1)}, bf16[15,320,128]{2,1,0:T(8,128)(2,1)S(1)}, u32[]{:S(2)}, u32[]{:S(2)}) collective-permute-start(bf16[15,320,128]{2,1,0:T(8,128)(2,1)S(1)} %get-tuple-element.52), channel_id=1, source_target_pairs={{0,16},{16,0},{1,17},{17,1},{2,18},{18,2},{3,19},{19,3},{4,20},{20... | collective-permute-start | bytes 3686408 | tf_op jit(solution)/shard_map/ppermute | solution.py:538
  15.8 1.5 %collective-permute-start.4 = (bf16[3,64,640]{2,1,0:T(8,128)(2,1)S(1)}, bf16[3,64,640]{2,1,0:T(8,128)(2,1)S(1)}, u32[]{:S(2)}, u32[]{:S(2)}) collective-permute-start(bf16[3,64,640]{2,1,0:T(8,128)(2,1)S(1)} %get-tuple-element.41.a_ref), channel_id=1, source_target_pairs={{0,4},{4,0},{8,12},{12,8},{1,5},{5,1},{9,13},{13,9},{2,6},{6,2},{1... | collective-permute-start | bytes 737288 | tf_op jit(solution)/shard_map/ppermute | solution.py:75
  15.8 42.6 %collective-permute-start.13 = (bf16[15,192,128]{2,1,0:T(8,128)(2,1)S(1)}, bf16[15,192,128]{2,1,0:T(8,128)(2,1)S(1)}, u32[]{:S(2)}, u32[]{:S(2)}) collective-permute-start(bf16[15,192,128]{2,1,0:T(8,128)(2,1)S(1)} %get-tuple-element.56), channel_id=1, source_target_pairs={{0,16},{16,0},{1,17},{17,1},{2,18},{18,2},{3,19},{19,3},{4,20},{20... | collective-permute-start | bytes 2211848 | tf_op jit(solution)/shard_map/ppermute | solution.py:538
  17.4 8.1 %collective-permute-start.5 = (bf16[3,64,640]{2,1,0:T(8,128)(2,1)S(1)}, bf16[3,64,640]{2,1,0:T(8,128)(2,1)S(1)}, u32[]{:S(2)}, u32[]{:S(2)}) collective-permute-start(bf16[3,64,640]{2,1,0:T(8,128)(2,1)S(1)} %add.4.refs_4_), channel_id=1, source_target_pairs={{0,8},{4,12},{8,0},{12,4},{1,9},{5,13},{9,1},{13,5},{2,10},{6,14},... | collective-permute-start | bytes 737288 | tf_op jit(solution)/shard_map/ppermute | solution.py:75
  19.5 3.1 %collective-permute-start.1 = (bf16[64,256]{1,0:T(8,128)(2,1)S(1)}, bf16[64,256]{1,0:T(8,128)(2,1)S(1)}, u32[]{:S(2)}, u32[]{:S(2)}) collective-permute-start(bf16[64,256]{1,0:T(8,128)(2,1)S(1)} %get-tuple-element.36), channel_id=1, source_target_pairs={{0,4},{4,8},{8,12},{1,5},{5,9},{9,13},{2,6},{6,10},{10,14},{3,7},{... | collective-permute-start | bytes 98312 | tf_op jit(solution)/shard_map/ppermute | solution.py:571
  21.3 3.4 %collective-permute-start.2 = (bf16[64,256]{1,0:T(8,128)(2,1)S(1)}, bf16[64,256]{1,0:T(8,128)(2,1)S(1)}, u32[]{:S(2)}, u32[]{:S(2)}) collective-permute-start(bf16[64,256]{1,0:T(8,128)(2,1)S(1)} %get-tuple-element.38), channel_id=1, source_target_pairs={{4,0},{8,4},{12,8},{5,1},{9,5},{13,9},{6,2},{10,6},{14,10},{7,3},{... | collective-permute-start | bytes 98312 | tf_op jit(solution)/shard_map/ppermute | solution.py:572
  29.1 5.4 %collective-permute-start.8 = (bf16[64,384]{1,0:T(8,128)(2,1)S(1)}, bf16[64,384]{1,0:T(8,128)(2,1)S(1)}, u32[]{:S(2)}, u32[]{:S(2)}) collective-permute-start(bf16[64,384]{1,0:T(8,128)(2,1)S(1)} %get-tuple-element.48.refs_11_), channel_id=1, source_target_pairs={{0,3},{1,0},{2,1},{3,2},{4,7},{5,4},{6,5},{7,6},{8,11},{9,8},{10,9... | collective-permute-start | bytes 147464 | tf_op jit(solution)/shard_map/ppermute | solution.py:577
  32.7 5.0 %collective-permute-start.7 = (bf16[64,384]{1,0:T(8,128)(2,1)S(1)}, bf16[64,384]{1,0:T(8,128)(2,1)S(1)}, u32[]{:S(2)}, u32[]{:S(2)}) collective-permute-start(bf16[64,384]{1,0:T(8,128)(2,1)S(1)} %get-tuple-element.48.refs_11_), channel_id=1, source_target_pairs={{0,2},{1,3},{2,0},{3,1},{4,6},{5,7},{6,4},{7,5},{8,10},{9,11},{10,... | collective-permute-start | bytes 147464 | tf_op jit(solution)/shard_map/ppermute | solution.py:577
  32.7 5.9 %collective-permute-start.6 = (bf16[64,384]{1,0:T(8,128)(2,1)S(1)}, bf16[64,384]{1,0:T(8,128)(2,1)S(1)}, u32[]{:S(2)}, u32[]{:S(2)}) collective-permute-start(bf16[64,384]{1,0:T(8,128)(2,1)S(1)} %get-tuple-element.48.refs_11_), channel_id=1, source_target_pairs={{0,1},{1,2},{2,3},{3,0},{4,5},{5,6},{6,7},{7,4},{8,9},{9,10},{10,1... | collective-permute-start | bytes 147464 | tf_op jit(solution)/shard_map/ppermute | solution.py:577
  41.6 1.8 %collective-permute-start.9 = (bf16[320,128]{1,0:T(8,128)(2,1)S(1)}, bf16[320,128]{1,0:T(8,128)(2,1)S(1)}, u32[]{:S(2)}, u32[]{:S(2)}) collective-permute-start(bf16[320,128]{1,0:T(8,128)(2,1)S(1)} %attend_grad.1.a_ref), channel_id=1, source_target_pairs={{0,4},{4,0},{8,12},{12,8},{1,5},{5,1},{9,13},{13,9},{2,6},{6,2},{1... | collective-permute-start | bytes 245768 | tf_op jit(solution)/shard_map/ppermute | solution.py:75
  43.4 4.8 %collective-permute-start.10 = (bf16[320,128]{1,0:T(8,128)(2,1)S(1)}, bf16[320,128]{1,0:T(8,128)(2,1)S(1)}, u32[]{:S(2)}, u32[]{:S(2)}) collective-permute-start(bf16[320,128]{1,0:T(8,128)(2,1)S(1)} %add.5.refs_4_), channel_id=1, source_target_pairs={{0,8},{4,12},{8,0},{12,4},{1,9},{5,13},{9,1},{13,5},{2,10},{6,14},... | collective-permute-start | bytes 245768 | tf_op jit(solution)/shard_map/ppermute | solution.py:75
  48.1 12.2 %collective-permute-start.12 = (bf16[15,32,128]{2,1,0:T(8,128)(2,1)S(1)}, bf16[15,32,128]{2,1,0:T(8,128)(2,1)S(1)}, u32[]{:S(2)}, u32[]{:S(2)}) collective-permute-start(bf16[15,32,128]{2,1,0:T(8,128)(2,1)S(1)} %get-tuple-element.55), channel_id=1, source_target_pairs={{0,16},{16,0},{1,17},{17,1},{2,18},{18,2},{3,19},{19,3},{4,20},{20... | collective-permute-start | bytes 368648 | tf_op jit(solution)/shard_map/ppermute | solution.py:538

commit v6 on v5

--- a/solution.py
+++ b/solution.py
@@ -557,12 +557,13 @@
     wot = w_out.T
     place = jnp.stack([seq_index, role_index])
 
+    mine = rollout[0].T
+    other = exchange(mine)
     piece = lead(mom, stride, unit, 3)
-    mine, piece = lax.optimization_barrier((rollout[0].T, piece))
-    other = exchange(mine)
     received = [exchange(piece)]
-    mom, other = lax.optimization_barrier((mom, other))
+    mom, piece = lax.optimization_barrier((mom, piece))
     m, et, w, mom, *pieces = prepare(place, w_embed, mom, w, sizes[1:], stride, sizes[0], unit)
+    other, pieces = lax.optimization_barrier((other, pieces))
     received += [exchange(p) for p in pieces[:-1]]
     m, received[0] = lax.optimization_barrier((m, received[0]))
     ma, mb = butterfly(m, "seq")

time: 62.1 us -> 62.2 us (level)
  waiting for transfers between devices: 17.5 us -> 19 us
  starting transfers between devices: 18.3 us -> 16.9 us
    ppermute x5, starting transfers between devices: 6.68 us -> 5.71 us  [exchange(): return lax.ppermute(x, 'role', [(0, 1), (1, 0)])]
    ppermute x5, waiting for transfers between devices: 5.14 us -> 5.87 us  [exchange(): return lax.ppermute(x, 'role', [(0, 1), (1, 0)])]
  transfers between devices with their start and end apart: 14 -> 14, of which waited for: 10 -> 10; matrix products, arithmetic and copies ran while one was open for 0% -> 0% of each run, Pallas kernels for 35% -> 37%
where the time goes in v6:
time: 62.2 us; the launch traced here: 62 us
  Pallas kernels  24.5 us (39%)
  waiting for transfers between devices  19 us (31%)
  starting transfers between devices  16.9 us (27%)
  between operations  1.55 us (2%)
    pallas_call x1, Pallas kernels, update(): pl.pallas_call(functools.partial(update_kernel, heads, unit, sizes), in_s...  6.57 us
    ppermute x4, waiting for transfers between devices, swap(): lax.ppermute(x, axis, [(i, i ^ bit) for i in range(lax.axis_size(axis))])  6.54 us
    pallas_call x1, Pallas kernels, prepare(): pl.pallas_call(functools.partial(prepare_kernel, sizes, stride, skip, uni...  6.16 us
    ppermute x5, waiting for transfers between devices, exchange(): return lax.ppermute(x, 'role', [(0, 1), (1, 0)])  5.87 us
    ppermute x5, starting transfers between devices, exchange(): return lax.ppermute(x, 'role', [(0, 1), (1, 0)])  5.71 us
    ppermute x3, starting transfers between devices, body(): lax.ppermute(partial_pred, 'mp', [(i, (i + d) % mp_count) for i in range(...  4.45 us
    ppermute x3, waiting for transfers between devices, body(): lax.ppermute(partial_pred, 'mp', [(i, (i + d) % mp_count) for i in range(...  4.28 us
    ppermute x4, starting transfers between devices, swap(): lax.ppermute(x, axis, [(i, i ^ bit) for i in range(lax.axis_size(axis))])  3.66 us
  transfers between devices with their start and end apart: 14, of which 10 were waited for; matrix products, arithmetic and copies ran while one was open for 0% of the time, Pallas kernels for 37%

profile of v6, /device:TPU:0, one launch (start us, length us, event | category | flops | bytes accessed | tf_op | source)
XLA Modules:
  0.0 62.0 jit_solution(15260841335332053386)
XLA Ops:
  0.6 3.0 %collective-permute-start = (bf16[64,384]{1,0:T(8,128)(2,1)}, bf16[64,384]{1,0:T(8,128)(2,1)S(1)}, u32[]{:S(2)}, u32[]{:S(2)}) collective-permute-start(bf16[64,384]{1,0:T(8,128)(2,1)} %bitcast.15), channel_id=1, source_target_pairs={{0,16},{16,0},{1,17},{17,1},{2,18},{18,2},{3,19},{19,3},{4,20},{20... | collective-permute-start | bytes 147464 | tf_op jit(solution)/shard_map/ppermute | solution.py:538
  3.6 1.2 %lead.1 = bf16[15,96,128]{2,1,0:T(8,128)(2,1)S(1)} custom-call(f32[9600,128]{1,0:T(8,128)} %bitcast.19), custom_call_target="tpu_custom_call" | custom-call | flops 184320 | bytes 1105920 | tf_op jit(solution)/shard_map/lead/pallas_call | solution.py:151
  4.9 0.1 collective-permute-start.3
  5.0 0.1 pad_add_fusion.place_ref.refs_0_
  5.0 0.0 copy-start.1
  5.0 0.0 copy-start
  5.0 0.0 copy-start.2
  5.0 0.0 copy-start.3
  5.0 6.2 %prepare.1 = (bf16[3,64,640]{2,1,0:T(8,128)(2,1)S(1)}, bf16[1280,64]{1,0:T(8,128)(2,1)S(1)}, bf16[3,1280,640]{2,1,0:T(8,128)(2,1)S(1)}, f32[9600,128]{1,0:T(8,12...) custom-call(s32[2]{0:T(128)S(1)} %pad_add_fusion.place_ref.refs_0_, ...), custom_call_target="tpu_custom_call" | custom-call | flops 314572800 | bytes 22118400 | tf_op jit(solution)/shard_map/prepare/pallas_call | solution.py:208
  11.2 0.0 collective-permute-done.other_ref
  11.2 2.1 %collective-permute-start.11 = (bf16[15,320,128]{2,1,0:T(8,128)(2,1)S(1)}, bf16[15,320,128]{2,1,0:T(8,128)(2,1)S(1)}, u32[]{:S(2)}, u32[]{:S(2)}) collective-permute-start(bf16[15,320,128]{2,1,0:T(8,128)(2,1)S(1)} %get-tuple-element.54), channel_id=1, source_target_pairs={{0,16},{16,0},{1,17},{17,1},{2,18},{18,2},{3,19},{19,3},{4,20},{20... | collective-permute-start | bytes 3686408 | tf_op jit(solution)/shard_map/ppermute | solution.py:538
  13.3 3.2 %collective-permute-done.3.refs_8_ = bf16[15,96,128]{2,1,0:T(8,128)(2,1)S(1)} collective-permute-done((bf16[15,96,128]{2,1,0:T(8,128)(2,1)S(1)}, bf16[15,96,128]{2,1,0:T(8,128)(2,1)S(1)}, u32[]{:S(2)}, u32[]{:S(2)}) %collective-permute-start.3) | collective-permute-done | bytes 368672 | tf_op jit(solution)/shard_map/ppermute | solution.py:538
  16.5 0.0 collective-permute-start.4
  16.5 0.0 collective-permute-start.13
  16.5 1.5 %collective-permute-done.4.b_ref = bf16[3,64,640]{2,1,0:T(8,128)(2,1)S(1)} collective-permute-done((bf16[3,64,640]{2,1,0:T(8,128)(2,1)S(1)}, bf16[3,64,640]{2,1,0:T(8,128)(2,1)S(1)}, u32[]{:S(2)}, u32[]{:S(2)}) %collective-permute-start.4) | collective-permute-done | bytes 245792 | tf_op jit(solution)/shard_map/ppermute | solution.py:75
  18.0 0.1 add.4.refs_4_
  18.0 1.4 %collective-permute-start.5 = (bf16[3,64,640]{2,1,0:T(8,128)(2,1)S(1)}, bf16[3,64,640]{2,1,0:T(8,128)(2,1)S(1)}, u32[]{:S(2)}, u32[]{:S(2)}) collective-permute-start(bf16[3,64,640]{2,1,0:T(8,128)(2,1)S(1)} %add.4.refs_4_), channel_id=1, source_target_pairs={{0,8},{4,12},{8,0},{12,4},{1,9},{5,13},{9,1},{13,5},{2,10},{6,14},... | collective-permute-start | bytes 737288 | tf_op jit(solution)/shard_map/ppermute | solution.py:75
  19.4 0.0 copy-done.1
  19.4 0.6 pick.1
  20.0 1.8 %collective-permute-start.1 = (bf16[64,256]{1,0:T(8,128)(2,1)S(1)}, bf16[64,256]{1,0:T(8,128)(2,1)S(1)}, u32[]{:S(2)}, u32[]{:S(2)}) collective-permute-start(bf16[64,256]{1,0:T(8,128)(2,1)S(1)} %get-tuple-element.39), channel_id=1, source_target_pairs={{0,4},{4,8},{8,12},{1,5},{5,9},{9,13},{2,6},{6,10},{10,14},{3,7},{... | collective-permute-start | bytes 98312 | tf_op jit(solution)/shard_map/ppermute | solution.py:572
  21.7 1.3 %collective-permute-start.2 = (bf16[64,256]{1,0:T(8,128)(2,1)S(1)}, bf16[64,256]{1,0:T(8,128)(2,1)S(1)}, u32[]{:S(2)}, u32[]{:S(2)}) collective-permute-start(bf16[64,256]{1,0:T(8,128)(2,1)S(1)} %get-tuple-element.41), channel_id=1, source_target_pairs={{4,0},{8,4},{12,8},{5,1},{9,5},{13,9},{6,2},{10,6},{14,10},{7,3},{... | collective-permute-start | bytes 98312 | tf_op jit(solution)/shard_map/ppermute | solution.py:573
  23.0 0.0 collective-permute-done.1.refs_1_
  23.1 2.3 %collective-permute-done.2.refs_3_ = bf16[64,256]{1,0:T(8,128)(2,1)S(1)} collective-permute-done((bf16[64,256]{1,0:T(8,128)(2,1)S(1)}, bf16[64,256]{1,0:T(8,128)(2,1)S(1)}, u32[]{:S(2)}, u32[]{:S(2)}) %collective-permute-start.2) | collective-permute-done | bytes 32800 | tf_op jit(solution)/shard_map/ppermute | solution.py:573
  25.3 0.8 %collective-permute-done.5.refs_5_ = bf16[3,64,640]{2,1,0:T(8,128)(2,1)S(1)} collective-permute-done((bf16[3,64,640]{2,1,0:T(8,128)(2,1)S(1)}, bf16[3,64,640]{2,1,0:T(8,128)(2,1)S(1)}, u32[]{:S(2)}, u32[]{:S(2)}) %collective-permute-start.5) | collective-permute-done | bytes 245792 | tf_op jit(solution)/shard_map/ppermute | solution.py:75
  26.1 0.0 copy-done
  26.1 3.6 %attend.1 = (bf16[3,64,640]{2,1,0:T(8,128)(2,1)S(1)}, bf16[2,640,128]{2,1,0:T(8,128)(2,1)S(1)}, bf16[2,960,640]{2,1,0:T(8,128)(2,1)S(1)}, bf16[1920,128]{1,0:T(8...) custom-call(s32[2]{0:T(128)S(1)} %pad_add_fusion.place_ref.refs_0_, ...), custom_call_target="tpu_custom_call" | custom-call | flops 692060160 | bytes 24576000 | tf_op jit(solution)/shard_map/attend/pallas_call | solution.py:293
  29.7 3.4 %collective-permute-start.8 = (bf16[64,384]{1,0:T(8,128)(2,1)S(1)}, bf16[64,384]{1,0:T(8,128)(2,1)S(1)}, u32[]{:S(2)}, u32[]{:S(2)}) collective-permute-start(bf16[64,384]{1,0:T(8,128)(2,1)S(1)} %get-tuple-element.50.refs_11_), channel_id=1, source_target_pairs={{0,3},{1,0},{2,1},{3,2},{4,7},{5,4},{6,5},{7,6},{8,11},{9,8},{10,9... | collective-permute-start | bytes 147464 | tf_op jit(solution)/shard_map/ppermute | solution.py:578
  33.2 0.0 collective-permute-start.7
  33.2 1.0 %collective-permute-start.6 = (bf16[64,384]{1,0:T(8,128)(2,1)S(1)}, bf16[64,384]{1,0:T(8,128)(2,1)S(1)}, u32[]{:S(2)}, u32[]{:S(2)}) collective-permute-start(bf16[64,384]{1,0:T(8,128)(2,1)S(1)} %get-tuple-element.50.refs_11_), channel_id=1, source_target_pairs={{0,1},{1,2},{2,3},{3,0},{4,5},{5,6},{6,7},{7,4},{8,9},{9,10},{10,1... | collective-permute-start | bytes 147464 | tf_op jit(solution)/shard_map/ppermute | solution.py:578
  34.8 0.1 collective-permute-done.8.refs_14_
  34.9 3.2 %collective-permute-done.7.refs_13_ = bf16[64,384]{1,0:T(8,128)(2,1)S(1)} collective-permute-done((bf16[64,384]{1,0:T(8,128)(2,1)S(1)}, bf16[64,384]{1,0:T(8,128)(2,1)S(1)}, u32[]{:S(2)}, u32[]{:S(2)}) %collective-permute-start.7) | collective-permute-done | bytes 49184 | tf_op jit(solution)/shard_map/ppermute | solution.py:578
  38.2 1.0 %collective-permute-done.6.refs_12_ = bf16[64,384]{1,0:T(8,128)(2,1)S(1)} collective-permute-done((bf16[64,384]{1,0:T(8,128)(2,1)S(1)}, bf16[64,384]{1,0:T(8,128)(2,1)S(1)}, u32[]{:S(2)}, u32[]{:S(2)}) %collective-permute-start.6) | collective-permute-done | bytes 49184 | tf_op jit(solution)/shard_map/ppermute | solution.py:578
  39.1 0.0 copy-done.2
  39.1 0.0 copy-done.3
  39.1 2.9 %attend_grad.1.a_ref = bf16[320,128]{1,0:T(8,128)(2,1)S(1)} custom-call(s32[1]{0:T(128)S(6)} %copy.16.refs_0_, f32[1,32]{1,0:T(1,128)S(1)} %bitcast.17, s32[1,32]{1,0:T(1,128)S(1)} %bitcast.18, bf16[2,640,128]{2,1,0:T(8,128)(2,1)S(1)} %get-tuple-element.44.refs_3_, bf16[3,64,640]{2,1,0:T(8,128)(2,1)S(1)} %get-tuple-element.45.refs_4_.refs_6_, ...), custom_call_target="tpu_custom_call" | custom-call | flops 692060160 | bytes 24576000 | tf_op jit(solution)/shard_map/attend_grad/pallas_call | solution.py:371
  42.0 0.9 %collective-permute-start.9 = (bf16[320,128]{1,0:T(8,128)(2,1)S(1)}, bf16[320,128]{1,0:T(8,128)(2,1)S(1)}, u32[]{:S(2)}, u32[]{:S(2)}) collective-permute-start(bf16[320,128]{1,0:T(8,128)(2,1)S(1)} %attend_grad.1.a_ref), channel_id=1, source_target_pairs={{0,4},{4,0},{8,12},{12,8},{1,5},{5,1},{9,13},{13,9},{2,6},{6,2},{1... | collective-permute-start | bytes 245768 | tf_op jit(solution)/shard_map/ppermute | solution.py:75
  42.9 0.9 %collective-permute-done.9.b_ref = bf16[320,128]{1,0:T(8,128)(2,1)S(1)} collective-permute-done((bf16[320,128]{1,0:T(8,128)(2,1)S(1)}, bf16[320,128]{1,0:T(8,128)(2,1)S(1)}, u32[]{:S(2)}, u32[]{:S(2)}) %collective-permute-start.9) | collective-permute-done | bytes 81952 | tf_op jit(solution)/shard_map/ppermute | solution.py:75
  43.8 1.4 %collective-permute-start.10 = (bf16[320,128]{1,0:T(8,128)(2,1)S(1)}, bf16[320,128]{1,0:T(8,128)(2,1)S(1)}, u32[]{:S(2)}, u32[]{:S(2)}) collective-permute-start(bf16[320,128]{1,0:T(8,128)(2,1)S(1)} %add.5.refs_4_), channel_id=1, source_target_pairs={{0,8},{4,12},{8,0},{12,4},{1,9},{5,13},{9,1},{13,5},{2,10},{6,14},... | collective-permute-start | bytes 245768 | tf_op jit(solution)/shard_map/ppermute | solution.py:75
  45.2 3.4 %collective-permute-done.10.refs_5_ = bf16[320,128]{1,0:T(8,128)(2,1)S(1)} collective-permute-done((bf16[320,128]{1,0:T(8,128)(2,1)S(1)}, bf16[320,128]{1,0:T(8,128)(2,1)S(1)}, u32[]{:S(2)}, u32[]{:S(2)}) %collective-permute-start.10) | collective-permute-done | bytes 81952 | tf_op jit(solution)/shard_map/ppermute | solution.py:75
  48.6 0.5 collective-permute-start.12
  49.1 0.0 collective-permute-done.11.refs_9_
  49.1 6.6 %update.1 = (f32[9600,128]{1,0:T(8,128)}, bf16[3,1280,640]{2,1,0:T(8,128)(2,1)}, f32[15,448,128]{2,1,0:T(8,128)S(1)}) custom-call(s32[2]{0:T(128)S(1)} %pad_add_fusion.place_ref.refs_0_, bf16[1280,64]{1,0:T(8,128)(2,1)S(1)} %get-tuple-element.32.refs_1_, f32[9600,128]{1,0:T(8,128)S(1)} %get-tuple-element.33.refs_2_, ...), custom_call_target="tpu_custom_call" | custom-call | flops 629145600 | bytes 27033600 | tf_op jit(solution)/shard_map/update/pallas_call | solution.py:472
  55.7 2.7 %collective-permute-done.13.recv_ref = bf16[15,192,128]{2,1,0:T(8,128)(2,1)S(1)} collective-permute-done((bf16[15,192,128]{2,1,0:T(8,128)(2,1)S(1)}, bf16[15,192,128]{2,1,0:T(8,128)(2,1)S(1)}, u32[]{:S(2)}, u32[]{:S(2)}) %collective-permute-start.13) | collective-permute-done | bytes 737312 | tf_op jit(solution)/shard_map/ppermute | solution.py:538
  58.4 2.0 %finish.2.old_hbm = bf16[3,1280,640]{2,1,0:T(8,128)(2,1)} custom-call(s32[2]{0:T(128)S(1)} %pad_add_fusion.place_ref.refs_0_, f32[15,448,128]{2,1,0:T(8,128)S(1)} %get-tuple-element.56.base_ref, bf16[15,192,128]{2,1,0:T(8,128)(2,1)S(1)} %collective-permute-done.13.recv_ref, ...), custom_call_target="tpu_custom_call", output_to_operand_aliasing={{}: (3, {})} | custom-call | flops 737280 | bytes 5160960 | tf_op jit(solution)/shard_map/finish/pallas_call | solution.py:520
  60.4 0.0 collective-permute-done.12.recv_ref
  60.4 1.4 %finish.3 = bf16[3,1280,640]{2,1,0:T(8,128)(2,1)} custom-call(s32[2]{0:T(128)S(1)} %pad_add_fusion.place_ref.refs_0_, f32[15,448,128]{2,1,0:T(8,128)S(1)} %get-tuple-element.56.base_ref, bf16[15,32,128]{2,1,0:T(8,128)(2,1)S(1)} %collective-permute-done.12.recv_ref, bf16[3,1280,640]{2,1,0:T(8,128)(2,1)} %finish.2.old_hbm), custom_call_target="tpu_custom_call", output_to_operand_aliasing={{}: (3, {})} | custom-call | flops 122880 | bytes 860160 | tf_op jit(solution)/shard_map/finish/pallas_call | solution.py:520
  (1 shorter events, 0.0 us)
Async XLA Ops:
  0.6 10.6 %collective-permute-start = (bf16[64,384]{1,0:T(8,128)(2,1)}, bf16[64,384]{1,0:T(8,128)(2,1)S(1)}, u32[]{:S(2)}, u32[]{:S(2)}) collective-permute-start(bf16[64,384]{1,0:T(8,128)(2,1)} %bitcast.15), channel_id=1, source_target_pairs={{0,16},{16,0},{1,17},{17,1},{2,18},{18,2},{3,19},{19,3},{4,20},{20... | collective-permute-start | bytes 147464 | tf_op jit(solution)/shard_map/ppermute | solution.py:538
  4.9 11.6 %collective-permute-start.3 = (bf16[15,96,128]{2,1,0:T(8,128)(2,1)S(1)}, bf16[15,96,128]{2,1,0:T(8,128)(2,1)S(1)}, u32[]{:S(2)}, u32[]{:S(2)}) collective-permute-start(bf16[15,96,128]{2,1,0:T(8,128)(2,1)S(1)} %lead.1), channel_id=1, source_target_pairs={{0,16},{16,0},{1,17},{17,1},{2,18},{18,2},{3,19},{19,3},{4,20},{20... | collective-permute-start | bytes 1105928 | tf_op jit(solution)/shard_map/ppermute | solution.py:538
  5.0 14.4 %copy-start.1 = (bf16[1,384,64]{1,2,0:T(8,128)(2,1)S(1)}, bf16[1,384,64]{1,2,0:T(8,128)(2,1)}, u32[]{:S(2)}) copy-start(bf16[1,384,64]{1,2,0:T(8,128)(2,1)} %param.8) | copy-start | bytes 147460
  5.0 21.1 %copy-start = (bf16[640,64]{0,1:T(8,128)(2,1)S(1)}, bf16[640,64]{0,1:T(8,128)(2,1)}, u32[]{:S(2)}) copy-start(bf16[640,64]{0,1:T(8,128)(2,1)} %param.11) | copy-start | bytes 245764
  5.0 34.1 %copy-start.2 = (f32[32]{0:T(128)S(1)}, f32[32]{0:T(128)}, u32[]{:S(2)}) copy-start(f32[32]{0:T(128)} %param.13) | copy-start | bytes 388
  5.0 34.1 %copy-start.3 = (s32[32]{0:T(128)S(1)}, s32[32]{0:T(128)}, u32[]{:S(2)}) copy-start(s32[32]{0:T(128)} %param.14) | copy-start | bytes 388
  11.2 37.9 %collective-permute-start.11 = (bf16[15,320,128]{2,1,0:T(8,128)(2,1)S(1)}, bf16[15,320,128]{2,1,0:T(8,128)(2,1)S(1)}, u32[]{:S(2)}, u32[]{:S(2)}) collective-permute-start(bf16[15,320,128]{2,1,0:T(8,128)(2,1)S(1)} %get-tuple-element.54), channel_id=1, source_target_pairs={{0,16},{16,0},{1,17},{17,1},{2,18},{18,2},{3,19},{19,3},{4,20},{20... | collective-permute-start | bytes 3686408 | tf_op jit(solution)/shard_map/ppermute | solution.py:538
  16.5 1.5 %collective-permute-start.4 = (bf16[3,64,640]{2,1,0:T(8,128)(2,1)S(1)}, bf16[3,64,640]{2,1,0:T(8,128)(2,1)S(1)}, u32[]{:S(2)}, u32[]{:S(2)}) collective-permute-start(bf16[3,64,640]{2,1,0:T(8,128)(2,1)S(1)} %get-tuple-element.43.a_ref), channel_id=1, source_target_pairs={{0,4},{4,0},{8,12},{12,8},{1,5},{5,1},{9,13},{13,9},{2,6},{6,2},{1... | collective-permute-start | bytes 737288 | tf_op jit(solution)/shard_map/ppermute | solution.py:75
  16.5 42.0 %collective-permute-start.13 = (bf16[15,192,128]{2,1,0:T(8,128)(2,1)S(1)}, bf16[15,192,128]{2,1,0:T(8,128)(2,1)S(1)}, u32[]{:S(2)}, u32[]{:S(2)}) collective-permute-start(bf16[15,192,128]{2,1,0:T(8,128)(2,1)S(1)} %get-tuple-element.58), channel_id=1, source_target_pairs={{0,16},{16,0},{1,17},{17,1},{2,18},{18,2},{3,19},{19,3},{4,20},{20... | collective-permute-start | bytes 2211848 | tf_op jit(solution)/shard_map/ppermute | solution.py:538
  18.0 8.1 %collective-permute-start.5 = (bf16[3,64,640]{2,1,0:T(8,128)(2,1)S(1)}, bf16[3,64,640]{2,1,0:T(8,128)(2,1)S(1)}, u32[]{:S(2)}, u32[]{:S(2)}) collective-permute-start(bf16[3,64,640]{2,1,0:T(8,128)(2,1)S(1)} %add.4.refs_4_), channel_id=1, source_target_pairs={{0,8},{4,12},{8,0},{12,4},{1,9},{5,13},{9,1},{13,5},{2,10},{6,14},... | collective-permute-start | bytes 737288 | tf_op jit(solution)/shard_map/ppermute | solution.py:75
  20.0 3.1 %collective-permute-start.1 = (bf16[64,256]{1,0:T(8,128)(2,1)S(1)}, bf16[64,256]{1,0:T(8,128)(2,1)S(1)}, u32[]{:S(2)}, u32[]{:S(2)}) collective-permute-start(bf16[64,256]{1,0:T(8,128)(2,1)S(1)} %get-tuple-element.39), channel_id=1, source_target_pairs={{0,4},{4,8},{8,12},{1,5},{5,9},{9,13},{2,6},{6,10},{10,14},{3,7},{... | collective-permute-start | bytes 98312 | tf_op jit(solution)/shard_map/ppermute | solution.py:572
  21.7 3.6 %collective-permute-start.2 = (bf16[64,256]{1,0:T(8,128)(2,1)S(1)}, bf16[64,256]{1,0:T(8,128)(2,1)S(1)}, u32[]{:S(2)}, u32[]{:S(2)}) collective-permute-start(bf16[64,256]{1,0:T(8,128)(2,1)S(1)} %get-tuple-element.41), channel_id=1, source_target_pairs={{4,0},{8,4},{12,8},{5,1},{9,5},{13,9},{6,2},{10,6},{14,10},{7,3},{... | collective-permute-start | bytes 98312 | tf_op jit(solution)/shard_map/ppermute | solution.py:573
  29.7 5.2 %collective-permute-start.8 = (bf16[64,384]{1,0:T(8,128)(2,1)S(1)}, bf16[64,384]{1,0:T(8,128)(2,1)S(1)}, u32[]{:S(2)}, u32[]{:S(2)}) collective-permute-start(bf16[64,384]{1,0:T(8,128)(2,1)S(1)} %get-tuple-element.50.refs_11_), channel_id=1, source_target_pairs={{0,3},{1,0},{2,1},{3,2},{4,7},{5,4},{6,5},{7,6},{8,11},{9,8},{10,9... | collective-permute-start | bytes 147464 | tf_op jit(solution)/shard_map/ppermute | solution.py:578
  33.2 5.0 %collective-permute-start.7 = (bf16[64,384]{1,0:T(8,128)(2,1)S(1)}, bf16[64,384]{1,0:T(8,128)(2,1)S(1)}, u32[]{:S(2)}, u32[]{:S(2)}) collective-permute-start(bf16[64,384]{1,0:T(8,128)(2,1)S(1)} %get-tuple-element.50.refs_11_), channel_id=1, source_target_pairs={{0,2},{1,3},{2,0},{3,1},{4,6},{5,7},{6,4},{7,5},{8,10},{9,11},{10,... | collective-permute-start | bytes 147464 | tf_op jit(solution)/shard_map/ppermute | solution.py:578
  33.2 5.9 %collective-permute-start.6 = (bf16[64,384]{1,0:T(8,128)(2,1)S(1)}, bf16[64,384]{1,0:T(8,128)(2,1)S(1)}, u32[]{:S(2)}, u32[]{:S(2)}) collective-permute-start(bf16[64,384]{1,0:T(8,128)(2,1)S(1)} %get-tuple-element.50.refs_11_), channel_id=1, source_target_pairs={{0,1},{1,2},{2,3},{3,0},{4,5},{5,6},{6,7},{7,4},{8,9},{9,10},{10,1... | collective-permute-start | bytes 147464 | tf_op jit(solution)/shard_map/ppermute | solution.py:578
  42.0 1.8 %collective-permute-start.9 = (bf16[320,128]{1,0:T(8,128)(2,1)S(1)}, bf16[320,128]{1,0:T(8,128)(2,1)S(1)}, u32[]{:S(2)}, u32[]{:S(2)}) collective-permute-start(bf16[320,128]{1,0:T(8,128)(2,1)S(1)} %attend_grad.1.a_ref), channel_id=1, source_target_pairs={{0,4},{4,0},{8,12},{12,8},{1,5},{5,1},{9,13},{13,9},{2,6},{6,2},{1... | collective-permute-start | bytes 245768 | tf_op jit(solution)/shard_map/ppermute | solution.py:75
  43.8 4.8 %collective-permute-start.10 = (bf16[320,128]{1,0:T(8,128)(2,1)S(1)}, bf16[320,128]{1,0:T(8,128)(2,1)S(1)}, u32[]{:S(2)}, u32[]{:S(2)}) collective-permute-start(bf16[320,128]{1,0:T(8,128)(2,1)S(1)} %add.5.refs_4_), channel_id=1, source_target_pairs={{0,8},{4,12},{8,0},{12,4},{1,9},{5,13},{9,1},{13,5},{2,10},{6,14},... | collective-permute-start | bytes 245768 | tf_op jit(solution)/shard_map/ppermute | solution.py:75
  48.6 11.8 %collective-permute-start.12 = (bf16[15,32,128]{2,1,0:T(8,128)(2,1)S(1)}, bf16[15,32,128]{2,1,0:T(8,128)(2,1)S(1)}, u32[]{:S(2)}, u32[]{:S(2)}) collective-permute-start(bf16[15,32,128]{2,1,0:T(8,128)(2,1)S(1)} %get-tuple-element.57), channel_id=1, source_target_pairs={{0,16},{16,0},{1,17},{17,1},{2,18},{18,2},{3,19},{19,3},{4,20},{20... | collective-permute-start | bytes 368648 | tf_op jit(solution)/shard_map/ppermute | solution.py:538

commit v7 on v6

--- a/solution.py
+++ b/solution.py
@@ -99,19 +99,23 @@
     return x, swap(x, axis, bit)
 
 
-def pick_kernel(place_ref, mine_ref, other_ref, now_ref, next_ref, head_ref, tail_ref):
+def pick_kernel(place_ref, mine_ref, piece_ref, now_ref, next_ref, head_ref, tail_ref):
     mine = mine_ref[...]
-    other = other_ref[...]
+    tok = mine.shape[1]
+    start = piece_ref.shape[0] - mine.size // HD
     sampler = place_ref[1] == 0
-    now = jnp.where(sampler, mine.astype(F32), other.astype(F32)).astype(BF16)
-    now_ref[...] = now
-    next_ref[...] = jnp.where(sampler, other.astype(F32), mine.astype(F32)).astype(BF16)
     spare = head_ref.shape[1]
-    head_ref[...] = now[:, :spare]
-    tail_ref[...] = now[:, now.shape[1] - spare :]
-
-
-def pick(place, mine, other, spare):
+    for k in range(tok // HD):
+        cols = slice(k * HD, (k + 1) * HD)
+        own = mine_ref[:, cols].astype(F32)
+        other = piece_ref[start + k * CH : start + (k + 1) * CH, :].astype(F32)
+        now_ref[:, cols] = jnp.where(sampler, own, other).astype(BF16)
+        next_ref[:, cols] = jnp.where(sampler, other, own).astype(BF16)
+    head_ref[...] = now_ref[:, :spare]
+    tail_ref[...] = now_ref[:, tok - spare :]
+
+
+def pick(place, mine, piece, spare):
     shape = pltpu.VMEM(mine.shape, BF16)
     edge = pltpu.VMEM((mine.shape[0], spare), BF16)
     return pl.pallas_call(
@@ -122,42 +126,53 @@
         compiler_params=params(4),
         cost_estimate=cost(mine.size, 10 * mine.size),
         name="pick",
-    )(place, mine, other)
+    )(place, mine, piece)
 
 
 def chunk_of(size, unit):
     return 2 * unit if size % (2 * unit) == 0 else unit
 
 
-def narrow(mom_ref, o_ref, stride, first, count, at=0):
+def narrow(mom_ref, o_ref, stride, first, count, at, size):
     for q in range(stride):
         part = mom_ref[pl.ds(first * stride + q, count, stride=stride), :]
-        o_ref[q, pl.ds(at, count), :] = (MOMENTUM_DECAY * part).astype(BF16)
-
-
-def lead_kernel(stride, count, steps, mom_hbm, o_ref, mom_ref, sems):
+        o_ref[pl.ds(q * size + at, count), :] = (MOMENTUM_DECAY * part).astype(BF16)
+
+
+def lead_kernel(stride, count, steps, mom_hbm, mine_hbm, o_ref, mom_ref, mine_ref, mine_sem, sems):
+    mine_copy = pltpu.make_async_copy(mine_hbm, mine_ref, mine_sem)
+    mine_copy.start()
     copies = []
     for k in range(steps):
         rows = pl.ds(k * count * stride, count * stride)
         copies.append(pltpu.make_async_copy(mom_hbm.at[rows], mom_ref.at[rows], sems.at[k]))
         copies[-1].start()
+    start = stride * count * steps
+    mine_copy.wait()
+    for k in range(mine_ref.shape[1] // HD):
+        o_ref[start + k * CH : start + (k + 1) * CH, :] = mine_ref[:, k * HD : (k + 1) * HD]
     for k in range(steps):
         copies[k].wait()
-        narrow(mom_ref, o_ref, stride, k * count, count, k * count)
-
-
-def lead(mom, stride, count, steps):
+        narrow(mom_ref, o_ref, stride, k * count, count, k * count, count * steps)
+
+
+def lead(mom, mine, stride, count, steps):
     pairs = count * steps
     return pl.pallas_call(
         functools.partial(lead_kernel, stride, count, steps),
-        in_specs=[HBM],
+        in_specs=[HBM, HBM],
         out_specs=VMEM,
-        out_shape=pltpu.VMEM((stride, pairs, HD), BF16),
-        scratch_shapes=[pltpu.VMEM((pairs * stride, HD), F32), pltpu.SemaphoreType.DMA((steps,))],
+        out_shape=pltpu.VMEM((stride * pairs + mine.size // HD, HD), BF16),
+        scratch_shapes=[
+            pltpu.VMEM((pairs * stride, HD), F32),
+            pltpu.VMEM(mine.shape, BF16),
+            pltpu.SemaphoreType.DMA(()),
+            pltpu.SemaphoreType.DMA((steps,)),
+        ],
         compiler_params=params(4),
         cost_estimate=cost(pairs * stride * HD, 6 * pairs * stride * HD),
         name="lead",
-    )(in_hbm(mom))
+    )(in_hbm(mom), in_hbm(mine))
 
 
 def prepare_kernel(sizes, stride, skip, unit, sliced, place_ref, e_hbm, mom_hbm, w_hbm, m_ref, et_ref, w_ref, mom_ref, *rest):
@@ -197,7 +212,7 @@
     for (first, count, k, at), copy in zip(cuts, mom_copies):
         copy.wait()
         if k >= 0:
-            narrow(mom_ref, pieces[k], stride, first, count, at)
+            narrow(mom_ref, pieces[k], stride, first, count, at, sizes[k])
 
 
 def prepare(place, w_embed, mom, w, sizes, stride, skip, unit):
@@ -215,7 +230,7 @@
             pltpu.VMEM(w.shape, BF16),
             pltpu.VMEM(mom.shape, F32),
         ]
-        + [pltpu.VMEM((stride, n, HD), BF16) for n in sizes],
+        + [pltpu.VMEM((stride * n, HD), BF16) for n in sizes],
         scratch_shapes=[
             pltpu.VMEM((CH, rows), BF16),
             pltpu.SemaphoreType.DMA(()),
@@ -448,7 +463,8 @@
             own = own + gs_ref[q, pl.ds(local + role, count, stride=2), :]
             other = gs_ref[q, pl.ds(local + 1 - role, count, stride=2), :]
             if k < here:
-                other = other + recv_refs[k][q, at : at + count, :].astype(F32)
+                row = q * sizes[k] + at
+                other = other + recv_refs[k][row : row + count, :].astype(F32)
             onm_ref[slot, pl.ds(q, count, stride=stride), :] = own
             fs_ref[q, mine, :] = own
             fs_ref[q, theirs, :] = other
@@ -464,8 +480,8 @@
             copy.wait()
 
 
-def update(place, et, mom, w, received, rest, unit, heads, sources):
-    sizes = [a.shape[1] for a in received] + [rest]
+def update(place, et, mom, w, received, sizes, rest, unit, heads, sources):
+    sizes = [*sizes, rest]
     _, rows, width = w.shape
     stride = 3 * heads
     slots = 4
@@ -494,7 +510,8 @@
 
 def finish_kernel(heads, unit, first, local, place_ref, base_ref, recv_ref, old_hbm, ow_hbm, fs_ref, ow_ref, sems):
     del old_hbm
-    stride, size, _ = recv_ref.shape
+    stride = base_ref.shape[0]
+    size = recv_ref.shape[0] // stride
     role = place_ref[1]
     count = chunk_of(size, unit)
     fs_ref[...] = jnp.zeros_like(fs_ref)
@@ -503,7 +520,8 @@
         at = 2 * step * count
         for q in range(stride):
             part, b = divmod(q, heads)
-            fs_ref[q, pl.ds(1 - role, count, stride=2), :] = recv_ref[q, at // 2 : at // 2 + count, :].astype(F32)
+            row = q * size + at // 2
+            fs_ref[q, pl.ds(1 - role, count, stride=2), :] = recv_ref[row : row + count, :].astype(F32)
             new = base_ref[q, 2 * local + at : 2 * local + at + 2 * count, :] - LEARNING_RATE * fs_ref[q]
             ow_ref[part, at : at + 2 * count, b * HD : (b + 1) * HD] = new.astype(BF16)
         source = ow_ref.at[:, pl.ds(at, 2 * count)]
@@ -515,7 +533,8 @@
 
 
 def finish(place, base, recv, old, first, local, unit, heads):
-    stride, size, _ = recv.shape
+    stride = base.shape[0]
+    size = recv.shape[0] // stride
     count = chunk_of(size, unit)
     return pl.pallas_call(
         functools.partial(finish_kernel, heads, unit, first, local),
@@ -551,33 +570,28 @@
 
     stride = 3 * heads
     unit = pair_rows // 20
-    sizes = (3 * unit, 10 * unit, 6 * unit, unit)
+    sizes = (3 * unit, 8 * unit, 6 * unit, 3 * unit)
     mom = momentum.reshape(pair_rows * stride, HD)
     w = w_qkv.transpose(1, 0, 2)
     wot = w_out.T
     place = jnp.stack([seq_index, role_index])
 
     mine = rollout[0].T
-    other = exchange(mine)
-    piece = lead(mom, stride, unit, 3)
+    piece = lead(mom, mine, stride, unit, sizes[0] // unit)
     received = [exchange(piece)]
     mom, piece = lax.optimization_barrier((mom, piece))
     m, et, w, mom, *pieces = prepare(place, w_embed, mom, w, sizes[1:], stride, sizes[0], unit)
-    other, pieces = lax.optimization_barrier((other, pieces))
-    received += [exchange(p) for p in pieces[:-1]]
+    received += [exchange(p) for p in pieces]
     m, received[0] = lax.optimization_barrier((m, received[0]))
     ma, mb = butterfly(m, "seq")
 
-    latent_now, latent_next, head, tail = pick(place, mine, other, min(2 * HD, tok_dev))
+    latent_now, latent_next, head, tail = pick(place, mine, received[0], min(2 * HD, tok_dev))
     left = lax.ppermute(tail, "seq", [(i, i + 1) for i in range(seq_count - 1)])
     right = lax.ppermute(head, "seq", [(i + 1, i) for i in range(seq_count - 1)])
 
     m, win, e, u, il, partial_pred = forward(place, left, latent_now, right, ma, mb, wot, tiles, heads, seq_count)
-    mp_count = lax.axis_size("mp")
-    preds = [partial_pred] + [
-        lax.ppermute(partial_pred, "mp", [(i, (i + d) % mp_count) for i in range(mp_count)])
-        for d in range(1, mp_count)
-    ]
+    preds = list(butterfly(partial_pred, "mp"))
+    preds, received[1] = lax.optimization_barrier((preds, received[1]))
     za, zb = butterfly(
         backward(
             timestep,
@@ -599,13 +613,10 @@
         "seq",
     )
 
-    zb, last = lax.optimization_barrier((zb, pieces[-1]))
-    received.append(exchange(last))
-    rest = sizes[2] + sizes[3]
-    nm, nw, base = update(place, et, mom, w, received[:2], rest, unit, heads, [za, zb, m, wot])
-    first = sizes[0] + sizes[1]
-    nw = finish(place, base, received[2], nw, first, 0, unit, heads)
-    nw = finish(place, base, received[3], nw, first + sizes[2], sizes[2], unit, heads)
+    rest = sizes[-1]
+    nm, nw, base = update(place, et, mom, w, received[:-1], sizes[:-1], rest, unit, heads, [za, zb, m, wot])
+    first = sum(sizes) - rest
+    nw = finish(place, base, received[-1], nw, first, 0, unit, heads)
     return nm.reshape(momentum.shape), nw.transpose(1, 0, 2)
 
 

time: 62.2 us -> 61.2 us (0.984)
  Pallas kernels: 24.5 us -> 22.6 us
    ppermute x5 -> x4, waiting for transfers between devices: 5.87 us -> 12.4 us  [exchange(): return lax.ppermute(x, 'role', [(0, 1), (1, 0)])]
    ppermute x3 -> x0, starting transfers between devices: 4.45 us -> none  [body(): lax.ppermute(partial_pred, 'mp', [(i, (i + d) % mp_count) for i in range(...]
    ppermute x3 -> x0, waiting for transfers between devices: 4.28 us -> none  [body(): lax.ppermute(partial_pred, 'mp', [(i, (i + d) % mp_count) for i in range(...]
    ppermute x4 -> x6, starting transfers between devices: 3.66 us -> 7.73 us  [swap(): lax.ppermute(x, axis, [(i, i ^ bit) for i in range(lax.axis_size(axis))])]
    pallas_call x2 -> x1, Pallas kernels: 3.36 us -> 1.65 us  [finish(): pl.pallas_call(functools.partial(finish_kernel, heads, unit, first, local...]
    ppermute x4 -> x6, waiting for transfers between devices: 6.54 us -> 5.11 us  [swap(): lax.ppermute(x, axis, [(i, i ^ bit) for i in range(lax.axis_size(axis))])]
    ppermute x5 -> x4, starting transfers between devices: 5.71 us -> 6.56 us  [exchange(): return lax.ppermute(x, 'role', [(0, 1), (1, 0)])]
  transfers between devices with their start and end apart: 14 -> 12, of which waited for: 10 -> 8; matrix products, arithmetic and copies ran while one was open for 0% -> 0% of each run, Pallas kernels for 37% -> 32%
where the time goes in v7:
time: 61.2 us; the launch traced here: 61 us
  Pallas kernels  22.6 us (37%)
  waiting for transfers between devices  19.4 us (32%)
  starting transfers between devices  17.4 us (28%)
  between operations  1.38 us (2%)
    ppermute x4, waiting for transfers between devices, exchange(): return lax.ppermute(x, 'role', [(0, 1), (1, 0)])  12.4 us
    ppermute x6, starting transfers between devices, swap(): lax.ppermute(x, axis, [(i, i ^ bit) for i in range(lax.axis_size(axis))])  7.73 us
    ppermute x4, starting transfers between devices, exchange(): return lax.ppermute(x, 'role', [(0, 1), (1, 0)])  6.56 us
    pallas_call x1, Pallas kernels, update(): pl.pallas_call(functools.partial(update_kernel, heads, unit, sizes), in_s...  6.38 us
    pallas_call x1, Pallas kernels, prepare(): pl.pallas_call(functools.partial(prepare_kernel, sizes, stride, skip, uni...  6.16 us
    ppermute x6, waiting for transfers between devices, swap(): lax.ppermute(x, axis, [(i, i ^ bit) for i in range(lax.axis_size(axis))])  5.11 us
    pallas_call x1, Pallas kernels, forward(): pl.pallas_call(functools.partial(forward_kernel, tiles, heads, seq_count...  3.63 us
    pallas_call x1, Pallas kernels, backward(): pl.pallas_call(functools.partial(backward_kernel, tiles, heads, tokens_al...  2.88 us
  transfers between devices with their start and end apart: 12, of which 8 were waited for; matrix products, arithmetic and copies ran while one was open for 0% of the time, Pallas kernels for 32%

profile of v7, /device:TPU:0, one launch (start us, length us, event | category | flops | bytes accessed | tf_op | source)
XLA Modules:
  0.0 61.0 jit_solution(10791019146569194236)
XLA Ops:
  0.6 1.3 %lead.1 = bf16[1632,128]{1,0:T(8,128)(2,1)S(1)} custom-call(f32[9600,128]{1,0:T(8,128)} %bitcast.19, bf16[64,384]{1,0:T(8,128)(2,1)} %bitcast.15), custom_call_target="tpu_custom_call" | custom-call | flops 184320 | bytes 1105920 | tf_op jit(solution)/shard_map/lead/pallas_call | solution.py:161
  1.9 3.0 %collective-permute-start = (bf16[1632,128]{1,0:T(8,128)(2,1)S(1)}, bf16[1632,128]{1,0:T(8,128)(2,1)S(1)}, u32[]{:S(2)}, u32[]{:S(2)}) collective-permute-start(bf16[1632,128]{1,0:T(8,128)(2,1)S(1)} %lead.1), channel_id=1, source_target_pairs={{0,16},{16,0},{1,17},{17,1},{2,18},{18,2},{3,19},{19,3},{4,20},{20... | collective-permute-start | bytes 1253384 | tf_op jit(solution)/shard_map/ppermute | solution.py:557
  4.9 0.1 pad_add_fusion.place_ref.refs_0_
  5.0 0.0 copy-start.1
  5.0 0.0 copy-start
  5.0 0.0 copy-start.2
  5.0 0.0 copy-start.3
  5.0 6.2 %prepare.1 = (bf16[3,64,640]{2,1,0:T(8,128)(2,1)S(1)}, bf16[1280,64]{1,0:T(8,128)(2,1)S(1)}, bf16[3,1280,640]{2,1,0:T(8,128)(2,1)S(1)}, f32[9600,128]{1,0:T(8,12...) custom-call(s32[2]{0:T(128)S(1)} %pad_add_fusion.place_ref.refs_0_, ...), custom_call_target="tpu_custom_call" | custom-call | flops 314572800 | bytes 22118400 | tf_op jit(solution)/shard_map/prepare/pallas_call | solution.py:223
  11.2 0.1 collective-permute-start.7
  11.3 4.1 %collective-permute-done.piece_ref.refs_8_ = bf16[1632,128]{1,0:T(8,128)(2,1)S(1)} collective-permute-done((bf16[1632,128]{1,0:T(8,128)(2,1)S(1)}, bf16[1632,128]{1,0:T(8,128)(2,1)S(1)}, u32[]{:S(2)}, u32[]{:S(2)}) %collective-permute-start) | collective-permute-done | bytes 417824 | tf_op jit(solution)/shard_map/ppermute | solution.py:557
  15.4 0.0 collective-permute-start.3
  15.4 2.1 %collective-permute-start.10 = (bf16[2880,128]{1,0:T(8,128)(2,1)S(1)}, bf16[2880,128]{1,0:T(8,128)(2,1)S(1)}, u32[]{:S(2)}, u32[]{:S(2)}) collective-permute-start(bf16[2880,128]{1,0:T(8,128)(2,1)S(1)} %get-tuple-element.49), channel_id=1, source_target_pairs={{0,16},{16,0},{1,17},{17,1},{2,18},{18,2},{3,19},{19,3},{4,20},{20... | collective-permute-start | bytes 2211848 | tf_op jit(solution)/shard_map/ppermute | solution.py:557
  17.5 0.0 collective-permute-done.3.b_ref
  17.5 0.1 add.5.refs_4_
  17.5 1.6 %collective-permute-start.4 = (bf16[3,64,640]{2,1,0:T(8,128)(2,1)S(1)}, bf16[3,64,640]{2,1,0:T(8,128)(2,1)S(1)}, u32[]{:S(2)}, u32[]{:S(2)}) collective-permute-start(bf16[3,64,640]{2,1,0:T(8,128)(2,1)S(1)} %add.5.refs_4_), channel_id=1, source_target_pairs={{0,8},{4,12},{8,0},{12,4},{1,9},{5,13},{9,1},{13,5},{2,10},{6,14},... | collective-permute-start | bytes 737288 | tf_op jit(solution)/shard_map/ppermute | solution.py:75
  19.1 0.0 copy-done.1
  19.1 0.6 pick.1
  19.7 1.8 %collective-permute-start.1 = (bf16[64,256]{1,0:T(8,128)(2,1)S(1)}, bf16[64,256]{1,0:T(8,128)(2,1)S(1)}, u32[]{:S(2)}, u32[]{:S(2)}) collective-permute-start(bf16[64,256]{1,0:T(8,128)(2,1)S(1)} %get-tuple-element.34), channel_id=1, source_target_pairs={{0,4},{4,8},{8,12},{1,5},{5,9},{9,13},{2,6},{6,10},{10,14},{3,7},{... | collective-permute-start | bytes 98312 | tf_op jit(solution)/shard_map/ppermute | solution.py:589
  21.5 1.3 %collective-permute-start.2 = (bf16[64,256]{1,0:T(8,128)(2,1)S(1)}, bf16[64,256]{1,0:T(8,128)(2,1)S(1)}, u32[]{:S(2)}, u32[]{:S(2)}) collective-permute-start(bf16[64,256]{1,0:T(8,128)(2,1)S(1)} %get-tuple-element.36), channel_id=1, source_target_pairs={{4,0},{8,4},{12,8},{5,1},{9,5},{13,9},{6,2},{10,6},{14,10},{7,3},{... | collective-permute-start | bytes 98312 | tf_op jit(solution)/shard_map/ppermute | solution.py:590
  22.8 0.0 collective-permute-done.1.refs_1_
  22.9 2.0 %collective-permute-done.2.refs_3_ = bf16[64,256]{1,0:T(8,128)(2,1)S(1)} collective-permute-done((bf16[64,256]{1,0:T(8,128)(2,1)S(1)}, bf16[64,256]{1,0:T(8,128)(2,1)S(1)}, u32[]{:S(2)}, u32[]{:S(2)}) %collective-permute-start.2) | collective-permute-done | bytes 32800 | tf_op jit(solution)/shard_map/ppermute | solution.py:590
  24.8 0.8 %collective-permute-done.4.refs_5_ = bf16[3,64,640]{2,1,0:T(8,128)(2,1)S(1)} collective-permute-done((bf16[3,64,640]{2,1,0:T(8,128)(2,1)S(1)}, bf16[3,64,640]{2,1,0:T(8,128)(2,1)S(1)}, u32[]{:S(2)}, u32[]{:S(2)}) %collective-permute-start.4) | collective-permute-done | bytes 245792 | tf_op jit(solution)/shard_map/ppermute | solution.py:75
  25.7 0.0 copy-done
  25.7 3.6 %attend.1 = (bf16[3,64,640]{2,1,0:T(8,128)(2,1)S(1)}, bf16[2,640,128]{2,1,0:T(8,128)(2,1)S(1)}, bf16[2,960,640]{2,1,0:T(8,128)(2,1)S(1)}, bf16[1920,128]{1,0:T(8...) custom-call(s32[2]{0:T(128)S(1)} %pad_add_fusion.place_ref.refs_0_, ...), custom_call_target="tpu_custom_call" | custom-call | flops 692060160 | bytes 24576000 | tf_op jit(solution)/shard_map/attend/pallas_call | solution.py:308
  29.3 1.6 %collective-permute-start.5 = (bf16[64,384]{1,0:T(8,128)(2,1)S(1)}, bf16[64,384]{1,0:T(8,128)(2,1)S(1)}, u32[]{:S(2)}, u32[]{:S(2)}) collective-permute-start(bf16[64,384]{1,0:T(8,128)(2,1)S(1)} %get-tuple-element.44.a_ref), channel_id=1, source_target_pairs={{0,1},{1,0},{2,3},{3,2},{4,5},{5,4},{6,7},{7,6},{8,9},{9,8},{10,11... | collective-permute-start | bytes 147464 | tf_op jit(solution)/shard_map/ppermute | solution.py:75
  31.0 1.4 %collective-permute-start.11 = (bf16[1440,128]{1,0:T(8,128)(2,1)S(1)}, bf16[1440,128]{1,0:T(8,128)(2,1)S(1)}, u32[]{:S(2)}, u32[]{:S(2)}) collective-permute-start(bf16[1440,128]{1,0:T(8,128)(2,1)S(1)} %get-tuple-element.52), channel_id=1, source_target_pairs={{0,16},{16,0},{1,17},{17,1},{2,18},{18,2},{3,19},{19,3},{4,20},{20... | collective-permute-start | bytes 1105928 | tf_op jit(solution)/shard_map/ppermute | solution.py:557
  32.4 1.1 %collective-permute-done.5.b_ref = bf16[64,384]{1,0:T(8,128)(2,1)S(1)} collective-permute-done((bf16[64,384]{1,0:T(8,128)(2,1)S(1)}, bf16[64,384]{1,0:T(8,128)(2,1)S(1)}, u32[]{:S(2)}, u32[]{:S(2)}) %collective-permute-start.5) | collective-permute-done | bytes 49184 | tf_op jit(solution)/shard_map/ppermute | solution.py:75
  33.5 2.7 %collective-permute-start.6 = (bf16[64,384]{1,0:T(8,128)(2,1)S(1)}, bf16[64,384]{1,0:T(8,128)(2,1)S(1)}, u32[]{:S(2)}, u32[]{:S(2)}) collective-permute-start(bf16[64,384]{1,0:T(8,128)(2,1)S(1)} %add.6.refs_11_), channel_id=1, source_target_pairs={{0,2},{1,3},{2,0},{3,1},{4,6},{5,7},{6,4},{7,5},{8,10},{9,11},{10,... | collective-permute-start | bytes 147464 | tf_op jit(solution)/shard_map/ppermute | solution.py:75
  36.8 0.0 collective-permute-done.7.refs_9_
  36.8 2.0 %collective-permute-done.6.refs_12_ = bf16[64,384]{1,0:T(8,128)(2,1)S(1)} collective-permute-done((bf16[64,384]{1,0:T(8,128)(2,1)S(1)}, bf16[64,384]{1,0:T(8,128)(2,1)S(1)}, u32[]{:S(2)}, u32[]{:S(2)}) %collective-permute-start.6) | collective-permute-done | bytes 49184 | tf_op jit(solution)/shard_map/ppermute | solution.py:75
  38.8 0.0 copy-done.2
  38.8 0.0 copy-done.3
  38.8 2.9 %attend_grad.1.a_ref = bf16[320,128]{1,0:T(8,128)(2,1)S(1)} custom-call(s32[1]{0:T(128)S(6)} %copy.14.refs_0_, f32[1,32]{1,0:T(1,128)S(1)} %bitcast.17, s32[1,32]{1,0:T(1,128)S(1)} %bitcast.18, bf16[2,640,128]{2,1,0:T(8,128)(2,1)S(1)} %get-tuple-element.38.refs_3_, bf16[3,64,640]{2,1,0:T(8,128)(2,1)S(1)} %get-tuple-element.39.refs_4_.refs_6_, ...), custom_call_target="tpu_custom_call" | custom-call | flops 692060160 | bytes 24576000 | tf_op jit(solution)/shard_map/attend_grad/pallas_call | solution.py:386
  41.7 0.2 collective-permute-start.8
  41.9 1.2 %collective-permute-done.8.b_ref = bf16[320,128]{1,0:T(8,128)(2,1)S(1)} collective-permute-done((bf16[320,128]{1,0:T(8,128)(2,1)S(1)}, bf16[320,128]{1,0:T(8,128)(2,1)S(1)}, u32[]{:S(2)}, u32[]{:S(2)}) %collective-permute-start.8) | collective-permute-done | bytes 81952 | tf_op jit(solution)/shard_map/ppermute | solution.py:75
  43.0 1.7 %collective-permute-start.9 = (bf16[320,128]{1,0:T(8,128)(2,1)S(1)}, bf16[320,128]{1,0:T(8,128)(2,1)S(1)}, u32[]{:S(2)}, u32[]{:S(2)}) collective-permute-start(bf16[320,128]{1,0:T(8,128)(2,1)S(1)} %add.7.refs_4_), channel_id=1, source_target_pairs={{0,8},{4,12},{8,0},{12,4},{1,9},{5,13},{9,1},{13,5},{2,10},{6,14},... | collective-permute-start | bytes 245768 | tf_op jit(solution)/shard_map/ppermute | solution.py:75
  44.7 7.5 %collective-permute-done.10.refs_10_ = bf16[2880,128]{1,0:T(8,128)(2,1)S(1)} collective-permute-done((bf16[2880,128]{1,0:T(8,128)(2,1)S(1)}, bf16[2880,128]{1,0:T(8,128)(2,1)S(1)}, u32[]{:S(2)}, u32[]{:S(2)}) %collective-permute-start.10) | collective-permute-done | bytes 737312 | tf_op jit(solution)/shard_map/ppermute | solution.py:557
  52.3 0.0 collective-permute-done.9.refs_5_
  52.3 6.4 %update.1 = (f32[9600,128]{1,0:T(8,128)}, bf16[3,1280,640]{2,1,0:T(8,128)(2,1)}, f32[15,192,128]{2,1,0:T(8,128)S(1)}) custom-call(s32[2]{0:T(128)S(1)} %pad_add_fusion.place_ref.refs_0_, bf16[1280,64]{1,0:T(8,128)(2,1)S(1)} %get-tuple-element.29.refs_1_, f32[9600,128]{1,0:T(8,128)S(1)} %get-tuple-element.30.refs_2_, ...), custom_call_target="tpu_custom_call" | custom-call | flops 629145600 | bytes 27033600 | tf_op jit(solution)/shard_map/update/pallas_call | solution.py:488
  58.6 0.7 %collective-permute-done.11.recv_ref = bf16[1440,128]{1,0:T(8,128)(2,1)S(1)} collective-permute-done((bf16[1440,128]{1,0:T(8,128)(2,1)S(1)}, bf16[1440,128]{1,0:T(8,128)(2,1)S(1)}, u32[]{:S(2)}, u32[]{:S(2)}) %collective-permute-start.11) | collective-permute-done | bytes 368672 | tf_op jit(solution)/shard_map/ppermute | solution.py:557
  59.3 1.6 %finish.1 = bf16[3,1280,640]{2,1,0:T(8,128)(2,1)} custom-call(s32[2]{0:T(128)S(1)} %pad_add_fusion.place_ref.refs_0_, f32[15,192,128]{2,1,0:T(8,128)S(1)} %get-tuple-element.51.base_ref, bf16[1440,128]{1,0:T(8,128)(2,1)S(1)} %collective-permute-done.11.recv_ref, bf16[3,1280,640]{2,1,0:T(8,128)(2,1)} %get-tuple-element.53.old_hbm), custom_call_target="tpu_custom_call", output_to_operand_aliasing={{}: (3, {})} | custom-call | flops 368640 | bytes 2580480 | tf_op jit(solution)/shard_map/finish/pallas_call | solution.py:539
  (2 shorter events, 0.0 us)
Async XLA Ops:
  1.9 13.5 %collective-permute-start = (bf16[1632,128]{1,0:T(8,128)(2,1)S(1)}, bf16[1632,128]{1,0:T(8,128)(2,1)S(1)}, u32[]{:S(2)}, u32[]{:S(2)}) collective-permute-start(bf16[1632,128]{1,0:T(8,128)(2,1)S(1)} %lead.1), channel_id=1, source_target_pairs={{0,16},{16,0},{1,17},{17,1},{2,18},{18,2},{3,19},{19,3},{4,20},{20... | collective-permute-start | bytes 1253384 | tf_op jit(solution)/shard_map/ppermute | solution.py:557
  5.0 14.1 %copy-start.1 = (bf16[1,384,64]{1,2,0:T(8,128)(2,1)S(1)}, bf16[1,384,64]{1,2,0:T(8,128)(2,1)}, u32[]{:S(2)}) copy-start(bf16[1,384,64]{1,2,0:T(8,128)(2,1)} %param.8) | copy-start | bytes 147460
  5.0 20.7 %copy-start = (bf16[640,64]{0,1:T(8,128)(2,1)S(1)}, bf16[640,64]{0,1:T(8,128)(2,1)}, u32[]{:S(2)}) copy-start(bf16[640,64]{0,1:T(8,128)(2,1)} %param.11) | copy-start | bytes 245764
  5.0 33.8 %copy-start.2 = (f32[32]{0:T(128)S(1)}, f32[32]{0:T(128)}, u32[]{:S(2)}) copy-start(f32[32]{0:T(128)} %param.13) | copy-start | bytes 388
  5.0 33.8 %copy-start.3 = (s32[32]{0:T(128)S(1)}, s32[32]{0:T(128)}, u32[]{:S(2)}) copy-start(s32[32]{0:T(128)} %param.14) | copy-start | bytes 388
  11.2 25.6 %collective-permute-start.7 = (bf16[3840,128]{1,0:T(8,128)(2,1)S(1)}, bf16[3840,128]{1,0:T(8,128)(2,1)S(1)}, u32[]{:S(2)}, u32[]{:S(2)}) collective-permute-start(bf16[3840,128]{1,0:T(8,128)(2,1)S(1)} %get-tuple-element.45), channel_id=1, source_target_pairs={{0,16},{16,0},{1,17},{17,1},{2,18},{18,2},{3,19},{19,3},{4,20},{20... | collective-permute-start | bytes 2949128 | tf_op jit(solution)/shard_map/ppermute | solution.py:557
  15.4 2.1 %collective-permute-start.3 = (bf16[3,64,640]{2,1,0:T(8,128)(2,1)S(1)}, bf16[3,64,640]{2,1,0:T(8,128)(2,1)S(1)}, u32[]{:S(2)}, u32[]{:S(2)}) collective-permute-start(bf16[3,64,640]{2,1,0:T(8,128)(2,1)S(1)} %get-tuple-element.37.a_ref), channel_id=1, source_target_pairs={{0,4},{4,0},{8,12},{12,8},{1,5},{5,1},{9,13},{13,9},{2,6},{6,2},{1... | collective-permute-start | bytes 737288 | tf_op jit(solution)/shard_map/ppermute | solution.py:75
  15.4 36.9 %collective-permute-start.10 = (bf16[2880,128]{1,0:T(8,128)(2,1)S(1)}, bf16[2880,128]{1,0:T(8,128)(2,1)S(1)}, u32[]{:S(2)}, u32[]{:S(2)}) collective-permute-start(bf16[2880,128]{1,0:T(8,128)(2,1)S(1)} %get-tuple-element.49), channel_id=1, source_target_pairs={{0,16},{16,0},{1,17},{17,1},{2,18},{18,2},{3,19},{19,3},{4,20},{20... | collective-permute-start | bytes 2211848 | tf_op jit(solution)/shard_map/ppermute | solution.py:557
  17.5 8.2 %collective-permute-start.4 = (bf16[3,64,640]{2,1,0:T(8,128)(2,1)S(1)}, bf16[3,64,640]{2,1,0:T(8,128)(2,1)S(1)}, u32[]{:S(2)}, u32[]{:S(2)}) collective-permute-start(bf16[3,64,640]{2,1,0:T(8,128)(2,1)S(1)} %add.5.refs_4_), channel_id=1, source_target_pairs={{0,8},{4,12},{8,0},{12,4},{1,9},{5,13},{9,1},{13,5},{2,10},{6,14},... | collective-permute-start | bytes 737288 | tf_op jit(solution)/shard_map/ppermute | solution.py:75
  19.7 3.1 %collective-permute-start.1 = (bf16[64,256]{1,0:T(8,128)(2,1)S(1)}, bf16[64,256]{1,0:T(8,128)(2,1)S(1)}, u32[]{:S(2)}, u32[]{:S(2)}) collective-permute-start(bf16[64,256]{1,0:T(8,128)(2,1)S(1)} %get-tuple-element.34), channel_id=1, source_target_pairs={{0,4},{4,8},{8,12},{1,5},{5,9},{9,13},{2,6},{6,10},{10,14},{3,7},{... | collective-permute-start | bytes 98312 | tf_op jit(solution)/shard_map/ppermute | solution.py:589
  21.5 3.3 %collective-permute-start.2 = (bf16[64,256]{1,0:T(8,128)(2,1)S(1)}, bf16[64,256]{1,0:T(8,128)(2,1)S(1)}, u32[]{:S(2)}, u32[]{:S(2)}) collective-permute-start(bf16[64,256]{1,0:T(8,128)(2,1)S(1)} %get-tuple-element.36), channel_id=1, source_target_pairs={{4,0},{8,4},{12,8},{5,1},{9,5},{13,9},{6,2},{10,6},{14,10},{7,3},{... | collective-permute-start | bytes 98312 | tf_op jit(solution)/shard_map/ppermute | solution.py:590
  29.3 4.2 %collective-permute-start.5 = (bf16[64,384]{1,0:T(8,128)(2,1)S(1)}, bf16[64,384]{1,0:T(8,128)(2,1)S(1)}, u32[]{:S(2)}, u32[]{:S(2)}) collective-permute-start(bf16[64,384]{1,0:T(8,128)(2,1)S(1)} %get-tuple-element.44.a_ref), channel_id=1, source_target_pairs={{0,1},{1,0},{2,3},{3,2},{4,5},{5,4},{6,7},{7,6},{8,9},{9,8},{10,11... | collective-permute-start | bytes 147464 | tf_op jit(solution)/shard_map/ppermute | solution.py:75
  31.0 28.4 %collective-permute-start.11 = (bf16[1440,128]{1,0:T(8,128)(2,1)S(1)}, bf16[1440,128]{1,0:T(8,128)(2,1)S(1)}, u32[]{:S(2)}, u32[]{:S(2)}) collective-permute-start(bf16[1440,128]{1,0:T(8,128)(2,1)S(1)} %get-tuple-element.52), channel_id=1, source_target_pairs={{0,16},{16,0},{1,17},{17,1},{2,18},{18,2},{3,19},{19,3},{4,20},{20... | collective-permute-start | bytes 1105928 | tf_op jit(solution)/shard_map/ppermute | solution.py:557
  33.5 5.3 %collective-permute-start.6 = (bf16[64,384]{1,0:T(8,128)(2,1)S(1)}, bf16[64,384]{1,0:T(8,128)(2,1)S(1)}, u32[]{:S(2)}, u32[]{:S(2)}) collective-permute-start(bf16[64,384]{1,0:T(8,128)(2,1)S(1)} %add.6.refs_11_), channel_id=1, source_target_pairs={{0,2},{1,3},{2,0},{3,1},{4,6},{5,7},{6,4},{7,5},{8,10},{9,11},{10,... | collective-permute-start | bytes 147464 | tf_op jit(solution)/shard_map/ppermute | solution.py:75
  41.7 1.3 %collective-permute-start.8 = (bf16[320,128]{1,0:T(8,128)(2,1)S(1)}, bf16[320,128]{1,0:T(8,128)(2,1)S(1)}, u32[]{:S(2)}, u32[]{:S(2)}) collective-permute-start(bf16[320,128]{1,0:T(8,128)(2,1)S(1)} %attend_grad.1.a_ref), channel_id=1, source_target_pairs={{0,4},{4,0},{8,12},{12,8},{1,5},{5,1},{9,13},{13,9},{2,6},{6,2},{1... | collective-permute-start | bytes 245768 | tf_op jit(solution)/shard_map/ppermute | solution.py:75
  43.0 9.2 %collective-permute-start.9 = (bf16[320,128]{1,0:T(8,128)(2,1)S(1)}, bf16[320,128]{1,0:T(8,128)(2,1)S(1)}, u32[]{:S(2)}, u32[]{:S(2)}) collective-permute-start(bf16[320,128]{1,0:T(8,128)(2,1)S(1)} %add.7.refs_4_), channel_id=1, source_target_pairs={{0,8},{4,12},{8,0},{12,4},{1,9},{5,13},{9,1},{13,5},{2,10},{6,14},... | collective-permute-start | bytes 245768 | tf_op jit(solution)/shard_map/ppermute | solution.py:75

commit v8 on v7

--- a/solution.py
+++ b/solution.py
@@ -570,7 +570,7 @@
 
     stride = 3 * heads
     unit = pair_rows // 20
-    sizes = (3 * unit, 8 * unit, 6 * unit, 3 * unit)
+    sizes = (3 * unit, 6 * unit, 6 * unit, 4 * unit, unit)
     mom = momentum.reshape(pair_rows * stride, HD)
     w = w_qkv.transpose(1, 0, 2)
     wot = w_out.T
@@ -581,7 +581,7 @@
     received = [exchange(piece)]
     mom, piece = lax.optimization_barrier((mom, piece))
     m, et, w, mom, *pieces = prepare(place, w_embed, mom, w, sizes[1:], stride, sizes[0], unit)
-    received += [exchange(p) for p in pieces]
+    received += [exchange(p) for p in pieces[:-1]]
     m, received[0] = lax.optimization_barrier((m, received[0]))
     ma, mb = butterfly(m, "seq")
 
@@ -613,10 +613,13 @@
         "seq",
     )
 
-    rest = sizes[-1]
-    nm, nw, base = update(place, et, mom, w, received[:-1], sizes[:-1], rest, unit, heads, [za, zb, m, wot])
+    zb, last = lax.optimization_barrier((zb, pieces[-1]))
+    received.append(exchange(last))
+    rest = sizes[-2] + sizes[-1]
+    nm, nw, base = update(place, et, mom, w, received[:-2], sizes[:-2], rest, unit, heads, [za, zb, m, wot])
     first = sum(sizes) - rest
-    nw = finish(place, base, received[-1], nw, first, 0, unit, heads)
+    nw = finish(place, base, received[-2], nw, first, 0, unit, heads)
+    nw = finish(place, base, received[-1], nw, first + sizes[-2], sizes[-2], unit, heads)
     return nm.reshape(momentum.shape), nw.transpose(1, 0, 2)
 
 

time: 61.2 us -> 60.9 us (level)
  waiting for transfers between devices: 19.4 us -> 15.7 us
  starting transfers between devices: 17.4 us -> 19.2 us
  Pallas kernels: 22.6 us -> 24.4 us
    ppermute x4 -> x5, waiting for transfers between devices: 12.4 us -> 5.87 us  [exchange(): return lax.ppermute(x, 'role', [(0, 1), (1, 0)])]
    ppermute x6, waiting for transfers between devices: 5.11 us -> 9.29 us  [swap(): lax.ppermute(x, axis, [(i, i ^ bit) for i in range(lax.axis_size(axis))])]
    pallas_call x1 -> x2, Pallas kernels: 1.65 us -> 3.16 us  [finish(): pl.pallas_call(functools.partial(finish_kernel, heads, unit, first, local...]
    ppermute x1, waiting for transfers between devices: 1.97 us -> 0.49 us  [body(): lax.ppermute(head, 'seq', [(i + 1, i) for i in range(seq_count - 1)])]
    ppermute x6, starting transfers between devices: 7.73 us -> 8.71 us  [swap(): lax.ppermute(x, axis, [(i, i ^ bit) for i in range(lax.axis_size(axis))])]
    ppermute x4 -> x5, starting transfers between devices: 6.56 us -> 7.32 us  [exchange(): return lax.ppermute(x, 'role', [(0, 1), (1, 0)])]
  transfers between devices with their start and end apart: 12 -> 13, of which waited for: 8 -> 8; matrix products, arithmetic and copies ran while one was open for 0% -> 0% of each run, Pallas kernels for 32% -> 36%
where the time goes in v8:
time: 60.9 us; the launch traced here: 60.7 us
  Pallas kernels  24.4 us (40%)
  starting transfers between devices  19.2 us (32%)
  waiting for transfers between devices  15.7 us (26%)
  between operations  1.38 us (2%)
    ppermute x6, waiting for transfers between devices, swap(): lax.ppermute(x, axis, [(i, i ^ bit) for i in range(lax.axis_size(axis))])  9.29 us
    ppermute x6, starting transfers between devices, swap(): lax.ppermute(x, axis, [(i, i ^ bit) for i in range(lax.axis_size(axis))])  8.71 us
    ppermute x5, starting transfers between devices, exchange(): return lax.ppermute(x, 'role', [(0, 1), (1, 0)])  7.32 us
    pallas_call x1, Pallas kernels, update(): pl.pallas_call(functools.partial(update_kernel, heads, unit, sizes), in_s...  6.64 us
    pallas_call x1, Pallas kernels, prepare(): pl.pallas_call(functools.partial(prepare_kernel, sizes, stride, skip, uni...  6.16 us
    ppermute x5, waiting for transfers between devices, exchange(): return lax.ppermute(x, 'role', [(0, 1), (1, 0)])  5.87 us
    pallas_call x1, Pallas kernels, forward(): pl.pallas_call(functools.partial(forward_kernel, tiles, heads, seq_count...  3.63 us
    pallas_call x2, Pallas kernels, finish(): pl.pallas_call(functools.partial(finish_kernel, heads, unit, first, local...  3.16 us
  transfers between devices with their start and end apart: 13, of which 8 were waited for; matrix products, arithmetic and copies ran while one was open for 0% of the time, Pallas kernels for 36%

profile of v8, /device:TPU:0, one launch (start us, length us, event | category | flops | bytes accessed | tf_op | source)
XLA Modules:
  0.0 60.7 jit_solution(4739165960912158502)
XLA Ops:
  0.6 1.3 %lead.1 = bf16[1632,128]{1,0:T(8,128)(2,1)S(1)} custom-call(f32[9600,128]{1,0:T(8,128)} %bitcast.20, bf16[64,384]{1,0:T(8,128)(2,1)} %bitcast.15), custom_call_target="tpu_custom_call" | custom-call | flops 184320 | bytes 1105920 | tf_op jit(solution)/shard_map/lead/pallas_call | solution.py:161
  1.9 3.0 %collective-permute-start = (bf16[1632,128]{1,0:T(8,128)(2,1)S(1)}, bf16[1632,128]{1,0:T(8,128)(2,1)S(1)}, u32[]{:S(2)}, u32[]{:S(2)}) collective-permute-start(bf16[1632,128]{1,0:T(8,128)(2,1)S(1)} %lead.1), channel_id=1, source_target_pairs={{0,16},{16,0},{1,17},{17,1},{2,18},{18,2},{3,19},{19,3},{4,20},{20... | collective-permute-start | bytes 1253384 | tf_op jit(solution)/shard_map/ppermute | solution.py:557
  4.9 0.1 pad_add_fusion.place_ref.refs_0_
  5.0 0.0 copy-start.1
  5.0 0.0 copy-start
  5.0 0.0 copy-start.2
  5.0 0.0 copy-start.3
  5.0 6.2 %prepare.1 = (bf16[3,64,640]{2,1,0:T(8,128)(2,1)S(1)}, bf16[1280,64]{1,0:T(8,128)(2,1)S(1)}, bf16[3,1280,640]{2,1,0:T(8,128)(2,1)S(1)}, f32[9600,128]{1,0:T(8,12...) custom-call(s32[2]{0:T(128)S(1)} %pad_add_fusion.place_ref.refs_0_, ...), custom_call_target="tpu_custom_call" | custom-call | flops 314572800 | bytes 22118400 | tf_op jit(solution)/shard_map/prepare/pallas_call | solution.py:223
  11.2 0.1 collective-permute-start.7
  11.3 4.1 %collective-permute-done.piece_ref.refs_8_ = bf16[1632,128]{1,0:T(8,128)(2,1)S(1)} collective-permute-done((bf16[1632,128]{1,0:T(8,128)(2,1)S(1)}, bf16[1632,128]{1,0:T(8,128)(2,1)S(1)}, u32[]{:S(2)}, u32[]{:S(2)}) %collective-permute-start) | collective-permute-done | bytes 417824 | tf_op jit(solution)/shard_map/ppermute | solution.py:557
  15.4 0.0 collective-permute-start.3
  15.4 2.1 %collective-permute-start.10 = (bf16[2880,128]{1,0:T(8,128)(2,1)S(1)}, bf16[2880,128]{1,0:T(8,128)(2,1)S(1)}, u32[]{:S(2)}, u32[]{:S(2)}) collective-permute-start(bf16[2880,128]{1,0:T(8,128)(2,1)S(1)} %get-tuple-element.54), channel_id=1, source_target_pairs={{0,16},{16,0},{1,17},{17,1},{2,18},{18,2},{3,19},{19,3},{4,20},{20... | collective-permute-start | bytes 2211848 | tf_op jit(solution)/shard_map/ppermute | solution.py:557
  17.5 0.0 collective-permute-done.3.b_ref
  17.5 0.1 add.5.refs_4_
  17.5 1.6 %collective-permute-start.4 = (bf16[3,64,640]{2,1,0:T(8,128)(2,1)S(1)}, bf16[3,64,640]{2,1,0:T(8,128)(2,1)S(1)}, u32[]{:S(2)}, u32[]{:S(2)}) collective-permute-start(bf16[3,64,640]{2,1,0:T(8,128)(2,1)S(1)} %add.5.refs_4_), channel_id=1, source_target_pairs={{0,8},{4,12},{8,0},{12,4},{1,9},{5,13},{9,1},{13,5},{2,10},{6,14},... | collective-permute-start | bytes 737288 | tf_op jit(solution)/shard_map/ppermute | solution.py:75
  19.1 0.0 copy-done.1
  19.1 0.6 pick.1
  19.7 1.8 %collective-permute-start.1 = (bf16[64,256]{1,0:T(8,128)(2,1)S(1)}, bf16[64,256]{1,0:T(8,128)(2,1)S(1)}, u32[]{:S(2)}, u32[]{:S(2)}) collective-permute-start(bf16[64,256]{1,0:T(8,128)(2,1)S(1)} %get-tuple-element.37), channel_id=1, source_target_pairs={{0,4},{4,8},{8,12},{1,5},{5,9},{9,13},{2,6},{6,10},{10,14},{3,7},{... | collective-permute-start | bytes 98312 | tf_op jit(solution)/shard_map/ppermute | solution.py:589
  21.6 1.3 %collective-permute-start.2 = (bf16[64,256]{1,0:T(8,128)(2,1)S(1)}, bf16[64,256]{1,0:T(8,128)(2,1)S(1)}, u32[]{:S(2)}, u32[]{:S(2)}) collective-permute-start(bf16[64,256]{1,0:T(8,128)(2,1)S(1)} %get-tuple-element.39), channel_id=1, source_target_pairs={{4,0},{8,4},{12,8},{5,1},{9,5},{13,9},{6,2},{10,6},{14,10},{7,3},{... | collective-permute-start | bytes 98312 | tf_op jit(solution)/shard_map/ppermute | solution.py:590
  22.9 0.0 collective-permute-done.1.refs_1_
  22.9 1.5 %collective-permute-start.12 = (bf16[1920,128]{1,0:T(8,128)(2,1)S(1)}, bf16[1920,128]{1,0:T(8,128)(2,1)S(1)}, u32[]{:S(2)}, u32[]{:S(2)}) collective-permute-start(bf16[1920,128]{1,0:T(8,128)(2,1)S(1)} %get-tuple-element.58), channel_id=1, source_target_pairs={{0,16},{16,0},{1,17},{17,1},{2,18},{18,2},{3,19},{19,3},{4,20},{20... | collective-permute-start | bytes 1474568 | tf_op jit(solution)/shard_map/ppermute | solution.py:557
  24.3 0.5 collective-permute-done.2.refs_3_
  24.8 0.8 %collective-permute-done.4.refs_5_ = bf16[3,64,640]{2,1,0:T(8,128)(2,1)S(1)} collective-permute-done((bf16[3,64,640]{2,1,0:T(8,128)(2,1)S(1)}, bf16[3,64,640]{2,1,0:T(8,128)(2,1)S(1)}, u32[]{:S(2)}, u32[]{:S(2)}) %collective-permute-start.4) | collective-permute-done | bytes 245792 | tf_op jit(solution)/shard_map/ppermute | solution.py:75
  25.7 0.0 copy-done
  25.7 3.6 %attend.1 = (bf16[3,64,640]{2,1,0:T(8,128)(2,1)S(1)}, bf16[2,640,128]{2,1,0:T(8,128)(2,1)S(1)}, bf16[2,960,640]{2,1,0:T(8,128)(2,1)S(1)}, bf16[1920,128]{1,0:T(8...) custom-call(s32[2]{0:T(128)S(1)} %pad_add_fusion.place_ref.refs_0_, ...), custom_call_target="tpu_custom_call" | custom-call | flops 692060160 | bytes 24576000 | tf_op jit(solution)/shard_map/attend/pallas_call | solution.py:308
  29.3 1.6 %collective-permute-start.5 = (bf16[64,384]{1,0:T(8,128)(2,1)S(1)}, bf16[64,384]{1,0:T(8,128)(2,1)S(1)}, u32[]{:S(2)}, u32[]{:S(2)}) collective-permute-start(bf16[64,384]{1,0:T(8,128)(2,1)S(1)} %get-tuple-element.47.a_ref), channel_id=1, source_target_pairs={{0,1},{1,0},{2,3},{3,2},{4,5},{5,4},{6,7},{7,6},{8,9},{9,8},{10,11... | collective-permute-start | bytes 147464 | tf_op jit(solution)/shard_map/ppermute | solution.py:75
  31.0 2.5 %collective-permute-done.5.b_ref = bf16[64,384]{1,0:T(8,128)(2,1)S(1)} collective-permute-done((bf16[64,384]{1,0:T(8,128)(2,1)S(1)}, bf16[64,384]{1,0:T(8,128)(2,1)S(1)}, u32[]{:S(2)}, u32[]{:S(2)}) %collective-permute-start.5) | collective-permute-done | bytes 49184 | tf_op jit(solution)/shard_map/ppermute | solution.py:75
  33.5 2.7 %collective-permute-start.6 = (bf16[64,384]{1,0:T(8,128)(2,1)S(1)}, bf16[64,384]{1,0:T(8,128)(2,1)S(1)}, u32[]{:S(2)}, u32[]{:S(2)}) collective-permute-start(bf16[64,384]{1,0:T(8,128)(2,1)S(1)} %add.6.refs_11_), channel_id=1, source_target_pairs={{0,2},{1,3},{2,0},{3,1},{4,6},{5,7},{6,4},{7,5},{8,10},{9,11},{10,... | collective-permute-start | bytes 147464 | tf_op jit(solution)/shard_map/ppermute | solution.py:75
  36.8 0.0 collective-permute-done.7.refs_9_
  36.8 2.0 %collective-permute-done.6.refs_12_ = bf16[64,384]{1,0:T(8,128)(2,1)S(1)} collective-permute-done((bf16[64,384]{1,0:T(8,128)(2,1)S(1)}, bf16[64,384]{1,0:T(8,128)(2,1)S(1)}, u32[]{:S(2)}, u32[]{:S(2)}) %collective-permute-start.6) | collective-permute-done | bytes 49184 | tf_op jit(solution)/shard_map/ppermute | solution.py:75
  38.8 0.0 copy-done.2
  38.8 0.0 copy-done.3
  38.8 2.9 %attend_grad.1.a_ref = bf16[320,128]{1,0:T(8,128)(2,1)S(1)} custom-call(s32[1]{0:T(128)S(6)} %copy.16.refs_0_, f32[1,32]{1,0:T(1,128)S(1)} %bitcast.17, s32[1,32]{1,0:T(1,128)S(1)} %bitcast.18, bf16[2,640,128]{2,1,0:T(8,128)(2,1)S(1)} %get-tuple-element.41.refs_3_, bf16[3,64,640]{2,1,0:T(8,128)(2,1)S(1)} %get-tuple-element.42.refs_4_.refs_6_, ...), custom_call_target="tpu_custom_call" | custom-call | flops 692060160 | bytes 24576000 | tf_op jit(solution)/shard_map/attend_grad/pallas_call | solution.py:386
  41.7 0.2 collective-permute-start.8
  41.9 1.2 %collective-permute-done.8.b_ref = bf16[320,128]{1,0:T(8,128)(2,1)S(1)} collective-permute-done((bf16[320,128]{1,0:T(8,128)(2,1)S(1)}, bf16[320,128]{1,0:T(8,128)(2,1)S(1)}, u32[]{:S(2)}, u32[]{:S(2)}) %collective-permute-start.8) | collective-permute-done | bytes 81952 | tf_op jit(solution)/shard_map/ppermute | solution.py:75
  43.1 2.6 %collective-permute-start.9 = (bf16[320,128]{1,0:T(8,128)(2,1)S(1)}, bf16[320,128]{1,0:T(8,128)(2,1)S(1)}, u32[]{:S(2)}, u32[]{:S(2)}) collective-permute-start(bf16[320,128]{1,0:T(8,128)(2,1)S(1)} %add.7.refs_4_), channel_id=1, source_target_pairs={{0,8},{4,12},{8,0},{12,4},{1,9},{5,13},{9,1},{13,5},{2,10},{6,14},... | collective-permute-start | bytes 245768 | tf_op jit(solution)/shard_map/ppermute | solution.py:75
  45.7 2.8 %collective-permute-done.9.refs_5_ = bf16[320,128]{1,0:T(8,128)(2,1)S(1)} collective-permute-done((bf16[320,128]{1,0:T(8,128)(2,1)S(1)}, bf16[320,128]{1,0:T(8,128)(2,1)S(1)}, u32[]{:S(2)}, u32[]{:S(2)}) %collective-permute-start.9) | collective-permute-done | bytes 81952 | tf_op jit(solution)/shard_map/ppermute | solution.py:75
  48.5 0.7 %collective-permute-start.11 = (bf16[480,128]{1,0:T(8,128)(2,1)S(1)}, bf16[480,128]{1,0:T(8,128)(2,1)S(1)}, u32[]{:S(2)}, u32[]{:S(2)}) collective-permute-start(bf16[480,128]{1,0:T(8,128)(2,1)S(1)} %get-tuple-element.57), channel_id=1, source_target_pairs={{0,16},{16,0},{1,17},{17,1},{2,18},{18,2},{3,19},{19,3},{4,20},{20... | collective-permute-start | bytes 368648 | tf_op jit(solution)/shard_map/ppermute | solution.py:557
  49.2 0.0 collective-permute-done.10.refs_10_
  49.2 6.6 %update.1 = (f32[9600,128]{1,0:T(8,128)}, bf16[3,1280,640]{2,1,0:T(8,128)(2,1)}, f32[15,320,128]{2,1,0:T(8,128)S(1)}) custom-call(s32[2]{0:T(128)S(1)} %pad_add_fusion.place_ref.refs_0_, bf16[1280,64]{1,0:T(8,128)(2,1)S(1)} %get-tuple-element.32.refs_1_, f32[9600,128]{1,0:T(8,128)S(1)} %get-tuple-element.33.refs_2_, ...), custom_call_target="tpu_custom_call" | custom-call | flops 629145600 | bytes 27033600 | tf_op jit(solution)/shard_map/update/pallas_call | solution.py:488
  55.8 1.7 %collective-permute-done.12.recv_ref = bf16[1920,128]{1,0:T(8,128)(2,1)S(1)} collective-permute-done((bf16[1920,128]{1,0:T(8,128)(2,1)S(1)}, bf16[1920,128]{1,0:T(8,128)(2,1)S(1)}, u32[]{:S(2)}, u32[]{:S(2)}) %collective-permute-start.12) | collective-permute-done | bytes 491552 | tf_op jit(solution)/shard_map/ppermute | solution.py:557
  57.5 1.8 %finish.2.old_hbm = bf16[3,1280,640]{2,1,0:T(8,128)(2,1)} custom-call(s32[2]{0:T(128)S(1)} %pad_add_fusion.place_ref.refs_0_, f32[15,320,128]{2,1,0:T(8,128)S(1)} %get-tuple-element.56.base_ref, bf16[1920,128]{1,0:T(8,128)(2,1)S(1)} %collective-permute-done.12.recv_ref, bf16[3,1280,640]{2,1,0:T(8,128)(2,1)} %get-tuple-element.59.old_hbm), custom_call_target="tpu_custom_call", output_to_operand_aliasing={{}: (3, {})} | custom-call | flops 491520 | bytes 3440640 | tf_op jit(solution)/shard_map/finish/pallas_call | solution.py:539
  59.3 0.0 collective-permute-done.11.recv_ref
  59.3 1.4 %finish.3 = bf16[3,1280,640]{2,1,0:T(8,128)(2,1)} custom-call(s32[2]{0:T(128)S(1)} %pad_add_fusion.place_ref.refs_0_, f32[15,320,128]{2,1,0:T(8,128)S(1)} %get-tuple-element.56.base_ref, bf16[480,128]{1,0:T(8,128)(2,1)S(1)} %collective-permute-done.11.recv_ref, bf16[3,1280,640]{2,1,0:T(8,128)(2,1)} %finish.2.old_hbm), custom_call_target="tpu_custom_call", output_to_operand_aliasing={{}: (3, {})} | custom-call | flops 122880 | bytes 860160 | tf_op jit(solution)/shard_map/finish/pallas_call | solution.py:539
  (2 shorter events, 0.0 us)
Async XLA Ops:
  1.9 13.5 %collective-permute-start = (bf16[1632,128]{1,0:T(8,128)(2,1)S(1)}, bf16[1632,128]{1,0:T(8,128)(2,1)S(1)}, u32[]{:S(2)}, u32[]{:S(2)}) collective-permute-start(bf16[1632,128]{1,0:T(8,128)(2,1)S(1)} %lead.1), channel_id=1, source_target_pairs={{0,16},{16,0},{1,17},{17,1},{2,18},{18,2},{3,19},{19,3},{4,20},{20... | collective-permute-start | bytes 1253384 | tf_op jit(solution)/shard_map/ppermute | solution.py:557
  5.0 14.1 %copy-start.1 = (bf16[1,384,64]{1,2,0:T(8,128)(2,1)S(1)}, bf16[1,384,64]{1,2,0:T(8,128)(2,1)}, u32[]{:S(2)}) copy-start(bf16[1,384,64]{1,2,0:T(8,128)(2,1)} %param.8) | copy-start | bytes 147460
  5.0 20.7 %copy-start = (bf16[640,64]{0,1:T(8,128)(2,1)S(1)}, bf16[640,64]{0,1:T(8,128)(2,1)}, u32[]{:S(2)}) copy-start(bf16[640,64]{0,1:T(8,128)(2,1)} %param.11) | copy-start | bytes 245764
  5.0 33.8 %copy-start.2 = (f32[32]{0:T(128)S(1)}, f32[32]{0:T(128)}, u32[]{:S(2)}) copy-start(f32[32]{0:T(128)} %param.13) | copy-start | bytes 388
  5.0 33.8 %copy-start.3 = (s32[32]{0:T(128)S(1)}, s32[32]{0:T(128)}, u32[]{:S(2)}) copy-start(s32[32]{0:T(128)} %param.14) | copy-start | bytes 388
  11.2 25.6 %collective-permute-start.7 = (bf16[2880,128]{1,0:T(8,128)(2,1)S(1)}, bf16[2880,128]{1,0:T(8,128)(2,1)S(1)}, u32[]{:S(2)}, u32[]{:S(2)}) collective-permute-start(bf16[2880,128]{1,0:T(8,128)(2,1)S(1)} %get-tuple-element.48), channel_id=1, source_target_pairs={{0,16},{16,0},{1,17},{17,1},{2,18},{18,2},{3,19},{19,3},{4,20},{20... | collective-permute-start | bytes 2211848 | tf_op jit(solution)/shard_map/ppermute | solution.py:557
  15.4 2.1 %collective-permute-start.3 = (bf16[3,64,640]{2,1,0:T(8,128)(2,1)S(1)}, bf16[3,64,640]{2,1,0:T(8,128)(2,1)S(1)}, u32[]{:S(2)}, u32[]{:S(2)}) collective-permute-start(bf16[3,64,640]{2,1,0:T(8,128)(2,1)S(1)} %get-tuple-element.40.a_ref), channel_id=1, source_target_pairs={{0,4},{4,0},{8,12},{12,8},{1,5},{5,1},{9,13},{13,9},{2,6},{6,2},{1... | collective-permute-start | bytes 737288 | tf_op jit(solution)/shard_map/ppermute | solution.py:75
  15.4 33.8 %collective-permute-start.10 = (bf16[2880,128]{1,0:T(8,128)(2,1)S(1)}, bf16[2880,128]{1,0:T(8,128)(2,1)S(1)}, u32[]{:S(2)}, u32[]{:S(2)}) collective-permute-start(bf16[2880,128]{1,0:T(8,128)(2,1)S(1)} %get-tuple-element.54), channel_id=1, source_target_pairs={{0,16},{16,0},{1,17},{17,1},{2,18},{18,2},{3,19},{19,3},{4,20},{20... | collective-permute-start | bytes 2211848 | tf_op jit(solution)/shard_map/ppermute | solution.py:557
  17.5 8.2 %collective-permute-start.4 = (bf16[3,64,640]{2,1,0:T(8,128)(2,1)S(1)}, bf16[3,64,640]{2,1,0:T(8,128)(2,1)S(1)}, u32[]{:S(2)}, u32[]{:S(2)}) collective-permute-start(bf16[3,64,640]{2,1,0:T(8,128)(2,1)S(1)} %add.5.refs_4_), channel_id=1, source_target_pairs={{0,8},{4,12},{8,0},{12,4},{1,9},{5,13},{9,1},{13,5},{2,10},{6,14},... | collective-permute-start | bytes 737288 | tf_op jit(solution)/shard_map/ppermute | solution.py:75
  19.7 3.1 %collective-permute-start.1 = (bf16[64,256]{1,0:T(8,128)(2,1)S(1)}, bf16[64,256]{1,0:T(8,128)(2,1)S(1)}, u32[]{:S(2)}, u32[]{:S(2)}) collective-permute-start(bf16[64,256]{1,0:T(8,128)(2,1)S(1)} %get-tuple-element.37), channel_id=1, source_target_pairs={{0,4},{4,8},{8,12},{1,5},{5,9},{9,13},{2,6},{6,10},{10,14},{3,7},{... | collective-permute-start | bytes 98312 | tf_op jit(solution)/shard_map/ppermute | solution.py:589
  21.6 3.3 %collective-permute-start.2 = (bf16[64,256]{1,0:T(8,128)(2,1)S(1)}, bf16[64,256]{1,0:T(8,128)(2,1)S(1)}, u32[]{:S(2)}, u32[]{:S(2)}) collective-permute-start(bf16[64,256]{1,0:T(8,128)(2,1)S(1)} %get-tuple-element.39), channel_id=1, source_target_pairs={{4,0},{8,4},{12,8},{5,1},{9,5},{13,9},{6,2},{10,6},{14,10},{7,3},{... | collective-permute-start | bytes 98312 | tf_op jit(solution)/shard_map/ppermute | solution.py:590
  22.9 34.7 %collective-permute-start.12 = (bf16[1920,128]{1,0:T(8,128)(2,1)S(1)}, bf16[1920,128]{1,0:T(8,128)(2,1)S(1)}, u32[]{:S(2)}, u32[]{:S(2)}) collective-permute-start(bf16[1920,128]{1,0:T(8,128)(2,1)S(1)} %get-tuple-element.58), channel_id=1, source_target_pairs={{0,16},{16,0},{1,17},{17,1},{2,18},{18,2},{3,19},{19,3},{4,20},{20... | collective-permute-start | bytes 1474568 | tf_op jit(solution)/shard_map/ppermute | solution.py:557
  29.3 4.2 %collective-permute-start.5 = (bf16[64,384]{1,0:T(8,128)(2,1)S(1)}, bf16[64,384]{1,0:T(8,128)(2,1)S(1)}, u32[]{:S(2)}, u32[]{:S(2)}) collective-permute-start(bf16[64,384]{1,0:T(8,128)(2,1)S(1)} %get-tuple-element.47.a_ref), channel_id=1, source_target_pairs={{0,1},{1,0},{2,3},{3,2},{4,5},{5,4},{6,7},{7,6},{8,9},{9,8},{10,11... | collective-permute-start | bytes 147464 | tf_op jit(solution)/shard_map/ppermute | solution.py:75
  33.5 5.3 %collective-permute-start.6 = (bf16[64,384]{1,0:T(8,128)(2,1)S(1)}, bf16[64,384]{1,0:T(8,128)(2,1)S(1)}, u32[]{:S(2)}, u32[]{:S(2)}) collective-permute-start(bf16[64,384]{1,0:T(8,128)(2,1)S(1)} %add.6.refs_11_), channel_id=1, source_target_pairs={{0,2},{1,3},{2,0},{3,1},{4,6},{5,7},{6,4},{7,5},{8,10},{9,11},{10,... | collective-permute-start | bytes 147464 | tf_op jit(solution)/shard_map/ppermute | solution.py:75
  41.7 1.3 %collective-permute-start.8 = (bf16[320,128]{1,0:T(8,128)(2,1)S(1)}, bf16[320,128]{1,0:T(8,128)(2,1)S(1)}, u32[]{:S(2)}, u32[]{:S(2)}) collective-permute-start(bf16[320,128]{1,0:T(8,128)(2,1)S(1)} %attend_grad.1.a_ref), channel_id=1, source_target_pairs={{0,4},{4,0},{8,12},{12,8},{1,5},{5,1},{9,13},{13,9},{2,6},{6,2},{1... | collective-permute-start | bytes 245768 | tf_op jit(solution)/shard_map/ppermute | solution.py:75
  43.1 5.4 %collective-permute-start.9 = (bf16[320,128]{1,0:T(8,128)(2,1)S(1)}, bf16[320,128]{1,0:T(8,128)(2,1)S(1)}, u32[]{:S(2)}, u32[]{:S(2)}) collective-permute-start(bf16[320,128]{1,0:T(8,128)(2,1)S(1)} %add.7.refs_4_), channel_id=1, source_target_pairs={{0,8},{4,12},{8,0},{12,4},{1,9},{5,13},{9,1},{13,5},{2,10},{6,14},... | collective-permute-start | bytes 245768 | tf_op jit(solution)/shard_map/ppermute | solution.py:75
  48.5 10.9 %collective-permute-start.11 = (bf16[480,128]{1,0:T(8,128)(2,1)S(1)}, bf16[480,128]{1,0:T(8,128)(2,1)S(1)}, u32[]{:S(2)}, u32[]{:S(2)}) collective-permute-start(bf16[480,128]{1,0:T(8,128)(2,1)S(1)} %get-tuple-element.57), channel_id=1, source_target_pairs={{0,16},{16,0},{1,17},{17,1},{2,18},{18,2},{3,19},{19,3},{4,20},{20... | collective-permute-start | bytes 368648 | tf_op jit(solution)/shard_map/ppermute | solution.py:557

commit v9 on v8

--- a/solution.py
+++ b/solution.py
@@ -524,10 +524,11 @@
             fs_ref[q, pl.ds(1 - role, count, stride=2), :] = recv_ref[row : row + count, :].astype(F32)
             new = base_ref[q, 2 * local + at : 2 * local + at + 2 * count, :] - LEARNING_RATE * fs_ref[q]
             ow_ref[part, at : at + 2 * count, b * HD : (b + 1) * HD] = new.astype(BF16)
-        source = ow_ref.at[:, pl.ds(at, 2 * count)]
-        target = ow_hbm.at[:, pl.ds(2 * first + at, 2 * count)]
-        copies.append(pltpu.make_async_copy(source, target, sems.at[step]))
-        copies[-1].start()
+            if b == heads - 1:
+                source = ow_ref.at[part, pl.ds(at, 2 * count)]
+                target = ow_hbm.at[part, pl.ds(2 * first + at, 2 * count)]
+                copies.append(pltpu.make_async_copy(source, target, sems.at[3 * step + part]))
+                copies[-1].start()
     for copy in copies:
         copy.wait()
 
@@ -545,7 +546,7 @@
         scratch_shapes=[
             pltpu.VMEM((stride, 2 * count, HD), F32),
             pltpu.VMEM((3, 2 * size, heads * HD), BF16),
-            pltpu.SemaphoreType.DMA((size // count,)),
+            pltpu.SemaphoreType.DMA((3 * size // count,)),
         ],
         compiler_params=params(4),
         cost_estimate=cost(2 * recv.size, 14 * recv.size),
@@ -591,7 +592,8 @@
 
     m, win, e, u, il, partial_pred = forward(place, left, latent_now, right, ma, mb, wot, tiles, heads, seq_count)
     preds = list(butterfly(partial_pred, "mp"))
-    preds, received[1] = lax.optimization_barrier((preds, received[1]))
+    preds, received[1], last = lax.optimization_barrier((preds, received[1], pieces[-1]))
+    received.append(exchange(last))
     za, zb = butterfly(
         backward(
             timestep,
@@ -613,8 +615,6 @@
         "seq",
     )
 
-    zb, last = lax.optimization_barrier((zb, pieces[-1]))
-    received.append(exchange(last))
     rest = sizes[-2] + sizes[-1]
     nm, nw, base = update(place, et, mom, w, received[:-2], sizes[:-2], rest, unit, heads, [za, zb, m, wot])
     first = sum(sizes) - rest

time: 60.9 us -> 60.9 us (level)
  starting transfers between devices: 19.2 us -> 20.7 us
  waiting for transfers between devices: 15.7 us -> 14.2 us
    ppermute x6, waiting for transfers between devices: 9.29 us -> 6.61 us  [swap(): lax.ppermute(x, axis, [(i, i ^ bit) for i in range(lax.axis_size(axis))])]
    ppermute x1, waiting for transfers between devices: 0.49 us -> 3.09 us  [body(): lax.ppermute(head, 'seq', [(i + 1, i) for i in range(seq_count - 1)])]
    ppermute x5, waiting for transfers between devices: 5.87 us -> 4.49 us  [exchange(): return lax.ppermute(x, 'role', [(0, 1), (1, 0)])]
    ppermute x6, starting transfers between devices: 8.71 us -> 9.63 us  [swap(): lax.ppermute(x, axis, [(i, i ^ bit) for i in range(lax.axis_size(axis))])]
    ppermute x5, starting transfers between devices: 7.32 us -> 7.96 us  [exchange(): return lax.ppermute(x, 'role', [(0, 1), (1, 0)])]
where the time goes in v9:
time: 60.9 us; the launch traced here: 60.7 us
  Pallas kernels  24.3 us (40%)
  starting transfers between devices  20.7 us (34%)
  waiting for transfers between devices  14.2 us (23%)
  between operations  1.38 us (2%)
    ppermute x6, starting transfers between devices, swap(): lax.ppermute(x, axis, [(i, i ^ bit) for i in range(lax.axis_size(axis))])  9.63 us
    ppermute x5, starting transfers between devices, exchange(): return lax.ppermute(x, 'role', [(0, 1), (1, 0)])  7.96 us
    pallas_call x1, Pallas kernels, update(): pl.pallas_call(functools.partial(update_kernel, heads, unit, sizes), in_s...  6.64 us
    ppermute x6, waiting for transfers between devices, swap(): lax.ppermute(x, axis, [(i, i ^ bit) for i in range(lax.axis_size(axis))])  6.61 us
    pallas_call x1, Pallas kernels, prepare(): pl.pallas_call(functools.partial(prepare_kernel, sizes, stride, skip, uni...  6.16 us
    ppermute x5, waiting for transfers between devices, exchange(): return lax.ppermute(x, 'role', [(0, 1), (1, 0)])  4.49 us
    pallas_call x1, Pallas kernels, forward(): pl.pallas_call(functools.partial(forward_kernel, tiles, heads, seq_count...  3.63 us
    ppermute x1, waiting for transfers between devices, body(): lax.ppermute(head, 'seq', [(i + 1, i) for i in range(seq_count - 1)])  3.09 us
  transfers between devices with their start and end apart: 13, of which 8 were waited for; matrix products, arithmetic and copies ran while one was open for 0% of the time, Pallas kernels for 36%

profile of v9, /device:TPU:0, one launch (start us, length us, event | category | flops | bytes accessed | tf_op | source)
XLA Modules:
  0.0 60.7 jit_solution(15332164378749057011)
XLA Ops:
  0.6 1.3 %lead.1 = bf16[1632,128]{1,0:T(8,128)(2,1)S(1)} custom-call(f32[9600,128]{1,0:T(8,128)} %bitcast.20, bf16[64,384]{1,0:T(8,128)(2,1)} %bitcast.15), custom_call_target="tpu_custom_call" | custom-call | flops 184320 | bytes 1105920 | tf_op jit(solution)/shard_map/lead/pallas_call | solution.py:161
  1.9 3.0 %collective-permute-start = (bf16[1632,128]{1,0:T(8,128)(2,1)S(1)}, bf16[1632,128]{1,0:T(8,128)(2,1)S(1)}, u32[]{:S(2)}, u32[]{:S(2)}) collective-permute-start(bf16[1632,128]{1,0:T(8,128)(2,1)S(1)} %lead.1), channel_id=1, source_target_pairs={{0,16},{16,0},{1,17},{17,1},{2,18},{18,2},{3,19},{19,3},{4,20},{20... | collective-permute-start | bytes 1253384 | tf_op jit(solution)/shard_map/ppermute | solution.py:558
  4.9 0.1 pad_add_fusion.place_ref.refs_0_
  5.0 0.0 copy-start.1
  5.0 0.0 copy-start
  5.0 0.0 copy-start.2
  5.0 0.0 copy-start.3
  5.0 6.2 %prepare.1 = (bf16[3,64,640]{2,1,0:T(8,128)(2,1)S(1)}, bf16[1280,64]{1,0:T(8,128)(2,1)S(1)}, bf16[3,1280,640]{2,1,0:T(8,128)(2,1)S(1)}, f32[9600,128]{1,0:T(8,12...) custom-call(s32[2]{0:T(128)S(1)} %pad_add_fusion.place_ref.refs_0_, ...), custom_call_target="tpu_custom_call" | custom-call | flops 314572800 | bytes 22118400 | tf_op jit(solution)/shard_map/prepare/pallas_call | solution.py:223
  11.2 0.1 collective-permute-start.7
  11.3 4.1 %collective-permute-done.piece_ref.refs_8_ = bf16[1632,128]{1,0:T(8,128)(2,1)S(1)} collective-permute-done((bf16[1632,128]{1,0:T(8,128)(2,1)S(1)}, bf16[1632,128]{1,0:T(8,128)(2,1)S(1)}, u32[]{:S(2)}, u32[]{:S(2)}) %collective-permute-start) | collective-permute-done | bytes 417824 | tf_op jit(solution)/shard_map/ppermute | solution.py:558
  15.4 0.0 collective-permute-start.3
  15.4 2.1 %collective-permute-start.10 = (bf16[2880,128]{1,0:T(8,128)(2,1)S(1)}, bf16[2880,128]{1,0:T(8,128)(2,1)S(1)}, u32[]{:S(2)}, u32[]{:S(2)}) collective-permute-start(bf16[2880,128]{1,0:T(8,128)(2,1)S(1)} %get-tuple-element.52), channel_id=1, source_target_pairs={{0,16},{16,0},{1,17},{17,1},{2,18},{18,2},{3,19},{19,3},{4,20},{20... | collective-permute-start | bytes 2211848 | tf_op jit(solution)/shard_map/ppermute | solution.py:558
  17.5 0.0 collective-permute-done.3.b_ref
  17.5 0.1 add.5.refs_4_
  17.5 1.6 %collective-permute-start.4 = (bf16[3,64,640]{2,1,0:T(8,128)(2,1)S(1)}, bf16[3,64,640]{2,1,0:T(8,128)(2,1)S(1)}, u32[]{:S(2)}, u32[]{:S(2)}) collective-permute-start(bf16[3,64,640]{2,1,0:T(8,128)(2,1)S(1)} %add.5.refs_4_), channel_id=1, source_target_pairs={{0,8},{4,12},{8,0},{12,4},{1,9},{5,13},{9,1},{13,5},{2,10},{6,14},... | collective-permute-start | bytes 737288 | tf_op jit(solution)/shard_map/ppermute | solution.py:75
  19.1 0.0 copy-done.1
  19.1 0.6 pick.1
  19.7 1.8 %collective-permute-start.1 = (bf16[64,256]{1,0:T(8,128)(2,1)S(1)}, bf16[64,256]{1,0:T(8,128)(2,1)S(1)}, u32[]{:S(2)}, u32[]{:S(2)}) collective-permute-start(bf16[64,256]{1,0:T(8,128)(2,1)S(1)} %get-tuple-element.36), channel_id=1, source_target_pairs={{0,4},{4,8},{8,12},{1,5},{5,9},{9,13},{2,6},{6,10},{10,14},{3,7},{... | collective-permute-start | bytes 98312 | tf_op jit(solution)/shard_map/ppermute | solution.py:590
  21.6 1.5 %collective-permute-start.12 = (bf16[1920,128]{1,0:T(8,128)(2,1)S(1)}, bf16[1920,128]{1,0:T(8,128)(2,1)S(1)}, u32[]{:S(2)}, u32[]{:S(2)}) collective-permute-start(bf16[1920,128]{1,0:T(8,128)(2,1)S(1)} %get-tuple-element.56), channel_id=1, source_target_pairs={{0,16},{16,0},{1,17},{17,1},{2,18},{18,2},{3,19},{19,3},{4,20},{20... | collective-permute-start | bytes 1474568 | tf_op jit(solution)/shard_map/ppermute | solution.py:558
  23.0 0.0 collective-permute-done.1.refs_1_
  23.0 1.3 %collective-permute-start.2 = (bf16[64,256]{1,0:T(8,128)(2,1)S(1)}, bf16[64,256]{1,0:T(8,128)(2,1)S(1)}, u32[]{:S(2)}, u32[]{:S(2)}) collective-permute-start(bf16[64,256]{1,0:T(8,128)(2,1)S(1)} %get-tuple-element.38), channel_id=1, source_target_pairs={{4,0},{8,4},{12,8},{5,1},{9,5},{13,9},{6,2},{10,6},{14,10},{7,3},{... | collective-permute-start | bytes 98312 | tf_op jit(solution)/shard_map/ppermute | solution.py:591
  24.3 3.1 %collective-permute-done.2.refs_3_ = bf16[64,256]{1,0:T(8,128)(2,1)S(1)} collective-permute-done((bf16[64,256]{1,0:T(8,128)(2,1)S(1)}, bf16[64,256]{1,0:T(8,128)(2,1)S(1)}, u32[]{:S(2)}, u32[]{:S(2)}) %collective-permute-start.2) | collective-permute-done | bytes 32800 | tf_op jit(solution)/shard_map/ppermute | solution.py:591
  27.4 0.0 collective-permute-done.4.refs_5_
  27.4 0.0 copy-done
  27.4 3.6 %attend.1 = (bf16[3,64,640]{2,1,0:T(8,128)(2,1)S(1)}, bf16[2,640,128]{2,1,0:T(8,128)(2,1)S(1)}, bf16[2,960,640]{2,1,0:T(8,128)(2,1)S(1)}, bf16[1920,128]{1,0:T(8...) custom-call(s32[2]{0:T(128)S(1)} %pad_add_fusion.place_ref.refs_0_, ...), custom_call_target="tpu_custom_call" | custom-call | flops 692060160 | bytes 24576000 | tf_op jit(solution)/shard_map/attend/pallas_call | solution.py:308
  31.1 1.6 %collective-permute-start.5 = (bf16[64,384]{1,0:T(8,128)(2,1)S(1)}, bf16[64,384]{1,0:T(8,128)(2,1)S(1)}, u32[]{:S(2)}, u32[]{:S(2)}) collective-permute-start(bf16[64,384]{1,0:T(8,128)(2,1)S(1)} %get-tuple-element.46.a_ref), channel_id=1, source_target_pairs={{0,1},{1,0},{2,3},{3,2},{4,5},{5,4},{6,7},{7,6},{8,9},{9,8},{10,11... | collective-permute-start | bytes 147464 | tf_op jit(solution)/shard_map/ppermute | solution.py:75
  32.7 2.5 %collective-permute-done.5.b_ref = bf16[64,384]{1,0:T(8,128)(2,1)S(1)} collective-permute-done((bf16[64,384]{1,0:T(8,128)(2,1)S(1)}, bf16[64,384]{1,0:T(8,128)(2,1)S(1)}, u32[]{:S(2)}, u32[]{:S(2)}) %collective-permute-start.5) | collective-permute-done | bytes 49184 | tf_op jit(solution)/shard_map/ppermute | solution.py:75
  35.2 2.7 %collective-permute-start.6 = (bf16[64,384]{1,0:T(8,128)(2,1)S(1)}, bf16[64,384]{1,0:T(8,128)(2,1)S(1)}, u32[]{:S(2)}, u32[]{:S(2)}) collective-permute-start(bf16[64,384]{1,0:T(8,128)(2,1)S(1)} %add.6.refs_11_), channel_id=1, source_target_pairs={{0,2},{1,3},{2,0},{3,1},{4,6},{5,7},{6,4},{7,5},{8,10},{9,11},{10,... | collective-permute-start | bytes 147464 | tf_op jit(solution)/shard_map/ppermute | solution.py:75
  38.5 0.0 collective-permute-done.7.refs_9_
  38.6 1.7 %collective-permute-done.6.refs_12_ = bf16[64,384]{1,0:T(8,128)(2,1)S(1)} collective-permute-done((bf16[64,384]{1,0:T(8,128)(2,1)S(1)}, bf16[64,384]{1,0:T(8,128)(2,1)S(1)}, u32[]{:S(2)}, u32[]{:S(2)}) %collective-permute-start.6) | collective-permute-done | bytes 49184 | tf_op jit(solution)/shard_map/ppermute | solution.py:75
  40.3 0.0 copy-done.2
  40.3 0.0 copy-done.3
  40.3 2.9 %attend_grad.1.a_ref = bf16[320,128]{1,0:T(8,128)(2,1)S(1)} custom-call(s32[1]{0:T(128)S(6)} %copy.16.refs_0_, f32[1,32]{1,0:T(1,128)S(1)} %bitcast.17, s32[1,32]{1,0:T(1,128)S(1)} %bitcast.18, bf16[2,640,128]{2,1,0:T(8,128)(2,1)S(1)} %get-tuple-element.40.refs_3_, bf16[3,64,640]{2,1,0:T(8,128)(2,1)S(1)} %get-tuple-element.41.refs_4_.refs_6_, ...), custom_call_target="tpu_custom_call" | custom-call | flops 692060160 | bytes 24576000 | tf_op jit(solution)/shard_map/attend_grad/pallas_call | solution.py:386
  43.2 1.7 %collective-permute-start.8 = (bf16[320,128]{1,0:T(8,128)(2,1)S(1)}, bf16[320,128]{1,0:T(8,128)(2,1)S(1)}, u32[]{:S(2)}, u32[]{:S(2)}) collective-permute-start(bf16[320,128]{1,0:T(8,128)(2,1)S(1)} %attend_grad.1.a_ref), channel_id=1, source_target_pairs={{0,4},{4,0},{8,12},{12,8},{1,5},{5,1},{9,13},{13,9},{2,6},{6,2},{1... | collective-permute-start | bytes 245768 | tf_op jit(solution)/shard_map/ppermute | solution.py:75
  44.9 0.9 %collective-permute-done.8.b_ref = bf16[320,128]{1,0:T(8,128)(2,1)S(1)} collective-permute-done((bf16[320,128]{1,0:T(8,128)(2,1)S(1)}, bf16[320,128]{1,0:T(8,128)(2,1)S(1)}, u32[]{:S(2)}, u32[]{:S(2)}) %collective-permute-start.8) | collective-permute-done | bytes 81952 | tf_op jit(solution)/shard_map/ppermute | solution.py:75
  45.8 2.0 %collective-permute-start.9 = (bf16[320,128]{1,0:T(8,128)(2,1)S(1)}, bf16[320,128]{1,0:T(8,128)(2,1)S(1)}, u32[]{:S(2)}, u32[]{:S(2)}) collective-permute-start(bf16[320,128]{1,0:T(8,128)(2,1)S(1)} %add.7.refs_4_), channel_id=1, source_target_pairs={{0,8},{4,12},{8,0},{12,4},{1,9},{5,13},{9,1},{13,5},{2,10},{6,14},... | collective-permute-start | bytes 245768 | tf_op jit(solution)/shard_map/ppermute | solution.py:75
  47.9 1.3 %collective-permute-start.11 = (bf16[480,128]{1,0:T(8,128)(2,1)S(1)}, bf16[480,128]{1,0:T(8,128)(2,1)S(1)}, u32[]{:S(2)}, u32[]{:S(2)}) collective-permute-start(bf16[480,128]{1,0:T(8,128)(2,1)S(1)} %get-tuple-element.55), channel_id=1, source_target_pairs={{0,16},{16,0},{1,17},{17,1},{2,18},{18,2},{3,19},{19,3},{4,20},{20... | collective-permute-start | bytes 368648 | tf_op jit(solution)/shard_map/ppermute | solution.py:558
  49.2 0.0 collective-permute-done.10.refs_10_
  49.2 1.4 %collective-permute-done.9.refs_5_ = bf16[320,128]{1,0:T(8,128)(2,1)S(1)} collective-permute-done((bf16[320,128]{1,0:T(8,128)(2,1)S(1)}, bf16[320,128]{1,0:T(8,128)(2,1)S(1)}, u32[]{:S(2)}, u32[]{:S(2)}) %collective-permute-start.9) | collective-permute-done | bytes 81952 | tf_op jit(solution)/shard_map/ppermute | solution.py:75
  50.6 6.6 %update.1 = (f32[9600,128]{1,0:T(8,128)}, bf16[3,1280,640]{2,1,0:T(8,128)(2,1)}, f32[15,320,128]{2,1,0:T(8,128)S(1)}) custom-call(s32[2]{0:T(128)S(1)} %pad_add_fusion.place_ref.refs_0_, bf16[1280,64]{1,0:T(8,128)(2,1)S(1)} %get-tuple-element.31.refs_1_, f32[9600,128]{1,0:T(8,128)S(1)} %get-tuple-element.32.refs_2_, ...), custom_call_target="tpu_custom_call" | custom-call | flops 629145600 | bytes 27033600 | tf_op jit(solution)/shard_map/update/pallas_call | solution.py:488
  57.3 0.3 collective-permute-done.12.recv_ref
  57.5 1.7 %finish.2.old_hbm = bf16[3,1280,640]{2,1,0:T(8,128)(2,1)} custom-call(s32[2]{0:T(128)S(1)} %pad_add_fusion.place_ref.refs_0_, f32[15,320,128]{2,1,0:T(8,128)S(1)} %get-tuple-element.54.base_ref, bf16[1920,128]{1,0:T(8,128)(2,1)S(1)} %collective-permute-done.12.recv_ref, bf16[3,1280,640]{2,1,0:T(8,128)(2,1)} %get-tuple-element.57.old_hbm), custom_call_target="tpu_custom_call", output_to_operand_aliasing={{}: (3, {})} | custom-call | flops 491520 | bytes 3440640 | tf_op jit(solution)/shard_map/finish/pallas_call | solution.py:540
  59.2 0.1 collective-permute-done.11.recv_ref
  59.3 1.3 %finish.3 = bf16[3,1280,640]{2,1,0:T(8,128)(2,1)} custom-call(s32[2]{0:T(128)S(1)} %pad_add_fusion.place_ref.refs_0_, f32[15,320,128]{2,1,0:T(8,128)S(1)} %get-tuple-element.54.base_ref, bf16[480,128]{1,0:T(8,128)(2,1)S(1)} %collective-permute-done.11.recv_ref, bf16[3,1280,640]{2,1,0:T(8,128)(2,1)} %finish.2.old_hbm), custom_call_target="tpu_custom_call", output_to_operand_aliasing={{}: (3, {})} | custom-call | flops 122880 | bytes 860160 | tf_op jit(solution)/shard_map/finish/pallas_call | solution.py:540
  (2 shorter events, 0.0 us)
Async XLA Ops:
  1.9 13.5 %collective-permute-start = (bf16[1632,128]{1,0:T(8,128)(2,1)S(1)}, bf16[1632,128]{1,0:T(8,128)(2,1)S(1)}, u32[]{:S(2)}, u32[]{:S(2)}) collective-permute-start(bf16[1632,128]{1,0:T(8,128)(2,1)S(1)} %lead.1), channel_id=1, source_target_pairs={{0,16},{16,0},{1,17},{17,1},{2,18},{18,2},{3,19},{19,3},{4,20},{20... | collective-permute-start | bytes 1253384 | tf_op jit(solution)/shard_map/ppermute | solution.py:558
  5.0 14.1 %copy-start.1 = (bf16[1,384,64]{1,2,0:T(8,128)(2,1)S(1)}, bf16[1,384,64]{1,2,0:T(8,128)(2,1)}, u32[]{:S(2)}) copy-start(bf16[1,384,64]{1,2,0:T(8,128)(2,1)} %param.8) | copy-start | bytes 147460
  5.0 22.4 %copy-start = (bf16[640,64]{0,1:T(8,128)(2,1)S(1)}, bf16[640,64]{0,1:T(8,128)(2,1)}, u32[]{:S(2)}) copy-start(bf16[640,64]{0,1:T(8,128)(2,1)} %param.11) | copy-start | bytes 245764
  5.0 35.3 %copy-start.2 = (f32[32]{0:T(128)S(1)}, f32[32]{0:T(128)}, u32[]{:S(2)}) copy-start(f32[32]{0:T(128)} %param.13) | copy-start | bytes 388
  5.0 35.3 %copy-start.3 = (s32[32]{0:T(128)S(1)}, s32[32]{0:T(128)}, u32[]{:S(2)}) copy-start(s32[32]{0:T(128)} %param.14) | copy-start | bytes 388
  11.2 27.4 %collective-permute-start.7 = (bf16[2880,128]{1,0:T(8,128)(2,1)S(1)}, bf16[2880,128]{1,0:T(8,128)(2,1)S(1)}, u32[]{:S(2)}, u32[]{:S(2)}) collective-permute-start(bf16[2880,128]{1,0:T(8,128)(2,1)S(1)} %get-tuple-element.47), channel_id=1, source_target_pairs={{0,16},{16,0},{1,17},{17,1},{2,18},{18,2},{3,19},{19,3},{4,20},{20... | collective-permute-start | bytes 2211848 | tf_op jit(solution)/shard_map/ppermute | solution.py:558
  15.4 2.1 %collective-permute-start.3 = (bf16[3,64,640]{2,1,0:T(8,128)(2,1)S(1)}, bf16[3,64,640]{2,1,0:T(8,128)(2,1)S(1)}, u32[]{:S(2)}, u32[]{:S(2)}) collective-permute-start(bf16[3,64,640]{2,1,0:T(8,128)(2,1)S(1)} %get-tuple-element.39.a_ref), channel_id=1, source_target_pairs={{0,4},{4,0},{8,12},{12,8},{1,5},{5,1},{9,13},{13,9},{2,6},{6,2},{1... | collective-permute-start | bytes 737288 | tf_op jit(solution)/shard_map/ppermute | solution.py:75
  15.4 33.8 %collective-permute-start.10 = (bf16[2880,128]{1,0:T(8,128)(2,1)S(1)}, bf16[2880,128]{1,0:T(8,128)(2,1)S(1)}, u32[]{:S(2)}, u32[]{:S(2)}) collective-permute-start(bf16[2880,128]{1,0:T(8,128)(2,1)S(1)} %get-tuple-element.52), channel_id=1, source_target_pairs={{0,16},{16,0},{1,17},{17,1},{2,18},{18,2},{3,19},{19,3},{4,20},{20... | collective-permute-start | bytes 2211848 | tf_op jit(solution)/shard_map/ppermute | solution.py:558
  17.5 9.9 %collective-permute-start.4 = (bf16[3,64,640]{2,1,0:T(8,128)(2,1)S(1)}, bf16[3,64,640]{2,1,0:T(8,128)(2,1)S(1)}, u32[]{:S(2)}, u32[]{:S(2)}) collective-permute-start(bf16[3,64,640]{2,1,0:T(8,128)(2,1)S(1)} %add.5.refs_4_), channel_id=1, source_target_pairs={{0,8},{4,12},{8,0},{12,4},{1,9},{5,13},{9,1},{13,5},{2,10},{6,14},... | collective-permute-start | bytes 737288 | tf_op jit(solution)/shard_map/ppermute | solution.py:75
  19.7 3.3 %collective-permute-start.1 = (bf16[64,256]{1,0:T(8,128)(2,1)S(1)}, bf16[64,256]{1,0:T(8,128)(2,1)S(1)}, u32[]{:S(2)}, u32[]{:S(2)}) collective-permute-start(bf16[64,256]{1,0:T(8,128)(2,1)S(1)} %get-tuple-element.36), channel_id=1, source_target_pairs={{0,4},{4,8},{8,12},{1,5},{5,9},{9,13},{2,6},{6,10},{10,14},{3,7},{... | collective-permute-start | bytes 98312 | tf_op jit(solution)/shard_map/ppermute | solution.py:590
  21.6 36.0 %collective-permute-start.12 = (bf16[1920,128]{1,0:T(8,128)(2,1)S(1)}, bf16[1920,128]{1,0:T(8,128)(2,1)S(1)}, u32[]{:S(2)}, u32[]{:S(2)}) collective-permute-start(bf16[1920,128]{1,0:T(8,128)(2,1)S(1)} %get-tuple-element.56), channel_id=1, source_target_pairs={{0,16},{16,0},{1,17},{17,1},{2,18},{18,2},{3,19},{19,3},{4,20},{20... | collective-permute-start | bytes 1474568 | tf_op jit(solution)/shard_map/ppermute | solution.py:558
  23.0 4.4 %collective-permute-start.2 = (bf16[64,256]{1,0:T(8,128)(2,1)S(1)}, bf16[64,256]{1,0:T(8,128)(2,1)S(1)}, u32[]{:S(2)}, u32[]{:S(2)}) collective-permute-start(bf16[64,256]{1,0:T(8,128)(2,1)S(1)} %get-tuple-element.38), channel_id=1, source_target_pairs={{4,0},{8,4},{12,8},{5,1},{9,5},{13,9},{6,2},{10,6},{14,10},{7,3},{... | collective-permute-start | bytes 98312 | tf_op jit(solution)/shard_map/ppermute | solution.py:591
  31.1 4.2 %collective-permute-start.5 = (bf16[64,384]{1,0:T(8,128)(2,1)S(1)}, bf16[64,384]{1,0:T(8,128)(2,1)S(1)}, u32[]{:S(2)}, u32[]{:S(2)}) collective-permute-start(bf16[64,384]{1,0:T(8,128)(2,1)S(1)} %get-tuple-element.46.a_ref), channel_id=1, source_target_pairs={{0,1},{1,0},{2,3},{3,2},{4,5},{5,4},{6,7},{7,6},{8,9},{9,8},{10,11... | collective-permute-start | bytes 147464 | tf_op jit(solution)/shard_map/ppermute | solution.py:75
  35.2 5.1 %collective-permute-start.6 = (bf16[64,384]{1,0:T(8,128)(2,1)S(1)}, bf16[64,384]{1,0:T(8,128)(2,1)S(1)}, u32[]{:S(2)}, u32[]{:S(2)}) collective-permute-start(bf16[64,384]{1,0:T(8,128)(2,1)S(1)} %add.6.refs_11_), channel_id=1, source_target_pairs={{0,2},{1,3},{2,0},{3,1},{4,6},{5,7},{6,4},{7,5},{8,10},{9,11},{10,... | collective-permute-start | bytes 147464 | tf_op jit(solution)/shard_map/ppermute | solution.py:75
  43.2 2.6 %collective-permute-start.8 = (bf16[320,128]{1,0:T(8,128)(2,1)S(1)}, bf16[320,128]{1,0:T(8,128)(2,1)S(1)}, u32[]{:S(2)}, u32[]{:S(2)}) collective-permute-start(bf16[320,128]{1,0:T(8,128)(2,1)S(1)} %attend_grad.1.a_ref), channel_id=1, source_target_pairs={{0,4},{4,0},{8,12},{12,8},{1,5},{5,1},{9,13},{13,9},{2,6},{6,2},{1... | collective-permute-start | bytes 245768 | tf_op jit(solution)/shard_map/ppermute | solution.py:75
  45.8 4.8 %collective-permute-start.9 = (bf16[320,128]{1,0:T(8,128)(2,1)S(1)}, bf16[320,128]{1,0:T(8,128)(2,1)S(1)}, u32[]{:S(2)}, u32[]{:S(2)}) collective-permute-start(bf16[320,128]{1,0:T(8,128)(2,1)S(1)} %add.7.refs_4_), channel_id=1, source_target_pairs={{0,8},{4,12},{8,0},{12,4},{1,9},{5,13},{9,1},{13,5},{2,10},{6,14},... | collective-permute-start | bytes 245768 | tf_op jit(solution)/shard_map/ppermute | solution.py:75
  47.9 11.5 %collective-permute-start.11 = (bf16[480,128]{1,0:T(8,128)(2,1)S(1)}, bf16[480,128]{1,0:T(8,128)(2,1)S(1)}, u32[]{:S(2)}, u32[]{:S(2)}) collective-permute-start(bf16[480,128]{1,0:T(8,128)(2,1)S(1)} %get-tuple-element.55), channel_id=1, source_target_pairs={{0,16},{16,0},{1,17},{17,1},{2,18},{18,2},{3,19},{19,3},{4,20},{20... | collective-permute-start | bytes 368648 | tf_op jit(solution)/shard_map/ppermute | solution.py:558
